TPU v7x, 32 devices: a whole 2x2x4 slice. The times are simulated.
32 devices in a mesh: tm: 4 (over y, core), head: 2 (over x), branch: 4 (over z).
Axes of the slice: x: 2, y: 2, z: 4, core: 2. Of those that a mesh axis runs over, the one named last changes fastest.
Arguments:
- queries: bfloat16 [4, 4, 512, 20, 128], P('branch', 'tm', 'head'), may hold values from -8 to 8
- keys: bfloat16 [4, 4, 512, 20, 128], P('branch', 'tm', 'head'), may hold values from -5 to 5
- values: bfloat16 [4, 4, 512, 20, 128], P('branch', 'tm', 'head'), may hold values from -6 to 6
- ctx_keys: bfloat16 [4, 512, 20, 128], P('tm', ('head', 'branch')), may hold values from -5 to 5
- ctx_values: bfloat16 [4, 512, 20, 128], P('tm', ('head', 'branch')), may hold values from -6 to 6
- hidden: bfloat16 [4, 4, 512, 5120], P('branch', 'tm', 'head'), may hold values from -6 to 6
- out_weight: bfloat16 [2560, 5120], P('head'), may hold values from -0.5 to 0.5
- gates: float32 [16, 5120], replicated, may hold values from 0.5 to 2
- levels: int32 [4], replicated, may hold values from 0 to 15
- span_mask: int32 [4, 4], replicated, may hold values from 0 to 1, as said below
- prefix: int32 [1], replicated, may hold values from 1 to 3
Outputs:
- updated: bfloat16 [4, 4, 512, 5120], P('branch', 'tm', 'head')
Inputs may be any that keep to these rules, and one draw needn't show every extreme that they name: `span_mask`: 1 on the diagonal and in the first column, 0 above the diagonal.
All inputs are finite; a program needn't handle non-finite values.
Results may differ from a plain program's by a relative error of at most 0.01.
Values may be sent and summed in bfloat16 or wider, within the bound.
No kernel may reach another device: no remote copies, remote signals or barrier semaphores. Data moves between devices by JAX's collectives and lax.ppermute only.
A program may use at most 256 MiB of HBM per device.

v0:
```python
import functools
import math

import jax
import jax.numpy as jnp
from jax import lax
from jax.experimental import pallas as pl
from jax.experimental.pallas import tpu as pltpu
from jax.sharding import PartitionSpec as P

NEG_BIG = -1e30
LOG2E = 1.4426950408889634
COL_BLOCKS = 8
HEAD_STEP_SCORES = 3 << 20
VMEM_LIMIT = 22 << 20


def flash_kernel(flags, *refs, layout, scale, step, first, last):
    count = sum(len(members) for _, members in layout)
    q_ref, kv_refs, refs = refs[0], refs[1 : 1 + count], refs[1 + count :]
    if not first:
        (max_in, sum_in, acc_in), refs = refs[:3], refs[3:]
    outs, score_ref = refs[:-1], refs[-1]
    dim = q_ref.shape[2]
    order = [(flag, i) for flag, members in layout for i in members]
    for h in range(step):
        block = jnp.concatenate([kv_refs[i][0, h] for _, i in order], axis=0)
        raw = lax.dot_general(
            q_ref[h], block, (((1,), (1,)), ((), ())), preferred_element_type=jnp.float32
        )
        at, top = 0, None
        for flag, i in order:
            bias = jnp.where(flags[flag] > 0, 0.0, NEG_BIG)
            for _ in range(0, kv_refs[i].shape[2], dim):
                piece = raw[:, at : at + dim] + bias
                score_ref[h, :, at : at + dim] = piece
                top = piece if top is None else jnp.maximum(top, piece)
                at += dim
        top = jnp.broadcast_to(jnp.max(top, axis=1, keepdims=True) * scale, top.shape)
        total = acc = None
        if not first:
            old = max_in[h]
            top = jnp.maximum(top, old)
            shrink = jnp.exp2(old - top)
            total, acc = sum_in[h] * shrink, acc_in[h] * shrink
        weights = []
        for j in range(0, at, dim):
            piece = jnp.exp2(score_ref[h, :, j : j + dim] * scale - top)
            total = piece if total is None else total + piece
            weights.append(piece.astype(jnp.bfloat16))
        block = jnp.concatenate([kv_refs[i][1, h] for _, i in order], axis=0)
        added = jnp.dot(
            jnp.concatenate(weights, axis=1), block, preferred_element_type=jnp.float32
        )
        acc = added if acc is None else acc + added
        if last:
            total = jnp.sum(total, axis=1, keepdims=True)
            outs[0][:, h * dim : (h + 1) * dim] = (acc / total).astype(outs[0].dtype)
        else:
            outs[0][h], outs[1][h], outs[2][h] = top, total, acc


def attend(queries, spans, flags, state, last):
    heads, rows, dim = queries.shape
    arrays, layout = [], []
    for flag, members in spans:
        layout.append((flag, tuple(range(len(arrays), len(arrays) + len(members)))))
        arrays += members
    keys = sum(array.shape[2] for array in arrays)
    step = max(s for s in range(1, heads + 1) if heads % s == 0 and s * rows * keys <= HEAD_STEP_SCORES)
    by_head = pl.BlockSpec((step, rows, dim), lambda h, f: (h, 0, 0))
    states = [] if state is None else list(state)
    return pl.pallas_call(
        functools.partial(
            flash_kernel,
            layout=tuple(layout),
            scale=LOG2E / math.sqrt(dim),
            step=step,
            first=state is None,
            last=last,
        ),
        out_shape=jax.ShapeDtypeStruct((rows, heads * dim), jnp.bfloat16)
        if last
        else [jax.ShapeDtypeStruct((heads, rows, dim), jnp.float32)] * 3,
        grid_spec=pltpu.PrefetchScalarGridSpec(
            num_scalar_prefetch=1,
            grid=(heads // step,),
            in_specs=[by_head]
            + [
                pl.BlockSpec((2, step, array.shape[2], dim), lambda h, f: (0, h, 0, 0))
                for array in arrays
            ]
            + [by_head] * len(states),
            out_specs=pl.BlockSpec((rows, step * dim), lambda h, f: (0, h)) if last else [by_head] * 3,
            scratch_shapes=[pltpu.VMEM((step, rows, keys), jnp.float32)],
        ),
        cost_estimate=pl.CostEstimate(
            flops=4 * heads * rows * keys * dim,
            bytes_accessed=2 * heads * dim * (2 * rows + 2 * keys),
            transcendentals=heads * rows * keys,
        ),
        compiler_params=pltpu.CompilerParams(vmem_limit_bytes=VMEM_LIMIT),
    )(flags, queries, *arrays, *states)


def body(sizes, queries, keys, values, ctx_keys, ctx_values, hidden, out_weight, gates, levels, span_mask, prefix):
    return sublayer(
        sizes, queries[0, 0], keys[0, 0], values[0, 0], ctx_keys[0], ctx_values[0], hidden[0, 0],
        out_weight, gates, levels, span_mask, prefix,
    )[None, None]


def sublayer(sizes, queries, keys, values, ctx_keys, ctx_values, hidden, out_weight, gates, levels, span_mask, prefix):
    spans, splits, branches = sizes
    span = lax.axis_index("tm")
    part = lax.axis_index("head")
    branch = lax.axis_index("branch")
    to_heads = lambda a: jnp.transpose(a, (1, 0, 2))
    q, k, v = to_heads(queries), to_heads(keys), to_heads(values)
    ck, cv = to_heads(ctx_keys), to_heads(ctx_values)
    group = q.shape[0] // splits
    take = lambda a, d: lax.dynamic_slice_in_dim(a, lax.rem(part + d, splits) * group, group, 0)
    pair = lambda a, b, d: jnp.stack([take(a, d), take(b, d)])
    cycle = lambda d: [(i, (i + d) % splits) for i in range(splits)]

    swap_up = [(i, i + 1) for i in range(0, spans, 2)]
    swap = swap_up + [(i + 1, i) for i in range(0, spans, 2)]
    mask_row = lax.dynamic_index_in_dim(span_mask, span, 0, keepdims=False)
    ids = jnp.arange(spans, dtype=jnp.int32)
    seen = lambda s: jnp.sum(jnp.where((ids == s) & (ids <= span), mask_row, 0))
    partner = span + 1 - 2 * lax.rem(span, 2)
    flags = [jnp.int32(1), seen(partner)]
    for s in range(2, spans, 2):
        flags += [seen(span - s), seen(partner - s)]
    flags = jnp.stack(flags)
    level_now = lax.dynamic_index_in_dim(levels, span, 0, keepdims=False)
    gate_row = lax.dynamic_index_in_dim(gates, level_now, 0, keepdims=False)

    ctx_parts, kv_parts, q_parts = [pair(ck, cv, 0)], [pair(k, v, 0)], [take(q, 0)]
    for d in range(1, splits):
        ctx_parts.append(lax.ppermute(pair(ck, cv, d), "head", cycle(d)))
    for d in range(1, splits):
        kv_parts.append(lax.ppermute(pair(k, v, d), "head", cycle(d)))
    for d in range(1, splits):
        q_parts.append(lax.ppermute(take(q, d), "head", cycle(d)))

    use_context = span < prefix[0]
    first = jnp.concatenate(ctx_parts, axis=2)
    piece_rows, rows = first.shape[2], k.shape[1]
    up, down, own, held = [first], [first], [], []
    for s in range(branches):
        piece = first
        if s > 0:
            if s == 2:
                up[-1], flags, gate_row = lax.optimization_barrier((up[-1], flags, gate_row))
            up.append(lax.ppermute(up[-1], "branch", [(i, i + 1) for i in range(s - 1, branches - 1)]))
            down.append(lax.ppermute(down[-1], "branch", [(i, i - 1) for i in range(1, branches - s + 1)]))
            held[-1], piece = lax.optimization_barrier((own[-1], up[s]))
            for t in range(1, s + 1):
                piece = jnp.where(branch == s - t, down[t], piece)
        d, at = divmod(s * piece_rows, rows)
        own.append(jnp.where(use_context, piece, kv_parts[d][:, :, at : at + piece_rows]))
        held.append(own[-1])

    groups = [held, []]
    for _ in range(2, spans, 2):
        groups += [[], []]
    for array in own:
        for s in range(2, spans, 2):
            far = lax.ppermute(array, "tm", [(i, i + s) for i in range(spans - s)])
            groups[s].append(far)
            groups[s + 1].append(lax.ppermute(far, "tm", swap))
        groups[1].append(lax.ppermute(array, "tm", swap_up))

    half = max(1, len(own) // 2)
    early = [(i, arrays[:half]) for i, arrays in enumerate(groups)]
    late = [(i, arrays[half:]) for i, arrays in enumerate(groups)]
    states = []
    for d in range(splits):
        states.append(attend(q_parts[d], early, flags, None, False))

    columns = out_weight.shape[1]
    width = columns // COL_BLOCKS
    project = lambda a, w: jnp.dot(a, w, preferred_element_type=jnp.float32).astype(jnp.bfloat16)
    returned = [[] for _ in range(COL_BLOCKS)]
    for d in range(1, splits):
        attended = attend(q_parts[d], late, flags, states[d], True)
        back = [((i + d) % splits, i) for i in range(splits)]
        for j in range(COL_BLOCKS):
            partial = project(attended, out_weight[:, j * width : (j + 1) * width])
            returned[j].append(lax.ppermute(partial, "head", back))
    attended = attend(q_parts[0], late, flags, states[0], True)
    kept = lax.optimization_barrier(project(attended, out_weight))
    updated = hidden
    for j in range(COL_BLOCKS):
        cols = slice(j * width, (j + 1) * width)
        total = kept[:, cols].astype(jnp.float32)
        for a in returned[j]:
            total = total + a.astype(jnp.float32)
        fresh = updated[:, cols].astype(jnp.float32) + gate_row[None, cols] * total
        updated = lax.dynamic_update_slice_in_dim(updated, fresh.astype(jnp.bfloat16), j * width, 1)
    return updated


def solution(mesh):
    sizes = (mesh.shape["tm"], mesh.shape["head"], mesh.shape["branch"])
    return jax.shard_map(
        functools.partial(body, sizes),
        mesh=mesh,
        in_specs=(
            P("branch", "tm", "head", None, None),
            P("branch", "tm", "head", None, None),
            P("branch", "tm", "head", None, None),
            P("tm", ("head", "branch"), None, None),
            P("tm", ("head", "branch"), None, None),
            P("branch", "tm", "head", None),
            P("head", None),
            P(),
            P(),
            P(),
            P(),
        ),
        out_specs=P("branch", "tm", "head", None),
        check_vma=False,
    )
```

profile of v0, /device:TPU:0, one launch (start us, length us, event | category | flops | bytes accessed | tf_op | source)
XLA Modules:
  0.0 189.3 jit_solution(6894159879220543713)
XLA Ops:
  0.0 1.0 copy-done.7
  1.2 0.8 pad_maximum_fusion.3
  1.9 3.0 %collective-permute-start = (bf16[2,10,64,128]{3,2,1,0:T(8,128)(2,1)}, bf16[2,10,64,128]{3,2,1,0:T(8,128)(2,1)}, u32[]{:S(2)}, u32[]{:S(2)}) collective-permute-start(bf16[2,10,64,128]{3,2,1,0:T(8,128)(2,1)} %pad_maximum_fusion.3), channel_id=1, source_target_pairs={{0,4},{4,0},{1,5},{5,1},{2,6},{6,2},{3,7},{7,3},{8,12},{12,8},{9,1... | collective-permute-start | bytes 983048 | tf_op jit(solution)/shard_map/ppermute | solution.py:141
  4.9 1.5 dynamic-slice_bitcast_fusion.3
  6.4 1.2 pad_maximum_fusion
  7.6 0.6 collective-permute-start.5
  8.9 0.6 dynamic_slice.47
  11.4 2.4 %collective-permute-done = bf16[2,10,64,128]{3,2,1,0:T(8,128)(2,1)} collective-permute-done((bf16[2,10,64,128]{3,2,1,0:T(8,128)(2,1)}, bf16[2,10,64,128]{3,2,1,0:T(8,128)(2,1)}, u32[]{:S(2)}, u32[]{:S(2)}) %collective-permute-start) | collective-permute-done | bytes 327712 | tf_op jit(solution)/shard_map/ppermute | solution.py:141
  13.8 1.3 fusion.41
  15.1 4.1 %collective-permute-start.1 = (bf16[2,10,128,128]{3,2,1,0:T(8,128)(2,1)S(1)}, bf16[2,10,128,128]{3,2,1,0:T(8,128)(2,1)S(1)}, u32[]{:S(2)}, u32[]{:S(2)}) collective-permute-start(bf16[2,10,128,128]{3,2,1,0:T(8,128)(2,1)S(1)} %get-tuple-element.45), channel_id=1, source_target_pairs={{0,1},{1,2},{2,3},{4,5},{5,6},{6,7},{8,9},{9,10},{10,11},{12,13},{... | collective-permute-start | bytes 1966088 | tf_op jit(solution)/shard_map/ppermute | solution.py:156
  19.1 1.3 collective-permute-start.2
  20.5 1.4 fusion.55
  21.9 1.9 pad_add_fusion.flags
  23.7 7.3 %collective-permute-done.1 = bf16[2,10,128,128]{3,2,1,0:T(8,128)(2,1)S(1)} collective-permute-done((bf16[2,10,128,128]{3,2,1,0:T(8,128)(2,1)S(1)}, bf16[2,10,128,128]{3,2,1,0:T(8,128)(2,1)S(1)}, u32[]{:S(2)}, u32[]{:S(2)}) %collective-permute-start.1) | collective-permute-done | bytes 655392 | tf_op jit(solution)/shard_map/ppermute | solution.py:156
  31.1 1.5 collective-permute-start.4
  32.6 2.8 %collective-permute-done.2 = bf16[2,10,128,128]{3,2,1,0:T(8,128)(2,1)} collective-permute-done((bf16[2,10,128,128]{3,2,1,0:T(8,128)(2,1)S(1)}, bf16[2,10,128,128]{3,2,1,0:T(8,128)(2,1)}, u32[]{:S(2)}, u32[]{:S(2)}) %collective-permute-start.2) | collective-permute-done | bytes 655392 | tf_op jit(solution)/shard_map/ppermute | solution.py:157
  35.3 1.3 collective-permute-start.3
  36.6 3.5 %collective-permute-start.16 = (bf16[2,10,128,128]{3,2,1,0:T(8,128)(2,1)S(1)}, bf16[2,10,128,128]{3,2,1,0:T(8,128)(2,1)S(1)}, u32[]{:S(2)}, u32[]{:S(2)}) collective-permute-start(bf16[2,10,128,128]{3,2,1,0:T(8,128)(2,1)S(1)} %get-tuple-element.27.refs_1_), channel_id=1, source_target_pairs={{0,16},{8,24},{1,17},{9,25},{2,18},{10,26},{3,19},{11,27},{4,20},{... | collective-permute-start | bytes 1966088 | tf_op jit(solution)/shard_map/ppermute | solution.py:170
  40.1 1.5 collective-permute-start.6
  41.6 1.5 fusion.42.refs_2_
  43.1 1.3 collective-permute-start.17
  44.5 7.3 %collective-permute-done.3 = bf16[2,10,128,128]{3,2,1,0:T(8,128)(2,1)} collective-permute-done((bf16[2,10,128,128]{3,2,1,0:T(8,128)(2,1)}, bf16[2,10,128,128]{3,2,1,0:T(8,128)(2,1)}, u32[]{:S(2)}, u32[]{:S(2)}) %collective-permute-start.3) | collective-permute-done | bytes 655392 | tf_op jit(solution)/shard_map/ppermute | solution.py:157
  51.8 1.3 collective-permute-start.7
  53.1 2.2 %collective-permute-start.14 = (bf16[2,10,128,128]{3,2,1,0:T(8,128)(2,1)S(1)}, bf16[2,10,128,128]{3,2,1,0:T(8,128)(2,1)}, u32[]{:S(2)}, u32[]{:S(2)}) collective-permute-start(bf16[2,10,128,128]{3,2,1,0:T(8,128)(2,1)S(1)} %get-tuple-element.27.refs_1_), channel_id=1, source_target_pairs={{0,8},{16,24},{1,9},{17,25},{2,10},{18,26},{3,11},{19,27},{4,12},{... | collective-permute-start | bytes 1966088 | tf_op jit(solution)/shard_map/ppermute | solution.py:173
  55.3 1.6 slice_select_fusion.1.refs_1_
  56.9 1.5 collective-permute-start.15
  58.5 6.5 %collective-permute-done.17.refs_6_ = bf16[2,10,128,128]{3,2,1,0:T(8,128)(2,1)S(1)} collective-permute-done((bf16[2,10,128,128]{3,2,1,0:T(8,128)(2,1)S(1)}, bf16[2,10,128,128]{3,2,1,0:T(8,128)(2,1)S(1)}, u32[]{:S(2)}, u32[]{:S(2)}) %collective-permute-start.17) | collective-permute-done | bytes 655392 | tf_op jit(solution)/shard_map/ppermute | solution.py:170
  65.0 4.4 %collective-permute-start.10 = (bf16[2,10,128,128]{3,2,1,0:T(8,128)(2,1)S(1)}, bf16[2,10,128,128]{3,2,1,0:T(8,128)(2,1)S(1)}, u32[]{:S(2)}, u32[]{:S(2)}) collective-permute-start(bf16[2,10,128,128]{3,2,1,0:T(8,128)(2,1)S(1)} %slice_select_fusion.1.refs_1_), channel_id=1, source_target_pairs={{0,16},{8,24},{1,17},{9,25},{2,18},{10,26},{3,19},{11,27},{4,20},{... | collective-permute-start | bytes 1966088 | tf_op jit(solution)/shard_map/ppermute | solution.py:170
  69.5 1.6 slice_select_fusion.refs_2_
  71.1 1.3 collective-permute-start.11
  72.6 1.6 collective-permute-start.20
  74.2 2.1 %collective-permute-start.8 = (bf16[2,10,128,128]{3,2,1,0:T(8,128)(2,1)S(1)}, bf16[2,10,128,128]{3,2,1,0:T(8,128)(2,1)S(1)}, u32[]{:S(2)}, u32[]{:S(2)}) collective-permute-start(bf16[2,10,128,128]{3,2,1,0:T(8,128)(2,1)S(1)} %slice_select_fusion.1.refs_1_), channel_id=1, source_target_pairs={{0,8},{16,24},{1,9},{17,25},{2,10},{18,26},{3,11},{19,27},{4,12},{... | collective-permute-start | bytes 1966088 | tf_op jit(solution)/shard_map/ppermute | solution.py:173
  76.3 1.5 collective-permute-start.9
  77.9 6.6 %collective-permute-done.10.refs_5_ = bf16[2,10,128,128]{3,2,1,0:T(8,128)(2,1)S(1)} collective-permute-done((bf16[2,10,128,128]{3,2,1,0:T(8,128)(2,1)S(1)}, bf16[2,10,128,128]{3,2,1,0:T(8,128)(2,1)S(1)}, u32[]{:S(2)}, u32[]{:S(2)}) %collective-permute-start.10) | collective-permute-done | bytes 655392 | tf_op jit(solution)/shard_map/ppermute | solution.py:170
  84.4 9.0 %collective-permute-done.11.refs_6_ = bf16[2,10,128,128]{3,2,1,0:T(8,128)(2,1)S(1)} collective-permute-done((bf16[2,10,128,128]{3,2,1,0:T(8,128)(2,1)S(1)}, bf16[2,10,128,128]{3,2,1,0:T(8,128)(2,1)S(1)}, u32[]{:S(2)}, u32[]{:S(2)}) %collective-permute-start.11) | collective-permute-done | bytes 655392 | tf_op jit(solution)/shard_map/ppermute | solution.py:170
  93.5 6.8 %shard_map.109 = (f32[10,256,128]{2,1,0:T(8,128)S(1)}, f32[10,256,128]{2,1,0:T(8,128)S(1)}, f32[10,256,128]{2,1,0:T(8,128)S(1)}) custom-call(s32[4]{0:T(128)S(1)} %pad_add_fusion.flags, bf16[10,256,128]{2,1,0:T(8,128)(2,1)S(1)} %get-tuple-element.38.refs_0_, bf16[2,10,128,128]{3,2,1,0:T(8,128)(2,1)S(1)} %get-tuple-element.27.refs_1_, ...), custom_call_target="tpu_custom_call" | custom-call | flops 1342177280 | bytes 6553600 | tf_op jit(solution)/shard_map/pallas_call | solution.py:73
  100.3 6.8 %shard_map.111 = (f32[10,256,128]{2,1,0:T(8,128)S(1)}, f32[10,256,128]{2,1,0:T(8,128)S(1)}, f32[10,256,128]{2,1,0:T(8,128)S(1)}) custom-call(s32[4]{0:T(128)S(1)} %pad_add_fusion.flags, bf16[10,256,128]{2,1,0:T(8,128)(2,1)S(1)} %collective-permute-done.20.refs_0_, bf16[2,10,128,128]{3,2,1,0:T(8,128)(2,1)S(1)} %get-tuple-element.27.refs_1_, ...), custom_call_target="tpu_custom_call" | custom-call | flops 1342177280 | bytes 6553600 | tf_op jit(solution)/shard_map/pallas_call | solution.py:73
  107.2 6.2 %shard_map.112 = bf16[256,1280]{1,0:T(8,128)(2,1)S(1)} custom-call(s32[4]{0:T(128)S(1)} %pad_add_fusion.flags, bf16[10,256,128]{2,1,0:T(8,128)(2,1)S(1)} %collective-permute-done.20.refs_0_, bf16[2,10,128,128]{3,2,1,0:T(8,128)(2,1)S(1)} %slice_select_fusion.1.refs_1_, bf16[2,10,128,128]{3,2,1,0:T(8,128)(2,1)S(1)} %slice_select_fusion.refs_2_, ...), custom_call_target="tpu_custom_call" | custom-call | flops 1342177280 | bytes 6553600 | tf_op jit(solution)/shard_map/pallas_call | solution.py:73
  113.4 2.1 %fusion.16 = bf16[256,640]{1,0:T(8,128)(2,1)S(1)} fusion(bf16[256,1280]{1,0:T(8,128)(2,1)S(1)} %shard_map.112, bf16[1280,5120]{1,0:T(8,128)(2,1)} %param.17), kind=kOutput, calls=%fused_computation.20 | convolution fusion | flops 419594240 | bytes 2621440 | tf_op jit(solution)/shard_map/dot_general | solution.py:184
  115.6 0.7 fusion.19
  116.3 0.7 fusion.22
  117.0 0.7 fusion.25
  117.7 0.7 fusion.28
  118.4 0.7 fusion.31
  119.0 5.9 %shard_map.110 = bf16[256,1280]{1,0:T(8,128)(2,1)S(1)} custom-call(s32[4]{0:T(128)S(1)} %pad_add_fusion.flags, bf16[10,256,128]{2,1,0:T(8,128)(2,1)S(1)} %get-tuple-element.38.refs_0_, bf16[2,10,128,128]{3,2,1,0:T(8,128)(2,1)S(1)} %slice_select_fusion.1.refs_1_, bf16[2,10,128,128]{3,2,1,0:T(8,128)(2,1)S(1)} %slice_select_fusion.refs_2_, ...), custom_call_target="tpu_custom_call" | custom-call | flops 1342177280 | bytes 6553600 | tf_op jit(solution)/shard_map/pallas_call | solution.py:73
  125.0 4.1 %convolution_convert_fusion = bf16[256,5120]{1,0:T(8,128)(2,1)S(1)} fusion(bf16[256,1280]{1,0:T(8,128)(2,1)S(1)} %shard_map.110, bf16[1280,5120]{1,0:T(8,128)(2,1)S(1)} %bitcast.91), kind=kOutput, calls=%fused_computation | convolution fusion | flops 3356753920 | bytes 16384000 | tf_op jit(solution)/shard_map/dot_general | solution.py:184
  129.1 1.6 collective-permute-start.21
  130.7 0.7 fusion.34
  132.0 0.7 fusion.37
  132.6 1.6 collective-permute-start.23
  134.7 1.5 collective-permute-start.25
  136.2 3.5 %collective-permute-done.21 = bf16[256,640]{1,0:T(8,128)(2,1)S(1)} collective-permute-done((bf16[256,640]{1,0:T(8,128)(2,1)S(1)}, bf16[256,640]{1,0:T(8,128)(2,1)S(1)}, u32[]{:S(2)}, u32[]{:S(2)}) %collective-permute-start.21) | collective-permute-done | bytes 327712 | tf_op jit(solution)/shard_map/ppermute | solution.py:191
  139.8 1.5 collective-permute-start.26
  141.6 5.2 %collective-permute-done.22 = bf16[256,640]{1,0:T(8,128)(2,1)S(1)} collective-permute-done((bf16[256,640]{1,0:T(8,128)(2,1)S(1)}, bf16[256,640]{1,0:T(8,128)(2,1)S(1)}, u32[]{:S(2)}, u32[]{:S(2)}) %collective-permute-start.22) | collective-permute-done | bytes 327712 | tf_op jit(solution)/shard_map/ppermute | solution.py:191
  146.8 1.5 collective-permute-start.27
  148.6 5.2 %collective-permute-done.23 = bf16[256,640]{1,0:T(8,128)(2,1)S(1)} collective-permute-done((bf16[256,640]{1,0:T(8,128)(2,1)S(1)}, bf16[256,640]{1,0:T(8,128)(2,1)S(1)}, u32[]{:S(2)}, u32[]{:S(2)}) %collective-permute-start.23) | collective-permute-done | bytes 327712 | tf_op jit(solution)/shard_map/ppermute | solution.py:191
  153.8 1.5 collective-permute-start.28
  155.6 5.2 %collective-permute-done.24 = bf16[256,640]{1,0:T(8,128)(2,1)S(1)} collective-permute-done((bf16[256,640]{1,0:T(8,128)(2,1)S(1)}, bf16[256,640]{1,0:T(8,128)(2,1)S(1)}, u32[]{:S(2)}, u32[]{:S(2)}) %collective-permute-start.24) | collective-permute-done | bytes 327712 | tf_op jit(solution)/shard_map/ppermute | solution.py:191
  161.1 6.7 %collective-permute-done.25 = bf16[256,640]{1,0:T(8,128)(2,1)S(1)} collective-permute-done((bf16[256,640]{1,0:T(8,128)(2,1)S(1)}, bf16[256,640]{1,0:T(8,128)(2,1)S(1)}, u32[]{:S(2)}, u32[]{:S(2)}) %collective-permute-start.25) | collective-permute-done | bytes 327712 | tf_op jit(solution)/shard_map/ppermute | solution.py:191
  168.1 6.7 %collective-permute-done.26 = bf16[256,640]{1,0:T(8,128)(2,1)S(1)} collective-permute-done((bf16[256,640]{1,0:T(8,128)(2,1)S(1)}, bf16[256,640]{1,0:T(8,128)(2,1)S(1)}, u32[]{:S(2)}, u32[]{:S(2)}) %collective-permute-start.26) | collective-permute-done | bytes 327712 | tf_op jit(solution)/shard_map/ppermute | solution.py:191
  175.2 6.7 %collective-permute-done.27 = bf16[256,640]{1,0:T(8,128)(2,1)S(1)} collective-permute-done((bf16[256,640]{1,0:T(8,128)(2,1)S(1)}, bf16[256,640]{1,0:T(8,128)(2,1)S(1)}, u32[]{:S(2)}, u32[]{:S(2)}) %collective-permute-start.27) | collective-permute-done | bytes 327712 | tf_op jit(solution)/shard_map/ppermute | solution.py:191
  182.2 1.5 copy.19
  183.7 4.7 %collective-permute-done.28 = bf16[256,640]{1,0:T(8,128)(2,1)S(1)} collective-permute-done((bf16[256,640]{1,0:T(8,128)(2,1)S(1)}, bf16[256,640]{1,0:T(8,128)(2,1)S(1)}, u32[]{:S(2)}, u32[]{:S(2)}) %collective-permute-start.28) | collective-permute-done | bytes 327712 | tf_op jit(solution)/shard_map/ppermute | solution.py:191
  188.4 0.9 fusion.51
  (57 shorter events, 3.8 us)
Async XLA Ops:
  0.0 20.4 %copy-start = (f32[16,5120]{1,0:T(8,128)S(1)}, f32[16,5120]{1,0:T(8,128)}, u32[]{:S(2)}) copy-start(f32[16,5120]{1,0:T(8,128)} %param.18) | copy-start | bytes 983044
  0.0 1.0 copy-start.7
  0.0 1.1 copy-start.6
  1.1 3.8 %copy-start.4 = (bf16[1,1,256,20,128]{4,2,3,1,0:T(8,128)(2,1)S(1)}, bf16[1,1,256,20,128]{4,2,3,1,0:T(8,128)(2,1)}, u32[]{:S(2)}) copy-start(bf16[1,1,256,20,128]{4,2,3,1,0:T(8,128)(2,1)} %param.13) | copy-start | bytes 3932164
  1.9 11.8 %collective-permute-start = (bf16[2,10,64,128]{3,2,1,0:T(8,128)(2,1)}, bf16[2,10,64,128]{3,2,1,0:T(8,128)(2,1)}, u32[]{:S(2)}, u32[]{:S(2)}) collective-permute-start(bf16[2,10,64,128]{3,2,1,0:T(8,128)(2,1)} %pad_maximum_fusion.3), channel_id=1, source_target_pairs={{0,4},{4,0},{1,5},{5,1},{2,6},{6,2},{3,7},{7,3},{8,12},{12,8},{9,1... | collective-permute-start | bytes 983048 | tf_op jit(solution)/shard_map/ppermute | solution.py:141
  6.4 8.7 %copy-start.2 = (bf16[1,10,256,128]{3,2,1,0:T(8,128)(2,1)}, bf16[1,10,256,128]{3,2,1,0:T(8,128)(2,1)S(1)}, u32[]{:S(2)}) copy-start(bf16[1,10,256,128]{3,2,1,0:T(8,128)(2,1)S(1)} %get-tuple-element.59) | copy-start | bytes 1966084
  6.4 2.5 %copy-start.8 = (s32[4]{0:T(128)S(1)}, s32[4]{0:T(128)}, u32[]{:S(2)}) copy-start(s32[4]{0:T(128)} %param.19) | copy-start | bytes 52
  7.6 45.5 %collective-permute-start.5 = (bf16[2,10,256,128]{3,2,1,0:T(8,128)(2,1)}, bf16[2,10,256,128]{3,2,1,0:T(8,128)(2,1)}, u32[]{:S(2)}, u32[]{:S(2)}) collective-permute-start(bf16[2,10,256,128]{3,2,1,0:T(8,128)(2,1)} %pad_maximum_fusion), channel_id=1, source_target_pairs={{0,4},{4,0},{1,5},{5,1},{2,6},{6,2},{3,7},{7,3},{8,12},{12,8},{9,1... | collective-permute-start | bytes 3932168 | tf_op jit(solution)/shard_map/ppermute | solution.py:143
  15.1 16.0 %collective-permute-start.1 = (bf16[2,10,128,128]{3,2,1,0:T(8,128)(2,1)S(1)}, bf16[2,10,128,128]{3,2,1,0:T(8,128)(2,1)S(1)}, u32[]{:S(2)}, u32[]{:S(2)}) collective-permute-start(bf16[2,10,128,128]{3,2,1,0:T(8,128)(2,1)S(1)} %get-tuple-element.45), channel_id=1, source_target_pairs={{0,1},{1,2},{2,3},{4,5},{5,6},{6,7},{8,9},{9,10},{10,11},{12,13},{... | collective-permute-start | bytes 1966088 | tf_op jit(solution)/shard_map/ppermute | solution.py:156
  19.1 16.2 %collective-permute-start.2 = (bf16[2,10,128,128]{3,2,1,0:T(8,128)(2,1)S(1)}, bf16[2,10,128,128]{3,2,1,0:T(8,128)(2,1)}, u32[]{:S(2)}, u32[]{:S(2)}) collective-permute-start(bf16[2,10,128,128]{3,2,1,0:T(8,128)(2,1)S(1)} %get-tuple-element.45), channel_id=1, source_target_pairs={{1,0},{2,1},{3,2},{5,4},{6,5},{7,6},{9,8},{10,9},{11,10},{13,12},{... | collective-permute-start | bytes 1966088 | tf_op jit(solution)/shard_map/ppermute | solution.py:157
  31.1 9.0 %copy-start.5 = (bf16[2,10,128,128]{3,2,1,0:T(8,128)(2,1)}, bf16[2,10,128,128]{3,2,1,0:T(8,128)(2,1)S(1)}, u32[]{:S(2)}) copy-start(bf16[2,10,128,128]{3,2,1,0:T(8,128)(2,1)S(1)} %collective-permute-done.1) | copy-start | bytes 1966084
  31.1 9.0 %collective-permute-start.4 = (bf16[2,10,128,128]{3,2,1,0:T(8,128)(2,1)S(1)}, bf16[2,10,128,128]{3,2,1,0:T(8,128)(2,1)}, u32[]{:S(2)}, u32[]{:S(2)}) collective-permute-start(bf16[2,10,128,128]{3,2,1,0:T(8,128)(2,1)S(1)} %collective-permute-done.1), channel_id=1, source_target_pairs={{1,2},{2,3},{5,6},{6,7},{9,10},{10,11},{13,14},{14,15},{17,18},{18... | collective-permute-start | bytes 1966088 | tf_op jit(solution)/shard_map/ppermute | solution.py:156
  35.3 16.5 %collective-permute-start.3 = (bf16[2,10,128,128]{3,2,1,0:T(8,128)(2,1)}, bf16[2,10,128,128]{3,2,1,0:T(8,128)(2,1)}, u32[]{:S(2)}, u32[]{:S(2)}) collective-permute-start(bf16[2,10,128,128]{3,2,1,0:T(8,128)(2,1)} %collective-permute-done.2), channel_id=1, source_target_pairs={{1,0},{2,1},{5,4},{6,5},{9,8},{10,9},{13,12},{14,13},{17,16},{18,1... | collective-permute-start | bytes 1966088 | tf_op jit(solution)/shard_map/ppermute | solution.py:157
  36.6 20.3 %collective-permute-start.16 = (bf16[2,10,128,128]{3,2,1,0:T(8,128)(2,1)S(1)}, bf16[2,10,128,128]{3,2,1,0:T(8,128)(2,1)S(1)}, u32[]{:S(2)}, u32[]{:S(2)}) collective-permute-start(bf16[2,10,128,128]{3,2,1,0:T(8,128)(2,1)S(1)} %get-tuple-element.27.refs_1_), channel_id=1, source_target_pairs={{0,16},{8,24},{1,17},{9,25},{2,18},{10,26},{3,19},{11,27},{4,20},{... | collective-permute-start | bytes 1966088 | tf_op jit(solution)/shard_map/ppermute | solution.py:170
  40.1 18.3 %collective-permute-start.6 = (bf16[2,10,128,128]{3,2,1,0:T(8,128)(2,1)}, bf16[2,10,128,128]{3,2,1,0:T(8,128)(2,1)}, u32[]{:S(2)}, u32[]{:S(2)}) collective-permute-start(bf16[2,10,128,128]{3,2,1,0:T(8,128)(2,1)} %collective-permute-done.4), channel_id=1, source_target_pairs={{2,3},{6,7},{10,11},{14,15},{18,19},{22,23},{26,27},{30,31}} | collective-permute-start | bytes 1966088 | tf_op jit(solution)/shard_map/ppermute | solution.py:156
  43.1 21.8 %collective-permute-start.17 = (bf16[2,10,128,128]{3,2,1,0:T(8,128)(2,1)S(1)}, bf16[2,10,128,128]{3,2,1,0:T(8,128)(2,1)S(1)}, u32[]{:S(2)}, u32[]{:S(2)}) collective-permute-start(bf16[2,10,128,128]{3,2,1,0:T(8,128)(2,1)S(1)} %fusion.42.refs_2_), channel_id=1, source_target_pairs={{0,16},{8,24},{1,17},{9,25},{2,18},{10,26},{3,19},{11,27},{4,20},{... | collective-permute-start | bytes 1966088 | tf_op jit(solution)/shard_map/ppermute | solution.py:170
  51.8 17.6 %collective-permute-start.7 = (bf16[2,10,128,128]{3,2,1,0:T(8,128)(2,1)}, bf16[2,10,128,128]{3,2,1,0:T(8,128)(2,1)}, u32[]{:S(2)}, u32[]{:S(2)}) collective-permute-start(bf16[2,10,128,128]{3,2,1,0:T(8,128)(2,1)} %collective-permute-done.3), channel_id=1, source_target_pairs={{1,0},{5,4},{9,8},{13,12},{17,16},{21,20},{25,24},{29,28}} | collective-permute-start | bytes 1966088 | tf_op jit(solution)/shard_map/ppermute | solution.py:157
  53.1 18.0 %collective-permute-start.14 = (bf16[2,10,128,128]{3,2,1,0:T(8,128)(2,1)S(1)}, bf16[2,10,128,128]{3,2,1,0:T(8,128)(2,1)}, u32[]{:S(2)}, u32[]{:S(2)}) collective-permute-start(bf16[2,10,128,128]{3,2,1,0:T(8,128)(2,1)S(1)} %get-tuple-element.27.refs_1_), channel_id=1, source_target_pairs={{0,8},{16,24},{1,9},{17,25},{2,10},{18,26},{3,11},{19,27},{4,12},{... | collective-permute-start | bytes 1966088 | tf_op jit(solution)/shard_map/ppermute | solution.py:173
  56.9 15.6 %copy-start.3 = (bf16[1,1,256,20,128]{4,2,3,1,0:T(8,128)(2,1)S(1)}, bf16[1,1,256,20,128]{4,2,3,1,0:T(8,128)(2,1)}, u32[]{:S(2)}) copy-start(bf16[1,1,256,20,128]{4,2,3,1,0:T(8,128)(2,1)} %param.11) | copy-start | bytes 3932164
  56.9 15.7 %collective-permute-start.15 = (bf16[2,10,128,128]{3,2,1,0:T(8,128)(2,1)S(1)}, bf16[2,10,128,128]{3,2,1,0:T(8,128)(2,1)S(1)}, u32[]{:S(2)}, u32[]{:S(2)}) collective-permute-start(bf16[2,10,128,128]{3,2,1,0:T(8,128)(2,1)S(1)} %fusion.42.refs_2_), channel_id=1, source_target_pairs={{0,8},{16,24},{1,9},{17,25},{2,10},{18,26},{3,11},{19,27},{4,12},{... | collective-permute-start | bytes 1966088 | tf_op jit(solution)/shard_map/ppermute | solution.py:173
  58.4 15.8 %collective-permute-start.18 = (bf16[2,10,128,128]{3,2,1,0:T(8,128)(2,1)S(1)}, bf16[2,10,128,128]{3,2,1,0:T(8,128)(2,1)S(1)}, u32[]{:S(2)}, u32[]{:S(2)}) collective-permute-start(bf16[2,10,128,128]{3,2,1,0:T(8,128)(2,1)S(1)} %collective-permute-done.16.refs_5_), channel_id=1, source_target_pairs={{0,8},{16,24},{8,0},{24,16},{1,9},{17,25},{9,1},{25,17},{2,10},{18... | collective-permute-start | bytes 1966088 | tf_op jit(solution)/shard_map/ppermute | solution.py:172
  65.0 19.5 %collective-permute-start.10 = (bf16[2,10,128,128]{3,2,1,0:T(8,128)(2,1)S(1)}, bf16[2,10,128,128]{3,2,1,0:T(8,128)(2,1)S(1)}, u32[]{:S(2)}, u32[]{:S(2)}) collective-permute-start(bf16[2,10,128,128]{3,2,1,0:T(8,128)(2,1)S(1)} %slice_select_fusion.1.refs_1_), channel_id=1, source_target_pairs={{0,16},{8,24},{1,17},{9,25},{2,18},{10,26},{3,19},{11,27},{4,20},{... | collective-permute-start | bytes 1966088 | tf_op jit(solution)/shard_map/ppermute | solution.py:170
  69.4 6.9 %collective-permute-start.19 = (bf16[2,10,128,128]{3,2,1,0:T(8,128)(2,1)S(1)}, bf16[2,10,128,128]{3,2,1,0:T(8,128)(2,1)S(1)}, u32[]{:S(2)}, u32[]{:S(2)}) collective-permute-start(bf16[2,10,128,128]{3,2,1,0:T(8,128)(2,1)S(1)} %collective-permute-done.17.refs_6_), channel_id=1, source_target_pairs={{0,8},{16,24},{8,0},{24,16},{1,9},{17,25},{9,1},{25,17},{2,10},{18... | collective-permute-start | bytes 1966088 | tf_op jit(solution)/shard_map/ppermute | solution.py:172
  71.1 22.4 %collective-permute-start.11 = (bf16[2,10,128,128]{3,2,1,0:T(8,128)(2,1)S(1)}, bf16[2,10,128,128]{3,2,1,0:T(8,128)(2,1)S(1)}, u32[]{:S(2)}, u32[]{:S(2)}) collective-permute-start(bf16[2,10,128,128]{3,2,1,0:T(8,128)(2,1)S(1)} %slice_select_fusion.refs_2_), channel_id=1, source_target_pairs={{0,16},{8,24},{1,17},{9,25},{2,18},{10,26},{3,19},{11,27},{4,20},{... | collective-permute-start | bytes 1966088 | tf_op jit(solution)/shard_map/ppermute | solution.py:170
  72.5 43.0 %slice-start = ((s8[13107200]{0:T(1024)(128)(4,1)}), s8[4194304]{0:T(1024)(128)(4,1)S(1)}, s32[]{:S(2)}) async-start(s8[13107200]{0:T(1024)(128)(4,1)} %bitcast.90), calls=%async_computation | async-start | bytes 8388608
  72.6 27.7 %collective-permute-start.20 = (bf16[10,256,128]{2,1,0:T(8,128)(2,1)S(1)}, bf16[10,256,128]{2,1,0:T(8,128)(2,1)S(1)}, u32[]{:S(2)}, u32[]{:S(2)}) collective-permute-start(bf16[10,256,128]{2,1,0:T(8,128)(2,1)S(1)} %get-tuple-element.39), channel_id=1, source_target_pairs={{0,4},{4,0},{1,5},{5,1},{2,6},{6,2},{3,7},{7,3},{8,12},{12,8},{9,1... | collective-permute-start | bytes 1966088 | tf_op jit(solution)/shard_map/ppermute | solution.py:145
  74.2 33.0 %collective-permute-start.8 = (bf16[2,10,128,128]{3,2,1,0:T(8,128)(2,1)S(1)}, bf16[2,10,128,128]{3,2,1,0:T(8,128)(2,1)S(1)}, u32[]{:S(2)}, u32[]{:S(2)}) collective-permute-start(bf16[2,10,128,128]{3,2,1,0:T(8,128)(2,1)S(1)} %slice_select_fusion.1.refs_1_), channel_id=1, source_target_pairs={{0,8},{16,24},{1,9},{17,25},{2,10},{18,26},{3,11},{19,27},{4,12},{... | collective-permute-start | bytes 1966088 | tf_op jit(solution)/shard_map/ppermute | solution.py:173
  76.3 30.8 %collective-permute-start.9 = (bf16[2,10,128,128]{3,2,1,0:T(8,128)(2,1)S(1)}, bf16[2,10,128,128]{3,2,1,0:T(8,128)(2,1)S(1)}, u32[]{:S(2)}, u32[]{:S(2)}) collective-permute-start(bf16[2,10,128,128]{3,2,1,0:T(8,128)(2,1)S(1)} %slice_select_fusion.refs_2_), channel_id=1, source_target_pairs={{0,8},{16,24},{1,9},{17,25},{2,10},{18,26},{3,11},{19,27},{4,12},{... | collective-permute-start | bytes 1966088 | tf_op jit(solution)/shard_map/ppermute | solution.py:173
  84.4 22.7 %collective-permute-start.12 = (bf16[2,10,128,128]{3,2,1,0:T(8,128)(2,1)S(1)}, bf16[2,10,128,128]{3,2,1,0:T(8,128)(2,1)S(1)}, u32[]{:S(2)}, u32[]{:S(2)}) collective-permute-start(bf16[2,10,128,128]{3,2,1,0:T(8,128)(2,1)S(1)} %collective-permute-done.10.refs_5_), channel_id=1, source_target_pairs={{0,8},{16,24},{8,0},{24,16},{1,9},{17,25},{9,1},{25,17},{2,10},{18... | collective-permute-start | bytes 1966088 | tf_op jit(solution)/shard_map/ppermute | solution.py:172
  93.5 13.7 %collective-permute-start.13 = (bf16[2,10,128,128]{3,2,1,0:T(8,128)(2,1)S(1)}, bf16[2,10,128,128]{3,2,1,0:T(8,128)(2,1)S(1)}, u32[]{:S(2)}, u32[]{:S(2)}) collective-permute-start(bf16[2,10,128,128]{3,2,1,0:T(8,128)(2,1)S(1)} %collective-permute-done.11.refs_6_), channel_id=1, source_target_pairs={{0,8},{16,24},{8,0},{24,16},{1,9},{17,25},{9,1},{25,17},{2,10},{18... | collective-permute-start | bytes 1966088 | tf_op jit(solution)/shard_map/ppermute | solution.py:172
  93.5 22.0 %slice-start.1 = ((s8[13107200]{0:T(1024)(128)(4,1)}), s8[4194304]{0:T(1024)(128)(4,1)S(1)}, s32[]{:S(2)}) async-start(s8[13107200]{0:T(1024)(128)(4,1)} %bitcast.90), calls=%async_computation.1 | async-start | bytes 8388608
  100.3 15.2 %slice-start.2 = ((s8[13107200]{0:T(1024)(128)(4,1)}), s8[4194304]{0:T(1024)(128)(4,1)S(1)}, s32[]{:S(2)}) async-start(s8[13107200]{0:T(1024)(128)(4,1)} %bitcast.90), calls=%async_computation.2 | async-start | bytes 8388608
  107.2 8.3 %slice-start.3 = ((s8[13107200]{0:T(1024)(128)(4,1)}), s8[524288]{0:T(1024)(128)(4,1)S(1)}, s32[]{:S(2)}) async-start(s8[13107200]{0:T(1024)(128)(4,1)} %bitcast.90), calls=%async_computation.3 | async-start | bytes 1048576
  129.1 12.2 %copy-start.1 = (bf16[1,1,256,5120]{3,2,1,0:T(8,128)(2,1)S(1)}, bf16[1,1,256,5120]{3,2,1,0:T(8,128)(2,1)}, u32[]{:S(2)}) copy-start(bf16[1,1,256,5120]{3,2,1,0:T(8,128)(2,1)} %param.16) | copy-start | bytes 7864324
  129.1 10.6 %collective-permute-start.21 = (bf16[256,640]{1,0:T(8,128)(2,1)S(1)}, bf16[256,640]{1,0:T(8,128)(2,1)S(1)}, u32[]{:S(2)}, u32[]{:S(2)}) collective-permute-start(bf16[256,640]{1,0:T(8,128)(2,1)S(1)} %fusion.16), channel_id=1, source_target_pairs={{4,0},{0,4},{5,1},{1,5},{6,2},{2,6},{7,3},{3,7},{12,8},{8,12},{13,... | collective-permute-start | bytes 983048 | tf_op jit(solution)/shard_map/ppermute | solution.py:191
  131.4 15.4 %collective-permute-start.22 = (bf16[256,640]{1,0:T(8,128)(2,1)S(1)}, bf16[256,640]{1,0:T(8,128)(2,1)S(1)}, u32[]{:S(2)}, u32[]{:S(2)}) collective-permute-start(bf16[256,640]{1,0:T(8,128)(2,1)S(1)} %fusion.19), channel_id=1, source_target_pairs={{4,0},{0,4},{5,1},{1,5},{6,2},{2,6},{7,3},{3,7},{12,8},{8,12},{13,... | collective-permute-start | bytes 983048 | tf_op jit(solution)/shard_map/ppermute | solution.py:191
  132.6 21.2 %collective-permute-start.23 = (bf16[256,640]{1,0:T(8,128)(2,1)S(1)}, bf16[256,640]{1,0:T(8,128)(2,1)S(1)}, u32[]{:S(2)}, u32[]{:S(2)}) collective-permute-start(bf16[256,640]{1,0:T(8,128)(2,1)S(1)} %fusion.22), channel_id=1, source_target_pairs={{4,0},{0,4},{5,1},{1,5},{6,2},{2,6},{7,3},{3,7},{12,8},{8,12},{13,... | collective-permute-start | bytes 983048 | tf_op jit(solution)/shard_map/ppermute | solution.py:191
  134.2 26.6 %collective-permute-start.24 = (bf16[256,640]{1,0:T(8,128)(2,1)S(1)}, bf16[256,640]{1,0:T(8,128)(2,1)S(1)}, u32[]{:S(2)}, u32[]{:S(2)}) collective-permute-start(bf16[256,640]{1,0:T(8,128)(2,1)S(1)} %fusion.25), channel_id=1, source_target_pairs={{4,0},{0,4},{5,1},{1,5},{6,2},{2,6},{7,3},{3,7},{12,8},{8,12},{13,... | collective-permute-start | bytes 983048 | tf_op jit(solution)/shard_map/ppermute | solution.py:191
  134.7 33.1 %collective-permute-start.25 = (bf16[256,640]{1,0:T(8,128)(2,1)S(1)}, bf16[256,640]{1,0:T(8,128)(2,1)S(1)}, u32[]{:S(2)}, u32[]{:S(2)}) collective-permute-start(bf16[256,640]{1,0:T(8,128)(2,1)S(1)} %fusion.28), channel_id=1, source_target_pairs={{4,0},{0,4},{5,1},{1,5},{6,2},{2,6},{7,3},{3,7},{12,8},{8,12},{13,... | collective-permute-start | bytes 983048 | tf_op jit(solution)/shard_map/ppermute | solution.py:191
  139.8 35.1 %collective-permute-start.26 = (bf16[256,640]{1,0:T(8,128)(2,1)S(1)}, bf16[256,640]{1,0:T(8,128)(2,1)S(1)}, u32[]{:S(2)}, u32[]{:S(2)}) collective-permute-start(bf16[256,640]{1,0:T(8,128)(2,1)S(1)} %fusion.31), channel_id=1, source_target_pairs={{4,0},{0,4},{5,1},{1,5},{6,2},{2,6},{7,3},{3,7},{12,8},{8,12},{13,... | collective-permute-start | bytes 983048 | tf_op jit(solution)/shard_map/ppermute | solution.py:191
  146.8 35.1 %collective-permute-start.27 = (bf16[256,640]{1,0:T(8,128)(2,1)S(1)}, bf16[256,640]{1,0:T(8,128)(2,1)S(1)}, u32[]{:S(2)}, u32[]{:S(2)}) collective-permute-start(bf16[256,640]{1,0:T(8,128)(2,1)S(1)} %fusion.34), channel_id=1, source_target_pairs={{4,0},{0,4},{5,1},{1,5},{6,2},{2,6},{7,3},{3,7},{12,8},{8,12},{13,... | collective-permute-start | bytes 983048 | tf_op jit(solution)/shard_map/ppermute | solution.py:191
  153.8 34.6 %collective-permute-start.28 = (bf16[256,640]{1,0:T(8,128)(2,1)S(1)}, bf16[256,640]{1,0:T(8,128)(2,1)S(1)}, u32[]{:S(2)}, u32[]{:S(2)}) collective-permute-start(bf16[256,640]{1,0:T(8,128)(2,1)S(1)} %fusion.37), channel_id=1, source_target_pairs={{4,0},{0,4},{5,1},{1,5},{6,2},{2,6},{7,3},{3,7},{12,8},{8,12},{13,... | collective-permute-start | bytes 983048 | tf_op jit(solution)/shard_map/ppermute | solution.py:191
where the time goes:
time: 192 us; the launch traced here: 189 us
  waiting for transfers between devices  86.1 us (45%)
  starting transfers between devices  44.2 us (23%)
  Pallas kernels  25.7 us (13%)
  other arithmetic  14.2 us (7%)
  matrix products  11.1 us (6%)
  local copies, waits for them, and re-layouts  4.94 us (3%)
  between operations  3.04 us (2%)
    ppermute x8, waiting for transfers between devices, sublayer(): returned[j].append(lax.ppermute(partial, 'head', back))  44.1 us
    pallas_call x4, Pallas kernels, attend(): pl.pallas_call(functools.partial(flash_kernel, layout=tuple(layout), scal...  25.7 us
    ppermute x4, waiting for transfers between devices, sublayer(): far = lax.ppermute(array, 'tm', [(i, i + s) for i in range(spans - s)])  22.1 us
    dot_general x9, matrix products, sublayer(): jnp.dot(a, w, preferred_element_type=jnp.float32).astype(jnp.bfloat16)  11.1 us
    ppermute x4, starting transfers between devices, sublayer(): far = lax.ppermute(array, 'tm', [(i, i + s) for i in range(spans - s)])  10.5 us
    ppermute x8, starting transfers between devices, sublayer(): returned[j].append(lax.ppermute(partial, 'head', back))  10.2 us
    ppermute x3, waiting for transfers between devices, sublayer(): lax.ppermute(down[-1], 'branch', [(i, i - 1) for i in range(1, branches -...  10.1 us
    ppermute x3, waiting for transfers between devices, sublayer(): lax.ppermute(up[-1], 'branch', [(i, i + 1) for i in range(s - 1, branches...  7.35 us
  transfers between devices with their start and end apart: 29, of which 15 were waited for; matrix products, arithmetic and copies ran while one was open for 9% of the time, Pallas kernels for 7%

commit v1 on v0

--- a/solution.py
+++ b/solution.py
@@ -10,7 +10,7 @@
 
 NEG_BIG = -1e30
 LOG2E = 1.4426950408889634
-COL_BLOCKS = 8
+COL_BLOCKS = 5
 HEAD_STEP_SCORES = 3 << 20
 VMEM_LIMIT = 22 << 20
 
@@ -145,21 +145,30 @@
         q_parts.append(lax.ppermute(take(q, d), "head", cycle(d)))
 
     use_context = span < prefix[0]
-    first = jnp.concatenate(ctx_parts, axis=2)
-    piece_rows, rows = first.shape[2], k.shape[1]
-    up, down, own, held = [first], [first], [], []
+    up, down = [[a] for a in ctx_parts], [[a] for a in ctx_parts]
+    piece_rows, rows = splits * ctx_parts[0].shape[2], k.shape[1]
+    own, held = [], []
     for s in range(branches):
-        piece = first
+        pieces = []
+        for d in range(splits):
+            piece = ctx_parts[d]
+            if s > 0:
+                if s == branches - 1 and d == 0:
+                    up[0][-1], flags, gate_row = lax.optimization_barrier((up[0][-1], flags, gate_row))
+                rise = [(i, i + 1) for i in range(s - 1, branches - 1)]
+                fall = [(i, i - 1) for i in range(1, branches - s + 1)]
+                up[d].append(lax.ppermute(up[d][-1], "branch", rise))
+                down[d].append(lax.ppermute(down[d][-1], "branch", fall))
+                piece = up[d][s]
+            pieces.append(piece)
         if s > 0:
-            if s == 2:
-                up[-1], flags, gate_row = lax.optimization_barrier((up[-1], flags, gate_row))
-            up.append(lax.ppermute(up[-1], "branch", [(i, i + 1) for i in range(s - 1, branches - 1)]))
-            down.append(lax.ppermute(down[-1], "branch", [(i, i - 1) for i in range(1, branches - s + 1)]))
-            held[-1], piece = lax.optimization_barrier((own[-1], up[s]))
-            for t in range(1, s + 1):
-                piece = jnp.where(branch == s - t, down[t], piece)
+            held[-1], *pieces = lax.optimization_barrier((own[-1], *pieces))
+            for d in range(splits):
+                for t in range(1, s + 1):
+                    pieces[d] = jnp.where(branch == s - t, down[d][t], pieces[d])
         d, at = divmod(s * piece_rows, rows)
-        own.append(jnp.where(use_context, piece, kv_parts[d][:, :, at : at + piece_rows]))
+        context = jnp.concatenate(pieces, axis=2)
+        own.append(jnp.where(use_context, context, kv_parts[d][:, :, at : at + piece_rows]))
         held.append(own[-1])
 
     groups = [held, []]

time: 192 us -> 206 us (1.073)
  the two profiles are of different devices: /device:TPU:0 before, /device:TPU:30 now
where the time goes in v1:
time: 206 us; the launch traced here: 205 us
  waiting for transfers between devices  113 us (55%)
  starting transfers between devices  38.9 us (19%)
  Pallas kernels  22.9 us (11%)
  other arithmetic  13.1 us (6%)
  matrix products  8.34 us (4%)
  local copies, waits for them, and re-layouts  5.36 us (3%)
  between operations  3.18 us (2%)
    ppermute x5, waiting for transfers between devices, sublayer(): returned[j].append(lax.ppermute(partial, 'head', back))  50.1 us
    ppermute x4, waiting for transfers between devices, sublayer(): far = lax.ppermute(array, 'tm', [(i, i + s) for i in range(spans - s)])  39.8 us
    ppermute x6, waiting for transfers between devices, sublayer(): up[d].append(lax.ppermute(up[d][-1], 'branch', rise))  23.4 us
    pallas_call x4, Pallas kernels, attend(): pl.pallas_call(functools.partial(flash_kernel, layout=tuple(layout), scal...  22.9 us
    ppermute x6, starting transfers between devices, sublayer(): down[d].append(lax.ppermute(down[d][-1], 'branch', fall))  11.9 us
    dot_general x6, matrix products, sublayer(): jnp.dot(a, w, preferred_element_type=jnp.float32).astype(jnp.bfloat16)  8.34 us
    ppermute x6, starting transfers between devices, sublayer(): up[d].append(lax.ppermute(up[d][-1], 'branch', rise))  7.73 us
    ppermute x4, starting transfers between devices, sublayer(): groups[1].append(lax.ppermute(array, 'tm', swap_up))  6.31 us
  transfers between devices with their start and end apart: 32, of which 12 were waited for; matrix products, arithmetic and copies ran while one was open for 9% of the time, Pallas kernels for 5%

profile of v1, /device:TPU:30, one launch (start us, length us, event | category | flops | bytes accessed | tf_op | source)
XLA Modules:
  0.0 205.2 jit_solution(2994587683329486589)
XLA Ops:
  0.0 1.0 copy-done.5
  1.2 0.6 collective-permute-start.4
  1.8 0.8 pad_maximum_fusion.2
  2.6 1.3 collective-permute-start
  3.9 4.6 %collective-permute-start.2 = (bf16[2,10,64,128]{3,2,1,0:T(8,128)(2,1)}, bf16[2,10,64,128]{3,2,1,0:T(8,128)(2,1)S(1)}, u32[]{:S(2)}, u32[]{:S(2)}) collective-permute-start(bf16[2,10,64,128]{3,2,1,0:T(8,128)(2,1)} %pad_maximum_fusion.2), channel_id=1, source_target_pairs={{1,0},{2,1},{3,2},{5,4},{6,5},{7,6},{9,8},{10,9},{11,10},{13,12},{... | collective-permute-start | bytes 983048 | tf_op jit(solution)/shard_map/ppermute | solution.py:161
  8.4 1.9 dynamic-slice_bitcast_fusion.3
  10.3 1.2 pad_maximum_fusion
  11.5 1.5 collective-permute-start.9
  13.0 0.6 dynamic_slice.45
  15.5 1.3 collective-permute-start.5
  16.8 4.6 %collective-permute-start.6 = (bf16[2,10,64,128]{3,2,1,0:T(8,128)(2,1)}, bf16[2,10,64,128]{3,2,1,0:T(8,128)(2,1)S(1)}, u32[]{:S(2)}, u32[]{:S(2)}) collective-permute-start(bf16[2,10,64,128]{3,2,1,0:T(8,128)(2,1)} %collective-permute-done.4), channel_id=1, source_target_pairs={{1,0},{2,1},{3,2},{5,4},{6,5},{7,6},{9,8},{10,9},{11,10},{13,12},{... | collective-permute-start | bytes 983048 | tf_op jit(solution)/shard_map/ppermute | solution.py:161
  21.4 1.3 collective-permute-start.1
  22.8 1.4 fusion.37
  24.2 1.9 pad_add_fusion.flags
  26.8 0.7 collective-permute-start.3
  27.4 1.2 fusion.26.refs_1_
  28.6 4.5 %collective-permute-done.1 = bf16[2,10,64,128]{3,2,1,0:T(8,128)(2,1)} collective-permute-done((bf16[2,10,64,128]{3,2,1,0:T(8,128)(2,1)S(1)}, bf16[2,10,64,128]{3,2,1,0:T(8,128)(2,1)}, u32[]{:S(2)}, u32[]{:S(2)}) %collective-permute-start.1) | collective-permute-done | bytes 327712 | tf_op jit(solution)/shard_map/ppermute | solution.py:160
  33.1 1.3 collective-permute-start.10
  34.4 1.3 collective-permute-start.7
  35.7 0.7 collective-permute-start.8
  36.7 13.4 %collective-permute-done.7 = bf16[2,10,64,128]{3,2,1,0:T(8,128)(2,1)S(1)} collective-permute-done((bf16[2,10,64,128]{3,2,1,0:T(8,128)(2,1)S(1)}, bf16[2,10,64,128]{3,2,1,0:T(8,128)(2,1)S(1)}, u32[]{:S(2)}, u32[]{:S(2)}) %collective-permute-start.7) | collective-permute-done | bytes 327712 | tf_op jit(solution)/shard_map/ppermute | solution.py:160
  50.0 1.3 collective-permute-start.22
  51.3 1.3 collective-permute-start.23
  52.6 1.1 select_select_fusion.3
  53.7 0.7 collective-permute-start.12
  54.4 1.3 collective-permute-start.11
  55.8 0.7 collective-permute-start.13
  56.5 1.3 slice_select_fusion.1.refs_1_
  57.8 5.6 %collective-permute-done.11 = bf16[2,10,64,128]{3,2,1,0:T(8,128)(2,1)S(1)} collective-permute-done((bf16[2,10,64,128]{3,2,1,0:T(8,128)(2,1)S(1)}, bf16[2,10,64,128]{3,2,1,0:T(8,128)(2,1)S(1)}, u32[]{:S(2)}, u32[]{:S(2)}) %collective-permute-start.11) | collective-permute-done | bytes 327712 | tf_op jit(solution)/shard_map/ppermute | solution.py:160
  63.4 1.3 collective-permute-start.20
  64.7 4.8 %collective-permute-done.22.refs_5_ = bf16[2,10,128,128]{3,2,1,0:T(8,128)(2,1)S(1)} collective-permute-done((bf16[2,10,128,128]{3,2,1,0:T(8,128)(2,1)S(1)}, bf16[2,10,128,128]{3,2,1,0:T(8,128)(2,1)S(1)}, u32[]{:S(2)}, u32[]{:S(2)}) %collective-permute-start.22) | collective-permute-done | bytes 655392 | tf_op jit(solution)/shard_map/ppermute | solution.py:179
  69.5 1.3 collective-permute-start.21
  70.9 9.0 %collective-permute-done.23.refs_6_ = bf16[2,10,128,128]{3,2,1,0:T(8,128)(2,1)S(1)} collective-permute-done((bf16[2,10,128,128]{3,2,1,0:T(8,128)(2,1)S(1)}, bf16[2,10,128,128]{3,2,1,0:T(8,128)(2,1)S(1)}, u32[]{:S(2)}, u32[]{:S(2)}) %collective-permute-start.23) | collective-permute-done | bytes 655392 | tf_op jit(solution)/shard_map/ppermute | solution.py:179
  80.2 1.4 slice_select_fusion.refs_2_
  81.6 1.6 collective-permute-start.17
  83.2 1.3 collective-permute-start.16
  84.7 0.6 collective-permute-start.26
  85.3 2.2 %collective-permute-start.15 = (bf16[2,10,128,128]{3,2,1,0:T(8,128)(2,1)S(1)}, bf16[2,10,128,128]{3,2,1,0:T(8,128)(2,1)S(1)}, u32[]{:S(2)}, u32[]{:S(2)}) collective-permute-start(bf16[2,10,128,128]{3,2,1,0:T(8,128)(2,1)S(1)} %slice_select_fusion.refs_2_), channel_id=1, source_target_pairs={{0,8},{16,24},{1,9},{17,25},{2,10},{18,26},{3,11},{19,27},{4,12},{... | collective-permute-start | bytes 1966088 | tf_op jit(solution)/shard_map/ppermute | solution.py:182
  87.5 1.5 collective-permute-start.14
  89.0 12.4 %collective-permute-done.17.refs_6_ = bf16[2,10,128,128]{3,2,1,0:T(8,128)(2,1)S(1)} collective-permute-done((bf16[2,10,128,128]{3,2,1,0:T(8,128)(2,1)S(1)}, bf16[2,10,128,128]{3,2,1,0:T(8,128)(2,1)S(1)}, u32[]{:S(2)}, u32[]{:S(2)}) %collective-permute-start.17) | collective-permute-done | bytes 655392 | tf_op jit(solution)/shard_map/ppermute | solution.py:179
  101.4 13.6 %collective-permute-done.16.refs_5_ = bf16[2,10,128,128]{3,2,1,0:T(8,128)(2,1)S(1)} collective-permute-done((bf16[2,10,128,128]{3,2,1,0:T(8,128)(2,1)S(1)}, bf16[2,10,128,128]{3,2,1,0:T(8,128)(2,1)S(1)}, u32[]{:S(2)}, u32[]{:S(2)}) %collective-permute-start.16) | collective-permute-done | bytes 655392 | tf_op jit(solution)/shard_map/ppermute | solution.py:179
  115.0 5.4 %shard_map.109 = (f32[10,256,128]{2,1,0:T(8,128)S(1)}, f32[10,256,128]{2,1,0:T(8,128)S(1)}, f32[10,256,128]{2,1,0:T(8,128)S(1)}) custom-call(s32[4]{0:T(128)S(1)} %pad_add_fusion.flags, bf16[10,256,128]{2,1,0:T(8,128)(2,1)S(1)} %get-tuple-element.44.refs_0_, bf16[2,10,128,128]{3,2,1,0:T(8,128)(2,1)S(1)} %fusion.26.refs_1_, ...), custom_call_target="tpu_custom_call" | custom-call | flops 1342177280 | bytes 6553600 | tf_op jit(solution)/shard_map/pallas_call | solution.py:73
  120.5 5.4 %shard_map.111 = (f32[10,256,128]{2,1,0:T(8,128)S(1)}, f32[10,256,128]{2,1,0:T(8,128)S(1)}, f32[10,256,128]{2,1,0:T(8,128)S(1)}) custom-call(s32[4]{0:T(128)S(1)} %pad_add_fusion.flags, bf16[10,256,128]{2,1,0:T(8,128)(2,1)S(1)} %collective-permute-done.26.refs_0_, bf16[2,10,128,128]{3,2,1,0:T(8,128)(2,1)S(1)} %fusion.26.refs_1_, ...), custom_call_target="tpu_custom_call" | custom-call | flops 1342177280 | bytes 6553600 | tf_op jit(solution)/shard_map/pallas_call | solution.py:73
  126.0 6.1 %shard_map.112 = bf16[256,1280]{1,0:T(8,128)(2,1)S(1)} custom-call(s32[4]{0:T(128)S(1)} %pad_add_fusion.flags, bf16[10,256,128]{2,1,0:T(8,128)(2,1)S(1)} %collective-permute-done.26.refs_0_, bf16[2,10,128,128]{3,2,1,0:T(8,128)(2,1)S(1)} %slice_select_fusion.1.refs_1_, bf16[2,10,128,128]{3,2,1,0:T(8,128)(2,1)S(1)} %slice_select_fusion.refs_2_, ...), custom_call_target="tpu_custom_call" | custom-call | flops 1342177280 | bytes 6553600 | tf_op jit(solution)/shard_map/pallas_call | solution.py:73
  132.2 0.8 fusion.10
  133.0 0.8 fusion.13
  133.9 0.8 fusion.16
  134.7 5.9 %shard_map.110 = bf16[256,1280]{1,0:T(8,128)(2,1)S(1)} custom-call(s32[4]{0:T(128)S(1)} %pad_add_fusion.flags, bf16[10,256,128]{2,1,0:T(8,128)(2,1)S(1)} %get-tuple-element.44.refs_0_, bf16[2,10,128,128]{3,2,1,0:T(8,128)(2,1)S(1)} %slice_select_fusion.1.refs_1_, bf16[2,10,128,128]{3,2,1,0:T(8,128)(2,1)S(1)} %slice_select_fusion.refs_2_, ...), custom_call_target="tpu_custom_call" | custom-call | flops 1342177280 | bytes 6553600 | tf_op jit(solution)/shard_map/pallas_call | solution.py:73
  140.6 4.1 %convolution_convert_fusion = bf16[256,5120]{1,0:T(8,128)(2,1)S(1)} fusion(bf16[256,1280]{1,0:T(8,128)(2,1)S(1)} %shard_map.110, bf16[1280,5120]{1,0:T(8,128)(2,1)S(1)} %bitcast.88), kind=kOutput, calls=%fused_computation | convolution fusion | flops 3356753920 | bytes 16384000 | tf_op jit(solution)/shard_map/dot_general | solution.py:193
  144.8 0.6 collective-permute-start.27
  145.4 1.5 collective-permute-start.28
  146.9 0.5 collective-permute-start.29
  147.4 0.8 fusion.19
  148.3 1.6 collective-permute-start.30
  149.8 0.8 fusion.22
  150.7 0.6 collective-permute-start.31
  151.3 8.4 %collective-permute-done.27 = bf16[256,1024]{1,0:T(8,128)(2,1)S(1)} collective-permute-done((bf16[256,1024]{1,0:T(8,128)(2,1)S(1)}, bf16[256,1024]{1,0:T(8,128)(2,1)S(1)}, u32[]{:S(2)}, u32[]{:S(2)}) %collective-permute-start.27) | collective-permute-done | bytes 524320 | tf_op jit(solution)/shard_map/ppermute | solution.py:200
  159.9 10.9 %collective-permute-done.28 = bf16[256,1024]{1,0:T(8,128)(2,1)S(1)} collective-permute-done((bf16[256,1024]{1,0:T(8,128)(2,1)S(1)}, bf16[256,1024]{1,0:T(8,128)(2,1)S(1)}, u32[]{:S(2)}, u32[]{:S(2)}) %collective-permute-start.28) | collective-permute-done | bytes 524320 | tf_op jit(solution)/shard_map/ppermute | solution.py:200
  170.9 0.3 fusion.29
  171.2 10.9 %collective-permute-done.29 = bf16[256,1024]{1,0:T(8,128)(2,1)S(1)} collective-permute-done((bf16[256,1024]{1,0:T(8,128)(2,1)S(1)}, bf16[256,1024]{1,0:T(8,128)(2,1)S(1)}, u32[]{:S(2)}, u32[]{:S(2)}) %collective-permute-start.29) | collective-permute-done | bytes 524320 | tf_op jit(solution)/shard_map/ppermute | solution.py:200
  182.4 10.9 %collective-permute-done.30 = bf16[256,1024]{1,0:T(8,128)(2,1)S(1)} collective-permute-done((bf16[256,1024]{1,0:T(8,128)(2,1)S(1)}, bf16[256,1024]{1,0:T(8,128)(2,1)S(1)}, u32[]{:S(2)}, u32[]{:S(2)}) %collective-permute-start.30) | collective-permute-done | bytes 524320 | tf_op jit(solution)/shard_map/ppermute | solution.py:200
  193.7 1.5 copy.16
  195.2 9.0 %collective-permute-done.31 = bf16[256,1024]{1,0:T(8,128)(2,1)S(1)} collective-permute-done((bf16[256,1024]{1,0:T(8,128)(2,1)S(1)}, bf16[256,1024]{1,0:T(8,128)(2,1)S(1)}, u32[]{:S(2)}, u32[]{:S(2)}) %collective-permute-start.31) | collective-permute-done | bytes 524320 | tf_op jit(solution)/shard_map/ppermute | solution.py:200
  204.1 1.1 fusion.33
  (60 shorter events, 2.0 us)
Async XLA Ops:
  0.0 22.7 %copy-start = (f32[16,5120]{1,0:T(8,128)S(1)}, f32[16,5120]{1,0:T(8,128)}, u32[]{:S(2)}) copy-start(f32[16,5120]{1,0:T(8,128)} %param.18) | copy-start | bytes 983044
  0.0 1.0 copy-start.5
  0.0 1.1 copy-start.4
  1.2 14.3 %collective-permute-start.4 = (bf16[2,10,64,128]{3,2,1,0:T(8,128)(2,1)S(1)}, bf16[2,10,64,128]{3,2,1,0:T(8,128)(2,1)}, u32[]{:S(2)}, u32[]{:S(2)}) collective-permute-start(bf16[2,10,64,128]{3,2,1,0:T(8,128)(2,1)S(1)} %pad_maximum_fusion.3), channel_id=1, source_target_pairs={{0,4},{4,0},{1,5},{5,1},{2,6},{6,2},{3,7},{7,3},{8,12},{12,8},{9,1... | collective-permute-start | bytes 983048 | tf_op jit(solution)/shard_map/ppermute | solution.py:141
  2.6 18.9 %collective-permute-start = (bf16[2,10,64,128]{3,2,1,0:T(8,128)(2,1)}, bf16[2,10,64,128]{3,2,1,0:T(8,128)(2,1)S(1)}, u32[]{:S(2)}, u32[]{:S(2)}) collective-permute-start(bf16[2,10,64,128]{3,2,1,0:T(8,128)(2,1)} %pad_maximum_fusion.2), channel_id=1, source_target_pairs={{0,1},{1,2},{2,3},{4,5},{5,6},{6,7},{8,9},{9,10},{10,11},{12,13},{... | collective-permute-start | bytes 983048 | tf_op jit(solution)/shard_map/ppermute | solution.py:160
  3.9 22.9 %collective-permute-start.2 = (bf16[2,10,64,128]{3,2,1,0:T(8,128)(2,1)}, bf16[2,10,64,128]{3,2,1,0:T(8,128)(2,1)S(1)}, u32[]{:S(2)}, u32[]{:S(2)}) collective-permute-start(bf16[2,10,64,128]{3,2,1,0:T(8,128)(2,1)} %pad_maximum_fusion.2), channel_id=1, source_target_pairs={{1,0},{2,1},{3,2},{5,4},{6,5},{7,6},{9,8},{10,9},{11,10},{13,12},{... | collective-permute-start | bytes 983048 | tf_op jit(solution)/shard_map/ppermute | solution.py:161
  10.3 2.7 %copy-start.6 = (s32[4]{0:T(128)S(1)}, s32[4]{0:T(128)}, u32[]{:S(2)}) copy-start(s32[4]{0:T(128)} %param.19) | copy-start | bytes 52
  11.5 44.3 %collective-permute-start.9 = (bf16[2,10,256,128]{3,2,1,0:T(8,128)(2,1)}, bf16[2,10,256,128]{3,2,1,0:T(8,128)(2,1)}, u32[]{:S(2)}, u32[]{:S(2)}) collective-permute-start(bf16[2,10,256,128]{3,2,1,0:T(8,128)(2,1)} %pad_maximum_fusion), channel_id=1, source_target_pairs={{0,4},{4,0},{1,5},{5,1},{2,6},{6,2},{3,7},{7,3},{8,12},{12,8},{9,1... | collective-permute-start | bytes 3932168 | tf_op jit(solution)/shard_map/ppermute | solution.py:143
  15.5 13.1 %collective-permute-start.5 = (bf16[2,10,64,128]{3,2,1,0:T(8,128)(2,1)}, bf16[2,10,64,128]{3,2,1,0:T(8,128)(2,1)S(1)}, u32[]{:S(2)}, u32[]{:S(2)}) collective-permute-start(bf16[2,10,64,128]{3,2,1,0:T(8,128)(2,1)} %collective-permute-done.4), channel_id=1, source_target_pairs={{0,1},{1,2},{2,3},{4,5},{5,6},{6,7},{8,9},{9,10},{10,11},{12,13},{... | collective-permute-start | bytes 983048 | tf_op jit(solution)/shard_map/ppermute | solution.py:160
  16.8 18.9 %collective-permute-start.6 = (bf16[2,10,64,128]{3,2,1,0:T(8,128)(2,1)}, bf16[2,10,64,128]{3,2,1,0:T(8,128)(2,1)S(1)}, u32[]{:S(2)}, u32[]{:S(2)}) collective-permute-start(bf16[2,10,64,128]{3,2,1,0:T(8,128)(2,1)} %collective-permute-done.4), channel_id=1, source_target_pairs={{1,0},{2,1},{3,2},{5,4},{6,5},{7,6},{9,8},{10,9},{11,10},{13,12},{... | collective-permute-start | bytes 983048 | tf_op jit(solution)/shard_map/ppermute | solution.py:161
  21.4 11.7 %collective-permute-start.1 = (bf16[2,10,64,128]{3,2,1,0:T(8,128)(2,1)S(1)}, bf16[2,10,64,128]{3,2,1,0:T(8,128)(2,1)}, u32[]{:S(2)}, u32[]{:S(2)}) collective-permute-start(bf16[2,10,64,128]{3,2,1,0:T(8,128)(2,1)S(1)} %collective-permute-done), channel_id=1, source_target_pairs={{1,2},{2,3},{5,6},{6,7},{9,10},{10,11},{13,14},{14,15},{17,18},{18... | collective-permute-start | bytes 983048 | tf_op jit(solution)/shard_map/ppermute | solution.py:160
  26.8 24.6 %collective-permute-start.3 = (bf16[2,10,64,128]{3,2,1,0:T(8,128)(2,1)S(1)}, bf16[2,10,64,128]{3,2,1,0:T(8,128)(2,1)S(1)}, u32[]{:S(2)}, u32[]{:S(2)}) collective-permute-start(bf16[2,10,64,128]{3,2,1,0:T(8,128)(2,1)S(1)} %collective-permute-done.2), channel_id=1, source_target_pairs={{1,0},{2,1},{5,4},{6,5},{9,8},{10,9},{13,12},{14,13},{17,16},{18,1... | collective-permute-start | bytes 983048 | tf_op jit(solution)/shard_map/ppermute | solution.py:161
  33.1 21.3 %collective-permute-start.10 = (bf16[2,10,64,128]{3,2,1,0:T(8,128)(2,1)}, bf16[2,10,64,128]{3,2,1,0:T(8,128)(2,1)S(1)}, u32[]{:S(2)}, u32[]{:S(2)}) collective-permute-start(bf16[2,10,64,128]{3,2,1,0:T(8,128)(2,1)} %collective-permute-done.1), channel_id=1, source_target_pairs={{2,3},{6,7},{10,11},{14,15},{18,19},{22,23},{26,27},{30,31}} | collective-permute-start | bytes 983048 | tf_op jit(solution)/shard_map/ppermute | solution.py:160
  34.4 15.6 %collective-permute-start.7 = (bf16[2,10,64,128]{3,2,1,0:T(8,128)(2,1)S(1)}, bf16[2,10,64,128]{3,2,1,0:T(8,128)(2,1)S(1)}, u32[]{:S(2)}, u32[]{:S(2)}) collective-permute-start(bf16[2,10,64,128]{3,2,1,0:T(8,128)(2,1)S(1)} %collective-permute-done.5), channel_id=1, source_target_pairs={{1,2},{2,3},{5,6},{6,7},{9,10},{10,11},{13,14},{14,15},{17,18},{18... | collective-permute-start | bytes 983048 | tf_op jit(solution)/shard_map/ppermute | solution.py:160
  35.7 18.0 %collective-permute-start.8 = (bf16[2,10,64,128]{3,2,1,0:T(8,128)(2,1)S(1)}, bf16[2,10,64,128]{3,2,1,0:T(8,128)(2,1)S(1)}, u32[]{:S(2)}, u32[]{:S(2)}) collective-permute-start(bf16[2,10,64,128]{3,2,1,0:T(8,128)(2,1)S(1)} %collective-permute-done.6), channel_id=1, source_target_pairs={{1,0},{2,1},{5,4},{6,5},{9,8},{10,9},{13,12},{14,13},{17,16},{18,1... | collective-permute-start | bytes 983048 | tf_op jit(solution)/shard_map/ppermute | solution.py:161
  50.0 19.5 %collective-permute-start.22 = (bf16[2,10,128,128]{3,2,1,0:T(8,128)(2,1)S(1)}, bf16[2,10,128,128]{3,2,1,0:T(8,128)(2,1)S(1)}, u32[]{:S(2)}, u32[]{:S(2)}) collective-permute-start(bf16[2,10,128,128]{3,2,1,0:T(8,128)(2,1)S(1)} %fusion.26.refs_1_), channel_id=1, source_target_pairs={{0,16},{8,24},{1,17},{9,25},{2,18},{10,26},{3,19},{11,27},{4,20},{... | collective-permute-start | bytes 1966088 | tf_op jit(solution)/shard_map/ppermute | solution.py:179
  51.3 28.6 %collective-permute-start.23 = (bf16[2,10,128,128]{3,2,1,0:T(8,128)(2,1)S(1)}, bf16[2,10,128,128]{3,2,1,0:T(8,128)(2,1)S(1)}, u32[]{:S(2)}, u32[]{:S(2)}) collective-permute-start(bf16[2,10,128,128]{3,2,1,0:T(8,128)(2,1)S(1)} %fusion.27.refs_2_), channel_id=1, source_target_pairs={{0,16},{8,24},{1,17},{9,25},{2,18},{10,26},{3,19},{11,27},{4,20},{... | collective-permute-start | bytes 1966088 | tf_op jit(solution)/shard_map/ppermute | solution.py:179
  53.7 17.1 %collective-permute-start.12 = (bf16[2,10,64,128]{3,2,1,0:T(8,128)(2,1)S(1)}, bf16[2,10,64,128]{3,2,1,0:T(8,128)(2,1)S(1)}, u32[]{:S(2)}, u32[]{:S(2)}) collective-permute-start(bf16[2,10,64,128]{3,2,1,0:T(8,128)(2,1)S(1)} %collective-permute-done.3), channel_id=1, source_target_pairs={{1,0},{5,4},{9,8},{13,12},{17,16},{21,20},{25,24},{29,28}} | collective-permute-start | bytes 983048 | tf_op jit(solution)/shard_map/ppermute | solution.py:161
  54.4 9.0 %collective-permute-start.11 = (bf16[2,10,64,128]{3,2,1,0:T(8,128)(2,1)S(1)}, bf16[2,10,64,128]{3,2,1,0:T(8,128)(2,1)S(1)}, u32[]{:S(2)}, u32[]{:S(2)}) collective-permute-start(bf16[2,10,64,128]{3,2,1,0:T(8,128)(2,1)S(1)} %collective-permute-done.7), channel_id=1, source_target_pairs={{2,3},{6,7},{10,11},{14,15},{18,19},{22,23},{26,27},{30,31}} | collective-permute-start | bytes 983048 | tf_op jit(solution)/shard_map/ppermute | solution.py:160
  55.8 24.3 %collective-permute-start.13 = (bf16[2,10,64,128]{3,2,1,0:T(8,128)(2,1)S(1)}, bf16[2,10,64,128]{3,2,1,0:T(8,128)(2,1)S(1)}, u32[]{:S(2)}, u32[]{:S(2)}) collective-permute-start(bf16[2,10,64,128]{3,2,1,0:T(8,128)(2,1)S(1)} %collective-permute-done.8), channel_id=1, source_target_pairs={{1,0},{5,4},{9,8},{13,12},{17,16},{21,20},{25,24},{29,28}} | collective-permute-start | bytes 983048 | tf_op jit(solution)/shard_map/ppermute | solution.py:161
  57.8 26.7 %copy-start.3 = (bf16[1,1,256,20,128]{4,2,3,1,0:T(8,128)(2,1)S(1)}, bf16[1,1,256,20,128]{4,2,3,1,0:T(8,128)(2,1)}, u32[]{:S(2)}) copy-start(bf16[1,1,256,20,128]{4,2,3,1,0:T(8,128)(2,1)} %param.11) | copy-start | bytes 3932164
  63.4 19.8 %collective-permute-start.20 = (bf16[2,10,128,128]{3,2,1,0:T(8,128)(2,1)S(1)}, bf16[2,10,128,128]{3,2,1,0:T(8,128)(2,1)S(1)}, u32[]{:S(2)}, u32[]{:S(2)}) collective-permute-start(bf16[2,10,128,128]{3,2,1,0:T(8,128)(2,1)S(1)} %fusion.26.refs_1_), channel_id=1, source_target_pairs={{0,8},{16,24},{1,9},{17,25},{2,10},{18,26},{3,11},{19,27},{4,12},{... | collective-permute-start | bytes 1966088 | tf_op jit(solution)/shard_map/ppermute | solution.py:182
  69.5 15.1 %collective-permute-start.21 = (bf16[2,10,128,128]{3,2,1,0:T(8,128)(2,1)S(1)}, bf16[2,10,128,128]{3,2,1,0:T(8,128)(2,1)S(1)}, u32[]{:S(2)}, u32[]{:S(2)}) collective-permute-start(bf16[2,10,128,128]{3,2,1,0:T(8,128)(2,1)S(1)} %fusion.27.refs_2_), channel_id=1, source_target_pairs={{0,8},{16,24},{1,9},{17,25},{2,10},{18,26},{3,11},{19,27},{4,12},{... | collective-permute-start | bytes 1966088 | tf_op jit(solution)/shard_map/ppermute | solution.py:182
  70.9 14.4 %collective-permute-start.24 = (bf16[2,10,128,128]{3,2,1,0:T(8,128)(2,1)S(1)}, bf16[2,10,128,128]{3,2,1,0:T(8,128)(2,1)S(1)}, u32[]{:S(2)}, u32[]{:S(2)}) collective-permute-start(bf16[2,10,128,128]{3,2,1,0:T(8,128)(2,1)S(1)} %collective-permute-done.22.refs_5_), channel_id=1, source_target_pairs={{0,8},{16,24},{8,0},{24,16},{1,9},{17,25},{9,1},{25,17},{2,10},{18... | collective-permute-start | bytes 1966088 | tf_op jit(solution)/shard_map/ppermute | solution.py:181
  80.0 7.5 %collective-permute-start.25 = (bf16[2,10,128,128]{3,2,1,0:T(8,128)(2,1)S(1)}, bf16[2,10,128,128]{3,2,1,0:T(8,128)(2,1)S(1)}, u32[]{:S(2)}, u32[]{:S(2)}) collective-permute-start(bf16[2,10,128,128]{3,2,1,0:T(8,128)(2,1)S(1)} %collective-permute-done.23.refs_6_), channel_id=1, source_target_pairs={{0,8},{16,24},{8,0},{24,16},{1,9},{17,25},{9,1},{25,17},{2,10},{18... | collective-permute-start | bytes 1966088 | tf_op jit(solution)/shard_map/ppermute | solution.py:181
  80.0 52.2 %slice-start = ((s8[13107200]{0:T(1024)(128)(4,1)}), s8[4194304]{0:T(1024)(128)(4,1)S(1)}, s32[]{:S(2)}) async-start(s8[13107200]{0:T(1024)(128)(4,1)} %bitcast.87), calls=%async_computation | async-start | bytes 8388608
  81.6 50.5 %slice-start.1 = ((s8[13107200]{0:T(1024)(128)(4,1)}), s8[4194304]{0:T(1024)(128)(4,1)S(1)}, s32[]{:S(2)}) async-start(s8[13107200]{0:T(1024)(128)(4,1)} %bitcast.87), calls=%async_computation.1 | async-start | bytes 8388608
  81.6 19.8 %collective-permute-start.17 = (bf16[2,10,128,128]{3,2,1,0:T(8,128)(2,1)S(1)}, bf16[2,10,128,128]{3,2,1,0:T(8,128)(2,1)S(1)}, u32[]{:S(2)}, u32[]{:S(2)}) collective-permute-start(bf16[2,10,128,128]{3,2,1,0:T(8,128)(2,1)S(1)} %slice_select_fusion.refs_2_), channel_id=1, source_target_pairs={{0,16},{8,24},{1,17},{9,25},{2,18},{10,26},{3,19},{11,27},{4,20},{... | collective-permute-start | bytes 1966088 | tf_op jit(solution)/shard_map/ppermute | solution.py:179
  83.2 31.8 %collective-permute-start.16 = (bf16[2,10,128,128]{3,2,1,0:T(8,128)(2,1)S(1)}, bf16[2,10,128,128]{3,2,1,0:T(8,128)(2,1)S(1)}, u32[]{:S(2)}, u32[]{:S(2)}) collective-permute-start(bf16[2,10,128,128]{3,2,1,0:T(8,128)(2,1)S(1)} %slice_select_fusion.1.refs_1_), channel_id=1, source_target_pairs={{0,16},{8,24},{1,17},{9,25},{2,18},{10,26},{3,19},{11,27},{4,20},{... | collective-permute-start | bytes 1966088 | tf_op jit(solution)/shard_map/ppermute | solution.py:179
  84.7 35.8 %collective-permute-start.26 = (bf16[10,256,128]{2,1,0:T(8,128)(2,1)S(1)}, bf16[10,256,128]{2,1,0:T(8,128)(2,1)S(1)}, u32[]{:S(2)}, u32[]{:S(2)}) collective-permute-start(bf16[10,256,128]{2,1,0:T(8,128)(2,1)S(1)} %get-tuple-element.45), channel_id=1, source_target_pairs={{0,4},{4,0},{1,5},{5,1},{2,6},{6,2},{3,7},{7,3},{8,12},{12,8},{9,1... | collective-permute-start | bytes 1966088 | tf_op jit(solution)/shard_map/ppermute | solution.py:145
  85.3 40.6 %collective-permute-start.15 = (bf16[2,10,128,128]{3,2,1,0:T(8,128)(2,1)S(1)}, bf16[2,10,128,128]{3,2,1,0:T(8,128)(2,1)S(1)}, u32[]{:S(2)}, u32[]{:S(2)}) collective-permute-start(bf16[2,10,128,128]{3,2,1,0:T(8,128)(2,1)S(1)} %slice_select_fusion.refs_2_), channel_id=1, source_target_pairs={{0,8},{16,24},{1,9},{17,25},{2,10},{18,26},{3,11},{19,27},{4,12},{... | collective-permute-start | bytes 1966088 | tf_op jit(solution)/shard_map/ppermute | solution.py:182
  87.5 38.5 %collective-permute-start.14 = (bf16[2,10,128,128]{3,2,1,0:T(8,128)(2,1)S(1)}, bf16[2,10,128,128]{3,2,1,0:T(8,128)(2,1)S(1)}, u32[]{:S(2)}, u32[]{:S(2)}) collective-permute-start(bf16[2,10,128,128]{3,2,1,0:T(8,128)(2,1)S(1)} %slice_select_fusion.1.refs_1_), channel_id=1, source_target_pairs={{0,8},{16,24},{1,9},{17,25},{2,10},{18,26},{3,11},{19,27},{4,12},{... | collective-permute-start | bytes 1966088 | tf_op jit(solution)/shard_map/ppermute | solution.py:182
  101.4 24.5 %collective-permute-start.19 = (bf16[2,10,128,128]{3,2,1,0:T(8,128)(2,1)S(1)}, bf16[2,10,128,128]{3,2,1,0:T(8,128)(2,1)S(1)}, u32[]{:S(2)}, u32[]{:S(2)}) collective-permute-start(bf16[2,10,128,128]{3,2,1,0:T(8,128)(2,1)S(1)} %collective-permute-done.17.refs_6_), channel_id=1, source_target_pairs={{0,8},{16,24},{8,0},{24,16},{1,9},{17,25},{9,1},{25,17},{2,10},{18... | collective-permute-start | bytes 1966088 | tf_op jit(solution)/shard_map/ppermute | solution.py:181
  115.0 11.0 %collective-permute-start.18 = (bf16[2,10,128,128]{3,2,1,0:T(8,128)(2,1)S(1)}, bf16[2,10,128,128]{3,2,1,0:T(8,128)(2,1)S(1)}, u32[]{:S(2)}, u32[]{:S(2)}) collective-permute-start(bf16[2,10,128,128]{3,2,1,0:T(8,128)(2,1)S(1)} %collective-permute-done.16.refs_5_), channel_id=1, source_target_pairs={{0,8},{16,24},{8,0},{24,16},{1,9},{17,25},{9,1},{25,17},{2,10},{18... | collective-permute-start | bytes 1966088 | tf_op jit(solution)/shard_map/ppermute | solution.py:181
  120.4 11.7 %slice-start.2 = ((s8[13107200]{0:T(1024)(128)(4,1)}), s8[4194304]{0:T(1024)(128)(4,1)S(1)}, s32[]{:S(2)}) async-start(s8[13107200]{0:T(1024)(128)(4,1)} %bitcast.87), calls=%async_computation.2 | async-start | bytes 8388608
  126.0 6.2 %slice-start.3 = ((s8[13107200]{0:T(1024)(128)(4,1)}), s8[524288]{0:T(1024)(128)(4,1)S(1)}, s32[]{:S(2)}) async-start(s8[13107200]{0:T(1024)(128)(4,1)} %bitcast.87), calls=%async_computation.3 | async-start | bytes 1048576
  144.8 14.9 %collective-permute-start.27 = (bf16[256,1024]{1,0:T(8,128)(2,1)S(1)}, bf16[256,1024]{1,0:T(8,128)(2,1)S(1)}, u32[]{:S(2)}, u32[]{:S(2)}) collective-permute-start(bf16[256,1024]{1,0:T(8,128)(2,1)S(1)} %fusion.10), channel_id=1, source_target_pairs={{4,0},{0,4},{5,1},{1,5},{6,2},{2,6},{7,3},{3,7},{12,8},{8,12},{13,... | collective-permute-start | bytes 1572872 | tf_op jit(solution)/shard_map/ppermute | solution.py:200
  145.4 25.5 %collective-permute-start.28 = (bf16[256,1024]{1,0:T(8,128)(2,1)S(1)}, bf16[256,1024]{1,0:T(8,128)(2,1)S(1)}, u32[]{:S(2)}, u32[]{:S(2)}) collective-permute-start(bf16[256,1024]{1,0:T(8,128)(2,1)S(1)} %fusion.13), channel_id=1, source_target_pairs={{4,0},{0,4},{5,1},{1,5},{6,2},{2,6},{7,3},{3,7},{12,8},{8,12},{13,... | collective-permute-start | bytes 1572872 | tf_op jit(solution)/shard_map/ppermute | solution.py:200
  146.9 35.2 %collective-permute-start.29 = (bf16[256,1024]{1,0:T(8,128)(2,1)S(1)}, bf16[256,1024]{1,0:T(8,128)(2,1)S(1)}, u32[]{:S(2)}, u32[]{:S(2)}) collective-permute-start(bf16[256,1024]{1,0:T(8,128)(2,1)S(1)} %fusion.16), channel_id=1, source_target_pairs={{4,0},{0,4},{5,1},{1,5},{6,2},{2,6},{7,3},{3,7},{12,8},{8,12},{13,... | collective-permute-start | bytes 1572872 | tf_op jit(solution)/shard_map/ppermute | solution.py:200
  148.3 11.4 %copy-start.2 = (bf16[1,1,256,5120]{3,2,1,0:T(8,128)(2,1)S(1)}, bf16[1,1,256,5120]{3,2,1,0:T(8,128)(2,1)}, u32[]{:S(2)}) copy-start(bf16[1,1,256,5120]{3,2,1,0:T(8,128)(2,1)} %param.16) | copy-start | bytes 7864324
  148.3 45.1 %collective-permute-start.30 = (bf16[256,1024]{1,0:T(8,128)(2,1)S(1)}, bf16[256,1024]{1,0:T(8,128)(2,1)S(1)}, u32[]{:S(2)}, u32[]{:S(2)}) collective-permute-start(bf16[256,1024]{1,0:T(8,128)(2,1)S(1)} %fusion.19), channel_id=1, source_target_pairs={{4,0},{0,4},{5,1},{1,5},{6,2},{2,6},{7,3},{3,7},{12,8},{8,12},{13,... | collective-permute-start | bytes 1572872 | tf_op jit(solution)/shard_map/ppermute | solution.py:200
  150.7 53.4 %collective-permute-start.31 = (bf16[256,1024]{1,0:T(8,128)(2,1)S(1)}, bf16[256,1024]{1,0:T(8,128)(2,1)S(1)}, u32[]{:S(2)}, u32[]{:S(2)}) collective-permute-start(bf16[256,1024]{1,0:T(8,128)(2,1)S(1)} %fusion.22), channel_id=1, source_target_pairs={{4,0},{0,4},{5,1},{1,5},{6,2},{2,6},{7,3},{3,7},{12,8},{8,12},{13,... | collective-permute-start | bytes 1572872 | tf_op jit(solution)/shard_map/ppermute | solution.py:200
  193.6 11.5 %copy-start.1 = (f32[16,5120]{1,0:T(8,128)S(1)}, f32[16,5120]{1,0:T(8,128)}, u32[]{:S(2)}) copy-start(f32[16,5120]{1,0:T(8,128)} %param.18) | copy-start | bytes 983044

commit v2 on v1

--- a/solution.py
+++ b/solution.py
@@ -15,24 +15,43 @@
 VMEM_LIMIT = 22 << 20
 
 
-def flash_kernel(flags, *refs, layout, scale, step, first, last):
-    count = sum(len(members) for _, members in layout)
+def hidden_bias(mask, span, origin):
+    source = origin(span)
+    return jnp.where((source >= 0) & (mask[span, jnp.maximum(source, 0)] > 0), 0.0, NEG_BIG)
+
+
+def flash_kernel(mask, *refs, layout, count, scale, step, first, last):
     q_ref, kv_refs, refs = refs[0], refs[1 : 1 + count], refs[1 + count :]
+    span = lax.axis_index("tm")
+    odd = lax.rem(span, 2) == 1
+    biases = [None if origin is None else hidden_bias(mask, span, origin) for origin, _ in layout]
+
+    def gather(kind, h):
+        blocks = []
+        for _, members in layout:
+            for i in members:
+                if isinstance(i, tuple):
+                    blocks.append(jnp.where(odd, kv_refs[i[0]][kind, h], kv_refs[i[1]][kind, h]))
+                else:
+                    blocks.append(kv_refs[i][kind, h])
+        return jnp.concatenate(blocks, axis=0)
+
     if not first:
         (max_in, sum_in, acc_in), refs = refs[:3], refs[3:]
     outs, score_ref = refs[:-1], refs[-1]
     dim = q_ref.shape[2]
-    order = [(flag, i) for flag, members in layout for i in members]
+    keys = kv_refs[0].shape[2]
+    order = [bias for bias, (_, members) in zip(biases, layout) for _ in members]
     for h in range(step):
-        block = jnp.concatenate([kv_refs[i][0, h] for _, i in order], axis=0)
         raw = lax.dot_general(
-            q_ref[h], block, (((1,), (1,)), ((), ())), preferred_element_type=jnp.float32
+            q_ref[h], gather(0, h), (((1,), (1,)), ((), ())), preferred_element_type=jnp.float32
         )
         at, top = 0, None
-        for flag, i in order:
-            bias = jnp.where(flags[flag] > 0, 0.0, NEG_BIG)
-            for _ in range(0, kv_refs[i].shape[2], dim):
-                piece = raw[:, at : at + dim] + bias
+        for bias in order:
+            for _ in range(0, keys, dim):
+                piece = raw[:, at : at + dim]
+                if bias is not None:
+                    piece = piece + bias
                 score_ref[h, :, at : at + dim] = piece
                 top = piece if top is None else jnp.maximum(top, piece)
                 at += dim
@@ -48,9 +67,8 @@
             piece = jnp.exp2(score_ref[h, :, j : j + dim] * scale - top)
             total = piece if total is None else total + piece
             weights.append(piece.astype(jnp.bfloat16))
-        block = jnp.concatenate([kv_refs[i][1, h] for _, i in order], axis=0)
         added = jnp.dot(
-            jnp.concatenate(weights, axis=1), block, preferred_element_type=jnp.float32
+            jnp.concatenate(weights, axis=1), gather(1, h), preferred_element_type=jnp.float32
         )
         acc = added if acc is None else acc + added
         if last:
@@ -60,20 +78,26 @@
             outs[0][h], outs[1][h], outs[2][h] = top, total, acc
 
 
-def attend(queries, spans, flags, state, last):
+def attend(queries, slots, span_mask, state, last):
     heads, rows, dim = queries.shape
     arrays, layout = [], []
-    for flag, members in spans:
-        layout.append((flag, tuple(range(len(arrays), len(arrays) + len(members)))))
-        arrays += members
-    keys = sum(array.shape[2] for array in arrays)
+    for origin, members in slots:
+        places = []
+        for member in members:
+            choices = member if isinstance(member, tuple) else (member,)
+            at = tuple(range(len(arrays), len(arrays) + len(choices)))
+            places.append(at if len(at) > 1 else at[0])
+            arrays += choices
+        layout.append((origin, places))
+    keys = arrays[0].shape[2] * sum(len(places) for _, places in layout)
     step = max(s for s in range(1, heads + 1) if heads % s == 0 and s * rows * keys <= HEAD_STEP_SCORES)
     by_head = pl.BlockSpec((step, rows, dim), lambda h, f: (h, 0, 0))
     states = [] if state is None else list(state)
     return pl.pallas_call(
         functools.partial(
             flash_kernel,
-            layout=tuple(layout),
+            layout=layout,
+            count=len(arrays),
             scale=LOG2E / math.sqrt(dim),
             step=step,
             first=state is None,
@@ -100,7 +124,7 @@
             transcendentals=heads * rows * keys,
         ),
         compiler_params=pltpu.CompilerParams(vmem_limit_bytes=VMEM_LIMIT),
-    )(flags, queries, *arrays, *states)
+    )(span_mask, queries, *arrays, *states)
 
 
 def body(sizes, queries, keys, values, ctx_keys, ctx_values, hidden, out_weight, gates, levels, span_mask, prefix):
@@ -123,16 +147,6 @@
     pair = lambda a, b, d: jnp.stack([take(a, d), take(b, d)])
     cycle = lambda d: [(i, (i + d) % splits) for i in range(splits)]
 
-    swap_up = [(i, i + 1) for i in range(0, spans, 2)]
-    swap = swap_up + [(i + 1, i) for i in range(0, spans, 2)]
-    mask_row = lax.dynamic_index_in_dim(span_mask, span, 0, keepdims=False)
-    ids = jnp.arange(spans, dtype=jnp.int32)
-    seen = lambda s: jnp.sum(jnp.where((ids == s) & (ids <= span), mask_row, 0))
-    partner = span + 1 - 2 * lax.rem(span, 2)
-    flags = [jnp.int32(1), seen(partner)]
-    for s in range(2, spans, 2):
-        flags += [seen(span - s), seen(partner - s)]
-    flags = jnp.stack(flags)
     level_now = lax.dynamic_index_in_dim(levels, span, 0, keepdims=False)
     gate_row = lax.dynamic_index_in_dim(gates, level_now, 0, keepdims=False)
 
@@ -145,16 +159,19 @@
         q_parts.append(lax.ppermute(take(q, d), "head", cycle(d)))
 
     use_context = span < prefix[0]
-    up, down = [[a] for a in ctx_parts], [[a] for a in ctx_parts]
-    piece_rows, rows = splits * ctx_parts[0].shape[2], k.shape[1]
-    own, held = [], []
+    final = spans - 1
+    stands_in = span == final
+    bases = [jnp.where(stands_in, lax.ppermute(a, "tm", [(0, final)]), a) for a in ctx_parts]
+    up, down = [[a] for a in bases], [[a] for a in bases]
+    piece_rows, rows = splits * bases[0].shape[2], k.shape[1]
+    own, passed, held = [], [], []
     for s in range(branches):
         pieces = []
         for d in range(splits):
-            piece = ctx_parts[d]
+            piece = bases[d]
             if s > 0:
                 if s == branches - 1 and d == 0:
-                    up[0][-1], flags, gate_row = lax.optimization_barrier((up[0][-1], flags, gate_row))
+                    up[0][-1], gate_row = lax.optimization_barrier((up[0][-1], gate_row))
                 rise = [(i, i + 1) for i in range(s - 1, branches - 1)]
                 fall = [(i, i - 1) for i in range(1, branches - s + 1)]
                 up[d].append(lax.ppermute(up[d][-1], "branch", rise))
@@ -162,43 +179,53 @@
                 piece = up[d][s]
             pieces.append(piece)
         if s > 0:
-            held[-1], *pieces = lax.optimization_barrier((own[-1], *pieces))
+            merged, *pieces = lax.optimization_barrier(((own[-1], passed[-1]), *pieces))
+            held[-1] = merged
             for d in range(splits):
                 for t in range(1, s + 1):
                     pieces[d] = jnp.where(branch == s - t, down[d][t], pieces[d])
         d, at = divmod(s * piece_rows, rows)
-        context = jnp.concatenate(pieces, axis=2)
-        own.append(jnp.where(use_context, context, kv_parts[d][:, :, at : at + piece_rows]))
-        held.append(own[-1])
-
-    groups = [held, []]
-    for _ in range(2, spans, 2):
-        groups += [[], []]
-    for array in own:
-        for s in range(2, spans, 2):
-            far = lax.ppermute(array, "tm", [(i, i + s) for i in range(spans - s)])
-            groups[s].append(far)
-            groups[s + 1].append(lax.ppermute(far, "tm", swap))
-        groups[1].append(lax.ppermute(array, "tm", swap_up))
+        context, mine = jnp.concatenate(pieces, axis=2), kv_parts[d][:, :, at : at + piece_rows]
+        own.append(jnp.where(use_context, context, mine))
+        passed.append(jnp.where(use_context | stands_in, context, mine))
+        held.append((own[-1], passed[-1]))
+
+    pairs = [(i, i + 1) for i in range(0, spans, 2)]
+    beside = [lax.ppermute(a, "tm", pairs + [(final, final - 1)]) for a in passed]
+    slots = [
+        (None, [a for a, _ in held]),
+        (lambda c: jnp.where(lax.rem(c, 2) == 1, c - 1, jnp.where(c == final - 1, 0, -1)), beside),
+    ]
+    for s in range(2, final - 1, 2):
+        far = [lax.ppermute(a, "tm", [(i, i + s) for i in range(spans - s)]) for a in own]
+        back = [(b, a) for a, b in pairs]
+        near = [lax.ppermute(a, "tm", pairs + back) for a in far]
+        slots.append((lambda c, s=s: c - s, far))
+        slots.append((lambda c, s=s: c + 1 - 2 * lax.rem(c, 2) - s, near))
+    s = final - 1
+    far = [lax.ppermute(a, "tm", [(1, final)]) for a in own]
+    near = [lax.ppermute(a, "tm", [(final, final - 1)]) for a in far]
+    slots.append((lambda c: jnp.where(c >= final - 1, 1, -1), list(zip(far, near))))
+    slots.append((lambda c: jnp.where(c == final, 0, -1), [a for _, a in held]))
 
     half = max(1, len(own) // 2)
-    early = [(i, arrays[:half]) for i, arrays in enumerate(groups)]
-    late = [(i, arrays[half:]) for i, arrays in enumerate(groups)]
+    early = [(origin, arrays[:half]) for origin, arrays in slots]
+    late = [(origin, arrays[half:]) for origin, arrays in slots]
     states = []
     for d in range(splits):
-        states.append(attend(q_parts[d], early, flags, None, False))
+        states.append(attend(q_parts[d], early, span_mask, None, False))
 
     columns = out_weight.shape[1]
     width = columns // COL_BLOCKS
     project = lambda a, w: jnp.dot(a, w, preferred_element_type=jnp.float32).astype(jnp.bfloat16)
     returned = [[] for _ in range(COL_BLOCKS)]
     for d in range(1, splits):
-        attended = attend(q_parts[d], late, flags, states[d], True)
+        attended = attend(q_parts[d], late, span_mask, states[d], True)
         back = [((i + d) % splits, i) for i in range(splits)]
         for j in range(COL_BLOCKS):
             partial = project(attended, out_weight[:, j * width : (j + 1) * width])
             returned[j].append(lax.ppermute(partial, "head", back))
-    attended = attend(q_parts[0], late, flags, states[0], True)
+    attended = attend(q_parts[0], late, span_mask, states[0], True)
     kept = lax.optimization_barrier(project(attended, out_weight))
     updated = hidden
     for j in range(COL_BLOCKS):

time: 206 us -> 182 us (0.88)
  the two profiles are of different devices: /device:TPU:30 before, /device:TPU:29 now
where the time goes in v2:
time: 182 us; the launch traced here: 181 us
  waiting for transfers between devices  80.6 us (44%)
  starting transfers between devices  49.2 us (27%)
  Pallas kernels  23.2 us (13%)
  other arithmetic  11.3 us (6%)
  matrix products  8.34 us (5%)
  local copies, waits for them, and re-layouts  4.95 us (3%)
  between operations  3.25 us (2%)
    ppermute x5, waiting for transfers between devices, sublayer(): returned[j].append(lax.ppermute(partial, 'head', back))  48.6 us
    ppermute x6, waiting for transfers between devices, sublayer(): up[d].append(lax.ppermute(up[d][-1], 'branch', rise))  23.5 us
    pallas_call x4, Pallas kernels, attend(): pl.pallas_call(functools.partial(flash_kernel, layout=layout, count=len(a...  23.2 us
    ppermute x6, starting transfers between devices, sublayer(): down[d].append(lax.ppermute(down[d][-1], 'branch', fall))  10.7 us
    ppermute x4, starting transfers between devices, sublayer(): lax.ppermute(a, 'tm', pairs + [(final, final - 1)])  9.71 us
    dot_general x6, matrix products, sublayer(): jnp.dot(a, w, preferred_element_type=jnp.float32).astype(jnp.bfloat16)  8.34 us
    ppermute x6, starting transfers between devices, sublayer(): up[d].append(lax.ppermute(up[d][-1], 'branch', rise))  7.74 us
    ppermute x4, starting transfers between devices, sublayer(): near = [lax.ppermute(a, 'tm', [(final, final - 1)]) for a in far]  7.13 us
  transfers between devices with their start and end apart: 34, of which 13 were waited for; matrix products, arithmetic and copies ran while one was open for 9% of the time, Pallas kernels for 6%

profile of v2, /device:TPU:29, one launch (start us, length us, event | category | flops | bytes accessed | tf_op | source)
XLA Modules:
  0.0 180.8 jit_solution(9798762493709287101)
XLA Ops:
  0.0 1.0 copy-done.7
  1.2 1.3 collective-permute-start.5
  2.5 0.8 pad_maximum_fusion.6
  3.2 1.3 collective-permute-start
  4.5 1.5 dynamic-slice_bitcast_fusion.3
  6.0 4.0 %collective-permute-done.5 = bf16[2,10,64,128]{3,2,1,0:T(8,128)(2,1)} collective-permute-done((bf16[2,10,64,128]{3,2,1,0:T(8,128)(2,1)S(1)}, bf16[2,10,64,128]{3,2,1,0:T(8,128)(2,1)}, u32[]{:S(2)}, u32[]{:S(2)}) %collective-permute-start.5) | collective-permute-done | bytes 327712 | tf_op jit(solution)/shard_map/ppermute | solution.py:155
  10.0 1.3 collective-permute-start.6
  11.3 1.2 pad_maximum_fusion
  12.4 1.2 collective-permute-start.11
  16.2 1.0 broadcast_select_fusion.11
  17.2 1.3 collective-permute-start.1
  18.5 4.0 %collective-permute-start.3 = (bf16[2,10,64,128]{3,2,1,0:T(8,128)(2,1)S(1)}, bf16[2,10,64,128]{3,2,1,0:T(8,128)(2,1)S(1)}, u32[]{:S(2)}, u32[]{:S(2)}) collective-permute-start(bf16[2,10,64,128]{3,2,1,0:T(8,128)(2,1)S(1)} %broadcast_select_fusion.11), channel_id=1, source_target_pairs={{1,0},{2,1},{3,2},{5,4},{6,5},{7,6},{9,8},{10,9},{11,10},{13,12},{... | collective-permute-start | bytes 983048 | tf_op jit(solution)/shard_map/ppermute | solution.py:178
  22.5 1.0 broadcast_select_fusion.10
  23.6 1.3 collective-permute-start.7
  24.9 4.0 %collective-permute-start.8 = (bf16[2,10,64,128]{3,2,1,0:T(8,128)(2,1)S(1)}, bf16[2,10,64,128]{3,2,1,0:T(8,128)(2,1)S(1)}, u32[]{:S(2)}, u32[]{:S(2)}) collective-permute-start(bf16[2,10,64,128]{3,2,1,0:T(8,128)(2,1)S(1)} %broadcast_select_fusion.10), channel_id=1, source_target_pairs={{1,0},{2,1},{3,2},{5,4},{6,5},{7,6},{9,8},{10,9},{11,10},{13,12},{... | collective-permute-start | bytes 983048 | tf_op jit(solution)/shard_map/ppermute | solution.py:178
  29.6 1.3 collective-permute-start.2
  30.9 0.7 collective-permute-start.4
  31.9 2.7 %collective-permute-done.7 = bf16[2,10,64,128]{3,2,1,0:T(8,128)(2,1)} collective-permute-done((bf16[2,10,64,128]{3,2,1,0:T(8,128)(2,1)S(1)}, bf16[2,10,64,128]{3,2,1,0:T(8,128)(2,1)}, u32[]{:S(2)}, u32[]{:S(2)}) %collective-permute-start.7) | collective-permute-done | bytes 327712 | tf_op jit(solution)/shard_map/ppermute | solution.py:177
  34.7 1.3 collective-permute-start.9
  36.0 0.7 collective-permute-start.10
  36.7 1.0 broadcast_select_fusion.8
  38.1 3.6 %collective-permute-done.2 = bf16[2,10,64,128]{3,2,1,0:T(8,128)(2,1)S(1)} collective-permute-done((bf16[2,10,64,128]{3,2,1,0:T(8,128)(2,1)S(1)}, bf16[2,10,64,128]{3,2,1,0:T(8,128)(2,1)S(1)}, u32[]{:S(2)}, u32[]{:S(2)}) %collective-permute-start.2) | collective-permute-done | bytes 327712 | tf_op jit(solution)/shard_map/ppermute | solution.py:177
  41.7 1.3 collective-permute-start.24
  43.0 5.6 %collective-permute-done.9 = bf16[2,10,64,128]{3,2,1,0:T(8,128)(2,1)S(1)} collective-permute-done((bf16[2,10,64,128]{3,2,1,0:T(8,128)(2,1)}, bf16[2,10,64,128]{3,2,1,0:T(8,128)(2,1)S(1)}, u32[]{:S(2)}, u32[]{:S(2)}) %collective-permute-start.9) | collective-permute-done | bytes 327712 | tf_op jit(solution)/shard_map/ppermute | solution.py:177
  48.6 1.3 collective-permute-start.26
  49.9 1.3 collective-permute-start.12
  51.3 0.7 collective-permute-start.14
  52.0 1.3 collective-permute-start.13
  53.4 6.6 %collective-permute-done.12 = bf16[2,10,64,128]{3,2,1,0:T(8,128)(2,1)S(1)} collective-permute-done((bf16[2,10,64,128]{3,2,1,0:T(8,128)(2,1)S(1)}, bf16[2,10,64,128]{3,2,1,0:T(8,128)(2,1)S(1)}, u32[]{:S(2)}, u32[]{:S(2)}) %collective-permute-start.12) | collective-permute-done | bytes 327712 | tf_op jit(solution)/shard_map/ppermute | solution.py:177
  60.0 0.7 collective-permute-start.15
  60.7 1.5 broadcast_select_fusion.1
  62.1 4.9 %collective-permute-done.13 = bf16[2,10,64,128]{3,2,1,0:T(8,128)(2,1)S(1)} collective-permute-done((bf16[2,10,64,128]{3,2,1,0:T(8,128)(2,1)S(1)}, bf16[2,10,64,128]{3,2,1,0:T(8,128)(2,1)S(1)}, u32[]{:S(2)}, u32[]{:S(2)}) %collective-permute-start.13) | collective-permute-done | bytes 327712 | tf_op jit(solution)/shard_map/ppermute | solution.py:177
  67.0 3.8 %collective-permute-start.22 = (bf16[2,10,128,128]{3,2,1,0:T(8,128)(2,1)S(1)}, bf16[2,10,128,128]{3,2,1,0:T(8,128)(2,1)S(1)}, u32[]{:S(2)}, u32[]{:S(2)}) collective-permute-start(bf16[2,10,128,128]{3,2,1,0:T(8,128)(2,1)S(1)} %get-tuple-element.37.refs_9_), channel_id=1, source_target_pairs={{0,8},{16,24},{24,16},{1,9},{17,25},{25,17},{2,10},{18,26},{26,18}... | collective-permute-start | bytes 1966088 | tf_op jit(solution)/shard_map/ppermute | solution.py:194
  70.9 2.1 %collective-permute-start.23 = (bf16[2,10,128,128]{3,2,1,0:T(8,128)(2,1)S(1)}, bf16[2,10,128,128]{3,2,1,0:T(8,128)(2,1)S(1)}, u32[]{:S(2)}, u32[]{:S(2)}) collective-permute-start(bf16[2,10,128,128]{3,2,1,0:T(8,128)(2,1)S(1)} %get-tuple-element.38.refs_10_), channel_id=1, source_target_pairs={{0,8},{16,24},{24,16},{1,9},{17,25},{25,17},{2,10},{18,26},{26,18}... | collective-permute-start | bytes 1966088 | tf_op jit(solution)/shard_map/ppermute | solution.py:194
  73.0 1.3 collective-permute-start.18
  74.4 1.9 %collective-permute-start.25 = (bf16[2,10,128,128]{3,2,1,0:T(8,128)(2,1)S(1)}, bf16[2,10,128,128]{3,2,1,0:T(8,128)(2,1)S(1)}, u32[]{:S(2)}, u32[]{:S(2)}) collective-permute-start(bf16[2,10,128,128]{3,2,1,0:T(8,128)(2,1)S(1)} %collective-permute-done.24.refs_5_), channel_id=1, source_target_pairs={{24,16},{25,17},{26,18},{27,19},{28,20},{29,21},{30,22},{31,23}} | collective-permute-start | bytes 1966088 | tf_op jit(solution)/shard_map/ppermute | solution.py:207
  76.2 1.3 collective-permute-start.27
  77.7 1.5 broadcast_select_fusion
  79.2 1.3 collective-permute-start.20
  80.9 1.9 %collective-permute-start.16 = (bf16[2,10,128,128]{3,2,1,0:T(8,128)(2,1)S(1)}, bf16[2,10,128,128]{3,2,1,0:T(8,128)(2,1)S(1)}, u32[]{:S(2)}, u32[]{:S(2)}) collective-permute-start(bf16[2,10,128,128]{3,2,1,0:T(8,128)(2,1)S(1)} %get-tuple-element.34.refs_9_), channel_id=1, source_target_pairs={{0,8},{16,24},{24,16},{1,9},{17,25},{25,17},{2,10},{18,26},{26,18}... | collective-permute-start | bytes 1966088 | tf_op jit(solution)/shard_map/ppermute | solution.py:194
  82.9 1.8 %collective-permute-done.18.refs_5_ = bf16[2,10,128,128]{3,2,1,0:T(8,128)(2,1)S(1)} collective-permute-done((bf16[2,10,128,128]{3,2,1,0:T(8,128)(2,1)S(1)}, bf16[2,10,128,128]{3,2,1,0:T(8,128)(2,1)S(1)}, u32[]{:S(2)}, u32[]{:S(2)}) %collective-permute-start.18) | collective-permute-done | bytes 655392 | tf_op jit(solution)/shard_map/ppermute | solution.py:206
  84.7 1.9 %collective-permute-start.17 = (bf16[2,10,128,128]{3,2,1,0:T(8,128)(2,1)S(1)}, bf16[2,10,128,128]{3,2,1,0:T(8,128)(2,1)S(1)}, u32[]{:S(2)}, u32[]{:S(2)}) collective-permute-start(bf16[2,10,128,128]{3,2,1,0:T(8,128)(2,1)S(1)} %get-tuple-element.45.refs_10_), channel_id=1, source_target_pairs={{0,8},{16,24},{24,16},{1,9},{17,25},{25,17},{2,10},{18,26},{26,18}... | collective-permute-start | bytes 1966088 | tf_op jit(solution)/shard_map/ppermute | solution.py:194
  86.6 2.4 %collective-permute-start.19 = (bf16[2,10,128,128]{3,2,1,0:T(8,128)(2,1)S(1)}, bf16[2,10,128,128]{3,2,1,0:T(8,128)(2,1)S(1)}, u32[]{:S(2)}, u32[]{:S(2)}) collective-permute-start(bf16[2,10,128,128]{3,2,1,0:T(8,128)(2,1)S(1)} %collective-permute-done.18.refs_5_), channel_id=1, source_target_pairs={{24,16},{25,17},{26,18},{27,19},{28,20},{29,21},{30,22},{31,23}} | collective-permute-start | bytes 1966088 | tf_op jit(solution)/shard_map/ppermute | solution.py:207
  89.1 2.6 %collective-permute-done.20.refs_7_ = bf16[2,10,128,128]{3,2,1,0:T(8,128)(2,1)S(1)} collective-permute-done((bf16[2,10,128,128]{3,2,1,0:T(8,128)(2,1)S(1)}, bf16[2,10,128,128]{3,2,1,0:T(8,128)(2,1)S(1)}, u32[]{:S(2)}, u32[]{:S(2)}) %collective-permute-start.20) | collective-permute-done | bytes 655392 | tf_op jit(solution)/shard_map/ppermute | solution.py:206
  91.7 1.5 collective-permute-start.21
  93.3 5.5 %shard_map.109 = (f32[10,256,128]{2,1,0:T(8,128)S(1)}, f32[10,256,128]{2,1,0:T(8,128)S(1)}, f32[10,256,128]{2,1,0:T(8,128)S(1)}) custom-call(s32[4,4]{1,0:T(4,128)S(1)} %copy-done.2, bf16[10,256,128]{2,1,0:T(8,128)(2,1)S(1)} %get-tuple-element.53.refs_0_, bf16[2,10,128,128]{3,2,1,0:T(8,128)(2,1)S(1)} %get-tuple-element.35.refs_1_, ...), custom_call_target="tpu_custom_call" | custom-call | flops 1342177280 | bytes 6553600 | tf_op jit(solution)/shard_map/pallas_call | solution.py:96
  98.8 5.5 %shard_map.111 = (f32[10,256,128]{2,1,0:T(8,128)S(1)}, f32[10,256,128]{2,1,0:T(8,128)S(1)}, f32[10,256,128]{2,1,0:T(8,128)S(1)}) custom-call(s32[4,4]{1,0:T(4,128)S(1)} %copy-done.2, bf16[10,256,128]{2,1,0:T(8,128)(2,1)S(1)} %collective-permute-done.28.refs_0_, bf16[2,10,128,128]{3,2,1,0:T(8,128)(2,1)S(1)} %get-tuple-element.35.refs_1_, ...), custom_call_target="tpu_custom_call" | custom-call | flops 1342177280 | bytes 6553600 | tf_op jit(solution)/shard_map/pallas_call | solution.py:96
  104.4 6.2 %shard_map.112 = bf16[256,1280]{1,0:T(8,128)(2,1)S(1)} custom-call(s32[4,4]{1,0:T(4,128)S(1)} %copy-done.2, bf16[10,256,128]{2,1,0:T(8,128)(2,1)S(1)} %collective-permute-done.28.refs_0_, bf16[2,10,128,128]{3,2,1,0:T(8,128)(2,1)S(1)} %get-tuple-element.31.refs_1_, bf16[2,10,128,128]{3,2,1,0:T(8,128)(2,1)S(1)} %get-tuple-element.46.refs_2_, ...), custom_call_target="tpu_custom_call" | custom-call | flops 1342177280 | bytes 6553600 | tf_op jit(solution)/shard_map/pallas_call | solution.py:96
  110.6 0.8 fusion.10
  111.5 0.8 fusion.13
  112.3 0.8 fusion.16
  113.2 5.9 %shard_map.110 = bf16[256,1280]{1,0:T(8,128)(2,1)S(1)} custom-call(s32[4,4]{1,0:T(4,128)S(1)} %copy-done.2, bf16[10,256,128]{2,1,0:T(8,128)(2,1)S(1)} %get-tuple-element.53.refs_0_, bf16[2,10,128,128]{3,2,1,0:T(8,128)(2,1)S(1)} %get-tuple-element.31.refs_1_, bf16[2,10,128,128]{3,2,1,0:T(8,128)(2,1)S(1)} %get-tuple-element.46.refs_2_, ...), custom_call_target="tpu_custom_call" | custom-call | flops 1342177280 | bytes 6553600 | tf_op jit(solution)/shard_map/pallas_call | solution.py:96
  119.1 4.1 %convolution_convert_fusion = bf16[256,5120]{1,0:T(8,128)(2,1)S(1)} fusion(bf16[256,1280]{1,0:T(8,128)(2,1)S(1)} %shard_map.110, bf16[1280,5120]{1,0:T(8,128)(2,1)S(1)} %bitcast.77), kind=kOutput, calls=%fused_computation | convolution fusion | flops 3356753920 | bytes 16384000 | tf_op jit(solution)/shard_map/dot_general | solution.py:220
  123.6 1.2 collective-permute-start.30
  125.0 0.8 fusion.19
  125.9 1.3 collective-permute-start.32
  127.2 0.8 fusion.22
  128.3 8.9 %collective-permute-done.29 = bf16[256,1024]{1,0:T(8,128)(2,1)S(1)} collective-permute-done((bf16[256,1024]{1,0:T(8,128)(2,1)S(1)}, bf16[256,1024]{1,0:T(8,128)(2,1)S(1)}, u32[]{:S(2)}, u32[]{:S(2)}) %collective-permute-start.29) | collective-permute-done | bytes 524320 | tf_op jit(solution)/shard_map/ppermute | solution.py:227
  137.6 10.9 %collective-permute-done.30 = bf16[256,1024]{1,0:T(8,128)(2,1)S(1)} collective-permute-done((bf16[256,1024]{1,0:T(8,128)(2,1)S(1)}, bf16[256,1024]{1,0:T(8,128)(2,1)S(1)}, u32[]{:S(2)}, u32[]{:S(2)}) %collective-permute-start.30) | collective-permute-done | bytes 524320 | tf_op jit(solution)/shard_map/ppermute | solution.py:227
  148.8 10.9 %collective-permute-done.31 = bf16[256,1024]{1,0:T(8,128)(2,1)S(1)} collective-permute-done((bf16[256,1024]{1,0:T(8,128)(2,1)S(1)}, bf16[256,1024]{1,0:T(8,128)(2,1)S(1)}, u32[]{:S(2)}, u32[]{:S(2)}) %collective-permute-start.31) | collective-permute-done | bytes 524320 | tf_op jit(solution)/shard_map/ppermute | solution.py:227
  160.0 10.9 %collective-permute-done.32 = bf16[256,1024]{1,0:T(8,128)(2,1)S(1)} collective-permute-done((bf16[256,1024]{1,0:T(8,128)(2,1)S(1)}, bf16[256,1024]{1,0:T(8,128)(2,1)S(1)}, u32[]{:S(2)}, u32[]{:S(2)}) %collective-permute-start.32) | collective-permute-done | bytes 524320 | tf_op jit(solution)/shard_map/ppermute | solution.py:227
  171.3 1.5 copy.16
  172.8 7.0 %collective-permute-done.33 = bf16[256,1024]{1,0:T(8,128)(2,1)S(1)} collective-permute-done((bf16[256,1024]{1,0:T(8,128)(2,1)S(1)}, bf16[256,1024]{1,0:T(8,128)(2,1)S(1)}, u32[]{:S(2)}, u32[]{:S(2)}) %collective-permute-start.33) | collective-permute-done | bytes 524320 | tf_op jit(solution)/shard_map/ppermute | solution.py:227
  179.7 1.1 fusion.31
  (68 shorter events, 4.6 us)
Async XLA Ops:
  0.0 28.9 %copy-start = (f32[16,5120]{1,0:T(8,128)S(1)}, f32[16,5120]{1,0:T(8,128)}, u32[]{:S(2)}) copy-start(f32[16,5120]{1,0:T(8,128)} %param.18) | copy-start | bytes 983044
  0.0 1.0 copy-start.7
  0.0 1.1 copy-start.6
  0.0 4.5 %copy-start.5 = (bf16[1,1,256,20,128]{4,2,3,1,0:T(8,128)(2,1)S(1)}, bf16[1,1,256,20,128]{4,2,3,1,0:T(8,128)(2,1)}, u32[]{:S(2)}) copy-start(bf16[1,1,256,20,128]{4,2,3,1,0:T(8,128)(2,1)} %param.13) | copy-start | bytes 3932164
  1.2 8.8 %collective-permute-start.5 = (bf16[2,10,64,128]{3,2,1,0:T(8,128)(2,1)S(1)}, bf16[2,10,64,128]{3,2,1,0:T(8,128)(2,1)}, u32[]{:S(2)}, u32[]{:S(2)}) collective-permute-start(bf16[2,10,64,128]{3,2,1,0:T(8,128)(2,1)S(1)} %pad_maximum_fusion.7), channel_id=1, source_target_pairs={{0,4},{4,0},{1,5},{5,1},{2,6},{6,2},{3,7},{7,3},{8,12},{12,8},{9,1... | collective-permute-start | bytes 983048 | tf_op jit(solution)/shard_map/ppermute | solution.py:155
  3.2 12.9 %collective-permute-start = (bf16[2,10,64,128]{3,2,1,0:T(8,128)(2,1)}, bf16[2,10,64,128]{3,2,1,0:T(8,128)(2,1)}, u32[]{:S(2)}, u32[]{:S(2)}) collective-permute-start(bf16[2,10,64,128]{3,2,1,0:T(8,128)(2,1)} %pad_maximum_fusion.6), channel_id=1, source_target_pairs={{0,24},{1,25},{2,26},{3,27},{4,28},{5,29},{6,30},{7,31}} | collective-permute-start | bytes 983048 | tf_op jit(solution)/shard_map/ppermute | solution.py:164
  6.0 7.6 %copy-start.8 = (s32[4]{0:T(128)S(1)}, s32[4]{0:T(128)}, u32[]{:S(2)}) copy-start(s32[4]{0:T(128)} %param.19) | copy-start | bytes 52
  10.0 12.5 %collective-permute-start.6 = (bf16[2,10,64,128]{3,2,1,0:T(8,128)(2,1)}, bf16[2,10,64,128]{3,2,1,0:T(8,128)(2,1)}, u32[]{:S(2)}, u32[]{:S(2)}) collective-permute-start(bf16[2,10,64,128]{3,2,1,0:T(8,128)(2,1)} %collective-permute-done.5), channel_id=1, source_target_pairs={{0,24},{1,25},{2,26},{3,27},{4,28},{5,29},{6,30},{7,31}} | collective-permute-start | bytes 983048 | tf_op jit(solution)/shard_map/ppermute | solution.py:164
  12.4 39.6 %collective-permute-start.11 = (bf16[2,10,256,128]{3,2,1,0:T(8,128)(2,1)}, bf16[2,10,256,128]{3,2,1,0:T(8,128)(2,1)}, u32[]{:S(2)}, u32[]{:S(2)}) collective-permute-start(bf16[2,10,256,128]{3,2,1,0:T(8,128)(2,1)} %pad_maximum_fusion), channel_id=1, source_target_pairs={{0,4},{4,0},{1,5},{5,1},{2,6},{6,2},{3,7},{7,3},{8,12},{12,8},{9,1... | collective-permute-start | bytes 3932168 | tf_op jit(solution)/shard_map/ppermute | solution.py:157
  17.2 12.4 %collective-permute-start.1 = (bf16[2,10,64,128]{3,2,1,0:T(8,128)(2,1)S(1)}, bf16[2,10,64,128]{3,2,1,0:T(8,128)(2,1)S(1)}, u32[]{:S(2)}, u32[]{:S(2)}) collective-permute-start(bf16[2,10,64,128]{3,2,1,0:T(8,128)(2,1)S(1)} %broadcast_select_fusion.11), channel_id=1, source_target_pairs={{0,1},{1,2},{2,3},{4,5},{5,6},{6,7},{8,9},{9,10},{10,11},{12,13},{... | collective-permute-start | bytes 983048 | tf_op jit(solution)/shard_map/ppermute | solution.py:177
  18.5 12.4 %collective-permute-start.3 = (bf16[2,10,64,128]{3,2,1,0:T(8,128)(2,1)S(1)}, bf16[2,10,64,128]{3,2,1,0:T(8,128)(2,1)S(1)}, u32[]{:S(2)}, u32[]{:S(2)}) collective-permute-start(bf16[2,10,64,128]{3,2,1,0:T(8,128)(2,1)S(1)} %broadcast_select_fusion.11), channel_id=1, source_target_pairs={{1,0},{2,1},{3,2},{5,4},{6,5},{7,6},{9,8},{10,9},{11,10},{13,12},{... | collective-permute-start | bytes 983048 | tf_op jit(solution)/shard_map/ppermute | solution.py:178
  23.6 11.1 %collective-permute-start.7 = (bf16[2,10,64,128]{3,2,1,0:T(8,128)(2,1)S(1)}, bf16[2,10,64,128]{3,2,1,0:T(8,128)(2,1)}, u32[]{:S(2)}, u32[]{:S(2)}) collective-permute-start(bf16[2,10,64,128]{3,2,1,0:T(8,128)(2,1)S(1)} %broadcast_select_fusion.10), channel_id=1, source_target_pairs={{0,1},{1,2},{2,3},{4,5},{5,6},{6,7},{8,9},{9,10},{10,11},{12,13},{... | collective-permute-start | bytes 983048 | tf_op jit(solution)/shard_map/ppermute | solution.py:177
  24.9 11.1 %collective-permute-start.8 = (bf16[2,10,64,128]{3,2,1,0:T(8,128)(2,1)S(1)}, bf16[2,10,64,128]{3,2,1,0:T(8,128)(2,1)S(1)}, u32[]{:S(2)}, u32[]{:S(2)}) collective-permute-start(bf16[2,10,64,128]{3,2,1,0:T(8,128)(2,1)S(1)} %broadcast_select_fusion.10), channel_id=1, source_target_pairs={{1,0},{2,1},{3,2},{5,4},{6,5},{7,6},{9,8},{10,9},{11,10},{13,12},{... | collective-permute-start | bytes 983048 | tf_op jit(solution)/shard_map/ppermute | solution.py:178
  29.6 12.1 %collective-permute-start.2 = (bf16[2,10,64,128]{3,2,1,0:T(8,128)(2,1)S(1)}, bf16[2,10,64,128]{3,2,1,0:T(8,128)(2,1)S(1)}, u32[]{:S(2)}, u32[]{:S(2)}) collective-permute-start(bf16[2,10,64,128]{3,2,1,0:T(8,128)(2,1)S(1)} %collective-permute-done.1), channel_id=1, source_target_pairs={{1,2},{2,3},{5,6},{6,7},{9,10},{10,11},{13,14},{14,15},{17,18},{18... | collective-permute-start | bytes 983048 | tf_op jit(solution)/shard_map/ppermute | solution.py:177
  30.9 19.0 %collective-permute-start.4 = (bf16[2,10,64,128]{3,2,1,0:T(8,128)(2,1)S(1)}, bf16[2,10,64,128]{3,2,1,0:T(8,128)(2,1)S(1)}, u32[]{:S(2)}, u32[]{:S(2)}) collective-permute-start(bf16[2,10,64,128]{3,2,1,0:T(8,128)(2,1)S(1)} %collective-permute-done.3), channel_id=1, source_target_pairs={{1,0},{2,1},{5,4},{6,5},{9,8},{10,9},{13,12},{14,13},{17,16},{18,1... | collective-permute-start | bytes 983048 | tf_op jit(solution)/shard_map/ppermute | solution.py:178
  34.7 13.9 %collective-permute-start.9 = (bf16[2,10,64,128]{3,2,1,0:T(8,128)(2,1)}, bf16[2,10,64,128]{3,2,1,0:T(8,128)(2,1)S(1)}, u32[]{:S(2)}, u32[]{:S(2)}) collective-permute-start(bf16[2,10,64,128]{3,2,1,0:T(8,128)(2,1)} %collective-permute-done.7), channel_id=1, source_target_pairs={{1,2},{2,3},{5,6},{6,7},{9,10},{10,11},{13,14},{14,15},{17,18},{18... | collective-permute-start | bytes 983048 | tf_op jit(solution)/shard_map/ppermute | solution.py:177
  36.0 15.3 %collective-permute-start.10 = (bf16[2,10,64,128]{3,2,1,0:T(8,128)(2,1)S(1)}, bf16[2,10,64,128]{3,2,1,0:T(8,128)(2,1)S(1)}, u32[]{:S(2)}, u32[]{:S(2)}) collective-permute-start(bf16[2,10,64,128]{3,2,1,0:T(8,128)(2,1)S(1)} %collective-permute-done.8), channel_id=1, source_target_pairs={{1,0},{2,1},{5,4},{6,5},{9,8},{10,9},{13,12},{14,13},{17,16},{18,1... | collective-permute-start | bytes 983048 | tf_op jit(solution)/shard_map/ppermute | solution.py:178
  41.7 31.3 %collective-permute-start.24 = (bf16[2,10,128,128]{3,2,1,0:T(8,128)(2,1)S(1)}, bf16[2,10,128,128]{3,2,1,0:T(8,128)(2,1)S(1)}, u32[]{:S(2)}, u32[]{:S(2)}) collective-permute-start(bf16[2,10,128,128]{3,2,1,0:T(8,128)(2,1)S(1)} %get-tuple-element.35.refs_1_), channel_id=1, source_target_pairs={{8,24},{9,25},{10,26},{11,27},{12,28},{13,29},{14,30},{15,31}} | collective-permute-start | bytes 1966088 | tf_op jit(solution)/shard_map/ppermute | solution.py:206
  48.6 25.7 %collective-permute-start.26 = (bf16[2,10,128,128]{3,2,1,0:T(8,128)(2,1)S(1)}, bf16[2,10,128,128]{3,2,1,0:T(8,128)(2,1)S(1)}, u32[]{:S(2)}, u32[]{:S(2)}) collective-permute-start(bf16[2,10,128,128]{3,2,1,0:T(8,128)(2,1)S(1)} %get-tuple-element.36.refs_2_), channel_id=1, source_target_pairs={{8,24},{9,25},{10,26},{11,27},{12,28},{13,29},{14,30},{15,31}} | collective-permute-start | bytes 1966088 | tf_op jit(solution)/shard_map/ppermute | solution.py:206
  49.9 10.1 %collective-permute-start.12 = (bf16[2,10,64,128]{3,2,1,0:T(8,128)(2,1)S(1)}, bf16[2,10,64,128]{3,2,1,0:T(8,128)(2,1)S(1)}, u32[]{:S(2)}, u32[]{:S(2)}) collective-permute-start(bf16[2,10,64,128]{3,2,1,0:T(8,128)(2,1)S(1)} %collective-permute-done.2), channel_id=1, source_target_pairs={{2,3},{6,7},{10,11},{14,15},{18,19},{22,23},{26,27},{30,31}} | collective-permute-start | bytes 983048 | tf_op jit(solution)/shard_map/ppermute | solution.py:177
  51.3 19.6 %collective-permute-start.14 = (bf16[2,10,64,128]{3,2,1,0:T(8,128)(2,1)S(1)}, bf16[2,10,64,128]{3,2,1,0:T(8,128)(2,1)S(1)}, u32[]{:S(2)}, u32[]{:S(2)}) collective-permute-start(bf16[2,10,64,128]{3,2,1,0:T(8,128)(2,1)S(1)} %collective-permute-done.4), channel_id=1, source_target_pairs={{1,0},{5,4},{9,8},{13,12},{17,16},{21,20},{25,24},{29,28}} | collective-permute-start | bytes 983048 | tf_op jit(solution)/shard_map/ppermute | solution.py:178
  52.0 15.0 %collective-permute-start.13 = (bf16[2,10,64,128]{3,2,1,0:T(8,128)(2,1)S(1)}, bf16[2,10,64,128]{3,2,1,0:T(8,128)(2,1)S(1)}, u32[]{:S(2)}, u32[]{:S(2)}) collective-permute-start(bf16[2,10,64,128]{3,2,1,0:T(8,128)(2,1)S(1)} %collective-permute-done.9), channel_id=1, source_target_pairs={{2,3},{6,7},{10,11},{14,15},{18,19},{22,23},{26,27},{30,31}} | collective-permute-start | bytes 983048 | tf_op jit(solution)/shard_map/ppermute | solution.py:177
  60.0 16.2 %collective-permute-start.15 = (bf16[2,10,64,128]{3,2,1,0:T(8,128)(2,1)S(1)}, bf16[2,10,64,128]{3,2,1,0:T(8,128)(2,1)S(1)}, u32[]{:S(2)}, u32[]{:S(2)}) collective-permute-start(bf16[2,10,64,128]{3,2,1,0:T(8,128)(2,1)S(1)} %collective-permute-done.10), channel_id=1, source_target_pairs={{1,0},{5,4},{9,8},{13,12},{17,16},{21,20},{25,24},{29,28}} | collective-permute-start | bytes 983048 | tf_op jit(solution)/shard_map/ppermute | solution.py:178
  67.0 12.2 %collective-permute-start.22 = (bf16[2,10,128,128]{3,2,1,0:T(8,128)(2,1)S(1)}, bf16[2,10,128,128]{3,2,1,0:T(8,128)(2,1)S(1)}, u32[]{:S(2)}, u32[]{:S(2)}) collective-permute-start(bf16[2,10,128,128]{3,2,1,0:T(8,128)(2,1)S(1)} %get-tuple-element.37.refs_9_), channel_id=1, source_target_pairs={{0,8},{16,24},{24,16},{1,9},{17,25},{25,17},{2,10},{18,26},{26,18}... | collective-permute-start | bytes 1966088 | tf_op jit(solution)/shard_map/ppermute | solution.py:194
  70.9 9.6 %copy-start.4 = (bf16[1,1,256,20,128]{4,2,3,1,0:T(8,128)(2,1)S(1)}, bf16[1,1,256,20,128]{4,2,3,1,0:T(8,128)(2,1)}, u32[]{:S(2)}) copy-start(bf16[1,1,256,20,128]{4,2,3,1,0:T(8,128)(2,1)} %param.11) | copy-start | bytes 3932164
  70.9 9.7 %collective-permute-start.23 = (bf16[2,10,128,128]{3,2,1,0:T(8,128)(2,1)S(1)}, bf16[2,10,128,128]{3,2,1,0:T(8,128)(2,1)S(1)}, u32[]{:S(2)}, u32[]{:S(2)}) collective-permute-start(bf16[2,10,128,128]{3,2,1,0:T(8,128)(2,1)S(1)} %get-tuple-element.38.refs_10_), channel_id=1, source_target_pairs={{0,8},{16,24},{24,16},{1,9},{17,25},{25,17},{2,10},{18,26},{26,18}... | collective-permute-start | bytes 1966088 | tf_op jit(solution)/shard_map/ppermute | solution.py:194
  73.0 11.6 %collective-permute-start.18 = (bf16[2,10,128,128]{3,2,1,0:T(8,128)(2,1)S(1)}, bf16[2,10,128,128]{3,2,1,0:T(8,128)(2,1)S(1)}, u32[]{:S(2)}, u32[]{:S(2)}) collective-permute-start(bf16[2,10,128,128]{3,2,1,0:T(8,128)(2,1)S(1)} %get-tuple-element.31.refs_1_), channel_id=1, source_target_pairs={{8,24},{9,25},{10,26},{11,27},{12,28},{13,29},{14,30},{15,31}} | collective-permute-start | bytes 1966088 | tf_op jit(solution)/shard_map/ppermute | solution.py:206
  74.4 6.6 %collective-permute-start.25 = (bf16[2,10,128,128]{3,2,1,0:T(8,128)(2,1)S(1)}, bf16[2,10,128,128]{3,2,1,0:T(8,128)(2,1)S(1)}, u32[]{:S(2)}, u32[]{:S(2)}) collective-permute-start(bf16[2,10,128,128]{3,2,1,0:T(8,128)(2,1)S(1)} %collective-permute-done.24.refs_5_), channel_id=1, source_target_pairs={{24,16},{25,17},{26,18},{27,19},{28,20},{29,21},{30,22},{31,23}} | collective-permute-start | bytes 1966088 | tf_op jit(solution)/shard_map/ppermute | solution.py:207
  76.2 10.4 %collective-permute-start.27 = (bf16[2,10,128,128]{3,2,1,0:T(8,128)(2,1)S(1)}, bf16[2,10,128,128]{3,2,1,0:T(8,128)(2,1)S(1)}, u32[]{:S(2)}, u32[]{:S(2)}) collective-permute-start(bf16[2,10,128,128]{3,2,1,0:T(8,128)(2,1)S(1)} %collective-permute-done.26.refs_7_), channel_id=1, source_target_pairs={{24,16},{25,17},{26,18},{27,19},{28,20},{29,21},{30,22},{31,23}} | collective-permute-start | bytes 1966088 | tf_op jit(solution)/shard_map/ppermute | solution.py:207
  77.7 15.5 %copy-start.2 = (s32[4,4]{1,0:T(4,128)S(1)}, s32[4,4]{1,0:T(4,128)}, u32[]{:S(2)}) copy-start(s32[4,4]{1,0:T(4,128)} %mask.7) | copy-start | bytes 196
  79.2 12.5 %collective-permute-start.20 = (bf16[2,10,128,128]{3,2,1,0:T(8,128)(2,1)S(1)}, bf16[2,10,128,128]{3,2,1,0:T(8,128)(2,1)S(1)}, u32[]{:S(2)}, u32[]{:S(2)}) collective-permute-start(bf16[2,10,128,128]{3,2,1,0:T(8,128)(2,1)S(1)} %get-tuple-element.46.refs_2_), channel_id=1, source_target_pairs={{8,24},{9,25},{10,26},{11,27},{12,28},{13,29},{14,30},{15,31}} | collective-permute-start | bytes 1966088 | tf_op jit(solution)/shard_map/ppermute | solution.py:206
  80.6 18.2 %collective-permute-start.28 = (bf16[10,256,128]{2,1,0:T(8,128)(2,1)S(1)}, bf16[10,256,128]{2,1,0:T(8,128)(2,1)S(1)}, u32[]{:S(2)}, u32[]{:S(2)}) collective-permute-start(bf16[10,256,128]{2,1,0:T(8,128)(2,1)S(1)} %get-tuple-element.54), channel_id=1, source_target_pairs={{0,4},{4,0},{1,5},{5,1},{2,6},{6,2},{3,7},{7,3},{8,12},{12,8},{9,1... | collective-permute-start | bytes 1966088 | tf_op jit(solution)/shard_map/ppermute | solution.py:159
  80.9 23.4 %collective-permute-start.16 = (bf16[2,10,128,128]{3,2,1,0:T(8,128)(2,1)S(1)}, bf16[2,10,128,128]{3,2,1,0:T(8,128)(2,1)S(1)}, u32[]{:S(2)}, u32[]{:S(2)}) collective-permute-start(bf16[2,10,128,128]{3,2,1,0:T(8,128)(2,1)S(1)} %get-tuple-element.34.refs_9_), channel_id=1, source_target_pairs={{0,8},{16,24},{24,16},{1,9},{17,25},{25,17},{2,10},{18,26},{26,18}... | collective-permute-start | bytes 1966088 | tf_op jit(solution)/shard_map/ppermute | solution.py:194
  84.7 19.7 %collective-permute-start.17 = (bf16[2,10,128,128]{3,2,1,0:T(8,128)(2,1)S(1)}, bf16[2,10,128,128]{3,2,1,0:T(8,128)(2,1)S(1)}, u32[]{:S(2)}, u32[]{:S(2)}) collective-permute-start(bf16[2,10,128,128]{3,2,1,0:T(8,128)(2,1)S(1)} %get-tuple-element.45.refs_10_), channel_id=1, source_target_pairs={{0,8},{16,24},{24,16},{1,9},{17,25},{25,17},{2,10},{18,26},{26,18}... | collective-permute-start | bytes 1966088 | tf_op jit(solution)/shard_map/ppermute | solution.py:194
  86.6 17.8 %collective-permute-start.19 = (bf16[2,10,128,128]{3,2,1,0:T(8,128)(2,1)S(1)}, bf16[2,10,128,128]{3,2,1,0:T(8,128)(2,1)S(1)}, u32[]{:S(2)}, u32[]{:S(2)}) collective-permute-start(bf16[2,10,128,128]{3,2,1,0:T(8,128)(2,1)S(1)} %collective-permute-done.18.refs_5_), channel_id=1, source_target_pairs={{24,16},{25,17},{26,18},{27,19},{28,20},{29,21},{30,22},{31,23}} | collective-permute-start | bytes 1966088 | tf_op jit(solution)/shard_map/ppermute | solution.py:207
  91.7 12.7 %collective-permute-start.21 = (bf16[2,10,128,128]{3,2,1,0:T(8,128)(2,1)S(1)}, bf16[2,10,128,128]{3,2,1,0:T(8,128)(2,1)S(1)}, u32[]{:S(2)}, u32[]{:S(2)}) collective-permute-start(bf16[2,10,128,128]{3,2,1,0:T(8,128)(2,1)S(1)} %collective-permute-done.20.refs_7_), channel_id=1, source_target_pairs={{24,16},{25,17},{26,18},{27,19},{28,20},{29,21},{30,22},{31,23}} | collective-permute-start | bytes 1966088 | tf_op jit(solution)/shard_map/ppermute | solution.py:207
  93.2 17.3 %slice-start = ((s8[13107200]{0:T(1024)(128)(4,1)}), s8[4194304]{0:T(1024)(128)(4,1)S(1)}, s32[]{:S(2)}) async-start(s8[13107200]{0:T(1024)(128)(4,1)} %bitcast.76), calls=%async_computation | async-start | bytes 8388608
  93.2 17.3 %slice-start.1 = ((s8[13107200]{0:T(1024)(128)(4,1)}), s8[4194304]{0:T(1024)(128)(4,1)S(1)}, s32[]{:S(2)}) async-start(s8[13107200]{0:T(1024)(128)(4,1)} %bitcast.76), calls=%async_computation.1 | async-start | bytes 8388608
  98.8 11.8 %slice-start.2 = ((s8[13107200]{0:T(1024)(128)(4,1)}), s8[4194304]{0:T(1024)(128)(4,1)S(1)}, s32[]{:S(2)}) async-start(s8[13107200]{0:T(1024)(128)(4,1)} %bitcast.76), calls=%async_computation.2 | async-start | bytes 8388608
  104.4 6.2 %slice-start.3 = ((s8[13107200]{0:T(1024)(128)(4,1)}), s8[524288]{0:T(1024)(128)(4,1)S(1)}, s32[]{:S(2)}) async-start(s8[13107200]{0:T(1024)(128)(4,1)} %bitcast.76), calls=%async_computation.3 | async-start | bytes 1048576
  123.2 14.0 %collective-permute-start.29 = (bf16[256,1024]{1,0:T(8,128)(2,1)S(1)}, bf16[256,1024]{1,0:T(8,128)(2,1)S(1)}, u32[]{:S(2)}, u32[]{:S(2)}) collective-permute-start(bf16[256,1024]{1,0:T(8,128)(2,1)S(1)} %fusion.10), channel_id=1, source_target_pairs={{4,0},{0,4},{5,1},{1,5},{6,2},{2,6},{7,3},{3,7},{12,8},{8,12},{13,... | collective-permute-start | bytes 1572872 | tf_op jit(solution)/shard_map/ppermute | solution.py:227
  123.6 24.9 %collective-permute-start.30 = (bf16[256,1024]{1,0:T(8,128)(2,1)S(1)}, bf16[256,1024]{1,0:T(8,128)(2,1)S(1)}, u32[]{:S(2)}, u32[]{:S(2)}) collective-permute-start(bf16[256,1024]{1,0:T(8,128)(2,1)S(1)} %fusion.13), channel_id=1, source_target_pairs={{4,0},{0,4},{5,1},{1,5},{6,2},{2,6},{7,3},{3,7},{12,8},{8,12},{13,... | collective-permute-start | bytes 1572872 | tf_op jit(solution)/shard_map/ppermute | solution.py:227
  124.8 34.9 %collective-permute-start.31 = (bf16[256,1024]{1,0:T(8,128)(2,1)S(1)}, bf16[256,1024]{1,0:T(8,128)(2,1)S(1)}, u32[]{:S(2)}, u32[]{:S(2)}) collective-permute-start(bf16[256,1024]{1,0:T(8,128)(2,1)S(1)} %fusion.16), channel_id=1, source_target_pairs={{4,0},{0,4},{5,1},{1,5},{6,2},{2,6},{7,3},{3,7},{12,8},{8,12},{13,... | collective-permute-start | bytes 1572872 | tf_op jit(solution)/shard_map/ppermute | solution.py:227
  125.9 11.4 %copy-start.3 = (bf16[1,1,256,5120]{3,2,1,0:T(8,128)(2,1)S(1)}, bf16[1,1,256,5120]{3,2,1,0:T(8,128)(2,1)}, u32[]{:S(2)}) copy-start(bf16[1,1,256,5120]{3,2,1,0:T(8,128)(2,1)} %param.16) | copy-start | bytes 7864324
  125.9 45.1 %collective-permute-start.32 = (bf16[256,1024]{1,0:T(8,128)(2,1)S(1)}, bf16[256,1024]{1,0:T(8,128)(2,1)S(1)}, u32[]{:S(2)}, u32[]{:S(2)}) collective-permute-start(bf16[256,1024]{1,0:T(8,128)(2,1)S(1)} %fusion.19), channel_id=1, source_target_pairs={{4,0},{0,4},{5,1},{1,5},{6,2},{2,6},{7,3},{3,7},{12,8},{8,12},{13,... | collective-permute-start | bytes 1572872 | tf_op jit(solution)/shard_map/ppermute | solution.py:227
  128.0 51.7 %collective-permute-start.33 = (bf16[256,1024]{1,0:T(8,128)(2,1)S(1)}, bf16[256,1024]{1,0:T(8,128)(2,1)S(1)}, u32[]{:S(2)}, u32[]{:S(2)}) collective-permute-start(bf16[256,1024]{1,0:T(8,128)(2,1)S(1)} %fusion.22), channel_id=1, source_target_pairs={{4,0},{0,4},{5,1},{1,5},{6,2},{2,6},{7,3},{3,7},{12,8},{8,12},{13,... | collective-permute-start | bytes 1572872 | tf_op jit(solution)/shard_map/ppermute | solution.py:227
  171.3 9.5 %copy-start.1 = (f32[16,5120]{1,0:T(8,128)S(1)}, f32[16,5120]{1,0:T(8,128)}, u32[]{:S(2)}) copy-start(f32[16,5120]{1,0:T(8,128)} %param.18) | copy-start | bytes 983044

commit v3 on v2

--- a/solution.py
+++ b/solution.py
@@ -134,11 +134,14 @@
     )[None, None]
 
 
+def permute(array, axis, pairs):
+    return lax.ppermute(array, axis, pairs)
+
+
 def sublayer(sizes, queries, keys, values, ctx_keys, ctx_values, hidden, out_weight, gates, levels, span_mask, prefix):
     spans, splits, branches = sizes
     span = lax.axis_index("tm")
     part = lax.axis_index("head")
-    branch = lax.axis_index("branch")
     to_heads = lambda a: jnp.transpose(a, (1, 0, 2))
     q, k, v = to_heads(queries), to_heads(keys), to_heads(values)
     ck, cv = to_heads(ctx_keys), to_heads(ctx_values)
@@ -152,65 +155,53 @@
 
     ctx_parts, kv_parts, q_parts = [pair(ck, cv, 0)], [pair(k, v, 0)], [take(q, 0)]
     for d in range(1, splits):
-        ctx_parts.append(lax.ppermute(pair(ck, cv, d), "head", cycle(d)))
-    for d in range(1, splits):
-        kv_parts.append(lax.ppermute(pair(k, v, d), "head", cycle(d)))
-    for d in range(1, splits):
-        q_parts.append(lax.ppermute(take(q, d), "head", cycle(d)))
+        ctx_parts.append(permute(pair(ck, cv, d), "head", cycle(d)))
+    for d in range(1, splits):
+        kv_parts.append(permute(pair(k, v, d), "head", cycle(d)))
+    for d in range(1, splits):
+        q_parts.append(permute(take(q, d), "head", cycle(d)))
 
     use_context = span < prefix[0]
     final = spans - 1
     stands_in = span == final
-    bases = [jnp.where(stands_in, lax.ppermute(a, "tm", [(0, final)]), a) for a in ctx_parts]
-    up, down = [[a] for a in bases], [[a] for a in bases]
-    piece_rows, rows = splits * bases[0].shape[2], k.shape[1]
-    own, passed, held = [], [], []
-    for s in range(branches):
-        pieces = []
-        for d in range(splits):
-            piece = bases[d]
-            if s > 0:
-                if s == branches - 1 and d == 0:
-                    up[0][-1], gate_row = lax.optimization_barrier((up[0][-1], gate_row))
-                rise = [(i, i + 1) for i in range(s - 1, branches - 1)]
-                fall = [(i, i - 1) for i in range(1, branches - s + 1)]
-                up[d].append(lax.ppermute(up[d][-1], "branch", rise))
-                down[d].append(lax.ppermute(down[d][-1], "branch", fall))
-                piece = up[d][s]
-            pieces.append(piece)
-        if s > 0:
-            merged, *pieces = lax.optimization_barrier(((own[-1], passed[-1]), *pieces))
-            held[-1] = merged
-            for d in range(splits):
-                for t in range(1, s + 1):
-                    pieces[d] = jnp.where(branch == s - t, down[d][t], pieces[d])
-        d, at = divmod(s * piece_rows, rows)
-        context, mine = jnp.concatenate(pieces, axis=2), kv_parts[d][:, :, at : at + piece_rows]
-        own.append(jnp.where(use_context, context, mine))
-        passed.append(jnp.where(use_context | stands_in, context, mine))
+    first = jnp.concatenate(ctx_parts, axis=2)
+    first = jnp.where(stands_in, permute(first, "tm", [(0, final)]), first)
+    pieces, own, passed, held = [first], [], [], []
+    piece_rows, rows = pieces[0].shape[2], k.shape[1]
+    for i in range(1, branches):
+        low = i & -i
+        pieces.append(permute(pieces[i - low], "branch", [(b, b ^ low) for b in range(branches)]))
+    for i, piece in enumerate(pieces):
+        if own:
+            held[-1], piece = lax.optimization_barrier(((own[-1], passed[-1]), piece))
+        d, at = divmod(i * piece_rows, rows)
+        mine = kv_parts[d][:, :, at : at + piece_rows]
+        own.append(jnp.where(use_context, piece, mine))
+        passed.append(jnp.where(use_context | stands_in, piece, mine))
         held.append((own[-1], passed[-1]))
 
     pairs = [(i, i + 1) for i in range(0, spans, 2)]
-    beside = [lax.ppermute(a, "tm", pairs + [(final, final - 1)]) for a in passed]
+    beside = [permute(a, "tm", pairs + [(final, final - 1)]) for a in passed]
     slots = [
         (None, [a for a, _ in held]),
         (lambda c: jnp.where(lax.rem(c, 2) == 1, c - 1, jnp.where(c == final - 1, 0, -1)), beside),
     ]
     for s in range(2, final - 1, 2):
-        far = [lax.ppermute(a, "tm", [(i, i + s) for i in range(spans - s)]) for a in own]
+        far = [permute(a, "tm", [(i, i + s) for i in range(spans - s)]) for a in own]
         back = [(b, a) for a, b in pairs]
-        near = [lax.ppermute(a, "tm", pairs + back) for a in far]
+        near = [permute(a, "tm", pairs + back) for a in far]
         slots.append((lambda c, s=s: c - s, far))
         slots.append((lambda c, s=s: c + 1 - 2 * lax.rem(c, 2) - s, near))
     s = final - 1
-    far = [lax.ppermute(a, "tm", [(1, final)]) for a in own]
-    near = [lax.ppermute(a, "tm", [(final, final - 1)]) for a in far]
+    far = [permute(a, "tm", [(1, final)]) for a in own]
+    near = [permute(a, "tm", [(final, final - 1)]) for a in far]
     slots.append((lambda c: jnp.where(c >= final - 1, 1, -1), list(zip(far, near))))
     slots.append((lambda c: jnp.where(c == final, 0, -1), [a for _, a in held]))
 
     half = max(1, len(own) // 2)
     early = [(origin, arrays[:half]) for origin, arrays in slots]
     late = [(origin, arrays[half:]) for origin, arrays in slots]
+    q_parts[0], gate_row = lax.optimization_barrier((q_parts[0], gate_row))
     states = []
     for d in range(splits):
         states.append(attend(q_parts[d], early, span_mask, None, False))
@@ -224,7 +215,7 @@
         back = [((i + d) % splits, i) for i in range(splits)]
         for j in range(COL_BLOCKS):
             partial = project(attended, out_weight[:, j * width : (j + 1) * width])
-            returned[j].append(lax.ppermute(partial, "head", back))
+            returned[j].append(permute(partial, "head", back))
     attended = attend(q_parts[0], late, span_mask, states[0], True)
     kept = lax.optimization_barrier(project(attended, out_weight))
     updated = hidden

time: 182 us -> 184 us (1.011)
  the two profiles are of different devices: /device:TPU:29 before, /device:TPU:0 now
where the time goes in v3:
time: 184 us; the launch traced here: 183 us
  waiting for transfers between devices  80.7 us (44%)
  starting transfers between devices  45.1 us (25%)
  Pallas kernels  30.4 us (17%)
  matrix products  8.47 us (5%)
  local copies, waits for them, and re-layouts  7.68 us (4%)
  other arithmetic  7.48 us (4%)
  between operations  3.09 us (2%)
    ppermute x24, waiting for transfers between devices, permute(): return lax.ppermute(array, axis, pairs)  80.7 us
    ppermute x24, starting transfers between devices, permute(): return lax.ppermute(array, axis, pairs)  45.1 us
    pallas_call x4, Pallas kernels, attend(): pl.pallas_call(functools.partial(flash_kernel, layout=layout, count=len(a...  30.4 us
    dot_general x6, matrix products, sublayer(): jnp.dot(a, w, preferred_element_type=jnp.float32).astype(jnp.bfloat16)  8.47 us
    select_n x4, other arithmetic, sublayer(): passed.append(jnp.where(use_context | stands_in, piece, mine))  3.85 us
  transfers between devices with their start and end apart: 24, of which 9 were waited for; matrix products, arithmetic and copies ran while one was open for 7% of the time, Pallas kernels for 9%

profile of v3, /device:TPU:0, one launch (start us, length us, event | category | flops | bytes accessed | tf_op | source)
XLA Modules:
  0.0 182.9 jit_solution(642707585727231046)
XLA Ops:
  0.0 1.0 copy-done.13
  1.0 0.1 copy-done.12
  1.2 3.0 %collective-permute-start = (bf16[2,10,64,128]{3,2,1,0:T(8,128)(2,1)S(1)}, bf16[2,10,64,128]{3,2,1,0:T(8,128)(2,1)S(1)}, u32[]{:S(2)}, u32[]{:S(2)}) collective-permute-start(bf16[2,10,64,128]{3,2,1,0:T(8,128)(2,1)S(1)} %pad_maximum_fusion.3), channel_id=1, source_target_pairs={{0,4},{4,0},{1,5},{5,1},{2,6},{6,2},{3,7},{7,3},{8,12},{12,8},{9,1... | collective-permute-start | bytes 983048 | tf_op jit(solution)/shard_map/ppermute | solution.py:138
  4.2 7.7 %collective-permute-done = bf16[2,10,64,128]{3,2,1,0:T(8,128)(2,1)S(1)} collective-permute-done((bf16[2,10,64,128]{3,2,1,0:T(8,128)(2,1)S(1)}, bf16[2,10,64,128]{3,2,1,0:T(8,128)(2,1)S(1)}, u32[]{:S(2)}, u32[]{:S(2)}) %collective-permute-start) | collective-permute-done | bytes 327712 | tf_op jit(solution)/shard_map/ppermute | solution.py:138
  12.0 3.1 %collective-permute-start.1 = (bf16[2,10,128,128]{3,2,1,0:T(8,128)(2,1)S(1)}, bf16[2,10,128,128]{3,2,1,0:T(8,128)(2,1)}, u32[]{:S(2)}, u32[]{:S(2)}) collective-permute-start(bf16[2,10,128,128]{3,2,1,0:T(8,128)(2,1)S(1)} %pad_maximum_fusion.2), channel_id=1, source_target_pairs={{0,24},{1,25},{2,26},{3,27},{4,28},{5,29},{6,30},{7,31}} | collective-permute-start | bytes 1966088 | tf_op jit(solution)/shard_map/ppermute | solution.py:138
  15.1 1.9 %dynamic-slice_bitcast_fusion.1 = (bf16[1,10,256,128]{3,2,1,0:T(8,128)(2,1)S(1)}, bf16[1,10,256,128]{3,2,1,0:T(8,128)(2,1)S(1)}, bf16[1,10,256,128]{3,2,1,0:T(8,128)(2,1)S(1)}, bf16[1,10,256,128]{3,2,1,0:T(8,128)(2,1)S(1)}) fusion(bf16[1,1,256,20,128]{4,2,3,1,0:T(8,128)(2,1)} %param.13, s32[]{:T(128)S(6)} %select_n.71, s32[]{:T(128)S(6)} %select_n.66, ...), kind=kLoop, calls=%fused_computation.28 | loop fusion | bytes 5242888 | tf_op jit(solution)/shard_map/stack | solution.py:150
  17.0 1.2 pad_maximum_fusion
  18.2 1.5 collective-permute-start.4
  20.3 2.0 %collective-permute-done.1 = bf16[2,10,128,128]{3,2,1,0:T(8,128)(2,1)} collective-permute-done((bf16[2,10,128,128]{3,2,1,0:T(8,128)(2,1)S(1)}, bf16[2,10,128,128]{3,2,1,0:T(8,128)(2,1)}, u32[]{:S(2)}, u32[]{:S(2)}) %collective-permute-start.1) | collective-permute-done | bytes 655392 | tf_op jit(solution)/shard_map/ppermute | solution.py:138
  22.4 0.4 broadcast_select_fusion.3
  22.8 1.6 collective-permute-start.2
  24.4 2.6 %collective-permute-start.3 = (bf16[2,10,128,128]{3,2,1,0:T(8,128)(2,1)S(1)}, bf16[2,10,128,128]{3,2,1,0:T(8,128)(2,1)S(1)}, u32[]{:S(2)}, u32[]{:S(2)}) collective-permute-start(bf16[2,10,128,128]{3,2,1,0:T(8,128)(2,1)S(1)} %get-tuple-element.40), channel_id=1, source_target_pairs={{0,2},{1,3},{2,0},{3,1},{4,6},{5,7},{6,4},{7,5},{8,10},{9,11},{10,... | collective-permute-start | bytes 1966088 | tf_op jit(solution)/shard_map/ppermute | solution.py:138
  27.0 0.1 broadcast_select_fusion.8.refs_1_
  27.1 1.5 collective-permute-start.14
  28.6 20.1 %collective-permute-done.2 = bf16[2,10,128,128]{3,2,1,0:T(8,128)(2,1)S(1)} collective-permute-done((bf16[2,10,128,128]{3,2,1,0:T(8,128)(2,1)S(1)}, bf16[2,10,128,128]{3,2,1,0:T(8,128)(2,1)S(1)}, u32[]{:S(2)}, u32[]{:S(2)}) %collective-permute-start.2) | collective-permute-done | bytes 655392 | tf_op jit(solution)/shard_map/ppermute | solution.py:138
  48.7 2.5 %collective-permute-done.3 = bf16[2,10,128,128]{3,2,1,0:T(8,128)(2,1)S(1)} collective-permute-done((bf16[2,10,128,128]{3,2,1,0:T(8,128)(2,1)S(1)}, bf16[2,10,128,128]{3,2,1,0:T(8,128)(2,1)S(1)}, u32[]{:S(2)}, u32[]{:S(2)}) %collective-permute-start.3) | collective-permute-done | bytes 655392 | tf_op jit(solution)/shard_map/ppermute | solution.py:138
  51.2 0.3 collective-permute-start.5
  51.6 1.1 broadcast_select_fusion.2
  52.7 1.5 collective-permute-start.16
  54.2 6.4 %collective-permute-start.12 = (bf16[2,10,128,128]{3,2,1,0:T(8,128)(2,1)S(1)}, bf16[2,10,128,128]{3,2,1,0:T(8,128)(2,1)S(1)}, u32[]{:S(2)}, u32[]{:S(2)}) collective-permute-start(bf16[2,10,128,128]{3,2,1,0:T(8,128)(2,1)S(1)} %get-tuple-element.31.refs_9_), channel_id=1, source_target_pairs={{0,8},{16,24},{24,16},{1,9},{17,25},{25,17},{2,10},{18,26},{26,18}... | collective-permute-start | bytes 1966088 | tf_op jit(solution)/shard_map/ppermute | solution.py:138
  60.7 2.1 %collective-permute-start.13 = (bf16[2,10,128,128]{3,2,1,0:T(8,128)(2,1)}, bf16[2,10,128,128]{3,2,1,0:T(8,128)(2,1)}, u32[]{:S(2)}, u32[]{:S(2)}) collective-permute-start(bf16[2,10,128,128]{3,2,1,0:T(8,128)(2,1)} %get-tuple-element.32.refs_10_), channel_id=1, source_target_pairs={{0,8},{16,24},{24,16},{1,9},{17,25},{25,17},{2,10},{18,26},{26,18}... | collective-permute-start | bytes 1966088 | tf_op jit(solution)/shard_map/ppermute | solution.py:138
  62.8 1.2 broadcast_select_fusion.1
  64.0 1.5 collective-permute-start.8
  65.6 1.5 collective-permute-start.15
  67.1 1.6 collective-permute-start.17
  68.7 1.2 broadcast_select_fusion
  69.9 0.8 copy-done.8
  70.7 1.5 collective-permute-start.10
  72.3 0.7 dynamic_slice.39
  74.9 1.6 dynamic-slice_bitcast_fusion.5
  76.5 0.6 collective-permute-start.18
  77.1 5.8 %collective-permute-start.6 = (bf16[2,10,128,128]{3,2,1,0:T(8,128)(2,1)S(1)}, bf16[2,10,128,128]{3,2,1,0:T(8,128)(2,1)S(1)}, u32[]{:S(2)}, u32[]{:S(2)}) collective-permute-start(bf16[2,10,128,128]{3,2,1,0:T(8,128)(2,1)S(1)} %get-tuple-element.28.refs_9_), channel_id=1, source_target_pairs={{0,8},{16,24},{24,16},{1,9},{17,25},{25,17},{2,10},{18,26},{26,18}... | collective-permute-start | bytes 1966088 | tf_op jit(solution)/shard_map/ppermute | solution.py:138
  82.9 1.3 collective-permute-start.7
  84.3 0.7 collective-permute-start.9
  85.0 0.9 collective-permute-start.11
  86.0 0.0 slice-start
  86.0 7.9 %shard_map.109 = (f32[10,256,128]{2,1,0:T(8,128)S(1)}, f32[10,256,128]{2,1,0:T(8,128)S(1)}, f32[10,256,128]{2,1,0:T(8,128)S(1)}) custom-call(s32[4,4]{1,0:T(4,128)S(1)} %copy-done.10, bf16[10,256,128]{2,1,0:T(8,128)(2,1)S(1)} %get-tuple-element.23.refs_0_, bf16[2,10,128,128]{3,2,1,0:T(8,128)(2,1)S(1)} %copy-done.5, bf16[2,10,128,128]{3,2,1,0:T(8,128)(2,1)S(1)} %copy-done.7, ...), custom_call_target="tpu_custom_call" | custom-call | flops 1342177280 | bytes 6553600 | tf_op jit(solution)/shard_map/pallas_call | solution.py:96
  93.9 0.0 slice-start.2
  93.9 7.9 %shard_map.111 = (f32[10,256,128]{2,1,0:T(8,128)S(1)}, f32[10,256,128]{2,1,0:T(8,128)S(1)}, f32[10,256,128]{2,1,0:T(8,128)S(1)}) custom-call(s32[4,4]{1,0:T(4,128)S(1)} %copy-done.10, bf16[10,256,128]{2,1,0:T(8,128)(2,1)S(1)} %collective-permute-done.18.refs_0_, bf16[2,10,128,128]{3,2,1,0:T(8,128)(2,1)S(1)} %copy-done.5, ...), custom_call_target="tpu_custom_call" | custom-call | flops 1342177280 | bytes 6553600 | tf_op jit(solution)/shard_map/pallas_call | solution.py:96
  101.9 0.0 slice-start.3
  101.9 7.4 %shard_map.112 = bf16[256,1280]{1,0:T(8,128)(2,1)S(1)} custom-call(s32[4,4]{1,0:T(4,128)S(1)} %copy-done.10, bf16[10,256,128]{2,1,0:T(8,128)(2,1)S(1)} %collective-permute-done.18.refs_0_, bf16[2,10,128,128]{3,2,1,0:T(8,128)(2,1)S(1)} %get-tuple-element.26.refs_1_, bf16[2,10,128,128]{3,2,1,0:T(8,128)(2,1)S(1)} %get-tuple-element.42.refs_2_, ...), custom_call_target="tpu_custom_call" | custom-call | flops 1342177280 | bytes 6553600 | tf_op jit(solution)/shard_map/pallas_call | solution.py:96
  109.4 0.9 fusion.10
  110.2 0.9 fusion.13
  111.1 0.9 fusion.16
  112.0 7.2 %shard_map.110 = bf16[256,1280]{1,0:T(8,128)(2,1)S(1)} custom-call(s32[4,4]{1,0:T(4,128)S(1)} %copy-done.10, bf16[10,256,128]{2,1,0:T(8,128)(2,1)S(1)} %get-tuple-element.23.refs_0_, bf16[2,10,128,128]{3,2,1,0:T(8,128)(2,1)S(1)} %get-tuple-element.26.refs_1_, bf16[2,10,128,128]{3,2,1,0:T(8,128)(2,1)S(1)} %get-tuple-element.42.refs_2_, ...), custom_call_target="tpu_custom_call" | custom-call | flops 1342177280 | bytes 6553600 | tf_op jit(solution)/shard_map/pallas_call | solution.py:96
  119.2 4.1 %convolution_convert_fusion = bf16[256,5120]{1,0:T(8,128)(2,1)S(1)} fusion(bf16[256,1280]{1,0:T(8,128)(2,1)S(1)} %shard_map.110, bf16[1280,5120]{1,0:T(8,128)(2,1)S(1)} %bitcast.77), kind=kOutput, calls=%fused_computation | convolution fusion | flops 3356753920 | bytes 16384000 | tf_op jit(solution)/shard_map/dot_general | solution.py:211
  123.3 1.6 collective-permute-start.19
  124.9 0.5 collective-permute-start.20
  125.4 1.5 collective-permute-start.21
  126.9 0.9 fusion.19
  127.8 0.6 collective-permute-start.22
  128.4 0.9 fusion.22
  129.3 1.6 collective-permute-start.23
  130.8 7.4 %collective-permute-done.19 = bf16[256,1024]{1,0:T(8,128)(2,1)S(1)} collective-permute-done((bf16[256,1024]{1,0:T(8,128)(2,1)S(1)}, bf16[256,1024]{1,0:T(8,128)(2,1)S(1)}, u32[]{:S(2)}, u32[]{:S(2)}) %collective-permute-start.19) | collective-permute-done | bytes 524320 | tf_op jit(solution)/shard_map/ppermute | solution.py:138
  138.2 0.3 fusion.26
  138.5 10.9 %collective-permute-done.20 = bf16[256,1024]{1,0:T(8,128)(2,1)S(1)} collective-permute-done((bf16[256,1024]{1,0:T(8,128)(2,1)S(1)}, bf16[256,1024]{1,0:T(8,128)(2,1)S(1)}, u32[]{:S(2)}, u32[]{:S(2)}) %collective-permute-start.20) | collective-permute-done | bytes 524320 | tf_op jit(solution)/shard_map/ppermute | solution.py:138
  149.4 0.3 fusion.27
  149.7 10.9 %collective-permute-done.21 = bf16[256,1024]{1,0:T(8,128)(2,1)S(1)} collective-permute-done((bf16[256,1024]{1,0:T(8,128)(2,1)S(1)}, bf16[256,1024]{1,0:T(8,128)(2,1)S(1)}, u32[]{:S(2)}, u32[]{:S(2)}) %collective-permute-start.21) | collective-permute-done | bytes 524320 | tf_op jit(solution)/shard_map/ppermute | solution.py:138
  160.7 0.3 fusion.28
  161.0 10.9 %collective-permute-done.22 = bf16[256,1024]{1,0:T(8,128)(2,1)S(1)} collective-permute-done((bf16[256,1024]{1,0:T(8,128)(2,1)S(1)}, bf16[256,1024]{1,0:T(8,128)(2,1)S(1)}, u32[]{:S(2)}, u32[]{:S(2)}) %collective-permute-start.22) | collective-permute-done | bytes 524320 | tf_op jit(solution)/shard_map/ppermute | solution.py:138
  171.9 0.3 fusion.29
  172.2 1.5 copy.16
  173.7 8.2 %collective-permute-done.23 = bf16[256,1024]{1,0:T(8,128)(2,1)S(1)} collective-permute-done((bf16[256,1024]{1,0:T(8,128)(2,1)S(1)}, bf16[256,1024]{1,0:T(8,128)(2,1)S(1)}, u32[]{:S(2)}, u32[]{:S(2)}) %collective-permute-start.23) | collective-permute-done | bytes 524320 | tf_op jit(solution)/shard_map/ppermute | solution.py:138
  181.9 1.1 fusion.31
  (53 shorter events, 0.3 us)
Async XLA Ops:
  0.0 85.9 %copy-start = (f32[16,5120]{1,0:T(8,128)S(1)}, f32[16,5120]{1,0:T(8,128)}, u32[]{:S(2)}) copy-start(f32[16,5120]{1,0:T(8,128)} %param.18) | copy-start | bytes 983044
  0.0 1.0 copy-start.13
  0.0 1.1 copy-start.12
  1.2 10.7 %collective-permute-start = (bf16[2,10,64,128]{3,2,1,0:T(8,128)(2,1)S(1)}, bf16[2,10,64,128]{3,2,1,0:T(8,128)(2,1)S(1)}, u32[]{:S(2)}, u32[]{:S(2)}) collective-permute-start(bf16[2,10,64,128]{3,2,1,0:T(8,128)(2,1)S(1)} %pad_maximum_fusion.3), channel_id=1, source_target_pairs={{0,4},{4,0},{1,5},{5,1},{2,6},{6,2},{3,7},{7,3},{8,12},{12,8},{9,1... | collective-permute-start | bytes 983048 | tf_op jit(solution)/shard_map/ppermute | solution.py:138
  12.0 10.4 %collective-permute-start.1 = (bf16[2,10,128,128]{3,2,1,0:T(8,128)(2,1)S(1)}, bf16[2,10,128,128]{3,2,1,0:T(8,128)(2,1)}, u32[]{:S(2)}, u32[]{:S(2)}) collective-permute-start(bf16[2,10,128,128]{3,2,1,0:T(8,128)(2,1)S(1)} %pad_maximum_fusion.2), channel_id=1, source_target_pairs={{0,24},{1,25},{2,26},{3,27},{4,28},{5,29},{6,30},{7,31}} | collective-permute-start | bytes 1966088 | tf_op jit(solution)/shard_map/ppermute | solution.py:138
  18.2 42.5 %collective-permute-start.4 = (bf16[2,10,256,128]{3,2,1,0:T(8,128)(2,1)}, bf16[2,10,256,128]{3,2,1,0:T(8,128)(2,1)}, u32[]{:S(2)}, u32[]{:S(2)}) collective-permute-start(bf16[2,10,256,128]{3,2,1,0:T(8,128)(2,1)} %pad_maximum_fusion), channel_id=1, source_target_pairs={{0,4},{4,0},{1,5},{5,1},{2,6},{6,2},{3,7},{7,3},{8,12},{12,8},{9,1... | collective-permute-start | bytes 3932168 | tf_op jit(solution)/shard_map/ppermute | solution.py:138
  22.8 31.4 %copy-start.2 = (bf16[2,10,128,128]{3,2,1,0:T(8,128)(2,1)}, bf16[2,10,128,128]{3,2,1,0:T(8,128)(2,1)S(1)}, u32[]{:S(2)}) copy-start(bf16[2,10,128,128]{3,2,1,0:T(8,128)(2,1)S(1)} %get-tuple-element.31.refs_9_) | copy-start | bytes 1966084
  22.8 26.0 %collective-permute-start.2 = (bf16[2,10,128,128]{3,2,1,0:T(8,128)(2,1)S(1)}, bf16[2,10,128,128]{3,2,1,0:T(8,128)(2,1)S(1)}, u32[]{:S(2)}, u32[]{:S(2)}) collective-permute-start(bf16[2,10,128,128]{3,2,1,0:T(8,128)(2,1)S(1)} %get-tuple-element.40), channel_id=1, source_target_pairs={{0,1},{1,0},{2,3},{3,2},{4,5},{5,4},{6,7},{7,6},{8,9},{9,8},{10,11... | collective-permute-start | bytes 1966088 | tf_op jit(solution)/shard_map/ppermute | solution.py:138
  24.4 26.8 %collective-permute-start.3 = (bf16[2,10,128,128]{3,2,1,0:T(8,128)(2,1)S(1)}, bf16[2,10,128,128]{3,2,1,0:T(8,128)(2,1)S(1)}, u32[]{:S(2)}, u32[]{:S(2)}) collective-permute-start(bf16[2,10,128,128]{3,2,1,0:T(8,128)(2,1)S(1)} %get-tuple-element.40), channel_id=1, source_target_pairs={{0,2},{1,3},{2,0},{3,1},{4,6},{5,7},{6,4},{7,5},{8,10},{9,11},{10,... | collective-permute-start | bytes 1966088 | tf_op jit(solution)/shard_map/ppermute | solution.py:138
  27.1 36.9 %copy-start.4 = (bf16[2,10,128,128]{3,2,1,0:T(8,128)(2,1)}, bf16[2,10,128,128]{3,2,1,0:T(8,128)(2,1)S(1)}, u32[]{:S(2)}) copy-start(bf16[2,10,128,128]{3,2,1,0:T(8,128)(2,1)S(1)} %broadcast_select_fusion.8.refs_1_) | copy-start | bytes 1966084
  27.1 36.9 %collective-permute-start.14 = (bf16[2,10,128,128]{3,2,1,0:T(8,128)(2,1)S(1)}, bf16[2,10,128,128]{3,2,1,0:T(8,128)(2,1)}, u32[]{:S(2)}, u32[]{:S(2)}) collective-permute-start(bf16[2,10,128,128]{3,2,1,0:T(8,128)(2,1)S(1)} %broadcast_select_fusion.8.refs_1_), channel_id=1, source_target_pairs={{8,24},{9,25},{10,26},{11,27},{12,28},{13,29},{14,30},{15,31}} | collective-permute-start | bytes 1966088 | tf_op jit(solution)/shard_map/ppermute | solution.py:138
  51.2 14.3 %collective-permute-start.5 = (bf16[2,10,128,128]{3,2,1,0:T(8,128)(2,1)S(1)}, bf16[2,10,128,128]{3,2,1,0:T(8,128)(2,1)S(1)}, u32[]{:S(2)}, u32[]{:S(2)}) collective-permute-start(bf16[2,10,128,128]{3,2,1,0:T(8,128)(2,1)S(1)} %collective-permute-done.3), channel_id=1, source_target_pairs={{0,1},{1,0},{2,3},{3,2},{4,5},{5,4},{6,7},{7,6},{8,9},{9,8},{10,11... | collective-permute-start | bytes 1966088 | tf_op jit(solution)/shard_map/ppermute | solution.py:138
  52.7 17.2 %copy-start.6 = (bf16[2,10,128,128]{3,2,1,0:T(8,128)(2,1)}, bf16[2,10,128,128]{3,2,1,0:T(8,128)(2,1)S(1)}, u32[]{:S(2)}) copy-start(bf16[2,10,128,128]{3,2,1,0:T(8,128)(2,1)S(1)} %get-tuple-element.30.refs_2_) | copy-start | bytes 1966084
  52.7 14.4 %collective-permute-start.16 = (bf16[2,10,128,128]{3,2,1,0:T(8,128)(2,1)S(1)}, bf16[2,10,128,128]{3,2,1,0:T(8,128)(2,1)}, u32[]{:S(2)}, u32[]{:S(2)}) collective-permute-start(bf16[2,10,128,128]{3,2,1,0:T(8,128)(2,1)S(1)} %get-tuple-element.30.refs_2_), channel_id=1, source_target_pairs={{8,24},{9,25},{10,26},{11,27},{12,28},{13,29},{14,30},{15,31}} | collective-permute-start | bytes 1966088 | tf_op jit(solution)/shard_map/ppermute | solution.py:138
  54.2 15.7 %collective-permute-start.12 = (bf16[2,10,128,128]{3,2,1,0:T(8,128)(2,1)S(1)}, bf16[2,10,128,128]{3,2,1,0:T(8,128)(2,1)S(1)}, u32[]{:S(2)}, u32[]{:S(2)}) collective-permute-start(bf16[2,10,128,128]{3,2,1,0:T(8,128)(2,1)S(1)} %get-tuple-element.31.refs_9_), channel_id=1, source_target_pairs={{0,8},{16,24},{24,16},{1,9},{17,25},{25,17},{2,10},{18,26},{26,18}... | collective-permute-start | bytes 1966088 | tf_op jit(solution)/shard_map/ppermute | solution.py:138
  60.6 11.6 %copy-start.14 = (s32[4]{0:T(128)S(1)}, s32[4]{0:T(128)}, u32[]{:S(2)}) copy-start(s32[4]{0:T(128)} %param.19) | copy-start | bytes 52
  60.7 15.8 %collective-permute-start.13 = (bf16[2,10,128,128]{3,2,1,0:T(8,128)(2,1)}, bf16[2,10,128,128]{3,2,1,0:T(8,128)(2,1)}, u32[]{:S(2)}, u32[]{:S(2)}) collective-permute-start(bf16[2,10,128,128]{3,2,1,0:T(8,128)(2,1)} %get-tuple-element.32.refs_10_), channel_id=1, source_target_pairs={{0,8},{16,24},{24,16},{1,9},{17,25},{25,17},{2,10},{18,26},{26,18}... | collective-permute-start | bytes 1966088 | tf_op jit(solution)/shard_map/ppermute | solution.py:138
  64.0 18.9 %collective-permute-start.8 = (bf16[2,10,128,128]{3,2,1,0:T(8,128)(2,1)S(1)}, bf16[2,10,128,128]{3,2,1,0:T(8,128)(2,1)}, u32[]{:S(2)}, u32[]{:S(2)}) collective-permute-start(bf16[2,10,128,128]{3,2,1,0:T(8,128)(2,1)S(1)} %get-tuple-element.26.refs_1_), channel_id=1, source_target_pairs={{8,24},{9,25},{10,26},{11,27},{12,28},{13,29},{14,30},{15,31}} | collective-permute-start | bytes 1966088 | tf_op jit(solution)/shard_map/ppermute | solution.py:138
  65.6 11.5 %collective-permute-start.15 = (bf16[2,10,128,128]{3,2,1,0:T(8,128)(2,1)}, bf16[2,10,128,128]{3,2,1,0:T(8,128)(2,1)}, u32[]{:S(2)}, u32[]{:S(2)}) collective-permute-start(bf16[2,10,128,128]{3,2,1,0:T(8,128)(2,1)} %collective-permute-done.14.refs_5_), channel_id=1, source_target_pairs={{24,16},{25,17},{26,18},{27,19},{28,20},{29,21},{30,22},{31,23}} | collective-permute-start | bytes 1966088 | tf_op jit(solution)/shard_map/ppermute | solution.py:138
  67.1 18.9 %copy-start.10 = (s32[4,4]{1,0:T(4,128)S(1)}, s32[4,4]{1,0:T(4,128)}, u32[]{:S(2)}) copy-start(s32[4,4]{1,0:T(4,128)} %mask.7) | copy-start | bytes 196
  67.1 17.2 %collective-permute-start.17 = (bf16[2,10,128,128]{3,2,1,0:T(8,128)(2,1)}, bf16[2,10,128,128]{3,2,1,0:T(8,128)(2,1)}, u32[]{:S(2)}, u32[]{:S(2)}) collective-permute-start(bf16[2,10,128,128]{3,2,1,0:T(8,128)(2,1)} %collective-permute-done.16.refs_7_), channel_id=1, source_target_pairs={{24,16},{25,17},{26,18},{27,19},{28,20},{29,21},{30,22},{31,23}} | collective-permute-start | bytes 1966088 | tf_op jit(solution)/shard_map/ppermute | solution.py:138
  69.9 0.8 copy-start.8
  70.7 14.2 %collective-permute-start.10 = (bf16[2,10,128,128]{3,2,1,0:T(8,128)(2,1)S(1)}, bf16[2,10,128,128]{3,2,1,0:T(8,128)(2,1)}, u32[]{:S(2)}, u32[]{:S(2)}) collective-permute-start(bf16[2,10,128,128]{3,2,1,0:T(8,128)(2,1)S(1)} %get-tuple-element.42.refs_2_), channel_id=1, source_target_pairs={{8,24},{9,25},{10,26},{11,27},{12,28},{13,29},{14,30},{15,31}} | collective-permute-start | bytes 1966088 | tf_op jit(solution)/shard_map/ppermute | solution.py:138
  74.8 11.1 %copy-start.3 = (bf16[2,10,128,128]{3,2,1,0:T(8,128)(2,1)S(1)}, bf16[2,10,128,128]{3,2,1,0:T(8,128)(2,1)}, u32[]{:S(2)}) copy-start(bf16[2,10,128,128]{3,2,1,0:T(8,128)(2,1)} %copy-done.2) | copy-start | bytes 1966084
  74.8 11.1 %copy-start.5 = (bf16[2,10,128,128]{3,2,1,0:T(8,128)(2,1)S(1)}, bf16[2,10,128,128]{3,2,1,0:T(8,128)(2,1)}, u32[]{:S(2)}) copy-start(bf16[2,10,128,128]{3,2,1,0:T(8,128)(2,1)} %copy-done.4) | copy-start | bytes 1966084
  74.9 11.1 %copy-start.7 = (bf16[2,10,128,128]{3,2,1,0:T(8,128)(2,1)S(1)}, bf16[2,10,128,128]{3,2,1,0:T(8,128)(2,1)}, u32[]{:S(2)}) copy-start(bf16[2,10,128,128]{3,2,1,0:T(8,128)(2,1)} %copy-done.6) | copy-start | bytes 1966084
  74.9 11.1 %copy-start.9 = (bf16[2,10,128,128]{3,2,1,0:T(8,128)(2,1)S(1)}, bf16[2,10,128,128]{3,2,1,0:T(8,128)(2,1)}, u32[]{:S(2)}) copy-start(bf16[2,10,128,128]{3,2,1,0:T(8,128)(2,1)} %copy-done.8) | copy-start | bytes 1966084
  76.5 17.5 %collective-permute-start.18 = (bf16[10,256,128]{2,1,0:T(8,128)(2,1)S(1)}, bf16[10,256,128]{2,1,0:T(8,128)(2,1)S(1)}, u32[]{:S(2)}, u32[]{:S(2)}) collective-permute-start(bf16[10,256,128]{2,1,0:T(8,128)(2,1)S(1)} %get-tuple-element.48), channel_id=1, source_target_pairs={{0,4},{4,0},{1,5},{5,1},{2,6},{6,2},{3,7},{7,3},{8,12},{12,8},{9,1... | collective-permute-start | bytes 1966088 | tf_op jit(solution)/shard_map/ppermute | solution.py:138
  77.1 24.8 %collective-permute-start.6 = (bf16[2,10,128,128]{3,2,1,0:T(8,128)(2,1)S(1)}, bf16[2,10,128,128]{3,2,1,0:T(8,128)(2,1)S(1)}, u32[]{:S(2)}, u32[]{:S(2)}) collective-permute-start(bf16[2,10,128,128]{3,2,1,0:T(8,128)(2,1)S(1)} %get-tuple-element.28.refs_9_), channel_id=1, source_target_pairs={{0,8},{16,24},{24,16},{1,9},{17,25},{25,17},{2,10},{18,26},{26,18}... | collective-permute-start | bytes 1966088 | tf_op jit(solution)/shard_map/ppermute | solution.py:138
  82.9 19.0 %collective-permute-start.7 = (bf16[2,10,128,128]{3,2,1,0:T(8,128)(2,1)S(1)}, bf16[2,10,128,128]{3,2,1,0:T(8,128)(2,1)S(1)}, u32[]{:S(2)}, u32[]{:S(2)}) collective-permute-start(bf16[2,10,128,128]{3,2,1,0:T(8,128)(2,1)S(1)} %get-tuple-element.41.refs_10_), channel_id=1, source_target_pairs={{0,8},{16,24},{24,16},{1,9},{17,25},{25,17},{2,10},{18,26},{26,18}... | collective-permute-start | bytes 1966088 | tf_op jit(solution)/shard_map/ppermute | solution.py:138
  84.3 17.6 %collective-permute-start.9 = (bf16[2,10,128,128]{3,2,1,0:T(8,128)(2,1)}, bf16[2,10,128,128]{3,2,1,0:T(8,128)(2,1)S(1)}, u32[]{:S(2)}, u32[]{:S(2)}) collective-permute-start(bf16[2,10,128,128]{3,2,1,0:T(8,128)(2,1)} %collective-permute-done.8.refs_5_), channel_id=1, source_target_pairs={{24,16},{25,17},{26,18},{27,19},{28,20},{29,21},{30,22},{31,23}} | collective-permute-start | bytes 1966088 | tf_op jit(solution)/shard_map/ppermute | solution.py:138
  85.0 16.9 %collective-permute-start.11 = (bf16[2,10,128,128]{3,2,1,0:T(8,128)(2,1)}, bf16[2,10,128,128]{3,2,1,0:T(8,128)(2,1)S(1)}, u32[]{:S(2)}, u32[]{:S(2)}) collective-permute-start(bf16[2,10,128,128]{3,2,1,0:T(8,128)(2,1)} %collective-permute-done.10.refs_7_), channel_id=1, source_target_pairs={{24,16},{25,17},{26,18},{27,19},{28,20},{29,21},{30,22},{31,23}} | collective-permute-start | bytes 1966088 | tf_op jit(solution)/shard_map/ppermute | solution.py:138
  86.0 23.3 %slice-start = ((s8[13107200]{0:T(1024)(128)(4,1)}), s8[4194304]{0:T(1024)(128)(4,1)S(1)}, s32[]{:S(2)}) async-start(s8[13107200]{0:T(1024)(128)(4,1)} %bitcast.76), calls=%async_computation | async-start | bytes 8388608
  86.0 23.3 %slice-start.1 = ((s8[13107200]{0:T(1024)(128)(4,1)}), s8[4194304]{0:T(1024)(128)(4,1)S(1)}, s32[]{:S(2)}) async-start(s8[13107200]{0:T(1024)(128)(4,1)} %bitcast.76), calls=%async_computation.1 | async-start | bytes 8388608
  93.9 15.4 %slice-start.2 = ((s8[13107200]{0:T(1024)(128)(4,1)}), s8[4194304]{0:T(1024)(128)(4,1)S(1)}, s32[]{:S(2)}) async-start(s8[13107200]{0:T(1024)(128)(4,1)} %bitcast.76), calls=%async_computation.2 | async-start | bytes 8388608
  101.9 7.4 %slice-start.3 = ((s8[13107200]{0:T(1024)(128)(4,1)}), s8[524288]{0:T(1024)(128)(4,1)S(1)}, s32[]{:S(2)}) async-start(s8[13107200]{0:T(1024)(128)(4,1)} %bitcast.76), calls=%async_computation.3 | async-start | bytes 1048576
  123.3 14.9 %collective-permute-start.19 = (bf16[256,1024]{1,0:T(8,128)(2,1)S(1)}, bf16[256,1024]{1,0:T(8,128)(2,1)S(1)}, u32[]{:S(2)}, u32[]{:S(2)}) collective-permute-start(bf16[256,1024]{1,0:T(8,128)(2,1)S(1)} %fusion.10), channel_id=1, source_target_pairs={{4,0},{0,4},{5,1},{1,5},{6,2},{2,6},{7,3},{3,7},{12,8},{8,12},{13,... | collective-permute-start | bytes 1572872 | tf_op jit(solution)/shard_map/ppermute | solution.py:138
  124.9 24.5 %collective-permute-start.20 = (bf16[256,1024]{1,0:T(8,128)(2,1)S(1)}, bf16[256,1024]{1,0:T(8,128)(2,1)S(1)}, u32[]{:S(2)}, u32[]{:S(2)}) collective-permute-start(bf16[256,1024]{1,0:T(8,128)(2,1)S(1)} %fusion.13), channel_id=1, source_target_pairs={{4,0},{0,4},{5,1},{1,5},{6,2},{2,6},{7,3},{3,7},{12,8},{8,12},{13,... | collective-permute-start | bytes 1572872 | tf_op jit(solution)/shard_map/ppermute | solution.py:138
  125.4 35.2 %collective-permute-start.21 = (bf16[256,1024]{1,0:T(8,128)(2,1)S(1)}, bf16[256,1024]{1,0:T(8,128)(2,1)S(1)}, u32[]{:S(2)}, u32[]{:S(2)}) collective-permute-start(bf16[256,1024]{1,0:T(8,128)(2,1)S(1)} %fusion.16), channel_id=1, source_target_pairs={{4,0},{0,4},{5,1},{1,5},{6,2},{2,6},{7,3},{3,7},{12,8},{8,12},{13,... | collective-permute-start | bytes 1572872 | tf_op jit(solution)/shard_map/ppermute | solution.py:138
  127.8 10.4 %copy-start.11 = (bf16[1,1,256,5120]{3,2,1,0:T(8,128)(2,1)S(1)}, bf16[1,1,256,5120]{3,2,1,0:T(8,128)(2,1)}, u32[]{:S(2)}) copy-start(bf16[1,1,256,5120]{3,2,1,0:T(8,128)(2,1)} %param.16) | copy-start | bytes 7864324
  127.8 44.1 %collective-permute-start.22 = (bf16[256,1024]{1,0:T(8,128)(2,1)S(1)}, bf16[256,1024]{1,0:T(8,128)(2,1)S(1)}, u32[]{:S(2)}, u32[]{:S(2)}) collective-permute-start(bf16[256,1024]{1,0:T(8,128)(2,1)S(1)} %fusion.19), channel_id=1, source_target_pairs={{4,0},{0,4},{5,1},{1,5},{6,2},{2,6},{7,3},{3,7},{12,8},{8,12},{13,... | collective-permute-start | bytes 1572872 | tf_op jit(solution)/shard_map/ppermute | solution.py:138
  129.3 52.6 %collective-permute-start.23 = (bf16[256,1024]{1,0:T(8,128)(2,1)S(1)}, bf16[256,1024]{1,0:T(8,128)(2,1)S(1)}, u32[]{:S(2)}, u32[]{:S(2)}) collective-permute-start(bf16[256,1024]{1,0:T(8,128)(2,1)S(1)} %fusion.22), channel_id=1, source_target_pairs={{4,0},{0,4},{5,1},{1,5},{6,2},{2,6},{7,3},{3,7},{12,8},{8,12},{13,... | collective-permute-start | bytes 1572872 | tf_op jit(solution)/shard_map/ppermute | solution.py:138
  172.2 10.7 %copy-start.1 = (f32[16,5120]{1,0:T(8,128)S(1)}, f32[16,5120]{1,0:T(8,128)}, u32[]{:S(2)}) copy-start(f32[16,5120]{1,0:T(8,128)} %param.18) | copy-start | bytes 983044

commit v4 on v2

--- a/solution.py
+++ b/solution.py
@@ -11,8 +11,8 @@
 NEG_BIG = -1e30
 LOG2E = 1.4426950408889634
 COL_BLOCKS = 5
-HEAD_STEP_SCORES = 3 << 20
-VMEM_LIMIT = 22 << 20
+HEAD_STEP_SCORES = 2 << 20
+VMEM_LIMIT = 28 << 20
 
 
 def hidden_bias(mask, span, origin):
@@ -29,26 +29,25 @@
     def gather(kind, h):
         blocks = []
         for _, members in layout:
-            for i in members:
-                if isinstance(i, tuple):
-                    blocks.append(jnp.where(odd, kv_refs[i[0]][kind, h], kv_refs[i[1]][kind, h]))
-                else:
-                    blocks.append(kv_refs[i][kind, h])
+            for choices, _ in members:
+                block = kv_refs[choices[0]][kind, h]
+                if len(choices) > 1:
+                    block = jnp.where(odd, block, kv_refs[choices[1]][kind, h])
+                blocks.append(block)
         return jnp.concatenate(blocks, axis=0)
 
     if not first:
         (max_in, sum_in, acc_in), refs = refs[:3], refs[3:]
     outs, score_ref = refs[:-1], refs[-1]
     dim = q_ref.shape[2]
-    keys = kv_refs[0].shape[2]
-    order = [bias for bias, (_, members) in zip(biases, layout) for _ in members]
+    order = [(bias, size) for bias, (_, members) in zip(biases, layout) for _, size in members]
     for h in range(step):
         raw = lax.dot_general(
             q_ref[h], gather(0, h), (((1,), (1,)), ((), ())), preferred_element_type=jnp.float32
         )
         at, top = 0, None
-        for bias in order:
-            for _ in range(0, keys, dim):
+        for bias, size in order:
+            for _ in range(0, size, dim):
                 piece = raw[:, at : at + dim]
                 if bias is not None:
                     piece = piece + bias
@@ -85,11 +84,10 @@
         places = []
         for member in members:
             choices = member if isinstance(member, tuple) else (member,)
-            at = tuple(range(len(arrays), len(arrays) + len(choices)))
-            places.append(at if len(at) > 1 else at[0])
+            places.append((tuple(range(len(arrays), len(arrays) + len(choices))), choices[0].shape[2]))
             arrays += choices
         layout.append((origin, places))
-    keys = arrays[0].shape[2] * sum(len(places) for _, places in layout)
+    keys = sum(size for _, places in layout for _, size in places)
     step = max(s for s in range(1, heads + 1) if heads % s == 0 and s * rows * keys <= HEAD_STEP_SCORES)
     by_head = pl.BlockSpec((step, rows, dim), lambda h, f: (h, 0, 0))
     states = [] if state is None else list(state)
@@ -138,7 +136,6 @@
     spans, splits, branches = sizes
     span = lax.axis_index("tm")
     part = lax.axis_index("head")
-    branch = lax.axis_index("branch")
     to_heads = lambda a: jnp.transpose(a, (1, 0, 2))
     q, k, v = to_heads(queries), to_heads(keys), to_heads(values)
     ck, cv = to_heads(ctx_keys), to_heads(ctx_values)
@@ -161,31 +158,24 @@
     use_context = span < prefix[0]
     final = spans - 1
     stands_in = span == final
-    bases = [jnp.where(stands_in, lax.ppermute(a, "tm", [(0, final)]), a) for a in ctx_parts]
-    up, down = [[a] for a in bases], [[a] for a in bases]
-    piece_rows, rows = splits * bases[0].shape[2], k.shape[1]
-    own, passed, held = [], [], []
-    for s in range(branches):
-        pieces = []
-        for d in range(splits):
-            piece = bases[d]
-            if s > 0:
-                if s == branches - 1 and d == 0:
-                    up[0][-1], gate_row = lax.optimization_barrier((up[0][-1], gate_row))
-                rise = [(i, i + 1) for i in range(s - 1, branches - 1)]
-                fall = [(i, i - 1) for i in range(1, branches - s + 1)]
-                up[d].append(lax.ppermute(up[d][-1], "branch", rise))
-                down[d].append(lax.ppermute(down[d][-1], "branch", fall))
-                piece = up[d][s]
-            pieces.append(piece)
-        if s > 0:
-            merged, *pieces = lax.optimization_barrier(((own[-1], passed[-1]), *pieces))
-            held[-1] = merged
-            for d in range(splits):
-                for t in range(1, s + 1):
-                    pieces[d] = jnp.where(branch == s - t, down[d][t], pieces[d])
-        d, at = divmod(s * piece_rows, rows)
-        context, mine = jnp.concatenate(pieces, axis=2), kv_parts[d][:, :, at : at + piece_rows]
+    lent = [lax.ppermute(a, "tm", [(0, final)]) for a in ctx_parts]
+    pieces = [jnp.concatenate([jnp.where(stands_in, b, a) for a, b in zip(ctx_parts, lent)], axis=2)]
+    piece_rows = pieces[0].shape[2]
+    for i in range(1, branches):
+        low = i & -i
+        pieces.append(lax.ppermute(pieces[i - low], "branch", [(b, b ^ low) for b in range(branches)]))
+    groups = [[i for i in range(branches) if i.bit_count() == n] for n in range(branches.bit_length())]
+    rows, at, own, passed, held = k.shape[1], 0, [], [], []
+    for members in groups:
+        contexts = [pieces[i] for i in members]
+        if own:
+            held[-1], *contexts = lax.optimization_barrier(((own[-1], passed[-1]), *contexts))
+        mine = []
+        for _ in members:
+            d, row = divmod(at, rows)
+            mine.append(kv_parts[d][:, :, row : row + piece_rows])
+            at += piece_rows
+        context, mine = jnp.concatenate(contexts, axis=2), jnp.concatenate(mine, axis=2)
         own.append(jnp.where(use_context, context, mine))
         passed.append(jnp.where(use_context | stands_in, context, mine))
         held.append((own[-1], passed[-1]))
@@ -208,12 +198,12 @@
     slots.append((lambda c: jnp.where(c >= final - 1, 1, -1), list(zip(far, near))))
     slots.append((lambda c: jnp.where(c == final, 0, -1), [a for _, a in held]))
 
-    half = max(1, len(own) // 2)
-    early = [(origin, arrays[:half]) for origin, arrays in slots]
-    late = [(origin, arrays[half:]) for origin, arrays in slots]
-    states = []
-    for d in range(splits):
-        states.append(attend(q_parts[d], early, span_mask, None, False))
+    early = [(origin, arrays[:-1]) for origin, arrays in slots]
+    late = [(origin, arrays[-1:]) for origin, arrays in slots]
+    q_parts[0], gate_row = lax.optimization_barrier((q_parts[0], gate_row))
+    states = {}
+    for d in range(1, splits):
+        states[d] = attend(q_parts[d], early, span_mask, None, False)
 
     columns = out_weight.shape[1]
     width = columns // COL_BLOCKS
@@ -225,7 +215,7 @@
         for j in range(COL_BLOCKS):
             partial = project(attended, out_weight[:, j * width : (j + 1) * width])
             returned[j].append(lax.ppermute(partial, "head", back))
-    attended = attend(q_parts[0], late, span_mask, states[0], True)
+    attended = attend(q_parts[0], slots, span_mask, None, True)
     kept = lax.optimization_barrier(project(attended, out_weight))
     updated = hidden
     for j in range(COL_BLOCKS):

time: 182 us -> 170 us (0.934)
  the two profiles are of different devices: /device:TPU:29 before, /device:TPU:0 now
where the time goes in v4:
time: 170 us; the launch traced here: 168 us
  waiting for transfers between devices  63 us (37%)
  starting transfers between devices  48.5 us (29%)
  Pallas kernels  27.5 us (16%)
  local copies, waits for them, and re-layouts  8.99 us (5%)
  other arithmetic  8.8 us (5%)
  matrix products  8.25 us (5%)
  between operations  3 us (2%)
    ppermute x5, waiting for transfers between devices, sublayer(): returned[j].append(lax.ppermute(partial, 'head', back))  33 us
    pallas_call x3, Pallas kernels, attend(): pl.pallas_call(functools.partial(flash_kernel, layout=layout, count=len(a...  27.5 us
    ppermute x3, waiting for transfers between devices, sublayer(): lax.ppermute(pieces[i - low], 'branch', [(b, b ^ low) for b in range(bran...  25.9 us
    ppermute x3, starting transfers between devices, sublayer(): lax.ppermute(a, 'tm', pairs + [(final, final - 1)])  18.5 us
    dot_general x6, matrix products, sublayer(): jnp.dot(a, w, preferred_element_type=jnp.float32).astype(jnp.bfloat16)  8.25 us
    ppermute x2, starting transfers between devices, sublayer(): lent = [lax.ppermute(a, 'tm', [(0, final)]) for a in ctx_parts]  6.3 us
    ppermute x3, starting transfers between devices, sublayer(): lax.ppermute(pieces[i - low], 'branch', [(b, b ^ low) for b in range(bran...  5.67 us
    ppermute x3, starting transfers between devices, sublayer(): far = [lax.ppermute(a, 'tm', [(1, final)]) for a in own]  4.98 us
  transfers between devices with their start and end apart: 22, of which 9 were waited for; matrix products, arithmetic and copies ran while one was open for 9% of the time, Pallas kernels for 13%

profile of v4, /device:TPU:0, one launch (start us, length us, event | category | flops | bytes accessed | tf_op | source)
XLA Modules:
  0.0 168.0 jit_solution(11532193341508665275)
XLA Ops:
  0.0 1.0 copy-done.14
  1.0 0.1 copy-done.13
  1.2 3.0 %collective-permute-start.1 = (bf16[2,10,64,128]{3,2,1,0:T(8,128)(2,1)S(1)}, bf16[2,10,64,128]{3,2,1,0:T(8,128)(2,1)}, u32[]{:S(2)}, u32[]{:S(2)}) collective-permute-start(bf16[2,10,64,128]{3,2,1,0:T(8,128)(2,1)S(1)} %pad_maximum_fusion.4), channel_id=1, source_target_pairs={{0,4},{4,0},{1,5},{5,1},{2,6},{6,2},{3,7},{7,3},{8,12},{12,8},{9,1... | collective-permute-start | bytes 983048 | tf_op jit(solution)/shard_map/ppermute | solution.py:152
  4.2 0.8 pad_maximum_fusion.3
  5.0 3.3 %collective-permute-start = (bf16[2,10,64,128]{3,2,1,0:T(8,128)(2,1)}, bf16[2,10,64,128]{3,2,1,0:T(8,128)(2,1)}, u32[]{:S(2)}, u32[]{:S(2)}) collective-permute-start(bf16[2,10,64,128]{3,2,1,0:T(8,128)(2,1)} %pad_maximum_fusion.3), channel_id=1, source_target_pairs={{0,24},{1,25},{2,26},{3,27},{4,28},{5,29},{6,30},{7,31}} | collective-permute-start | bytes 983048 | tf_op jit(solution)/shard_map/ppermute | solution.py:161
  8.3 1.5 dynamic-slice_bitcast_fusion.1
  9.8 0.0 copy-start.7
  9.8 2.3 %collective-permute-done.1 = bf16[2,10,64,128]{3,2,1,0:T(8,128)(2,1)} collective-permute-done((bf16[2,10,64,128]{3,2,1,0:T(8,128)(2,1)S(1)}, bf16[2,10,64,128]{3,2,1,0:T(8,128)(2,1)}, u32[]{:S(2)}, u32[]{:S(2)}) %collective-permute-start.1) | collective-permute-done | bytes 327712 | tf_op jit(solution)/shard_map/ppermute | solution.py:152
  12.1 3.0 %collective-permute-start.2 = (bf16[2,10,64,128]{3,2,1,0:T(8,128)(2,1)}, bf16[2,10,64,128]{3,2,1,0:T(8,128)(2,1)}, u32[]{:S(2)}, u32[]{:S(2)}) collective-permute-start(bf16[2,10,64,128]{3,2,1,0:T(8,128)(2,1)} %collective-permute-done.1), channel_id=1, source_target_pairs={{0,24},{1,25},{2,26},{3,27},{4,28},{5,29},{6,30},{7,31}} | collective-permute-start | bytes 983048 | tf_op jit(solution)/shard_map/ppermute | solution.py:161
  15.1 0.1 pad_maximum_fusion.1
  15.2 1.6 collective-permute-start.5
  17.4 0.1 broadcast_select_fusion.7
  17.5 1.7 %collective-permute-done.2 = bf16[2,10,64,128]{3,2,1,0:T(8,128)(2,1)} collective-permute-done((bf16[2,10,64,128]{3,2,1,0:T(8,128)(2,1)}, bf16[2,10,64,128]{3,2,1,0:T(8,128)(2,1)}, u32[]{:S(2)}, u32[]{:S(2)}) %collective-permute-start.2) | collective-permute-done | bytes 327712 | tf_op jit(solution)/shard_map/ppermute | solution.py:161
  19.2 1.0 broadcast_select_fusion.6
  20.2 1.6 broadcast_select_fusion.3
  21.8 2.7 %collective-permute-start.4 = (bf16[2,10,128,128]{3,2,1,0:T(8,128)(2,1)S(1)}, bf16[2,10,128,128]{3,2,1,0:T(8,128)(2,1)S(1)}, u32[]{:S(2)}, u32[]{:S(2)}) collective-permute-start(bf16[2,10,128,128]{3,2,1,0:T(8,128)(2,1)S(1)} %get-tuple-element.41), channel_id=1, source_target_pairs={{0,2},{1,3},{2,0},{3,1},{4,6},{5,7},{6,4},{7,5},{8,10},{9,11},{10,... | collective-permute-start | bytes 1966088 | tf_op jit(solution)/shard_map/ppermute | solution.py:166
  24.4 1.6 collective-permute-start.3
  26.0 23.2 %collective-permute-done.4 = bf16[2,10,128,128]{3,2,1,0:T(8,128)(2,1)S(1)} collective-permute-done((bf16[2,10,128,128]{3,2,1,0:T(8,128)(2,1)S(1)}, bf16[2,10,128,128]{3,2,1,0:T(8,128)(2,1)S(1)}, u32[]{:S(2)}, u32[]{:S(2)}) %collective-permute-start.4) | collective-permute-done | bytes 655392 | tf_op jit(solution)/shard_map/ppermute | solution.py:166
  49.2 0.2 collective-permute-done.3
  49.4 0.1 constant_dynamic-update-slice_fusion.1
  49.4 0.1 constant_dynamic-update-slice_fusion
  49.6 1.1 slice.99
  50.7 0.7 broadcast_select_fusion
  51.5 1.9 %collective-permute-start.12 = (bf16[2,10,256,128]{3,2,1,0:T(8,128)(2,1)S(1)}, bf16[2,10,256,128]{3,2,1,0:T(8,128)(2,1)}, u32[]{:S(2)}, u32[]{:S(2)}) collective-permute-start(bf16[2,10,256,128]{3,2,1,0:T(8,128)(2,1)S(1)} %get-tuple-element.22.refs_2_), channel_id=1, source_target_pairs={{8,24},{9,25},{10,26},{11,27},{12,28},{13,29},{14,30},{15,31}} | collective-permute-start | bytes 3932168 | tf_op jit(solution)/shard_map/ppermute | solution.py:196
  53.4 1.4 collective-permute-start.6
  54.9 0.9 dynamic-slice_bitcast_fusion.5
  55.8 0.5 collective-permute-start.16
  56.3 6.8 %collective-permute-start.7 = (bf16[2,10,128,128]{3,2,1,0:T(8,128)(2,1)}, bf16[2,10,128,128]{3,2,1,0:T(8,128)(2,1)}, u32[]{:S(2)}, u32[]{:S(2)}) collective-permute-start(bf16[2,10,128,128]{3,2,1,0:T(8,128)(2,1)} %get-tuple-element.24.refs_13_.refs_9_), channel_id=1, source_target_pairs={{0,8},{16,24},{24,16},{1,9},{17,25},{25,17},{2,10},{18,26},{26,18}... | collective-permute-start | bytes 1966088 | tf_op jit(solution)/shard_map/ppermute | solution.py:184
  63.1 1.5 collective-permute-start.10
  64.6 2.5 %collective-permute-done.6 = bf16[2,10,128,128]{3,2,1,0:T(8,128)(2,1)S(1)} collective-permute-done((bf16[2,10,128,128]{3,2,1,0:T(8,128)(2,1)S(1)}, bf16[2,10,128,128]{3,2,1,0:T(8,128)(2,1)S(1)}, u32[]{:S(2)}, u32[]{:S(2)}) %collective-permute-start.6) | collective-permute-done | bytes 655392 | tf_op jit(solution)/shard_map/ppermute | solution.py:166
  67.1 2.3 %broadcast_select_fusion.2 = (bf16[2,10,128,128]{3,2,1,0:T(8,128)(2,1)}, bf16[2,10,128,128]{3,2,1,0:T(8,128)(2,1)}) fusion(bf16[2,10,128,128]{3,2,1,0:T(8,128)(2,1)S(1)} %collective-permute-done.6, pred[]{:T(512)S(6)} %or.2, bf16[2,10,256,128]{3,2,1,0:T(8,128)(2,1)} %collective-permute-done.5, pred[]{:T(512)S(6)} %lt.28), kind=kLoop, calls=%fused_computation.36 | loop fusion | flops 655360 | bytes 2621442 | tf_op jit(solution)/shard_map/jit(_where)/select_n | solution.py:180
  69.4 1.5 collective-permute-start.14
  70.9 0.8 copy-done.2
  71.8 10.4 %collective-permute-start.8 = (bf16[2,10,256,128]{3,2,1,0:T(8,128)(2,1)S(1)}, bf16[2,10,256,128]{3,2,1,0:T(8,128)(2,1)}, u32[]{:S(2)}, u32[]{:S(2)}) collective-permute-start(bf16[2,10,256,128]{3,2,1,0:T(8,128)(2,1)S(1)} %get-tuple-element.25.refs_14_.refs_10_), channel_id=1, source_target_pairs={{0,8},{16,24},{24,16},{1,9},{17,25},{25,17},{2,10},{18,26},{26,18}... | collective-permute-start | bytes 3932168 | tf_op jit(solution)/shard_map/ppermute | solution.py:184
  82.2 1.7 %collective-permute-start.13 = (bf16[2,10,256,128]{3,2,1,0:T(8,128)(2,1)}, bf16[2,10,256,128]{3,2,1,0:T(8,128)(2,1)}, u32[]{:S(2)}, u32[]{:S(2)}) collective-permute-start(bf16[2,10,256,128]{3,2,1,0:T(8,128)(2,1)} %collective-permute-done.12.refs_9_.refs_7_), channel_id=1, source_target_pairs={{24,16},{25,17},{26,18},{27,19},{28,20},{29,21},{30,22},{31,23}} | collective-permute-start | bytes 3932168 | tf_op jit(solution)/shard_map/ppermute | solution.py:197
  83.9 0.6 dynamic_slice.39
  86.4 0.7 collective-permute-start.11
  87.2 1.3 collective-permute-start.9
  88.5 0.9 collective-permute-start.15
  89.5 1.1 copy-done.3
  90.7 9.3 %shard_map.110 = (f32[10,256,128]{2,1,0:T(8,128)S(1)}, f32[10,256,128]{2,1,0:T(8,128)S(1)}, f32[10,256,128]{2,1,0:T(8,128)S(1)}) custom-call(s32[4,4]{1,0:T(4,128)S(1)} %copy-done.5, bf16[10,256,128]{2,1,0:T(8,128)(2,1)S(1)} %copy-done.3, bf16[2,10,128,128]{3,2,1,0:T(8,128)(2,1)} %get-tuple-element.19.refs_1_, ...), custom_call_target="tpu_custom_call" | custom-call | flops 2013265920 | bytes 9175040 | tf_op jit(solution)/shard_map/pallas_call | solution.py:94
  100.0 5.4 %shard_map.111 = bf16[256,1280]{1,0:T(8,128)(2,1)S(1)} custom-call(s32[4,4]{1,0:T(4,128)S(1)} %copy-done.5, bf16[10,256,128]{2,1,0:T(8,128)(2,1)S(1)} %copy-done.3, bf16[2,10,128,128]{3,2,1,0:T(8,128)(2,1)} %get-tuple-element.32.refs_3_.refs_1_, bf16[2,10,128,128]{3,2,1,0:T(8,128)(2,1)S(1)} %collective-permute-done.9.refs_6_.refs_2_, ...), custom_call_target="tpu_custom_call" | custom-call | flops 671088640 | bytes 3932160 | tf_op jit(solution)/shard_map/pallas_call | solution.py:94
  105.4 0.9 fusion.23
  106.3 0.9 fusion.20
  107.2 0.9 fusion.17
  108.1 0.9 fusion.14
  108.9 0.9 fusion.11
  109.8 0.6 collective-permute-start.17
  110.4 1.5 collective-permute-start.18
  111.9 0.5 collective-permute-start.19
  112.5 1.5 collective-permute-start.20
  114.0 0.5 collective-permute-start.21
  114.5 12.8 %shard_map.109 = bf16[256,1280]{1,0:T(8,128)(2,1)S(1)} custom-call(s32[4,4]{1,0:T(4,128)S(1)} %copy-done.5, bf16[10,256,128]{2,1,0:T(8,128)(2,1)S(1)} %copy-done.4, bf16[2,10,128,128]{3,2,1,0:T(8,128)(2,1)} %get-tuple-element.19.refs_1_, bf16[2,10,256,128]{3,2,1,0:T(8,128)(2,1)S(1)} %get-tuple-element.22.refs_2_, ...), custom_call_target="tpu_custom_call" | custom-call | flops 2684354560 | bytes 11796480 | tf_op jit(solution)/shard_map/pallas_call | solution.py:94
  127.3 3.9 %convolution_convert_fusion = bf16[256,5120]{1,0:T(8,128)(2,1)S(1)} fusion(bf16[256,1280]{1,0:T(8,128)(2,1)S(1)} %shard_map.109, bf16[1280,5120]{1,0:T(8,128)(2,1)S(1)} %copy-done.15), kind=kOutput, calls=%fused_computation | convolution fusion | flops 3356753920 | bytes 16384000 | tf_op jit(solution)/shard_map/dot_general | solution.py:210
  131.2 0.3 fusion.27
  131.5 4.4 %collective-permute-done.18 = bf16[256,1024]{1,0:T(8,128)(2,1)S(1)} collective-permute-done((bf16[256,1024]{1,0:T(8,128)(2,1)S(1)}, bf16[256,1024]{1,0:T(8,128)(2,1)S(1)}, u32[]{:S(2)}, u32[]{:S(2)}) %collective-permute-start.18) | collective-permute-done | bytes 524320 | tf_op jit(solution)/shard_map/ppermute | solution.py:217
  135.9 0.3 fusion.28
  136.2 10.9 %collective-permute-done.19 = bf16[256,1024]{1,0:T(8,128)(2,1)S(1)} collective-permute-done((bf16[256,1024]{1,0:T(8,128)(2,1)S(1)}, bf16[256,1024]{1,0:T(8,128)(2,1)S(1)}, u32[]{:S(2)}, u32[]{:S(2)}) %collective-permute-start.19) | collective-permute-done | bytes 524320 | tf_op jit(solution)/shard_map/ppermute | solution.py:217
  147.2 0.3 fusion.29
  147.5 10.9 %collective-permute-done.20 = bf16[256,1024]{1,0:T(8,128)(2,1)S(1)} collective-permute-done((bf16[256,1024]{1,0:T(8,128)(2,1)S(1)}, bf16[256,1024]{1,0:T(8,128)(2,1)S(1)}, u32[]{:S(2)}, u32[]{:S(2)}) %collective-permute-start.20) | collective-permute-done | bytes 524320 | tf_op jit(solution)/shard_map/ppermute | solution.py:217
  158.4 0.3 fusion.30
  158.7 1.5 copy.17
  160.2 6.8 %collective-permute-done.21 = bf16[256,1024]{1,0:T(8,128)(2,1)S(1)} collective-permute-done((bf16[256,1024]{1,0:T(8,128)(2,1)S(1)}, bf16[256,1024]{1,0:T(8,128)(2,1)S(1)}, u32[]{:S(2)}, u32[]{:S(2)}) %collective-permute-start.21) | collective-permute-done | bytes 524320 | tf_op jit(solution)/shard_map/ppermute | solution.py:217
  167.0 1.1 fusion.32
  (46 shorter events, 0.2 us)
Async XLA Ops:
  0.0 89.4 %copy-start = (f32[16,5120]{1,0:T(8,128)S(1)}, f32[16,5120]{1,0:T(8,128)}, u32[]{:S(2)}) copy-start(f32[16,5120]{1,0:T(8,128)} %param.18) | copy-start | bytes 983044
  0.0 1.0 copy-start.14
  0.0 1.1 copy-start.13
  0.0 8.3 %copy-start.12 = (bf16[1,1,256,20,128]{4,2,3,1,0:T(8,128)(2,1)S(1)}, bf16[1,1,256,20,128]{4,2,3,1,0:T(8,128)(2,1)}, u32[]{:S(2)}) copy-start(bf16[1,1,256,20,128]{4,2,3,1,0:T(8,128)(2,1)} %param.13) | copy-start | bytes 3932164
  1.2 10.8 %collective-permute-start.1 = (bf16[2,10,64,128]{3,2,1,0:T(8,128)(2,1)S(1)}, bf16[2,10,64,128]{3,2,1,0:T(8,128)(2,1)}, u32[]{:S(2)}, u32[]{:S(2)}) collective-permute-start(bf16[2,10,64,128]{3,2,1,0:T(8,128)(2,1)S(1)} %pad_maximum_fusion.4), channel_id=1, source_target_pairs={{0,4},{4,0},{1,5},{5,1},{2,6},{6,2},{3,7},{7,3},{8,12},{12,8},{9,1... | collective-permute-start | bytes 983048 | tf_op jit(solution)/shard_map/ppermute | solution.py:152
  5.0 12.4 %collective-permute-start = (bf16[2,10,64,128]{3,2,1,0:T(8,128)(2,1)}, bf16[2,10,64,128]{3,2,1,0:T(8,128)(2,1)}, u32[]{:S(2)}, u32[]{:S(2)}) collective-permute-start(bf16[2,10,64,128]{3,2,1,0:T(8,128)(2,1)} %pad_maximum_fusion.3), channel_id=1, source_target_pairs={{0,24},{1,25},{2,26},{3,27},{4,28},{5,29},{6,30},{7,31}} | collective-permute-start | bytes 983048 | tf_op jit(solution)/shard_map/ppermute | solution.py:161
  9.8 12.0 %copy-start.7 = (bf16[1,10,256,128]{3,2,1,0:T(8,128)(2,1)}, bf16[1,10,256,128]{3,2,1,0:T(8,128)(2,1)S(1)}, u32[]{:S(2)}) copy-start(bf16[1,10,256,128]{3,2,1,0:T(8,128)(2,1)S(1)} %get-tuple-element.40) | copy-start | bytes 1966084
  9.8 12.0 %copy-start.9 = (bf16[1,10,256,128]{3,2,1,0:T(8,128)(2,1)}, bf16[1,10,256,128]{3,2,1,0:T(8,128)(2,1)S(1)}, u32[]{:S(2)}) copy-start(bf16[1,10,256,128]{3,2,1,0:T(8,128)(2,1)S(1)} %get-tuple-element.51) | copy-start | bytes 1966084
  12.1 7.1 %collective-permute-start.2 = (bf16[2,10,64,128]{3,2,1,0:T(8,128)(2,1)}, bf16[2,10,64,128]{3,2,1,0:T(8,128)(2,1)}, u32[]{:S(2)}, u32[]{:S(2)}) collective-permute-start(bf16[2,10,64,128]{3,2,1,0:T(8,128)(2,1)} %collective-permute-done.1), channel_id=1, source_target_pairs={{0,24},{1,25},{2,26},{3,27},{4,28},{5,29},{6,30},{7,31}} | collective-permute-start | bytes 983048 | tf_op jit(solution)/shard_map/ppermute | solution.py:161
  15.2 34.4 %collective-permute-start.5 = (bf16[2,10,256,128]{3,2,1,0:T(8,128)(2,1)S(1)}, bf16[2,10,256,128]{3,2,1,0:T(8,128)(2,1)}, u32[]{:S(2)}, u32[]{:S(2)}) collective-permute-start(bf16[2,10,256,128]{3,2,1,0:T(8,128)(2,1)S(1)} %pad_maximum_fusion.1), channel_id=1, source_target_pairs={{0,4},{4,0},{1,5},{5,1},{2,6},{6,2},{3,7},{7,3},{8,12},{12,8},{9,1... | collective-permute-start | bytes 3932168 | tf_op jit(solution)/shard_map/ppermute | solution.py:154
  21.8 28.9 %copy-start.8 = (bf16[1,10,256,128]{3,2,1,0:T(8,128)(2,1)S(1)}, bf16[1,10,256,128]{3,2,1,0:T(8,128)(2,1)}, u32[]{:S(2)}) copy-start(bf16[1,10,256,128]{3,2,1,0:T(8,128)(2,1)} %copy-done.7) | copy-start | bytes 1966084
  21.8 28.9 %copy-start.10 = (bf16[1,10,256,128]{3,2,1,0:T(8,128)(2,1)S(1)}, bf16[1,10,256,128]{3,2,1,0:T(8,128)(2,1)}, u32[]{:S(2)}) copy-start(bf16[1,10,256,128]{3,2,1,0:T(8,128)(2,1)} %copy-done.9) | copy-start | bytes 1966084
  21.8 27.4 %collective-permute-start.4 = (bf16[2,10,128,128]{3,2,1,0:T(8,128)(2,1)S(1)}, bf16[2,10,128,128]{3,2,1,0:T(8,128)(2,1)S(1)}, u32[]{:S(2)}, u32[]{:S(2)}) collective-permute-start(bf16[2,10,128,128]{3,2,1,0:T(8,128)(2,1)S(1)} %get-tuple-element.41), channel_id=1, source_target_pairs={{0,2},{1,3},{2,0},{3,1},{4,6},{5,7},{6,4},{7,5},{8,10},{9,11},{10,... | collective-permute-start | bytes 1966088 | tf_op jit(solution)/shard_map/ppermute | solution.py:166
  24.4 24.9 %collective-permute-start.3 = (bf16[2,10,128,128]{3,2,1,0:T(8,128)(2,1)S(1)}, bf16[2,10,128,128]{3,2,1,0:T(8,128)(2,1)S(1)}, u32[]{:S(2)}, u32[]{:S(2)}) collective-permute-start(bf16[2,10,128,128]{3,2,1,0:T(8,128)(2,1)S(1)} %get-tuple-element.41), channel_id=1, source_target_pairs={{0,1},{1,0},{2,3},{3,2},{4,5},{5,4},{6,7},{7,6},{8,9},{9,8},{10,11... | collective-permute-start | bytes 1966088 | tf_op jit(solution)/shard_map/ppermute | solution.py:166
  50.7 4.1 %copy-start.11 = (bf16[1,1,256,20,128]{4,2,3,1,0:T(8,128)(2,1)S(1)}, bf16[1,1,256,20,128]{4,2,3,1,0:T(8,128)(2,1)}, u32[]{:S(2)}) copy-start(bf16[1,1,256,20,128]{4,2,3,1,0:T(8,128)(2,1)} %param.11) | copy-start | bytes 3932164
  51.5 32.4 %copy-start.16 = (s32[4]{0:T(128)S(1)}, s32[4]{0:T(128)}, u32[]{:S(2)}) copy-start(s32[4]{0:T(128)} %param.19) | copy-start | bytes 52
  51.5 38.0 %copy-start.5 = (s32[4,4]{1,0:T(4,128)S(1)}, s32[4,4]{1,0:T(4,128)}, u32[]{:S(2)}) copy-start(s32[4,4]{1,0:T(4,128)} %mask.5) | copy-start | bytes 196
  51.5 30.7 %collective-permute-start.12 = (bf16[2,10,256,128]{3,2,1,0:T(8,128)(2,1)S(1)}, bf16[2,10,256,128]{3,2,1,0:T(8,128)(2,1)}, u32[]{:S(2)}, u32[]{:S(2)}) collective-permute-start(bf16[2,10,256,128]{3,2,1,0:T(8,128)(2,1)S(1)} %get-tuple-element.22.refs_2_), channel_id=1, source_target_pairs={{8,24},{9,25},{10,26},{11,27},{12,28},{13,29},{14,30},{15,31}} | collective-permute-start | bytes 3932168 | tf_op jit(solution)/shard_map/ppermute | solution.py:196
  53.4 13.7 %collective-permute-start.6 = (bf16[2,10,128,128]{3,2,1,0:T(8,128)(2,1)S(1)}, bf16[2,10,128,128]{3,2,1,0:T(8,128)(2,1)S(1)}, u32[]{:S(2)}, u32[]{:S(2)}) collective-permute-start(bf16[2,10,128,128]{3,2,1,0:T(8,128)(2,1)S(1)} %collective-permute-done.4), channel_id=1, source_target_pairs={{0,1},{1,0},{2,3},{3,2},{4,5},{5,4},{6,7},{7,6},{8,9},{9,8},{10,11... | collective-permute-start | bytes 1966088 | tf_op jit(solution)/shard_map/ppermute | solution.py:166
  55.8 15.2 %collective-permute-start.16 = (bf16[10,256,128]{2,1,0:T(8,128)(2,1)S(1)}, bf16[10,256,128]{2,1,0:T(8,128)(2,1)S(1)}, u32[]{:S(2)}, u32[]{:S(2)}) collective-permute-start(bf16[10,256,128]{2,1,0:T(8,128)(2,1)S(1)} %get-tuple-element.36), channel_id=1, source_target_pairs={{0,4},{4,0},{1,5},{5,1},{2,6},{6,2},{3,7},{7,3},{8,12},{12,8},{9,1... | collective-permute-start | bytes 1966088 | tf_op jit(solution)/shard_map/ppermute | solution.py:156
  56.3 30.8 %collective-permute-start.7 = (bf16[2,10,128,128]{3,2,1,0:T(8,128)(2,1)}, bf16[2,10,128,128]{3,2,1,0:T(8,128)(2,1)}, u32[]{:S(2)}, u32[]{:S(2)}) collective-permute-start(bf16[2,10,128,128]{3,2,1,0:T(8,128)(2,1)} %get-tuple-element.24.refs_13_.refs_9_), channel_id=1, source_target_pairs={{0,8},{16,24},{24,16},{1,9},{17,25},{25,17},{2,10},{18,26},{26,18}... | collective-permute-start | bytes 1966088 | tf_op jit(solution)/shard_map/ppermute | solution.py:184
  63.1 23.4 %collective-permute-start.10 = (bf16[2,10,128,128]{3,2,1,0:T(8,128)(2,1)}, bf16[2,10,128,128]{3,2,1,0:T(8,128)(2,1)}, u32[]{:S(2)}, u32[]{:S(2)}) collective-permute-start(bf16[2,10,128,128]{3,2,1,0:T(8,128)(2,1)} %get-tuple-element.19.refs_1_), channel_id=1, source_target_pairs={{8,24},{9,25},{10,26},{11,27},{12,28},{13,29},{14,30},{15,31}} | collective-permute-start | bytes 1966088 | tf_op jit(solution)/shard_map/ppermute | solution.py:196
  69.4 19.1 %collective-permute-start.14 = (bf16[2,10,128,128]{3,2,1,0:T(8,128)(2,1)}, bf16[2,10,128,128]{3,2,1,0:T(8,128)(2,1)}, u32[]{:S(2)}, u32[]{:S(2)}) collective-permute-start(bf16[2,10,128,128]{3,2,1,0:T(8,128)(2,1)} %get-tuple-element.32.refs_3_.refs_1_), channel_id=1, source_target_pairs={{8,24},{9,25},{10,26},{11,27},{12,28},{13,29},{14,30},{15,31}} | collective-permute-start | bytes 1966088 | tf_op jit(solution)/shard_map/ppermute | solution.py:196
  70.9 0.8 copy-start.2
  71.8 17.7 %collective-permute-start.8 = (bf16[2,10,256,128]{3,2,1,0:T(8,128)(2,1)S(1)}, bf16[2,10,256,128]{3,2,1,0:T(8,128)(2,1)}, u32[]{:S(2)}, u32[]{:S(2)}) collective-permute-start(bf16[2,10,256,128]{3,2,1,0:T(8,128)(2,1)S(1)} %get-tuple-element.25.refs_14_.refs_10_), channel_id=1, source_target_pairs={{0,8},{16,24},{24,16},{1,9},{17,25},{25,17},{2,10},{18,26},{26,18}... | collective-permute-start | bytes 3932168 | tf_op jit(solution)/shard_map/ppermute | solution.py:184
  82.2 7.3 %collective-permute-start.13 = (bf16[2,10,256,128]{3,2,1,0:T(8,128)(2,1)}, bf16[2,10,256,128]{3,2,1,0:T(8,128)(2,1)}, u32[]{:S(2)}, u32[]{:S(2)}) collective-permute-start(bf16[2,10,256,128]{3,2,1,0:T(8,128)(2,1)} %collective-permute-done.12.refs_9_.refs_7_), channel_id=1, source_target_pairs={{24,16},{25,17},{26,18},{27,19},{28,20},{29,21},{30,22},{31,23}} | collective-permute-start | bytes 3932168 | tf_op jit(solution)/shard_map/ppermute | solution.py:197
  86.4 3.0 %collective-permute-start.11 = (bf16[2,10,128,128]{3,2,1,0:T(8,128)(2,1)}, bf16[2,10,128,128]{3,2,1,0:T(8,128)(2,1)S(1)}, u32[]{:S(2)}, u32[]{:S(2)}) collective-permute-start(bf16[2,10,128,128]{3,2,1,0:T(8,128)(2,1)} %collective-permute-done.10.refs_7_.refs_5_), channel_id=1, source_target_pairs={{24,16},{25,17},{26,18},{27,19},{28,20},{29,21},{30,22},{31,23}} | collective-permute-start | bytes 1966088 | tf_op jit(solution)/shard_map/ppermute | solution.py:197
  87.2 12.8 %collective-permute-start.9 = (bf16[2,10,128,128]{3,2,1,0:T(8,128)(2,1)}, bf16[2,10,128,128]{3,2,1,0:T(8,128)(2,1)S(1)}, u32[]{:S(2)}, u32[]{:S(2)}) collective-permute-start(bf16[2,10,128,128]{3,2,1,0:T(8,128)(2,1)} %get-tuple-element.31.refs_15_.refs_5_), channel_id=1, source_target_pairs={{0,8},{16,24},{24,16},{1,9},{17,25},{25,17},{2,10},{18,26},{26,18}... | collective-permute-start | bytes 1966088 | tf_op jit(solution)/shard_map/ppermute | solution.py:184
  88.5 11.4 %collective-permute-start.15 = (bf16[2,10,128,128]{3,2,1,0:T(8,128)(2,1)}, bf16[2,10,128,128]{3,2,1,0:T(8,128)(2,1)S(1)}, u32[]{:S(2)}, u32[]{:S(2)}) collective-permute-start(bf16[2,10,128,128]{3,2,1,0:T(8,128)(2,1)} %collective-permute-done.14.refs_11_.refs_3_), channel_id=1, source_target_pairs={{24,16},{25,17},{26,18},{27,19},{28,20},{29,21},{30,22},{31,23}} | collective-permute-start | bytes 1966088 | tf_op jit(solution)/shard_map/ppermute | solution.py:197
  89.5 10.5 %copy-start.1 = (bf16[2,10,128,128]{3,2,1,0:T(8,128)(2,1)S(1)}, bf16[2,10,128,128]{3,2,1,0:T(8,128)(2,1)}, u32[]{:S(2)}) copy-start(bf16[2,10,128,128]{3,2,1,0:T(8,128)(2,1)} %get-tuple-element.31.refs_15_.refs_5_) | copy-start | bytes 1966084
  89.5 1.1 copy-start.3
  90.6 14.7 %copy-start.15 = (bf16[1280,5120]{1,0:T(8,128)(2,1)S(1)}, bf16[1280,5120]{1,0:T(8,128)(2,1)}, u32[]{:S(2)}) copy-start(bf16[1280,5120]{1,0:T(8,128)(2,1)} %param.17) | copy-start | bytes 39321604
  108.9 5.6 %copy-start.4 = (bf16[10,256,128]{2,1,0:T(8,128)(2,1)S(1)}, bf16[10,256,128]{2,1,0:T(8,128)(2,1)}, u32[]{:S(2)}) copy-start(bf16[10,256,128]{2,1,0:T(8,128)(2,1)} %get-tuple-element.18.refs_0_) | copy-start | bytes 1966084
  109.8 21.4 %collective-permute-start.17 = (bf16[256,1024]{1,0:T(8,128)(2,1)S(1)}, bf16[256,1024]{1,0:T(8,128)(2,1)S(1)}, u32[]{:S(2)}, u32[]{:S(2)}) collective-permute-start(bf16[256,1024]{1,0:T(8,128)(2,1)S(1)} %fusion.11), channel_id=1, source_target_pairs={{4,0},{0,4},{5,1},{1,5},{6,2},{2,6},{7,3},{3,7},{12,8},{8,12},{13,... | collective-permute-start | bytes 1572872 | tf_op jit(solution)/shard_map/ppermute | solution.py:217
  110.4 25.5 %collective-permute-start.18 = (bf16[256,1024]{1,0:T(8,128)(2,1)S(1)}, bf16[256,1024]{1,0:T(8,128)(2,1)S(1)}, u32[]{:S(2)}, u32[]{:S(2)}) collective-permute-start(bf16[256,1024]{1,0:T(8,128)(2,1)S(1)} %fusion.14), channel_id=1, source_target_pairs={{4,0},{0,4},{5,1},{1,5},{6,2},{2,6},{7,3},{3,7},{12,8},{8,12},{13,... | collective-permute-start | bytes 1572872 | tf_op jit(solution)/shard_map/ppermute | solution.py:217
  111.9 35.2 %collective-permute-start.19 = (bf16[256,1024]{1,0:T(8,128)(2,1)S(1)}, bf16[256,1024]{1,0:T(8,128)(2,1)S(1)}, u32[]{:S(2)}, u32[]{:S(2)}) collective-permute-start(bf16[256,1024]{1,0:T(8,128)(2,1)S(1)} %fusion.17), channel_id=1, source_target_pairs={{4,0},{0,4},{5,1},{1,5},{6,2},{2,6},{7,3},{3,7},{12,8},{8,12},{13,... | collective-permute-start | bytes 1572872 | tf_op jit(solution)/shard_map/ppermute | solution.py:217
  112.5 45.9 %collective-permute-start.20 = (bf16[256,1024]{1,0:T(8,128)(2,1)S(1)}, bf16[256,1024]{1,0:T(8,128)(2,1)S(1)}, u32[]{:S(2)}, u32[]{:S(2)}) collective-permute-start(bf16[256,1024]{1,0:T(8,128)(2,1)S(1)} %fusion.20), channel_id=1, source_target_pairs={{4,0},{0,4},{5,1},{1,5},{6,2},{2,6},{7,3},{3,7},{12,8},{8,12},{13,... | collective-permute-start | bytes 1572872 | tf_op jit(solution)/shard_map/ppermute | solution.py:217
  114.0 53.0 %collective-permute-start.21 = (bf16[256,1024]{1,0:T(8,128)(2,1)S(1)}, bf16[256,1024]{1,0:T(8,128)(2,1)S(1)}, u32[]{:S(2)}, u32[]{:S(2)}) collective-permute-start(bf16[256,1024]{1,0:T(8,128)(2,1)S(1)} %fusion.23), channel_id=1, source_target_pairs={{4,0},{0,4},{5,1},{1,5},{6,2},{2,6},{7,3},{3,7},{12,8},{8,12},{13,... | collective-permute-start | bytes 1572872 | tf_op jit(solution)/shard_map/ppermute | solution.py:217
  127.3 3.9 %copy-start.6 = (bf16[1,1,256,5120]{3,2,1,0:T(8,128)(2,1)S(1)}, bf16[1,1,256,5120]{3,2,1,0:T(8,128)(2,1)}, u32[]{:S(2)}) copy-start(bf16[1,1,256,5120]{3,2,1,0:T(8,128)(2,1)} %param.16) | copy-start | bytes 7864324

commit v5 on v4

--- a/solution.py
+++ b/solution.py
@@ -144,8 +144,6 @@
     pair = lambda a, b, d: jnp.stack([take(a, d), take(b, d)])
     cycle = lambda d: [(i, (i + d) % splits) for i in range(splits)]
 
-    level_now = lax.dynamic_index_in_dim(levels, span, 0, keepdims=False)
-    gate_row = lax.dynamic_index_in_dim(gates, level_now, 0, keepdims=False)
 
     ctx_parts, kv_parts, q_parts = [pair(ck, cv, 0)], [pair(k, v, 0)], [take(q, 0)]
     for d in range(1, splits):
@@ -198,9 +196,9 @@
     slots.append((lambda c: jnp.where(c >= final - 1, 1, -1), list(zip(far, near))))
     slots.append((lambda c: jnp.where(c == final, 0, -1), [a for _, a in held]))
 
-    early = [(origin, arrays[:-1]) for origin, arrays in slots]
-    late = [(origin, arrays[-1:]) for origin, arrays in slots]
-    q_parts[0], gate_row = lax.optimization_barrier((q_parts[0], gate_row))
+    cuts = [len(groups) - 1 if i in (0, 1, len(slots) - 1) else len(groups) - 2 for i in range(len(slots))]
+    early = [(origin, arrays[:cut]) for (origin, arrays), cut in zip(slots, cuts)]
+    late = [(origin, arrays[cut:]) for (origin, arrays), cut in zip(slots, cuts)]
     states = {}
     for d in range(1, splits):
         states[d] = attend(q_parts[d], early, span_mask, None, False)
@@ -216,6 +214,9 @@
             partial = project(attended, out_weight[:, j * width : (j + 1) * width])
             returned[j].append(lax.ppermute(partial, "head", back))
     attended = attend(q_parts[0], slots, span_mask, None, True)
+    attended, levels = lax.optimization_barrier((attended, levels))
+    level_now = lax.dynamic_index_in_dim(levels, span, 0, keepdims=False)
+    gate_row = lax.dynamic_index_in_dim(gates, level_now, 0, keepdims=False)
     kept = lax.optimization_barrier(project(attended, out_weight))
     updated = hidden
     for j in range(COL_BLOCKS):

time: 170 us -> 191 us (1.12)
  matrix products: 8.25 us -> 18.2 us
  local copies, waits for them, and re-layouts: 8.99 us -> 14.7 us
  other arithmetic: 8.8 us -> 12 us
    dot_general x6, matrix products: 8.25 us -> 18.2 us  [sublayer(): jnp.dot(a, w, preferred_element_type=jnp.float32).astype(jnp.bfloat16)]
    unnamed x36 -> x52, local copies, waits for them, and re-layouts: 4.68 us -> 9.3 us
    dynamic_update_slice x5, other arithmetic: 2.29 us -> 6.76 us  [sublayer(): lax.dynamic_update_slice_in_dim(updated, fresh.astype(jnp.bfloat16), j *...]
  transfers between devices with their start and end apart: 22 -> 22, of which waited for: 9 -> 9; matrix products, arithmetic and copies ran while one was open for 9% -> 13% of each run, Pallas kernels for 13% -> 4%
where the time goes in v5:
time: 191 us
  waiting for transfers between devices  64.9 us (34%)
  starting transfers between devices  49.1 us (26%)
  Pallas kernels  28.6 us (15%)
  matrix products  18.2 us (10%)
  local copies, waits for them, and re-layouts  14.7 us (8%)
  other arithmetic  12 us (6%)
  between operations  3.1 us (2%)
    ppermute x5, waiting for transfers between devices, sublayer(): returned[j].append(lax.ppermute(partial, 'head', back))  34.3 us
    pallas_call x3, Pallas kernels, attend(): pl.pallas_call(functools.partial(flash_kernel, layout=layout, count=len(a...  28.6 us
    ppermute x3, waiting for transfers between devices, sublayer(): lax.ppermute(pieces[i - low], 'branch', [(b, b ^ low) for b in range(bran...  27.2 us
    ppermute x3, starting transfers between devices, sublayer(): lax.ppermute(a, 'tm', pairs + [(final, final - 1)])  18.5 us
    dot_general x6, matrix products, sublayer(): jnp.dot(a, w, preferred_element_type=jnp.float32).astype(jnp.bfloat16)  18.2 us
    unnamed x52, local copies, waits for them, and re-layouts  9.3 us
    dynamic_update_slice x5, other arithmetic, sublayer(): lax.dynamic_update_slice_in_dim(updated, fresh.astype(jnp.bfloat16), j *...  6.76 us
    ppermute x3, starting transfers between devices, sublayer(): lax.ppermute(pieces[i - low], 'branch', [(b, b ^ low) for b in range(bran...  5.67 us
  transfers between devices with their start and end apart: 22, of which 9 were waited for; matrix products, arithmetic and copies ran while one was open for 13% of the time, Pallas kernels for 4%

profile of v5, /device:TPU:0, one launch (start us, length us, event | category | flops | bytes accessed | tf_op | source)
XLA Modules:
  0.0 190.6 jit_solution(16065154557761984117)
XLA Ops:
  0.0 1.0 copy-done.22
  1.2 3.0 %collective-permute-start.1 = (bf16[2,10,64,128]{3,2,1,0:T(8,128)(2,1)S(1)}, bf16[2,10,64,128]{3,2,1,0:T(8,128)(2,1)S(1)}, u32[]{:S(2)}, u32[]{:S(2)}) collective-permute-start(bf16[2,10,64,128]{3,2,1,0:T(8,128)(2,1)S(1)} %pad_maximum_fusion.4), channel_id=1, source_target_pairs={{0,4},{4,0},{1,5},{5,1},{2,6},{6,2},{3,7},{7,3},{8,12},{12,8},{9,1... | collective-permute-start | bytes 983048 | tf_op jit(solution)/shard_map/ppermute | solution.py:150
  4.2 0.8 pad_maximum_fusion.3
  5.0 3.3 %collective-permute-start = (bf16[2,10,64,128]{3,2,1,0:T(8,128)(2,1)}, bf16[2,10,64,128]{3,2,1,0:T(8,128)(2,1)}, u32[]{:S(2)}, u32[]{:S(2)}) collective-permute-start(bf16[2,10,64,128]{3,2,1,0:T(8,128)(2,1)} %pad_maximum_fusion.3), channel_id=1, source_target_pairs={{0,24},{1,25},{2,26},{3,27},{4,28},{5,29},{6,30},{7,31}} | collective-permute-start | bytes 983048 | tf_op jit(solution)/shard_map/ppermute | solution.py:159
  8.3 1.5 dynamic-slice_bitcast_fusion.1
  9.7 2.2 %collective-permute-done.1 = bf16[2,10,64,128]{3,2,1,0:T(8,128)(2,1)S(1)} collective-permute-done((bf16[2,10,64,128]{3,2,1,0:T(8,128)(2,1)S(1)}, bf16[2,10,64,128]{3,2,1,0:T(8,128)(2,1)S(1)}, u32[]{:S(2)}, u32[]{:S(2)}) %collective-permute-start.1) | collective-permute-done | bytes 327712 | tf_op jit(solution)/shard_map/ppermute | solution.py:150
  11.9 2.3 %collective-permute-start.2 = (bf16[2,10,64,128]{3,2,1,0:T(8,128)(2,1)S(1)}, bf16[2,10,64,128]{3,2,1,0:T(8,128)(2,1)S(1)}, u32[]{:S(2)}, u32[]{:S(2)}) collective-permute-start(bf16[2,10,64,128]{3,2,1,0:T(8,128)(2,1)S(1)} %collective-permute-done.1), channel_id=1, source_target_pairs={{0,24},{1,25},{2,26},{3,27},{4,28},{5,29},{6,30},{7,31}} | collective-permute-start | bytes 983048 | tf_op jit(solution)/shard_map/ppermute | solution.py:159
  14.2 1.2 pad_maximum_fusion.1
  15.4 1.5 collective-permute-start.5
  17.6 1.2 collective-permute-done.2
  18.8 0.4 broadcast_select_fusion.3
  19.2 2.7 %collective-permute-start.4 = (bf16[2,10,128,128]{3,2,1,0:T(8,128)(2,1)S(1)}, bf16[2,10,128,128]{3,2,1,0:T(8,128)(2,1)S(1)}, u32[]{:S(2)}, u32[]{:S(2)}) collective-permute-start(bf16[2,10,128,128]{3,2,1,0:T(8,128)(2,1)S(1)} %get-tuple-element.41), channel_id=1, source_target_pairs={{0,2},{1,3},{2,0},{3,1},{4,6},{5,7},{6,4},{7,5},{8,10},{9,11},{10,... | collective-permute-start | bytes 1966088 | tf_op jit(solution)/shard_map/ppermute | solution.py:164
  21.8 1.6 collective-permute-start.3
  23.4 23.7 %collective-permute-done.4 = bf16[2,10,128,128]{3,2,1,0:T(8,128)(2,1)S(1)} collective-permute-done((bf16[2,10,128,128]{3,2,1,0:T(8,128)(2,1)S(1)}, bf16[2,10,128,128]{3,2,1,0:T(8,128)(2,1)S(1)}, u32[]{:S(2)}, u32[]{:S(2)}) %collective-permute-start.4) | collective-permute-done | bytes 655392 | tf_op jit(solution)/shard_map/ppermute | solution.py:164
  47.1 0.2 collective-permute-done.3
  47.5 1.1 slice.104
  48.7 0.7 broadcast_select_fusion
  49.4 1.8 collective-permute-start.12
  51.2 1.4 collective-permute-start.6
  52.7 1.0 dynamic-slice_bitcast_fusion.5
  53.6 0.5 collective-permute-start.16
  54.2 5.9 %collective-permute-start.7 = (bf16[2,10,128,128]{3,2,1,0:T(8,128)(2,1)S(1)}, bf16[2,10,128,128]{3,2,1,0:T(8,128)(2,1)S(1)}, u32[]{:S(2)}, u32[]{:S(2)}) collective-permute-start(bf16[2,10,128,128]{3,2,1,0:T(8,128)(2,1)S(1)} %get-tuple-element.22.refs_13_.refs_7_), channel_id=1, source_target_pairs={{0,8},{16,24},{24,16},{1,9},{17,25},{25,17},{2,10},{18,26},{26,18}... | collective-permute-start | bytes 1966088 | tf_op jit(solution)/shard_map/ppermute | solution.py:182
  60.1 1.5 collective-permute-start.10
  61.7 3.3 %collective-permute-done.6 = bf16[2,10,128,128]{3,2,1,0:T(8,128)(2,1)S(1)} collective-permute-done((bf16[2,10,128,128]{3,2,1,0:T(8,128)(2,1)S(1)}, bf16[2,10,128,128]{3,2,1,0:T(8,128)(2,1)S(1)}, u32[]{:S(2)}, u32[]{:S(2)}) %collective-permute-start.6) | collective-permute-done | bytes 655392 | tf_op jit(solution)/shard_map/ppermute | solution.py:164
  65.0 6.7 %collective-permute-start.8 = (bf16[2,10,256,128]{3,2,1,0:T(8,128)(2,1)S(1)}, bf16[2,10,256,128]{3,2,1,0:T(8,128)(2,1)}, u32[]{:S(2)}, u32[]{:S(2)}) collective-permute-start(bf16[2,10,256,128]{3,2,1,0:T(8,128)(2,1)S(1)} %get-tuple-element.23.refs_14_.refs_8_), channel_id=1, source_target_pairs={{0,8},{16,24},{24,16},{1,9},{17,25},{25,17},{2,10},{18,26},{26,18}... | collective-permute-start | bytes 3932168 | tf_op jit(solution)/shard_map/ppermute | solution.py:182
  71.6 2.1 %broadcast_select_fusion.2 = (bf16[2,10,128,128]{3,2,1,0:T(8,128)(2,1)}, bf16[2,10,128,128]{3,2,1,0:T(8,128)(2,1)S(1)}) fusion(bf16[2,10,128,128]{3,2,1,0:T(8,128)(2,1)S(1)} %collective-permute-done.6, pred[]{:T(512)S(6)} %or.2, bf16[2,10,256,128]{3,2,1,0:T(8,128)(2,1)} %collective-permute-done.5, pred[]{:T(512)S(6)} %lt.26), kind=kLoop, calls=%fused_computation.36 | loop fusion | flops 655360 | bytes 2621442 | tf_op jit(solution)/shard_map/jit(_where)/select_n | solution.py:178
  73.8 0.8 copy-done.5
  74.6 1.5 collective-permute-start.14
  76.1 0.8 copy-done.3
  76.9 1.7 collective-permute-start.13
  78.7 1.5 collective-permute-start.11
  80.2 0.8 copy-done.7
  81.0 5.9 %collective-permute-start.9 = (bf16[2,10,128,128]{3,2,1,0:T(8,128)(2,1)}, bf16[2,10,128,128]{3,2,1,0:T(8,128)(2,1)}, u32[]{:S(2)}, u32[]{:S(2)}) collective-permute-start(bf16[2,10,128,128]{3,2,1,0:T(8,128)(2,1)} %get-tuple-element.31.refs_15_.refs_7_), channel_id=1, source_target_pairs={{0,8},{16,24},{24,16},{1,9},{17,25},{25,17},{2,10},{18,26},{26,18}... | collective-permute-start | bytes 1966088 | tf_op jit(solution)/shard_map/ppermute | solution.py:182
  86.9 1.6 collective-permute-start.15
  88.5 1.1 copy-done.1
  89.6 1.1 copy-done.6
  90.7 1.1 copy-done.8
  91.7 8.0 %shard_map.110 = (f32[10,256,128]{2,1,0:T(8,128)S(1)}, f32[10,256,128]{2,1,0:T(8,128)S(1)}, f32[10,256,128]{2,1,0:T(8,128)S(1)}) custom-call(s32[4,4]{1,0:T(4,128)S(1)} %copy-done.12, bf16[10,256,128]{2,1,0:T(8,128)(2,1)S(1)} %copy-done.6, bf16[2,10,128,128]{3,2,1,0:T(8,128)(2,1)S(1)} %copy-done.1, bf16[2,10,256,128]{3,2,1,0:T(8,128)(2,1)S(1)} %get-tuple-element.20.refs_2_, ...), custom_call_target="tpu_custom_call" | custom-call | flops 1677721600 | bytes 7864320 | tf_op jit(solution)/shard_map/pallas_call | solution.py:94
  99.8 7.6 %shard_map.111 = bf16[256,1280]{1,0:T(8,128)(2,1)S(1)} custom-call(s32[4,4]{1,0:T(4,128)S(1)} %copy-done.12, bf16[10,256,128]{2,1,0:T(8,128)(2,1)S(1)} %copy-done.6, bf16[2,10,128,128]{3,2,1,0:T(8,128)(2,1)S(1)} %copy-done.4, bf16[2,10,128,128]{3,2,1,0:T(8,128)(2,1)} %collective-permute-done.9.refs_6_.refs_2_, ...), custom_call_target="tpu_custom_call" | custom-call | flops 1006632960 | bytes 5242880 | tf_op jit(solution)/shard_map/pallas_call | solution.py:94
  107.5 1.6 fusion.23
  109.1 1.7 fusion.20
  110.8 1.6 fusion.17
  112.5 1.6 fusion.14
  114.1 1.7 fusion.11
  115.8 12.9 %shard_map.109 = bf16[256,1280]{1,0:T(8,128)(2,1)S(1)} custom-call(s32[4,4]{1,0:T(4,128)S(1)} %copy-done.12, bf16[10,256,128]{2,1,0:T(8,128)(2,1)S(1)} %copy-done.10, bf16[2,10,128,128]{3,2,1,0:T(8,128)(2,1)S(1)} %copy-done.2, bf16[2,10,256,128]{3,2,1,0:T(8,128)(2,1)S(1)} %get-tuple-element.20.refs_2_, bf16[2,10,128,128]{3,2,1,0:T(8,128)(2,1)S(1)} %copy-done.4, ...), custom_call_target="tpu_custom_call" | custom-call | flops 2684354560 | bytes 11796480 | tf_op jit(solution)/shard_map/pallas_call | solution.py:94
  128.7 0.8 copy-done.11
  129.5 0.7 dynamic_slice.47
  131.6 0.6 collective-permute-start.17
  132.2 1.5 collective-permute-start.18
  133.7 0.5 collective-permute-start.19
  134.2 1.5 collective-permute-start.20
  135.7 0.5 collective-permute-start.21
  136.2 10.0 %convolution_convert_fusion = bf16[256,5120]{1,0:T(8,128)(2,1)} fusion(bf16[256,1280]{1,0:T(8,128)(2,1)} %copy-done.11, bf16[1280,5120]{1,0:T(8,128)(2,1)} %param.17), kind=kOutput, calls=%fused_computation | convolution fusion | flops 3356753920 | bytes 16384000 | tf_op jit(solution)/shard_map/dot_general | solution.py:208
  146.9 1.1 fusion.33
  148.0 1.5 fusion.27
  149.5 8.4 %collective-permute-done.18 = bf16[256,1024]{1,0:T(8,128)(2,1)} collective-permute-done((bf16[256,1024]{1,0:T(8,128)(2,1)}, bf16[256,1024]{1,0:T(8,128)(2,1)}, u32[]{:S(2)}, u32[]{:S(2)}) %collective-permute-start.18) | collective-permute-done | bytes 524320 | tf_op jit(solution)/shard_map/ppermute | solution.py:215
  158.0 1.5 fusion.28
  159.5 9.7 %collective-permute-done.19 = bf16[256,1024]{1,0:T(8,128)(2,1)} collective-permute-done((bf16[256,1024]{1,0:T(8,128)(2,1)}, bf16[256,1024]{1,0:T(8,128)(2,1)}, u32[]{:S(2)}, u32[]{:S(2)}) %collective-permute-start.19) | collective-permute-done | bytes 524320 | tf_op jit(solution)/shard_map/ppermute | solution.py:215
  169.2 1.3 fusion.29
  170.6 9.9 %collective-permute-done.20 = bf16[256,1024]{1,0:T(8,128)(2,1)} collective-permute-done((bf16[256,1024]{1,0:T(8,128)(2,1)}, bf16[256,1024]{1,0:T(8,128)(2,1)}, u32[]{:S(2)}, u32[]{:S(2)}) %collective-permute-start.20) | collective-permute-done | bytes 524320 | tf_op jit(solution)/shard_map/ppermute | solution.py:215
  180.5 1.3 fusion.30
  181.8 1.5 copy.17
  183.3 6.3 %collective-permute-done.21 = bf16[256,1024]{1,0:T(8,128)(2,1)S(1)} collective-permute-done((bf16[256,1024]{1,0:T(8,128)(2,1)}, bf16[256,1024]{1,0:T(8,128)(2,1)S(1)}, u32[]{:S(2)}, u32[]{:S(2)}) %collective-permute-start.21) | collective-permute-done | bytes 524320 | tf_op jit(solution)/shard_map/ppermute | solution.py:215
  189.6 1.1 fusion.32
  (61 shorter events, 0.5 us)
Async XLA Ops:
  0.0 1.0 copy-start.22
  0.0 1.1 copy-start.21
  0.0 8.3 %copy-start.20 = (bf16[1,1,256,20,128]{4,2,3,1,0:T(8,128)(2,1)S(1)}, bf16[1,1,256,20,128]{4,2,3,1,0:T(8,128)(2,1)}, u32[]{:S(2)}) copy-start(bf16[1,1,256,20,128]{4,2,3,1,0:T(8,128)(2,1)} %param.13) | copy-start | bytes 3932164
  1.2 10.7 %collective-permute-start.1 = (bf16[2,10,64,128]{3,2,1,0:T(8,128)(2,1)S(1)}, bf16[2,10,64,128]{3,2,1,0:T(8,128)(2,1)S(1)}, u32[]{:S(2)}, u32[]{:S(2)}) collective-permute-start(bf16[2,10,64,128]{3,2,1,0:T(8,128)(2,1)S(1)} %pad_maximum_fusion.4), channel_id=1, source_target_pairs={{0,4},{4,0},{1,5},{5,1},{2,6},{6,2},{3,7},{7,3},{8,12},{12,8},{9,1... | collective-permute-start | bytes 983048 | tf_op jit(solution)/shard_map/ppermute | solution.py:150
  5.0 12.5 %collective-permute-start = (bf16[2,10,64,128]{3,2,1,0:T(8,128)(2,1)}, bf16[2,10,64,128]{3,2,1,0:T(8,128)(2,1)}, u32[]{:S(2)}, u32[]{:S(2)}) collective-permute-start(bf16[2,10,64,128]{3,2,1,0:T(8,128)(2,1)} %pad_maximum_fusion.3), channel_id=1, source_target_pairs={{0,24},{1,25},{2,26},{3,27},{4,28},{5,29},{6,30},{7,31}} | collective-permute-start | bytes 983048 | tf_op jit(solution)/shard_map/ppermute | solution.py:159
  9.7 9.4 %copy-start.14 = (bf16[1,10,256,128]{3,2,1,0:T(8,128)(2,1)}, bf16[1,10,256,128]{3,2,1,0:T(8,128)(2,1)S(1)}, u32[]{:S(2)}) copy-start(bf16[1,10,256,128]{3,2,1,0:T(8,128)(2,1)S(1)} %get-tuple-element.40) | copy-start | bytes 1966084
  9.7 9.4 %copy-start.16 = (bf16[1,10,256,128]{3,2,1,0:T(8,128)(2,1)}, bf16[1,10,256,128]{3,2,1,0:T(8,128)(2,1)S(1)}, u32[]{:S(2)}) copy-start(bf16[1,10,256,128]{3,2,1,0:T(8,128)(2,1)S(1)} %get-tuple-element.51) | copy-start | bytes 1966084
  11.9 6.8 %collective-permute-start.2 = (bf16[2,10,64,128]{3,2,1,0:T(8,128)(2,1)S(1)}, bf16[2,10,64,128]{3,2,1,0:T(8,128)(2,1)S(1)}, u32[]{:S(2)}, u32[]{:S(2)}) collective-permute-start(bf16[2,10,64,128]{3,2,1,0:T(8,128)(2,1)S(1)} %collective-permute-done.1), channel_id=1, source_target_pairs={{0,24},{1,25},{2,26},{3,27},{4,28},{5,29},{6,30},{7,31}} | collective-permute-start | bytes 983048 | tf_op jit(solution)/shard_map/ppermute | solution.py:159
  15.4 32.2 %collective-permute-start.5 = (bf16[2,10,256,128]{3,2,1,0:T(8,128)(2,1)}, bf16[2,10,256,128]{3,2,1,0:T(8,128)(2,1)}, u32[]{:S(2)}, u32[]{:S(2)}) collective-permute-start(bf16[2,10,256,128]{3,2,1,0:T(8,128)(2,1)} %pad_maximum_fusion.1), channel_id=1, source_target_pairs={{0,4},{4,0},{1,5},{5,1},{2,6},{6,2},{3,7},{7,3},{8,12},{12,8},{9,1... | collective-permute-start | bytes 3932168 | tf_op jit(solution)/shard_map/ppermute | solution.py:152
  19.2 41.0 %copy-start = (bf16[2,10,128,128]{3,2,1,0:T(8,128)(2,1)}, bf16[2,10,128,128]{3,2,1,0:T(8,128)(2,1)S(1)}, u32[]{:S(2)}) copy-start(bf16[2,10,128,128]{3,2,1,0:T(8,128)(2,1)S(1)} %get-tuple-element.17.refs_1_) | copy-start | bytes 1966084
  19.2 29.5 %copy-start.15 = (bf16[1,10,256,128]{3,2,1,0:T(8,128)(2,1)S(1)}, bf16[1,10,256,128]{3,2,1,0:T(8,128)(2,1)}, u32[]{:S(2)}) copy-start(bf16[1,10,256,128]{3,2,1,0:T(8,128)(2,1)} %copy-done.14) | copy-start | bytes 1966084
  19.2 29.5 %copy-start.17 = (bf16[1,10,256,128]{3,2,1,0:T(8,128)(2,1)S(1)}, bf16[1,10,256,128]{3,2,1,0:T(8,128)(2,1)}, u32[]{:S(2)}) copy-start(bf16[1,10,256,128]{3,2,1,0:T(8,128)(2,1)} %copy-done.16) | copy-start | bytes 1966084
  19.2 28.0 %collective-permute-start.4 = (bf16[2,10,128,128]{3,2,1,0:T(8,128)(2,1)S(1)}, bf16[2,10,128,128]{3,2,1,0:T(8,128)(2,1)S(1)}, u32[]{:S(2)}, u32[]{:S(2)}) collective-permute-start(bf16[2,10,128,128]{3,2,1,0:T(8,128)(2,1)S(1)} %get-tuple-element.41), channel_id=1, source_target_pairs={{0,2},{1,3},{2,0},{3,1},{4,6},{5,7},{6,4},{7,5},{8,10},{9,11},{10,... | collective-permute-start | bytes 1966088 | tf_op jit(solution)/shard_map/ppermute | solution.py:164
  21.8 25.5 %collective-permute-start.3 = (bf16[2,10,128,128]{3,2,1,0:T(8,128)(2,1)S(1)}, bf16[2,10,128,128]{3,2,1,0:T(8,128)(2,1)S(1)}, u32[]{:S(2)}, u32[]{:S(2)}) collective-permute-start(bf16[2,10,128,128]{3,2,1,0:T(8,128)(2,1)S(1)} %get-tuple-element.41), channel_id=1, source_target_pairs={{0,1},{1,0},{2,3},{3,2},{4,5},{5,4},{6,7},{7,6},{8,9},{9,8},{10,11... | collective-permute-start | bytes 1966088 | tf_op jit(solution)/shard_map/ppermute | solution.py:164
  48.7 4.0 %copy-start.19 = (bf16[1,1,256,20,128]{4,2,3,1,0:T(8,128)(2,1)S(1)}, bf16[1,1,256,20,128]{4,2,3,1,0:T(8,128)(2,1)}, u32[]{:S(2)}) copy-start(bf16[1,1,256,20,128]{4,2,3,1,0:T(8,128)(2,1)} %param.11) | copy-start | bytes 3932164
  49.4 39.0 %copy-start.12 = (s32[4,4]{1,0:T(4,128)S(1)}, s32[4,4]{1,0:T(4,128)}, u32[]{:S(2)}) copy-start(s32[4,4]{1,0:T(4,128)} %mask.5) | copy-start | bytes 196
  49.4 27.5 %collective-permute-start.12 = (bf16[2,10,256,128]{3,2,1,0:T(8,128)(2,1)S(1)}, bf16[2,10,256,128]{3,2,1,0:T(8,128)(2,1)}, u32[]{:S(2)}, u32[]{:S(2)}) collective-permute-start(bf16[2,10,256,128]{3,2,1,0:T(8,128)(2,1)S(1)} %get-tuple-element.20.refs_2_), channel_id=1, source_target_pairs={{8,24},{9,25},{10,26},{11,27},{12,28},{13,29},{14,30},{15,31}} | collective-permute-start | bytes 3932168 | tf_op jit(solution)/shard_map/ppermute | solution.py:194
  51.2 13.7 %collective-permute-start.6 = (bf16[2,10,128,128]{3,2,1,0:T(8,128)(2,1)S(1)}, bf16[2,10,128,128]{3,2,1,0:T(8,128)(2,1)S(1)}, u32[]{:S(2)}, u32[]{:S(2)}) collective-permute-start(bf16[2,10,128,128]{3,2,1,0:T(8,128)(2,1)S(1)} %collective-permute-done.4), channel_id=1, source_target_pairs={{0,1},{1,0},{2,3},{3,2},{4,5},{5,4},{6,7},{7,6},{8,9},{9,8},{10,11... | collective-permute-start | bytes 1966088 | tf_op jit(solution)/shard_map/ppermute | solution.py:164
  53.6 20.1 %collective-permute-start.16 = (bf16[10,256,128]{2,1,0:T(8,128)(2,1)S(1)}, bf16[10,256,128]{2,1,0:T(8,128)(2,1)S(1)}, u32[]{:S(2)}, u32[]{:S(2)}) collective-permute-start(bf16[10,256,128]{2,1,0:T(8,128)(2,1)S(1)} %get-tuple-element.36), channel_id=1, source_target_pairs={{0,4},{4,0},{1,5},{5,1},{2,6},{6,2},{3,7},{7,3},{8,12},{12,8},{9,1... | collective-permute-start | bytes 1966088 | tf_op jit(solution)/shard_map/ppermute | solution.py:154
  54.2 26.0 %collective-permute-start.7 = (bf16[2,10,128,128]{3,2,1,0:T(8,128)(2,1)S(1)}, bf16[2,10,128,128]{3,2,1,0:T(8,128)(2,1)S(1)}, u32[]{:S(2)}, u32[]{:S(2)}) collective-permute-start(bf16[2,10,128,128]{3,2,1,0:T(8,128)(2,1)S(1)} %get-tuple-element.22.refs_13_.refs_7_), channel_id=1, source_target_pairs={{0,8},{16,24},{24,16},{1,9},{17,25},{25,17},{2,10},{18,26},{26,18}... | collective-permute-start | bytes 1966088 | tf_op jit(solution)/shard_map/ppermute | solution.py:182
  60.1 18.5 %collective-permute-start.10 = (bf16[2,10,128,128]{3,2,1,0:T(8,128)(2,1)S(1)}, bf16[2,10,128,128]{3,2,1,0:T(8,128)(2,1)}, u32[]{:S(2)}, u32[]{:S(2)}) collective-permute-start(bf16[2,10,128,128]{3,2,1,0:T(8,128)(2,1)S(1)} %get-tuple-element.17.refs_1_), channel_id=1, source_target_pairs={{8,24},{9,25},{10,26},{11,27},{12,28},{13,29},{14,30},{15,31}} | collective-permute-start | bytes 1966088 | tf_op jit(solution)/shard_map/ppermute | solution.py:194
  65.0 23.5 %collective-permute-start.8 = (bf16[2,10,256,128]{3,2,1,0:T(8,128)(2,1)S(1)}, bf16[2,10,256,128]{3,2,1,0:T(8,128)(2,1)}, u32[]{:S(2)}, u32[]{:S(2)}) collective-permute-start(bf16[2,10,256,128]{3,2,1,0:T(8,128)(2,1)S(1)} %get-tuple-element.23.refs_14_.refs_8_), channel_id=1, source_target_pairs={{0,8},{16,24},{24,16},{1,9},{17,25},{25,17},{2,10},{18,26},{26,18}... | collective-permute-start | bytes 3932168 | tf_op jit(solution)/shard_map/ppermute | solution.py:182
  73.8 0.8 copy-start.5
  74.6 12.3 %collective-permute-start.14 = (bf16[2,10,128,128]{3,2,1,0:T(8,128)(2,1)S(1)}, bf16[2,10,128,128]{3,2,1,0:T(8,128)(2,1)}, u32[]{:S(2)}, u32[]{:S(2)}) collective-permute-start(bf16[2,10,128,128]{3,2,1,0:T(8,128)(2,1)S(1)} %get-tuple-element.32.refs_3_.refs_1_), channel_id=1, source_target_pairs={{8,24},{9,25},{10,26},{11,27},{12,28},{13,29},{14,30},{15,31}} | collective-permute-start | bytes 1966088 | tf_op jit(solution)/shard_map/ppermute | solution.py:194
  76.1 0.8 copy-start.3
  76.9 22.9 %collective-permute-start.13 = (bf16[2,10,256,128]{3,2,1,0:T(8,128)(2,1)}, bf16[2,10,256,128]{3,2,1,0:T(8,128)(2,1)}, u32[]{:S(2)}, u32[]{:S(2)}) collective-permute-start(bf16[2,10,256,128]{3,2,1,0:T(8,128)(2,1)} %collective-permute-done.12.refs_9_.refs_3_), channel_id=1, source_target_pairs={{24,16},{25,17},{26,18},{27,19},{28,20},{29,21},{30,22},{31,23}} | collective-permute-start | bytes 3932168 | tf_op jit(solution)/shard_map/ppermute | solution.py:195
  78.7 9.8 %collective-permute-start.11 = (bf16[2,10,128,128]{3,2,1,0:T(8,128)(2,1)}, bf16[2,10,128,128]{3,2,1,0:T(8,128)(2,1)}, u32[]{:S(2)}, u32[]{:S(2)}) collective-permute-start(bf16[2,10,128,128]{3,2,1,0:T(8,128)(2,1)} %collective-permute-done.10.refs_7_.refs_5_), channel_id=1, source_target_pairs={{24,16},{25,17},{26,18},{27,19},{28,20},{29,21},{30,22},{31,23}} | collective-permute-start | bytes 1966088 | tf_op jit(solution)/shard_map/ppermute | solution.py:195
  80.2 0.8 copy-start.7
  81.0 18.8 %collective-permute-start.9 = (bf16[2,10,128,128]{3,2,1,0:T(8,128)(2,1)}, bf16[2,10,128,128]{3,2,1,0:T(8,128)(2,1)}, u32[]{:S(2)}, u32[]{:S(2)}) collective-permute-start(bf16[2,10,128,128]{3,2,1,0:T(8,128)(2,1)} %get-tuple-element.31.refs_15_.refs_7_), channel_id=1, source_target_pairs={{0,8},{16,24},{24,16},{1,9},{17,25},{25,17},{2,10},{18,26},{26,18}... | collective-permute-start | bytes 1966088 | tf_op jit(solution)/shard_map/ppermute | solution.py:182
  86.9 12.9 %collective-permute-start.15 = (bf16[2,10,128,128]{3,2,1,0:T(8,128)(2,1)}, bf16[2,10,128,128]{3,2,1,0:T(8,128)(2,1)}, u32[]{:S(2)}, u32[]{:S(2)}) collective-permute-start(bf16[2,10,128,128]{3,2,1,0:T(8,128)(2,1)} %collective-permute-done.14.refs_11_.refs_5_), channel_id=1, source_target_pairs={{24,16},{25,17},{26,18},{27,19},{28,20},{29,21},{30,22},{31,23}} | collective-permute-start | bytes 1966088 | tf_op jit(solution)/shard_map/ppermute | solution.py:195
  88.5 1.1 copy-start.1
  89.6 1.1 copy-start.6
  90.7 1.1 copy-start.8
  91.7 8.1 %copy-start.4 = (bf16[2,10,128,128]{3,2,1,0:T(8,128)(2,1)S(1)}, bf16[2,10,128,128]{3,2,1,0:T(8,128)(2,1)}, u32[]{:S(2)}) copy-start(bf16[2,10,128,128]{3,2,1,0:T(8,128)(2,1)} %copy-done.3) | copy-start | bytes 1966084
  91.7 15.8 %copy-start.23 = (bf16[1280,5120]{1,0:T(8,128)(2,1)S(1)}, bf16[1280,5120]{1,0:T(8,128)(2,1)}, u32[]{:S(2)}) copy-start(bf16[1280,5120]{1,0:T(8,128)(2,1)} %param.17) | copy-start | bytes 39321604
  114.1 1.7 copy-start.2
  114.1 1.7 copy-start.9
  114.1 1.7 copy-start.10
  115.7 13.8 %copy-start.24 = (s32[4]{0:T(128)S(1)}, s32[4]{0:T(128)}, u32[]{:S(2)}) copy-start(s32[4]{0:T(128)} %param.19) | copy-start | bytes 52
  128.7 0.9 copy-start.11
  131.6 16.5 %copy-start.13 = (bf16[1,1,256,5120]{3,2,1,0:T(8,128)(2,1)S(1)}, bf16[1,1,256,5120]{3,2,1,0:T(8,128)(2,1)}, u32[]{:S(2)}) copy-start(bf16[1,1,256,5120]{3,2,1,0:T(8,128)(2,1)} %param.16) | copy-start | bytes 7864324
  131.6 16.4 %collective-permute-start.17 = (bf16[256,1024]{1,0:T(8,128)(2,1)}, bf16[256,1024]{1,0:T(8,128)(2,1)}, u32[]{:S(2)}, u32[]{:S(2)}) collective-permute-start(bf16[256,1024]{1,0:T(8,128)(2,1)} %fusion.11), channel_id=1, source_target_pairs={{4,0},{0,4},{5,1},{1,5},{6,2},{2,6},{7,3},{3,7},{12,8},{8,12},{13,... | collective-permute-start | bytes 1572872 | tf_op jit(solution)/shard_map/ppermute | solution.py:215
  132.2 25.8 %collective-permute-start.18 = (bf16[256,1024]{1,0:T(8,128)(2,1)}, bf16[256,1024]{1,0:T(8,128)(2,1)}, u32[]{:S(2)}, u32[]{:S(2)}) collective-permute-start(bf16[256,1024]{1,0:T(8,128)(2,1)} %fusion.14), channel_id=1, source_target_pairs={{4,0},{0,4},{5,1},{1,5},{6,2},{2,6},{7,3},{3,7},{12,8},{8,12},{13,... | collective-permute-start | bytes 1572872 | tf_op jit(solution)/shard_map/ppermute | solution.py:215
  133.7 35.6 %collective-permute-start.19 = (bf16[256,1024]{1,0:T(8,128)(2,1)}, bf16[256,1024]{1,0:T(8,128)(2,1)}, u32[]{:S(2)}, u32[]{:S(2)}) collective-permute-start(bf16[256,1024]{1,0:T(8,128)(2,1)} %fusion.17), channel_id=1, source_target_pairs={{4,0},{0,4},{5,1},{1,5},{6,2},{2,6},{7,3},{3,7},{12,8},{8,12},{13,... | collective-permute-start | bytes 1572872 | tf_op jit(solution)/shard_map/ppermute | solution.py:215
  134.2 46.3 %collective-permute-start.20 = (bf16[256,1024]{1,0:T(8,128)(2,1)}, bf16[256,1024]{1,0:T(8,128)(2,1)}, u32[]{:S(2)}, u32[]{:S(2)}) collective-permute-start(bf16[256,1024]{1,0:T(8,128)(2,1)} %fusion.20), channel_id=1, source_target_pairs={{4,0},{0,4},{5,1},{1,5},{6,2},{2,6},{7,3},{3,7},{12,8},{8,12},{13,... | collective-permute-start | bytes 1572872 | tf_op jit(solution)/shard_map/ppermute | solution.py:215
  135.7 53.9 %collective-permute-start.21 = (bf16[256,1024]{1,0:T(8,128)(2,1)}, bf16[256,1024]{1,0:T(8,128)(2,1)S(1)}, u32[]{:S(2)}, u32[]{:S(2)}) collective-permute-start(bf16[256,1024]{1,0:T(8,128)(2,1)} %fusion.23), channel_id=1, source_target_pairs={{4,0},{0,4},{5,1},{1,5},{6,2},{2,6},{7,3},{3,7},{12,8},{8,12},{13,... | collective-permute-start | bytes 1572872 | tf_op jit(solution)/shard_map/ppermute | solution.py:215
  146.9 22.3 %copy-start.18 = (bf16[256,5120]{1,0:T(8,128)(2,1)S(1)}, bf16[256,5120]{1,0:T(8,128)(2,1)}, u32[]{:S(2)}) copy-start(bf16[256,5120]{1,0:T(8,128)(2,1)} %convolution_convert_fusion) | copy-start | bytes 7864324

commit v6 on v5

--- a/solution.py
+++ b/solution.py
@@ -11,8 +11,8 @@
 NEG_BIG = -1e30
 LOG2E = 1.4426950408889634
 COL_BLOCKS = 5
-HEAD_STEP_SCORES = 2 << 20
-VMEM_LIMIT = 28 << 20
+HEAD_STEP_SCORES = 1 << 20
+VMEM_MARGIN = 3 << 20
 
 
 def hidden_bias(mask, span, origin):
@@ -89,6 +89,9 @@
         layout.append((origin, places))
     keys = sum(size for _, places in layout for _, size in places)
     step = max(s for s in range(1, heads + 1) if heads % s == 0 and s * rows * keys <= HEAD_STEP_SCORES)
+    read = sum(array.shape[2] for array in arrays)
+    blocks = step * dim * (2 * 2 * read + 2 * 2 * rows + 3 * 4 * rows)
+    grant = 4 * step * rows * keys + 2 * blocks + VMEM_MARGIN
     by_head = pl.BlockSpec((step, rows, dim), lambda h, f: (h, 0, 0))
     states = [] if state is None else list(state)
     return pl.pallas_call(
@@ -121,7 +124,7 @@
             bytes_accessed=2 * heads * dim * (2 * rows + 2 * keys),
             transcendentals=heads * rows * keys,
         ),
-        compiler_params=pltpu.CompilerParams(vmem_limit_bytes=VMEM_LIMIT),
+        compiler_params=pltpu.CompilerParams(vmem_limit_bytes=grant),
     )(span_mask, queries, *arrays, *states)
 
 
@@ -154,8 +157,11 @@
         q_parts.append(lax.ppermute(take(q, d), "head", cycle(d)))
 
     use_context = span < prefix[0]
+    level_now = lax.dynamic_index_in_dim(levels, span, 0, keepdims=False)
+    gate_row = lax.dynamic_index_in_dim(gates, level_now, 0, keepdims=False)
     final = spans - 1
     stands_in = span == final
+    ctx_parts[0], gate_row = lax.optimization_barrier((ctx_parts[0], gate_row))
     lent = [lax.ppermute(a, "tm", [(0, final)]) for a in ctx_parts]
     pieces = [jnp.concatenate([jnp.where(stands_in, b, a) for a, b in zip(ctx_parts, lent)], axis=2)]
     piece_rows = pieces[0].shape[2]
@@ -214,9 +220,6 @@
             partial = project(attended, out_weight[:, j * width : (j + 1) * width])
             returned[j].append(lax.ppermute(partial, "head", back))
     attended = attend(q_parts[0], slots, span_mask, None, True)
-    attended, levels = lax.optimization_barrier((attended, levels))
-    level_now = lax.dynamic_index_in_dim(levels, span, 0, keepdims=False)
-    gate_row = lax.dynamic_index_in_dim(gates, level_now, 0, keepdims=False)
     kept = lax.optimization_barrier(project(attended, out_weight))
     updated = hidden
     for j in range(COL_BLOCKS):

time: 191 us -> 162 us (0.85)
  the two profiles are of different devices: /device:TPU:0 before, /device:TPU:5 now
where the time goes in v6:
time: 162 us; the launch traced here: 161 us
  waiting for transfers between devices  82.8 us (51%)
  starting transfers between devices  27.8 us (17%)
  Pallas kernels  25.4 us (16%)
  matrix products  8.08 us (5%)
  other arithmetic  7.72 us (5%)
  local copies, waits for them, and re-layouts  6.23 us (4%)
  between operations  3.2 us (2%)
    ppermute x3, waiting for transfers between devices, sublayer(): lax.ppermute(pieces[i - low], 'branch', [(b, b ^ low) for b in range(bran...  36.3 us
    ppermute x5, waiting for transfers between devices, sublayer(): returned[j].append(lax.ppermute(partial, 'head', back))  34 us
    pallas_call x3, Pallas kernels, attend(): pl.pallas_call(functools.partial(flash_kernel, layout=layout, count=len(a...  25.4 us
    dot_general x6, matrix products, sublayer(): jnp.dot(a, w, preferred_element_type=jnp.float32).astype(jnp.bfloat16)  8.08 us
    ppermute x3, starting transfers between devices, sublayer(): lax.ppermute(a, 'tm', pairs + [(final, final - 1)])  5.74 us
    ppermute x3, waiting for transfers between devices, sublayer(): far = [lax.ppermute(a, 'tm', [(1, final)]) for a in own]  5.72 us
    ppermute x3, starting transfers between devices, sublayer(): near = [lax.ppermute(a, 'tm', [(final, final - 1)]) for a in far]  4.72 us
    ppermute x2, waiting for transfers between devices, sublayer(): lent = [lax.ppermute(a, 'tm', [(0, final)]) for a in ctx_parts]  4.63 us
  transfers between devices with their start and end apart: 22, of which 12 were waited for; matrix products, arithmetic and copies ran while one was open for 8% of the time, Pallas kernels for 12%

profile of v6, /device:TPU:5, one launch (start us, length us, event | category | flops | bytes accessed | tf_op | source)
XLA Modules:
  0.0 161.3 jit_solution(9679243900132674223)
XLA Ops:
  0.0 1.0 copy-done.6
  1.0 0.1 copy-done.5
  1.2 0.8 pad_maximum_fusion.4
  1.9 1.2 collective-permute-start.1
  3.1 0.6 dynamic_slice.40
  5.9 1.3 collective-permute-start
  7.2 1.5 dynamic-slice_bitcast_fusion.1
  8.7 2.2 %collective-permute-done.1 = bf16[2,10,64,128]{3,2,1,0:T(8,128)(2,1)} collective-permute-done((bf16[2,10,64,128]{3,2,1,0:T(8,128)(2,1)}, bf16[2,10,64,128]{3,2,1,0:T(8,128)(2,1)}, u32[]{:S(2)}, u32[]{:S(2)}) %collective-permute-start.1) | collective-permute-done | bytes 327712 | tf_op jit(solution)/shard_map/ppermute | solution.py:153
  10.8 1.3 collective-permute-start.2
  12.1 0.1 pad_maximum_fusion.1
  12.3 1.3 collective-permute-start.5
  14.2 0.2 collective-permute-done
  14.4 1.0 broadcast_select_fusion.7
  15.4 4.4 %collective-permute-done.2 = bf16[2,10,64,128]{3,2,1,0:T(8,128)(2,1)} collective-permute-done((bf16[2,10,64,128]{3,2,1,0:T(8,128)(2,1)}, bf16[2,10,64,128]{3,2,1,0:T(8,128)(2,1)}, u32[]{:S(2)}, u32[]{:S(2)}) %collective-permute-start.2) | collective-permute-done | bytes 327712 | tf_op jit(solution)/shard_map/ppermute | solution.py:165
  19.8 1.0 broadcast_select_fusion.6
  20.8 0.4 broadcast_select_fusion.3
  21.3 2.4 %collective-permute-start.4 = (bf16[2,10,128,128]{3,2,1,0:T(8,128)(2,1)S(1)}, bf16[2,10,128,128]{3,2,1,0:T(8,128)(2,1)S(1)}, u32[]{:S(2)}, u32[]{:S(2)}) collective-permute-start(bf16[2,10,128,128]{3,2,1,0:T(8,128)(2,1)S(1)} %get-tuple-element.41), channel_id=1, source_target_pairs={{0,2},{1,3},{2,0},{3,1},{4,6},{5,7},{6,4},{7,5},{8,10},{9,11},{10,... | collective-permute-start | bytes 1966088 | tf_op jit(solution)/shard_map/ppermute | solution.py:170
  23.7 1.3 collective-permute-start.3
  25.0 24.7 %collective-permute-done.4 = bf16[2,10,128,128]{3,2,1,0:T(8,128)(2,1)S(1)} collective-permute-done((bf16[2,10,128,128]{3,2,1,0:T(8,128)(2,1)S(1)}, bf16[2,10,128,128]{3,2,1,0:T(8,128)(2,1)S(1)}, u32[]{:S(2)}, u32[]{:S(2)}) %collective-permute-start.4) | collective-permute-done | bytes 655392 | tf_op jit(solution)/shard_map/ppermute | solution.py:170
  49.7 0.5 collective-permute-done.3
  50.1 0.1 constant_dynamic-update-slice_fusion.1
  50.2 0.1 constant_dynamic-update-slice_fusion
  50.3 1.1 slice.99
  51.5 0.8 broadcast_select_fusion
  52.3 1.6 collective-permute-start.12
  53.9 0.9 collective-permute-start.6
  54.8 0.1 dynamic-slice_bitcast_fusion.5
  54.9 0.3 collective-permute-start.16
  55.3 1.9 %collective-permute-start.7 = (bf16[2,10,128,128]{3,2,1,0:T(8,128)(2,1)S(1)}, bf16[2,10,128,128]{3,2,1,0:T(8,128)(2,1)S(1)}, u32[]{:S(2)}, u32[]{:S(2)}) collective-permute-start(bf16[2,10,128,128]{3,2,1,0:T(8,128)(2,1)S(1)} %get-tuple-element.24.refs_13_.refs_7_), channel_id=1, source_target_pairs={{0,8},{16,24},{24,16},{1,9},{17,25},{25,17},{2,10},{18,26},{26,18}... | collective-permute-start | bytes 1966088 | tf_op jit(solution)/shard_map/ppermute | solution.py:188
  57.2 1.3 collective-permute-start.10
  58.5 11.1 %collective-permute-done.6 = bf16[2,10,128,128]{3,2,1,0:T(8,128)(2,1)S(1)} collective-permute-done((bf16[2,10,128,128]{3,2,1,0:T(8,128)(2,1)S(1)}, bf16[2,10,128,128]{3,2,1,0:T(8,128)(2,1)S(1)}, u32[]{:S(2)}, u32[]{:S(2)}) %collective-permute-start.6) | collective-permute-done | bytes 655392 | tf_op jit(solution)/shard_map/ppermute | solution.py:170
  69.6 1.9 %collective-permute-start.8 = (bf16[2,10,256,128]{3,2,1,0:T(8,128)(2,1)S(1)}, bf16[2,10,256,128]{3,2,1,0:T(8,128)(2,1)S(1)}, u32[]{:S(2)}, u32[]{:S(2)}) collective-permute-start(bf16[2,10,256,128]{3,2,1,0:T(8,128)(2,1)S(1)} %get-tuple-element.25.refs_14_.refs_8_), channel_id=1, source_target_pairs={{0,8},{16,24},{24,16},{1,9},{17,25},{25,17},{2,10},{18,26},{26,18}... | collective-permute-start | bytes 3932168 | tf_op jit(solution)/shard_map/ppermute | solution.py:188
  71.5 1.3 broadcast_select_fusion.2
  72.8 1.3 collective-permute-start.14
  74.1 1.9 %collective-permute-start.13 = (bf16[2,10,256,128]{3,2,1,0:T(8,128)(2,1)S(1)}, bf16[2,10,256,128]{3,2,1,0:T(8,128)(2,1)S(1)}, u32[]{:S(2)}, u32[]{:S(2)}) collective-permute-start(bf16[2,10,256,128]{3,2,1,0:T(8,128)(2,1)S(1)} %collective-permute-done.12.refs_9_.refs_3_), channel_id=1, source_target_pairs={{24,16},{25,17},{26,18},{27,19},{28,20},{29,21},{30,22},{31,23}} | collective-permute-start | bytes 3932168 | tf_op jit(solution)/shard_map/ppermute | solution.py:201
  76.0 2.0 %collective-permute-done.10.refs_7_.refs_5_ = bf16[2,10,128,128]{3,2,1,0:T(8,128)(2,1)S(1)} collective-permute-done((bf16[2,10,128,128]{3,2,1,0:T(8,128)(2,1)S(1)}, bf16[2,10,128,128]{3,2,1,0:T(8,128)(2,1)S(1)}, u32[]{:S(2)}, u32[]{:S(2)}) %collective-permute-start.10) | collective-permute-done | bytes 655392 | tf_op jit(solution)/shard_map/ppermute | solution.py:200
  78.0 1.3 collective-permute-start.11
  79.3 1.9 %collective-permute-start.9 = (bf16[2,10,128,128]{3,2,1,0:T(8,128)(2,1)S(1)}, bf16[2,10,128,128]{3,2,1,0:T(8,128)(2,1)S(1)}, u32[]{:S(2)}, u32[]{:S(2)}) collective-permute-start(bf16[2,10,128,128]{3,2,1,0:T(8,128)(2,1)S(1)} %get-tuple-element.31.refs_15_.refs_7_), channel_id=1, source_target_pairs={{0,8},{16,24},{24,16},{1,9},{17,25},{25,17},{2,10},{18,26},{26,18}... | collective-permute-start | bytes 1966088 | tf_op jit(solution)/shard_map/ppermute | solution.py:188
  81.2 3.8 %collective-permute-done.14.refs_11_.refs_5_ = bf16[2,10,128,128]{3,2,1,0:T(8,128)(2,1)S(1)} collective-permute-done((bf16[2,10,128,128]{3,2,1,0:T(8,128)(2,1)S(1)}, bf16[2,10,128,128]{3,2,1,0:T(8,128)(2,1)S(1)}, u32[]{:S(2)}, u32[]{:S(2)}) %collective-permute-start.14) | collective-permute-done | bytes 655392 | tf_op jit(solution)/shard_map/ppermute | solution.py:200
  85.0 1.5 collective-permute-start.15
  86.5 7.7 %shard_map.110 = (f32[10,256,128]{2,1,0:T(8,128)S(1)}, f32[10,256,128]{2,1,0:T(8,128)S(1)}, f32[10,256,128]{2,1,0:T(8,128)S(1)}) custom-call(s32[4,4]{1,0:T(4,128)S(1)} %copy-done.1, bf16[10,256,128]{2,1,0:T(8,128)(2,1)S(1)} %collective-permute-done.16.refs_0_, bf16[2,10,128,128]{3,2,1,0:T(8,128)(2,1)S(1)} %get-tuple-element.19.refs_1_, ...), custom_call_target="tpu_custom_call" | custom-call | flops 1677721600 | bytes 7864320 | tf_op jit(solution)/shard_map/pallas_call | solution.py:97
  94.3 5.8 %shard_map.111 = bf16[256,1280]{1,0:T(8,128)(2,1)S(1)} custom-call(s32[4,4]{1,0:T(4,128)S(1)} %copy-done.1, bf16[10,256,128]{2,1,0:T(8,128)(2,1)S(1)} %collective-permute-done.16.refs_0_, bf16[2,10,128,128]{3,2,1,0:T(8,128)(2,1)S(1)} %get-tuple-element.32.refs_3_.refs_1_, bf16[2,10,128,128]{3,2,1,0:T(8,128)(2,1)S(1)} %collective-permute-done.9.refs_6_.refs_2_, ...), custom_call_target="tpu_custom_call" | custom-call | flops 1006632960 | bytes 5242880 | tf_op jit(solution)/shard_map/pallas_call | solution.py:97
  100.1 0.8 fusion.23
  101.0 0.8 fusion.20
  101.8 0.8 fusion.17
  102.7 0.8 fusion.14
  103.5 0.8 fusion.11
  104.4 0.3 collective-permute-start.17
  104.7 1.2 collective-permute-start.18
  105.9 0.3 collective-permute-start.19
  106.2 1.2 collective-permute-start.20
  107.4 0.3 collective-permute-start.21
  107.7 11.9 %shard_map.109 = bf16[256,1280]{1,0:T(8,128)(2,1)S(1)} custom-call(s32[4,4]{1,0:T(4,128)S(1)} %copy-done.1, bf16[10,256,128]{2,1,0:T(8,128)(2,1)S(1)} %get-tuple-element.35.refs_0_, bf16[2,10,128,128]{3,2,1,0:T(8,128)(2,1)S(1)} %get-tuple-element.19.refs_1_, bf16[2,10,256,128]{3,2,1,0:T(8,128)(2,1)S(1)} %get-tuple-element.22.refs_2_, ...), custom_call_target="tpu_custom_call" | custom-call | flops 2684354560 | bytes 11796480 | tf_op jit(solution)/shard_map/pallas_call | solution.py:97
  119.6 3.9 %convolution_convert_fusion = bf16[256,5120]{1,0:T(8,128)(2,1)S(1)} fusion(bf16[256,1280]{1,0:T(8,128)(2,1)S(1)} %shard_map.109, bf16[1280,5120]{1,0:T(8,128)(2,1)S(1)} %bitcast.77), kind=kOutput, calls=%fused_computation | convolution fusion | flops 3356753920 | bytes 16384000 | tf_op jit(solution)/shard_map/dot_general | solution.py:214
  123.5 0.3 fusion.27
  123.8 5.8 %collective-permute-done.18 = bf16[256,1024]{1,0:T(8,128)(2,1)S(1)} collective-permute-done((bf16[256,1024]{1,0:T(8,128)(2,1)S(1)}, bf16[256,1024]{1,0:T(8,128)(2,1)S(1)}, u32[]{:S(2)}, u32[]{:S(2)}) %collective-permute-start.18) | collective-permute-done | bytes 524320 | tf_op jit(solution)/shard_map/ppermute | solution.py:221
  129.6 0.3 fusion.28
  130.0 10.9 %collective-permute-done.19 = bf16[256,1024]{1,0:T(8,128)(2,1)S(1)} collective-permute-done((bf16[256,1024]{1,0:T(8,128)(2,1)S(1)}, bf16[256,1024]{1,0:T(8,128)(2,1)S(1)}, u32[]{:S(2)}, u32[]{:S(2)}) %collective-permute-start.19) | collective-permute-done | bytes 524320 | tf_op jit(solution)/shard_map/ppermute | solution.py:221
  140.9 0.3 fusion.29
  141.2 10.9 %collective-permute-done.20 = bf16[256,1024]{1,0:T(8,128)(2,1)S(1)} collective-permute-done((bf16[256,1024]{1,0:T(8,128)(2,1)S(1)}, bf16[256,1024]{1,0:T(8,128)(2,1)S(1)}, u32[]{:S(2)}, u32[]{:S(2)}) %collective-permute-start.20) | collective-permute-done | bytes 524320 | tf_op jit(solution)/shard_map/ppermute | solution.py:221
  152.1 0.3 fusion.30
  152.4 1.5 copy.17
  153.9 6.3 %collective-permute-done.21 = bf16[256,1024]{1,0:T(8,128)(2,1)S(1)} collective-permute-done((bf16[256,1024]{1,0:T(8,128)(2,1)S(1)}, bf16[256,1024]{1,0:T(8,128)(2,1)S(1)}, u32[]{:S(2)}, u32[]{:S(2)}) %collective-permute-start.21) | collective-permute-done | bytes 524320 | tf_op jit(solution)/shard_map/ppermute | solution.py:221
  160.2 1.1 fusion.32
  (37 shorter events, 0.2 us)
Async XLA Ops:
  0.0 5.8 %copy-start = (f32[16,5120]{1,0:T(8,128)S(1)}, f32[16,5120]{1,0:T(8,128)}, u32[]{:S(2)}) copy-start(f32[16,5120]{1,0:T(8,128)} %param.18) | copy-start | bytes 983044
  0.0 1.0 copy-start.6
  0.0 1.1 copy-start.5
  0.0 3.1 %copy-start.7 = (s32[4]{0:T(128)S(1)}, s32[4]{0:T(128)}, u32[]{:S(2)}) copy-start(s32[4]{0:T(128)} %param.19) | copy-start | bytes 52
  0.0 7.2 %copy-start.4 = (bf16[1,1,256,20,128]{4,2,3,1,0:T(8,128)(2,1)S(1)}, bf16[1,1,256,20,128]{4,2,3,1,0:T(8,128)(2,1)}, u32[]{:S(2)}) copy-start(bf16[1,1,256,20,128]{4,2,3,1,0:T(8,128)(2,1)} %param.13) | copy-start | bytes 3932164
  1.9 8.9 %collective-permute-start.1 = (bf16[2,10,64,128]{3,2,1,0:T(8,128)(2,1)}, bf16[2,10,64,128]{3,2,1,0:T(8,128)(2,1)}, u32[]{:S(2)}, u32[]{:S(2)}) collective-permute-start(bf16[2,10,64,128]{3,2,1,0:T(8,128)(2,1)} %pad_maximum_fusion.4), channel_id=1, source_target_pairs={{0,4},{4,0},{1,5},{5,1},{2,6},{6,2},{3,7},{7,3},{8,12},{12,8},{9,1... | collective-permute-start | bytes 983048 | tf_op jit(solution)/shard_map/ppermute | solution.py:153
  5.9 8.5 %collective-permute-start = (bf16[2,10,64,128]{3,2,1,0:T(8,128)(2,1)S(1)}, bf16[2,10,64,128]{3,2,1,0:T(8,128)(2,1)}, u32[]{:S(2)}, u32[]{:S(2)}) collective-permute-start(bf16[2,10,64,128]{3,2,1,0:T(8,128)(2,1)S(1)} %pad_maximum_fusion.3), channel_id=1, source_target_pairs={{0,24},{1,25},{2,26},{3,27},{4,28},{5,29},{6,30},{7,31}} | collective-permute-start | bytes 983048 | tf_op jit(solution)/shard_map/ppermute | solution.py:165
  10.8 9.0 %collective-permute-start.2 = (bf16[2,10,64,128]{3,2,1,0:T(8,128)(2,1)}, bf16[2,10,64,128]{3,2,1,0:T(8,128)(2,1)}, u32[]{:S(2)}, u32[]{:S(2)}) collective-permute-start(bf16[2,10,64,128]{3,2,1,0:T(8,128)(2,1)} %collective-permute-done.1), channel_id=1, source_target_pairs={{0,24},{1,25},{2,26},{3,27},{4,28},{5,29},{6,30},{7,31}} | collective-permute-start | bytes 983048 | tf_op jit(solution)/shard_map/ppermute | solution.py:165
  12.3 38.1 %collective-permute-start.5 = (bf16[2,10,256,128]{3,2,1,0:T(8,128)(2,1)S(1)}, bf16[2,10,256,128]{3,2,1,0:T(8,128)(2,1)}, u32[]{:S(2)}, u32[]{:S(2)}) collective-permute-start(bf16[2,10,256,128]{3,2,1,0:T(8,128)(2,1)S(1)} %pad_maximum_fusion.1), channel_id=1, source_target_pairs={{0,4},{4,0},{1,5},{5,1},{2,6},{6,2},{3,7},{7,3},{8,12},{12,8},{9,1... | collective-permute-start | bytes 3932168 | tf_op jit(solution)/shard_map/ppermute | solution.py:155
  21.3 28.4 %collective-permute-start.4 = (bf16[2,10,128,128]{3,2,1,0:T(8,128)(2,1)S(1)}, bf16[2,10,128,128]{3,2,1,0:T(8,128)(2,1)S(1)}, u32[]{:S(2)}, u32[]{:S(2)}) collective-permute-start(bf16[2,10,128,128]{3,2,1,0:T(8,128)(2,1)S(1)} %get-tuple-element.41), channel_id=1, source_target_pairs={{0,2},{1,3},{2,0},{3,1},{4,6},{5,7},{6,4},{7,5},{8,10},{9,11},{10,... | collective-permute-start | bytes 1966088 | tf_op jit(solution)/shard_map/ppermute | solution.py:170
  23.7 26.5 %collective-permute-start.3 = (bf16[2,10,128,128]{3,2,1,0:T(8,128)(2,1)S(1)}, bf16[2,10,128,128]{3,2,1,0:T(8,128)(2,1)S(1)}, u32[]{:S(2)}, u32[]{:S(2)}) collective-permute-start(bf16[2,10,128,128]{3,2,1,0:T(8,128)(2,1)S(1)} %get-tuple-element.41), channel_id=1, source_target_pairs={{0,1},{1,0},{2,3},{3,2},{4,5},{5,4},{6,7},{7,6},{8,9},{9,8},{10,11... | collective-permute-start | bytes 1966088 | tf_op jit(solution)/shard_map/ppermute | solution.py:170
  51.5 3.3 %copy-start.3 = (bf16[1,1,256,20,128]{4,2,3,1,0:T(8,128)(2,1)S(1)}, bf16[1,1,256,20,128]{4,2,3,1,0:T(8,128)(2,1)}, u32[]{:S(2)}) copy-start(bf16[1,1,256,20,128]{4,2,3,1,0:T(8,128)(2,1)} %param.11) | copy-start | bytes 3932164
  51.5 48.6 %slice-start = ((s8[13107200]{0:T(1024)(128)(4,1)}), s8[4194304]{0:T(1024)(128)(4,1)S(1)}, s32[]{:S(2)}) async-start(s8[13107200]{0:T(1024)(128)(4,1)} %bitcast.76), calls=%async_computation | async-start | bytes 8388608
  52.3 34.2 %copy-start.1 = (s32[4,4]{1,0:T(4,128)S(1)}, s32[4,4]{1,0:T(4,128)}, u32[]{:S(2)}) copy-start(s32[4,4]{1,0:T(4,128)} %mask.5) | copy-start | bytes 196
  52.3 47.8 %slice-start.1 = ((s8[13107200]{0:T(1024)(128)(4,1)}), s8[4194304]{0:T(1024)(128)(4,1)S(1)}, s32[]{:S(2)}) async-start(s8[13107200]{0:T(1024)(128)(4,1)} %bitcast.76), calls=%async_computation.1 | async-start | bytes 8388608
  52.3 21.8 %collective-permute-start.12 = (bf16[2,10,256,128]{3,2,1,0:T(8,128)(2,1)S(1)}, bf16[2,10,256,128]{3,2,1,0:T(8,128)(2,1)S(1)}, u32[]{:S(2)}, u32[]{:S(2)}) collective-permute-start(bf16[2,10,256,128]{3,2,1,0:T(8,128)(2,1)S(1)} %get-tuple-element.22.refs_2_), channel_id=1, source_target_pairs={{8,24},{9,25},{10,26},{11,27},{12,28},{13,29},{14,30},{15,31}} | collective-permute-start | bytes 3932168 | tf_op jit(solution)/shard_map/ppermute | solution.py:200
  53.9 15.7 %collective-permute-start.6 = (bf16[2,10,128,128]{3,2,1,0:T(8,128)(2,1)S(1)}, bf16[2,10,128,128]{3,2,1,0:T(8,128)(2,1)S(1)}, u32[]{:S(2)}, u32[]{:S(2)}) collective-permute-start(bf16[2,10,128,128]{3,2,1,0:T(8,128)(2,1)S(1)} %collective-permute-done.4), channel_id=1, source_target_pairs={{0,1},{1,0},{2,3},{3,2},{4,5},{5,4},{6,7},{7,6},{8,9},{9,8},{10,11... | collective-permute-start | bytes 1966088 | tf_op jit(solution)/shard_map/ppermute | solution.py:170
  54.9 17.8 %collective-permute-start.16 = (bf16[10,256,128]{2,1,0:T(8,128)(2,1)S(1)}, bf16[10,256,128]{2,1,0:T(8,128)(2,1)S(1)}, u32[]{:S(2)}, u32[]{:S(2)}) collective-permute-start(bf16[10,256,128]{2,1,0:T(8,128)(2,1)S(1)} %get-tuple-element.36), channel_id=1, source_target_pairs={{0,4},{4,0},{1,5},{5,1},{2,6},{6,2},{3,7},{7,3},{8,12},{12,8},{9,1... | collective-permute-start | bytes 1966088 | tf_op jit(solution)/shard_map/ppermute | solution.py:157
  55.3 24.0 %collective-permute-start.7 = (bf16[2,10,128,128]{3,2,1,0:T(8,128)(2,1)S(1)}, bf16[2,10,128,128]{3,2,1,0:T(8,128)(2,1)S(1)}, u32[]{:S(2)}, u32[]{:S(2)}) collective-permute-start(bf16[2,10,128,128]{3,2,1,0:T(8,128)(2,1)S(1)} %get-tuple-element.24.refs_13_.refs_7_), channel_id=1, source_target_pairs={{0,8},{16,24},{24,16},{1,9},{17,25},{25,17},{2,10},{18,26},{26,18}... | collective-permute-start | bytes 1966088 | tf_op jit(solution)/shard_map/ppermute | solution.py:188
  57.2 20.8 %collective-permute-start.10 = (bf16[2,10,128,128]{3,2,1,0:T(8,128)(2,1)S(1)}, bf16[2,10,128,128]{3,2,1,0:T(8,128)(2,1)S(1)}, u32[]{:S(2)}, u32[]{:S(2)}) collective-permute-start(bf16[2,10,128,128]{3,2,1,0:T(8,128)(2,1)S(1)} %get-tuple-element.19.refs_1_), channel_id=1, source_target_pairs={{8,24},{9,25},{10,26},{11,27},{12,28},{13,29},{14,30},{15,31}} | collective-permute-start | bytes 1966088 | tf_op jit(solution)/shard_map/ppermute | solution.py:200
  69.6 16.9 %collective-permute-start.8 = (bf16[2,10,256,128]{3,2,1,0:T(8,128)(2,1)S(1)}, bf16[2,10,256,128]{3,2,1,0:T(8,128)(2,1)S(1)}, u32[]{:S(2)}, u32[]{:S(2)}) collective-permute-start(bf16[2,10,256,128]{3,2,1,0:T(8,128)(2,1)S(1)} %get-tuple-element.25.refs_14_.refs_8_), channel_id=1, source_target_pairs={{0,8},{16,24},{24,16},{1,9},{17,25},{25,17},{2,10},{18,26},{26,18}... | collective-permute-start | bytes 3932168 | tf_op jit(solution)/shard_map/ppermute | solution.py:188
  72.8 12.2 %collective-permute-start.14 = (bf16[2,10,128,128]{3,2,1,0:T(8,128)(2,1)S(1)}, bf16[2,10,128,128]{3,2,1,0:T(8,128)(2,1)S(1)}, u32[]{:S(2)}, u32[]{:S(2)}) collective-permute-start(bf16[2,10,128,128]{3,2,1,0:T(8,128)(2,1)S(1)} %get-tuple-element.32.refs_3_.refs_1_), channel_id=1, source_target_pairs={{8,24},{9,25},{10,26},{11,27},{12,28},{13,29},{14,30},{15,31}} | collective-permute-start | bytes 1966088 | tf_op jit(solution)/shard_map/ppermute | solution.py:200
  74.1 20.1 %collective-permute-start.13 = (bf16[2,10,256,128]{3,2,1,0:T(8,128)(2,1)S(1)}, bf16[2,10,256,128]{3,2,1,0:T(8,128)(2,1)S(1)}, u32[]{:S(2)}, u32[]{:S(2)}) collective-permute-start(bf16[2,10,256,128]{3,2,1,0:T(8,128)(2,1)S(1)} %collective-permute-done.12.refs_9_.refs_3_), channel_id=1, source_target_pairs={{24,16},{25,17},{26,18},{27,19},{28,20},{29,21},{30,22},{31,23}} | collective-permute-start | bytes 3932168 | tf_op jit(solution)/shard_map/ppermute | solution.py:201
  78.0 8.6 %collective-permute-start.11 = (bf16[2,10,128,128]{3,2,1,0:T(8,128)(2,1)S(1)}, bf16[2,10,128,128]{3,2,1,0:T(8,128)(2,1)S(1)}, u32[]{:S(2)}, u32[]{:S(2)}) collective-permute-start(bf16[2,10,128,128]{3,2,1,0:T(8,128)(2,1)S(1)} %collective-permute-done.10.refs_7_.refs_5_), channel_id=1, source_target_pairs={{24,16},{25,17},{26,18},{27,19},{28,20},{29,21},{30,22},{31,23}} | collective-permute-start | bytes 1966088 | tf_op jit(solution)/shard_map/ppermute | solution.py:201
  79.3 14.9 %collective-permute-start.9 = (bf16[2,10,128,128]{3,2,1,0:T(8,128)(2,1)S(1)}, bf16[2,10,128,128]{3,2,1,0:T(8,128)(2,1)S(1)}, u32[]{:S(2)}, u32[]{:S(2)}) collective-permute-start(bf16[2,10,128,128]{3,2,1,0:T(8,128)(2,1)S(1)} %get-tuple-element.31.refs_15_.refs_7_), channel_id=1, source_target_pairs={{0,8},{16,24},{24,16},{1,9},{17,25},{25,17},{2,10},{18,26},{26,18}... | collective-permute-start | bytes 1966088 | tf_op jit(solution)/shard_map/ppermute | solution.py:188
  85.0 9.2 %collective-permute-start.15 = (bf16[2,10,128,128]{3,2,1,0:T(8,128)(2,1)S(1)}, bf16[2,10,128,128]{3,2,1,0:T(8,128)(2,1)S(1)}, u32[]{:S(2)}, u32[]{:S(2)}) collective-permute-start(bf16[2,10,128,128]{3,2,1,0:T(8,128)(2,1)S(1)} %collective-permute-done.14.refs_11_.refs_5_), channel_id=1, source_target_pairs={{24,16},{25,17},{26,18},{27,19},{28,20},{29,21},{30,22},{31,23}} | collective-permute-start | bytes 1966088 | tf_op jit(solution)/shard_map/ppermute | solution.py:201
  86.5 13.6 %slice-start.2 = ((s8[13107200]{0:T(1024)(128)(4,1)}), s8[4194304]{0:T(1024)(128)(4,1)S(1)}, s32[]{:S(2)}) async-start(s8[13107200]{0:T(1024)(128)(4,1)} %bitcast.76), calls=%async_computation.2 | async-start | bytes 8388608
  94.2 5.9 %slice-start.3 = ((s8[13107200]{0:T(1024)(128)(4,1)}), s8[524288]{0:T(1024)(128)(4,1)S(1)}, s32[]{:S(2)}) async-start(s8[13107200]{0:T(1024)(128)(4,1)} %bitcast.76), calls=%async_computation.3 | async-start | bytes 1048576
  104.4 19.1 %collective-permute-start.17 = (bf16[256,1024]{1,0:T(8,128)(2,1)S(1)}, bf16[256,1024]{1,0:T(8,128)(2,1)S(1)}, u32[]{:S(2)}, u32[]{:S(2)}) collective-permute-start(bf16[256,1024]{1,0:T(8,128)(2,1)S(1)} %fusion.11), channel_id=1, source_target_pairs={{4,0},{0,4},{5,1},{1,5},{6,2},{2,6},{7,3},{3,7},{12,8},{8,12},{13,... | collective-permute-start | bytes 1572872 | tf_op jit(solution)/shard_map/ppermute | solution.py:221
  104.7 24.9 %collective-permute-start.18 = (bf16[256,1024]{1,0:T(8,128)(2,1)S(1)}, bf16[256,1024]{1,0:T(8,128)(2,1)S(1)}, u32[]{:S(2)}, u32[]{:S(2)}) collective-permute-start(bf16[256,1024]{1,0:T(8,128)(2,1)S(1)} %fusion.14), channel_id=1, source_target_pairs={{4,0},{0,4},{5,1},{1,5},{6,2},{2,6},{7,3},{3,7},{12,8},{8,12},{13,... | collective-permute-start | bytes 1572872 | tf_op jit(solution)/shard_map/ppermute | solution.py:221
  105.9 34.9 %collective-permute-start.19 = (bf16[256,1024]{1,0:T(8,128)(2,1)S(1)}, bf16[256,1024]{1,0:T(8,128)(2,1)S(1)}, u32[]{:S(2)}, u32[]{:S(2)}) collective-permute-start(bf16[256,1024]{1,0:T(8,128)(2,1)S(1)} %fusion.17), channel_id=1, source_target_pairs={{4,0},{0,4},{5,1},{1,5},{6,2},{2,6},{7,3},{3,7},{12,8},{8,12},{13,... | collective-permute-start | bytes 1572872 | tf_op jit(solution)/shard_map/ppermute | solution.py:221
  106.2 45.9 %collective-permute-start.20 = (bf16[256,1024]{1,0:T(8,128)(2,1)S(1)}, bf16[256,1024]{1,0:T(8,128)(2,1)S(1)}, u32[]{:S(2)}, u32[]{:S(2)}) collective-permute-start(bf16[256,1024]{1,0:T(8,128)(2,1)S(1)} %fusion.20), channel_id=1, source_target_pairs={{4,0},{0,4},{5,1},{1,5},{6,2},{2,6},{7,3},{3,7},{12,8},{8,12},{13,... | collective-permute-start | bytes 1572872 | tf_op jit(solution)/shard_map/ppermute | solution.py:221
  107.4 52.8 %collective-permute-start.21 = (bf16[256,1024]{1,0:T(8,128)(2,1)S(1)}, bf16[256,1024]{1,0:T(8,128)(2,1)S(1)}, u32[]{:S(2)}, u32[]{:S(2)}) collective-permute-start(bf16[256,1024]{1,0:T(8,128)(2,1)S(1)} %fusion.23), channel_id=1, source_target_pairs={{4,0},{0,4},{5,1},{1,5},{6,2},{2,6},{7,3},{3,7},{12,8},{8,12},{13,... | collective-permute-start | bytes 1572872 | tf_op jit(solution)/shard_map/ppermute | solution.py:221
  119.6 3.9 %copy-start.2 = (bf16[1,1,256,5120]{3,2,1,0:T(8,128)(2,1)S(1)}, bf16[1,1,256,5120]{3,2,1,0:T(8,128)(2,1)}, u32[]{:S(2)}) copy-start(bf16[1,1,256,5120]{3,2,1,0:T(8,128)(2,1)} %param.16) | copy-start | bytes 7864324

commit v7 on v6

--- a/solution.py
+++ b/solution.py
@@ -197,9 +197,9 @@
         slots.append((lambda c, s=s: c - s, far))
         slots.append((lambda c, s=s: c + 1 - 2 * lax.rem(c, 2) - s, near))
     s = final - 1
-    far = [lax.ppermute(a, "tm", [(1, final)]) for a in own]
-    near = [lax.ppermute(a, "tm", [(final, final - 1)]) for a in far]
-    slots.append((lambda c: jnp.where(c >= final - 1, 1, -1), list(zip(far, near))))
+    far = [lax.ppermute(a, "tm", [(1, final - 1)]) for a in own]
+    near = [lax.ppermute(a, "tm", [(final - 1, final)]) for a in far]
+    slots.append((lambda c: jnp.where(c >= final - 1, 1, -1), list(zip(near, far))))
     slots.append((lambda c: jnp.where(c == final, 0, -1), [a for _, a in held]))
 
     cuts = [len(groups) - 1 if i in (0, 1, len(slots) - 1) else len(groups) - 2 for i in range(len(slots))]

time: 162 us -> 161 us (level)
  the two profiles are of different devices: /device:TPU:5 before, /device:TPU:28 now
where the time goes in v7:
time: 161 us
  waiting for transfers between devices  84.5 us (52%)
  starting transfers between devices  26.6 us (17%)
  Pallas kernels  25.4 us (16%)
  matrix products  8.09 us (5%)
  other arithmetic  6.78 us (4%)
  local copies, waits for them, and re-layouts  6.23 us (4%)
  between operations  3.2 us (2%)
    ppermute x3, waiting for transfers between devices, sublayer(): lax.ppermute(pieces[i - low], 'branch', [(b, b ^ low) for b in range(bran...  43.7 us
    ppermute x5, waiting for transfers between devices, sublayer(): returned[j].append(lax.ppermute(partial, 'head', back))  32.3 us
    pallas_call x3, Pallas kernels, attend(): pl.pallas_call(functools.partial(flash_kernel, layout=layout, count=len(a...  25.4 us
    dot_general x6, matrix products, sublayer(): jnp.dot(a, w, preferred_element_type=jnp.float32).astype(jnp.bfloat16)  8.09 us
    ppermute x3, waiting for transfers between devices, sublayer(): far = [lax.ppermute(a, 'tm', [(1, final - 1)]) for a in own]  5.86 us
    ppermute x3, starting transfers between devices, sublayer(): lax.ppermute(a, 'tm', pairs + [(final, final - 1)])  5.74 us
    ppermute x3, starting transfers between devices, sublayer(): near = [lax.ppermute(a, 'tm', [(final - 1, final)]) for a in far]  4.72 us
    ppermute x5, starting transfers between devices, sublayer(): returned[j].append(lax.ppermute(partial, 'head', back))  4.66 us
  transfers between devices with their start and end apart: 22, of which 9 were waited for; matrix products, arithmetic and copies ran while one was open for 7% of the time, Pallas kernels for 12%

profile of v7, /device:TPU:28, one launch (start us, length us, event | category | flops | bytes accessed | tf_op | source)
XLA Modules:
  0.0 160.8 jit_solution(15889979535429367810)
XLA Ops:
  0.0 1.0 copy-done.6
  1.0 0.1 copy-done.5
  1.2 0.8 pad_maximum_fusion.4
  1.9 1.5 collective-permute-start.1
  3.4 0.6 dynamic_slice.40
  6.2 1.4 collective-permute-start
  7.6 1.5 dynamic-slice_bitcast_fusion.1
  9.0 2.7 %collective-permute-done.1 = bf16[2,10,64,128]{3,2,1,0:T(8,128)(2,1)} collective-permute-done((bf16[2,10,64,128]{3,2,1,0:T(8,128)(2,1)}, bf16[2,10,64,128]{3,2,1,0:T(8,128)(2,1)}, u32[]{:S(2)}, u32[]{:S(2)}) %collective-permute-start.1) | collective-permute-done | bytes 327712 | tf_op jit(solution)/shard_map/ppermute | solution.py:153
  11.7 1.4 collective-permute-start.2
  13.1 0.1 pad_maximum_fusion.1
  13.2 1.6 collective-permute-start.5
  15.5 1.0 broadcast_select_fusion.6
  16.5 0.4 broadcast_select_fusion.3
  17.0 0.4 collective-permute-start.4
  17.4 0.4 collective-permute-start.3
  17.8 31.6 %collective-permute-done.4 = bf16[2,10,128,128]{3,2,1,0:T(8,128)(2,1)S(1)} collective-permute-done((bf16[2,10,128,128]{3,2,1,0:T(8,128)(2,1)S(1)}, bf16[2,10,128,128]{3,2,1,0:T(8,128)(2,1)S(1)}, u32[]{:S(2)}, u32[]{:S(2)}) %collective-permute-start.4) | collective-permute-done | bytes 655392 | tf_op jit(solution)/shard_map/ppermute | solution.py:170
  49.4 0.1 constant_dynamic-update-slice_fusion.1
  49.4 0.1 constant_dynamic-update-slice_fusion
  49.5 1.1 slice.99
  50.7 0.0 slice-start
  50.7 0.8 broadcast_select_fusion
  51.5 0.0 slice-start.1
  51.5 1.6 collective-permute-start.12
  53.1 0.1 collective-permute-start.6
  53.2 0.1 dynamic-slice_bitcast_fusion.5
  53.3 0.6 collective-permute-start.16
  53.9 1.9 %collective-permute-start.7 = (bf16[2,10,128,128]{3,2,1,0:T(8,128)(2,1)S(1)}, bf16[2,10,128,128]{3,2,1,0:T(8,128)(2,1)S(1)}, u32[]{:S(2)}, u32[]{:S(2)}) collective-permute-start(bf16[2,10,128,128]{3,2,1,0:T(8,128)(2,1)S(1)} %get-tuple-element.24.refs_13_.refs_7_), channel_id=1, source_target_pairs={{0,8},{16,24},{24,16},{1,9},{17,25},{25,17},{2,10},{18,26},{26,18}... | collective-permute-start | bytes 1966088 | tf_op jit(solution)/shard_map/ppermute | solution.py:188
  55.8 1.3 collective-permute-start.10
  57.1 12.1 %collective-permute-done.6 = bf16[2,10,128,128]{3,2,1,0:T(8,128)(2,1)S(1)} collective-permute-done((bf16[2,10,128,128]{3,2,1,0:T(8,128)(2,1)S(1)}, bf16[2,10,128,128]{3,2,1,0:T(8,128)(2,1)S(1)}, u32[]{:S(2)}, u32[]{:S(2)}) %collective-permute-start.6) | collective-permute-done | bytes 655392 | tf_op jit(solution)/shard_map/ppermute | solution.py:170
  69.2 1.9 %collective-permute-start.8 = (bf16[2,10,256,128]{3,2,1,0:T(8,128)(2,1)S(1)}, bf16[2,10,256,128]{3,2,1,0:T(8,128)(2,1)S(1)}, u32[]{:S(2)}, u32[]{:S(2)}) collective-permute-start(bf16[2,10,256,128]{3,2,1,0:T(8,128)(2,1)S(1)} %get-tuple-element.25.refs_14_.refs_8_), channel_id=1, source_target_pairs={{0,8},{16,24},{24,16},{1,9},{17,25},{25,17},{2,10},{18,26},{26,18}... | collective-permute-start | bytes 3932168 | tf_op jit(solution)/shard_map/ppermute | solution.py:188
  71.2 1.3 broadcast_select_fusion.2
  72.4 1.3 collective-permute-start.14
  73.8 1.9 %collective-permute-start.13 = (bf16[2,10,256,128]{3,2,1,0:T(8,128)(2,1)S(1)}, bf16[2,10,256,128]{3,2,1,0:T(8,128)(2,1)S(1)}, u32[]{:S(2)}, u32[]{:S(2)}) collective-permute-start(bf16[2,10,256,128]{3,2,1,0:T(8,128)(2,1)S(1)} %collective-permute-done.12.refs_10_.refs_4_), channel_id=1, source_target_pairs={{16,24},{17,25},{18,26},{19,27},{20,28},{21,29},{22,30},{23,31}} | collective-permute-start | bytes 3932168 | tf_op jit(solution)/shard_map/ppermute | solution.py:201
  75.7 2.1 %collective-permute-done.10.refs_8_.refs_6_ = bf16[2,10,128,128]{3,2,1,0:T(8,128)(2,1)S(1)} collective-permute-done((bf16[2,10,128,128]{3,2,1,0:T(8,128)(2,1)S(1)}, bf16[2,10,128,128]{3,2,1,0:T(8,128)(2,1)S(1)}, u32[]{:S(2)}, u32[]{:S(2)}) %collective-permute-start.10) | collective-permute-done | bytes 655392 | tf_op jit(solution)/shard_map/ppermute | solution.py:200
  77.8 1.3 collective-permute-start.11
  79.1 1.9 %collective-permute-start.9 = (bf16[2,10,128,128]{3,2,1,0:T(8,128)(2,1)S(1)}, bf16[2,10,128,128]{3,2,1,0:T(8,128)(2,1)S(1)}, u32[]{:S(2)}, u32[]{:S(2)}) collective-permute-start(bf16[2,10,128,128]{3,2,1,0:T(8,128)(2,1)S(1)} %get-tuple-element.31.refs_15_.refs_7_), channel_id=1, source_target_pairs={{0,8},{16,24},{24,16},{1,9},{17,25},{25,17},{2,10},{18,26},{26,18}... | collective-permute-start | bytes 1966088 | tf_op jit(solution)/shard_map/ppermute | solution.py:188
  81.0 3.8 %collective-permute-done.14.refs_12_.refs_6_ = bf16[2,10,128,128]{3,2,1,0:T(8,128)(2,1)S(1)} collective-permute-done((bf16[2,10,128,128]{3,2,1,0:T(8,128)(2,1)S(1)}, bf16[2,10,128,128]{3,2,1,0:T(8,128)(2,1)S(1)}, u32[]{:S(2)}, u32[]{:S(2)}) %collective-permute-start.14) | collective-permute-done | bytes 655392 | tf_op jit(solution)/shard_map/ppermute | solution.py:200
  84.8 1.5 collective-permute-start.15
  86.3 0.0 slice-start.2
  86.3 7.7 %shard_map.110 = (f32[10,256,128]{2,1,0:T(8,128)S(1)}, f32[10,256,128]{2,1,0:T(8,128)S(1)}, f32[10,256,128]{2,1,0:T(8,128)S(1)}) custom-call(s32[4,4]{1,0:T(4,128)S(1)} %copy-done.1, bf16[10,256,128]{2,1,0:T(8,128)(2,1)S(1)} %collective-permute-done.16.refs_0_, bf16[2,10,128,128]{3,2,1,0:T(8,128)(2,1)S(1)} %get-tuple-element.19.refs_1_, ...), custom_call_target="tpu_custom_call" | custom-call | flops 1677721600 | bytes 7864320 | tf_op jit(solution)/shard_map/pallas_call | solution.py:97
  94.0 0.0 slice-start.3
  94.0 5.8 %shard_map.111 = bf16[256,1280]{1,0:T(8,128)(2,1)S(1)} custom-call(s32[4,4]{1,0:T(4,128)S(1)} %copy-done.1, bf16[10,256,128]{2,1,0:T(8,128)(2,1)S(1)} %collective-permute-done.16.refs_0_, bf16[2,10,128,128]{3,2,1,0:T(8,128)(2,1)S(1)} %get-tuple-element.32.refs_3_.refs_1_, bf16[2,10,128,128]{3,2,1,0:T(8,128)(2,1)S(1)} %collective-permute-done.9.refs_6_.refs_2_, ...), custom_call_target="tpu_custom_call" | custom-call | flops 1006632960 | bytes 5242880 | tf_op jit(solution)/shard_map/pallas_call | solution.py:97
  99.9 0.8 fusion.23
  100.8 0.8 fusion.20
  101.6 0.8 fusion.17
  102.5 0.8 fusion.14
  103.3 0.8 fusion.11
  104.2 0.6 collective-permute-start.17
  104.8 1.5 collective-permute-start.18
  106.3 0.5 collective-permute-start.19
  106.8 1.5 collective-permute-start.20
  108.3 0.5 collective-permute-start.21
  108.9 11.9 %shard_map.109 = bf16[256,1280]{1,0:T(8,128)(2,1)S(1)} custom-call(s32[4,4]{1,0:T(4,128)S(1)} %copy-done.1, bf16[10,256,128]{2,1,0:T(8,128)(2,1)S(1)} %get-tuple-element.35.refs_0_, bf16[2,10,128,128]{3,2,1,0:T(8,128)(2,1)S(1)} %get-tuple-element.19.refs_1_, bf16[2,10,256,128]{3,2,1,0:T(8,128)(2,1)S(1)} %get-tuple-element.22.refs_2_, ...), custom_call_target="tpu_custom_call" | custom-call | flops 2684354560 | bytes 11796480 | tf_op jit(solution)/shard_map/pallas_call | solution.py:97
  120.8 3.9 %convolution_convert_fusion = bf16[256,5120]{1,0:T(8,128)(2,1)S(1)} fusion(bf16[256,1280]{1,0:T(8,128)(2,1)S(1)} %shard_map.109, bf16[1280,5120]{1,0:T(8,128)(2,1)S(1)} %bitcast.77), kind=kOutput, calls=%fused_computation | convolution fusion | flops 3356753920 | bytes 16384000 | tf_op jit(solution)/shard_map/dot_general | solution.py:214
  124.7 0.3 fusion.27
  125.0 5.3 %collective-permute-done.18 = bf16[256,1024]{1,0:T(8,128)(2,1)S(1)} collective-permute-done((bf16[256,1024]{1,0:T(8,128)(2,1)S(1)}, bf16[256,1024]{1,0:T(8,128)(2,1)S(1)}, u32[]{:S(2)}, u32[]{:S(2)}) %collective-permute-start.18) | collective-permute-done | bytes 524320 | tf_op jit(solution)/shard_map/ppermute | solution.py:221
  130.3 0.3 fusion.28
  130.6 10.9 %collective-permute-done.19 = bf16[256,1024]{1,0:T(8,128)(2,1)S(1)} collective-permute-done((bf16[256,1024]{1,0:T(8,128)(2,1)S(1)}, bf16[256,1024]{1,0:T(8,128)(2,1)S(1)}, u32[]{:S(2)}, u32[]{:S(2)}) %collective-permute-start.19) | collective-permute-done | bytes 524320 | tf_op jit(solution)/shard_map/ppermute | solution.py:221
  141.5 0.3 fusion.29
  141.8 10.9 %collective-permute-done.20 = bf16[256,1024]{1,0:T(8,128)(2,1)S(1)} collective-permute-done((bf16[256,1024]{1,0:T(8,128)(2,1)S(1)}, bf16[256,1024]{1,0:T(8,128)(2,1)S(1)}, u32[]{:S(2)}, u32[]{:S(2)}) %collective-permute-start.20) | collective-permute-done | bytes 524320 | tf_op jit(solution)/shard_map/ppermute | solution.py:221
  152.8 0.3 fusion.30
  153.1 1.5 copy.17
  154.6 5.2 %collective-permute-done.21 = bf16[256,1024]{1,0:T(8,128)(2,1)S(1)} collective-permute-done((bf16[256,1024]{1,0:T(8,128)(2,1)S(1)}, bf16[256,1024]{1,0:T(8,128)(2,1)S(1)}, u32[]{:S(2)}, u32[]{:S(2)}) %collective-permute-start.21) | collective-permute-done | bytes 524320 | tf_op jit(solution)/shard_map/ppermute | solution.py:221
  159.8 1.1 fusion.32
  (37 shorter events, 0.2 us)
Async XLA Ops:
  0.0 6.1 %copy-start = (f32[16,5120]{1,0:T(8,128)S(1)}, f32[16,5120]{1,0:T(8,128)}, u32[]{:S(2)}) copy-start(f32[16,5120]{1,0:T(8,128)} %param.18) | copy-start | bytes 983044
  0.0 1.0 copy-start.6
  0.0 1.1 copy-start.5
  0.0 3.4 %copy-start.7 = (s32[4]{0:T(128)S(1)}, s32[4]{0:T(128)}, u32[]{:S(2)}) copy-start(s32[4]{0:T(128)} %param.19) | copy-start | bytes 52
  0.0 7.6 %copy-start.4 = (bf16[1,1,256,20,128]{4,2,3,1,0:T(8,128)(2,1)S(1)}, bf16[1,1,256,20,128]{4,2,3,1,0:T(8,128)(2,1)}, u32[]{:S(2)}) copy-start(bf16[1,1,256,20,128]{4,2,3,1,0:T(8,128)(2,1)} %param.13) | copy-start | bytes 3932164
  1.9 9.8 %collective-permute-start.1 = (bf16[2,10,64,128]{3,2,1,0:T(8,128)(2,1)}, bf16[2,10,64,128]{3,2,1,0:T(8,128)(2,1)}, u32[]{:S(2)}, u32[]{:S(2)}) collective-permute-start(bf16[2,10,64,128]{3,2,1,0:T(8,128)(2,1)} %pad_maximum_fusion.4), channel_id=1, source_target_pairs={{0,4},{4,0},{1,5},{5,1},{2,6},{6,2},{3,7},{7,3},{8,12},{12,8},{9,1... | collective-permute-start | bytes 983048 | tf_op jit(solution)/shard_map/ppermute | solution.py:153
  6.2 9.2 %collective-permute-start = (bf16[2,10,64,128]{3,2,1,0:T(8,128)(2,1)S(1)}, bf16[2,10,64,128]{3,2,1,0:T(8,128)(2,1)}, u32[]{:S(2)}, u32[]{:S(2)}) collective-permute-start(bf16[2,10,64,128]{3,2,1,0:T(8,128)(2,1)S(1)} %pad_maximum_fusion.3), channel_id=1, source_target_pairs={{0,24},{1,25},{2,26},{3,27},{4,28},{5,29},{6,30},{7,31}} | collective-permute-start | bytes 983048 | tf_op jit(solution)/shard_map/ppermute | solution.py:165
  11.7 3.8 %collective-permute-start.2 = (bf16[2,10,64,128]{3,2,1,0:T(8,128)(2,1)}, bf16[2,10,64,128]{3,2,1,0:T(8,128)(2,1)}, u32[]{:S(2)}, u32[]{:S(2)}) collective-permute-start(bf16[2,10,64,128]{3,2,1,0:T(8,128)(2,1)} %collective-permute-done.1), channel_id=1, source_target_pairs={{0,24},{1,25},{2,26},{3,27},{4,28},{5,29},{6,30},{7,31}} | collective-permute-start | bytes 983048 | tf_op jit(solution)/shard_map/ppermute | solution.py:165
  13.2 36.3 %collective-permute-start.5 = (bf16[2,10,256,128]{3,2,1,0:T(8,128)(2,1)S(1)}, bf16[2,10,256,128]{3,2,1,0:T(8,128)(2,1)}, u32[]{:S(2)}, u32[]{:S(2)}) collective-permute-start(bf16[2,10,256,128]{3,2,1,0:T(8,128)(2,1)S(1)} %pad_maximum_fusion.1), channel_id=1, source_target_pairs={{0,4},{4,0},{1,5},{5,1},{2,6},{6,2},{3,7},{7,3},{8,12},{12,8},{9,1... | collective-permute-start | bytes 3932168 | tf_op jit(solution)/shard_map/ppermute | solution.py:155
  17.0 32.4 %collective-permute-start.4 = (bf16[2,10,128,128]{3,2,1,0:T(8,128)(2,1)S(1)}, bf16[2,10,128,128]{3,2,1,0:T(8,128)(2,1)S(1)}, u32[]{:S(2)}, u32[]{:S(2)}) collective-permute-start(bf16[2,10,128,128]{3,2,1,0:T(8,128)(2,1)S(1)} %get-tuple-element.41), channel_id=1, source_target_pairs={{0,2},{1,3},{2,0},{3,1},{4,6},{5,7},{6,4},{7,5},{8,10},{9,11},{10,... | collective-permute-start | bytes 1966088 | tf_op jit(solution)/shard_map/ppermute | solution.py:170
  17.4 32.0 %collective-permute-start.3 = (bf16[2,10,128,128]{3,2,1,0:T(8,128)(2,1)S(1)}, bf16[2,10,128,128]{3,2,1,0:T(8,128)(2,1)S(1)}, u32[]{:S(2)}, u32[]{:S(2)}) collective-permute-start(bf16[2,10,128,128]{3,2,1,0:T(8,128)(2,1)S(1)} %get-tuple-element.41), channel_id=1, source_target_pairs={{0,1},{1,0},{2,3},{3,2},{4,5},{5,4},{6,7},{7,6},{8,9},{9,8},{10,11... | collective-permute-start | bytes 1966088 | tf_op jit(solution)/shard_map/ppermute | solution.py:170
  50.7 2.5 %copy-start.3 = (bf16[1,1,256,20,128]{4,2,3,1,0:T(8,128)(2,1)S(1)}, bf16[1,1,256,20,128]{4,2,3,1,0:T(8,128)(2,1)}, u32[]{:S(2)}) copy-start(bf16[1,1,256,20,128]{4,2,3,1,0:T(8,128)(2,1)} %param.11) | copy-start | bytes 3932164
  50.7 49.2 %slice-start = ((s8[13107200]{0:T(1024)(128)(4,1)}), s8[4194304]{0:T(1024)(128)(4,1)S(1)}, s32[]{:S(2)}) async-start(s8[13107200]{0:T(1024)(128)(4,1)} %bitcast.76), calls=%async_computation | async-start | bytes 8388608
  51.5 34.8 %copy-start.1 = (s32[4,4]{1,0:T(4,128)S(1)}, s32[4,4]{1,0:T(4,128)}, u32[]{:S(2)}) copy-start(s32[4,4]{1,0:T(4,128)} %mask.5) | copy-start | bytes 196
  51.5 48.4 %slice-start.1 = ((s8[13107200]{0:T(1024)(128)(4,1)}), s8[4194304]{0:T(1024)(128)(4,1)S(1)}, s32[]{:S(2)}) async-start(s8[13107200]{0:T(1024)(128)(4,1)} %bitcast.76), calls=%async_computation.1 | async-start | bytes 8388608
  51.5 22.2 %collective-permute-start.12 = (bf16[2,10,256,128]{3,2,1,0:T(8,128)(2,1)S(1)}, bf16[2,10,256,128]{3,2,1,0:T(8,128)(2,1)S(1)}, u32[]{:S(2)}, u32[]{:S(2)}) collective-permute-start(bf16[2,10,256,128]{3,2,1,0:T(8,128)(2,1)S(1)} %get-tuple-element.22.refs_2_), channel_id=1, source_target_pairs={{8,16},{9,17},{10,18},{11,19},{12,20},{13,21},{14,22},{15,23}} | collective-permute-start | bytes 3932168 | tf_op jit(solution)/shard_map/ppermute | solution.py:200
  53.1 16.1 %collective-permute-start.6 = (bf16[2,10,128,128]{3,2,1,0:T(8,128)(2,1)S(1)}, bf16[2,10,128,128]{3,2,1,0:T(8,128)(2,1)S(1)}, u32[]{:S(2)}, u32[]{:S(2)}) collective-permute-start(bf16[2,10,128,128]{3,2,1,0:T(8,128)(2,1)S(1)} %collective-permute-done.4), channel_id=1, source_target_pairs={{0,1},{1,0},{2,3},{3,2},{4,5},{5,4},{6,7},{7,6},{8,9},{9,8},{10,11... | collective-permute-start | bytes 1966088 | tf_op jit(solution)/shard_map/ppermute | solution.py:170
  53.3 19.1 %collective-permute-start.16 = (bf16[10,256,128]{2,1,0:T(8,128)(2,1)S(1)}, bf16[10,256,128]{2,1,0:T(8,128)(2,1)S(1)}, u32[]{:S(2)}, u32[]{:S(2)}) collective-permute-start(bf16[10,256,128]{2,1,0:T(8,128)(2,1)S(1)} %get-tuple-element.36), channel_id=1, source_target_pairs={{0,4},{4,0},{1,5},{5,1},{2,6},{6,2},{3,7},{7,3},{8,12},{12,8},{9,1... | collective-permute-start | bytes 1966088 | tf_op jit(solution)/shard_map/ppermute | solution.py:157
  53.9 25.2 %collective-permute-start.7 = (bf16[2,10,128,128]{3,2,1,0:T(8,128)(2,1)S(1)}, bf16[2,10,128,128]{3,2,1,0:T(8,128)(2,1)S(1)}, u32[]{:S(2)}, u32[]{:S(2)}) collective-permute-start(bf16[2,10,128,128]{3,2,1,0:T(8,128)(2,1)S(1)} %get-tuple-element.24.refs_13_.refs_7_), channel_id=1, source_target_pairs={{0,8},{16,24},{24,16},{1,9},{17,25},{25,17},{2,10},{18,26},{26,18}... | collective-permute-start | bytes 1966088 | tf_op jit(solution)/shard_map/ppermute | solution.py:188
  55.8 21.9 %collective-permute-start.10 = (bf16[2,10,128,128]{3,2,1,0:T(8,128)(2,1)S(1)}, bf16[2,10,128,128]{3,2,1,0:T(8,128)(2,1)S(1)}, u32[]{:S(2)}, u32[]{:S(2)}) collective-permute-start(bf16[2,10,128,128]{3,2,1,0:T(8,128)(2,1)S(1)} %get-tuple-element.19.refs_1_), channel_id=1, source_target_pairs={{8,16},{9,17},{10,18},{11,19},{12,20},{13,21},{14,22},{15,23}} | collective-permute-start | bytes 1966088 | tf_op jit(solution)/shard_map/ppermute | solution.py:200
  69.2 17.1 %collective-permute-start.8 = (bf16[2,10,256,128]{3,2,1,0:T(8,128)(2,1)S(1)}, bf16[2,10,256,128]{3,2,1,0:T(8,128)(2,1)S(1)}, u32[]{:S(2)}, u32[]{:S(2)}) collective-permute-start(bf16[2,10,256,128]{3,2,1,0:T(8,128)(2,1)S(1)} %get-tuple-element.25.refs_14_.refs_8_), channel_id=1, source_target_pairs={{0,8},{16,24},{24,16},{1,9},{17,25},{25,17},{2,10},{18,26},{26,18}... | collective-permute-start | bytes 3932168 | tf_op jit(solution)/shard_map/ppermute | solution.py:188
  72.4 12.3 %collective-permute-start.14 = (bf16[2,10,128,128]{3,2,1,0:T(8,128)(2,1)S(1)}, bf16[2,10,128,128]{3,2,1,0:T(8,128)(2,1)S(1)}, u32[]{:S(2)}, u32[]{:S(2)}) collective-permute-start(bf16[2,10,128,128]{3,2,1,0:T(8,128)(2,1)S(1)} %get-tuple-element.32.refs_3_.refs_1_), channel_id=1, source_target_pairs={{8,16},{9,17},{10,18},{11,19},{12,20},{13,21},{14,22},{15,23}} | collective-permute-start | bytes 1966088 | tf_op jit(solution)/shard_map/ppermute | solution.py:200
  73.8 20.3 %collective-permute-start.13 = (bf16[2,10,256,128]{3,2,1,0:T(8,128)(2,1)S(1)}, bf16[2,10,256,128]{3,2,1,0:T(8,128)(2,1)S(1)}, u32[]{:S(2)}, u32[]{:S(2)}) collective-permute-start(bf16[2,10,256,128]{3,2,1,0:T(8,128)(2,1)S(1)} %collective-permute-done.12.refs_10_.refs_4_), channel_id=1, source_target_pairs={{16,24},{17,25},{18,26},{19,27},{20,28},{21,29},{22,30},{23,31}} | collective-permute-start | bytes 3932168 | tf_op jit(solution)/shard_map/ppermute | solution.py:201
  77.8 8.6 %collective-permute-start.11 = (bf16[2,10,128,128]{3,2,1,0:T(8,128)(2,1)S(1)}, bf16[2,10,128,128]{3,2,1,0:T(8,128)(2,1)S(1)}, u32[]{:S(2)}, u32[]{:S(2)}) collective-permute-start(bf16[2,10,128,128]{3,2,1,0:T(8,128)(2,1)S(1)} %collective-permute-done.10.refs_8_.refs_6_), channel_id=1, source_target_pairs={{16,24},{17,25},{18,26},{19,27},{20,28},{21,29},{22,30},{23,31}} | collective-permute-start | bytes 1966088 | tf_op jit(solution)/shard_map/ppermute | solution.py:201
  79.1 14.9 %collective-permute-start.9 = (bf16[2,10,128,128]{3,2,1,0:T(8,128)(2,1)S(1)}, bf16[2,10,128,128]{3,2,1,0:T(8,128)(2,1)S(1)}, u32[]{:S(2)}, u32[]{:S(2)}) collective-permute-start(bf16[2,10,128,128]{3,2,1,0:T(8,128)(2,1)S(1)} %get-tuple-element.31.refs_15_.refs_7_), channel_id=1, source_target_pairs={{0,8},{16,24},{24,16},{1,9},{17,25},{25,17},{2,10},{18,26},{26,18}... | collective-permute-start | bytes 1966088 | tf_op jit(solution)/shard_map/ppermute | solution.py:188
  84.8 9.2 %collective-permute-start.15 = (bf16[2,10,128,128]{3,2,1,0:T(8,128)(2,1)S(1)}, bf16[2,10,128,128]{3,2,1,0:T(8,128)(2,1)S(1)}, u32[]{:S(2)}, u32[]{:S(2)}) collective-permute-start(bf16[2,10,128,128]{3,2,1,0:T(8,128)(2,1)S(1)} %collective-permute-done.14.refs_12_.refs_6_), channel_id=1, source_target_pairs={{16,24},{17,25},{18,26},{19,27},{20,28},{21,29},{22,30},{23,31}} | collective-permute-start | bytes 1966088 | tf_op jit(solution)/shard_map/ppermute | solution.py:201
  86.3 13.6 %slice-start.2 = ((s8[13107200]{0:T(1024)(128)(4,1)}), s8[4194304]{0:T(1024)(128)(4,1)S(1)}, s32[]{:S(2)}) async-start(s8[13107200]{0:T(1024)(128)(4,1)} %bitcast.76), calls=%async_computation.2 | async-start | bytes 8388608
  94.0 5.9 %slice-start.3 = ((s8[13107200]{0:T(1024)(128)(4,1)}), s8[524288]{0:T(1024)(128)(4,1)S(1)}, s32[]{:S(2)}) async-start(s8[13107200]{0:T(1024)(128)(4,1)} %bitcast.76), calls=%async_computation.3 | async-start | bytes 1048576
  104.2 20.5 %collective-permute-start.17 = (bf16[256,1024]{1,0:T(8,128)(2,1)S(1)}, bf16[256,1024]{1,0:T(8,128)(2,1)S(1)}, u32[]{:S(2)}, u32[]{:S(2)}) collective-permute-start(bf16[256,1024]{1,0:T(8,128)(2,1)S(1)} %fusion.11), channel_id=1, source_target_pairs={{4,0},{0,4},{5,1},{1,5},{6,2},{2,6},{7,3},{3,7},{12,8},{8,12},{13,... | collective-permute-start | bytes 1572872 | tf_op jit(solution)/shard_map/ppermute | solution.py:221
  104.8 25.5 %collective-permute-start.18 = (bf16[256,1024]{1,0:T(8,128)(2,1)S(1)}, bf16[256,1024]{1,0:T(8,128)(2,1)S(1)}, u32[]{:S(2)}, u32[]{:S(2)}) collective-permute-start(bf16[256,1024]{1,0:T(8,128)(2,1)S(1)} %fusion.14), channel_id=1, source_target_pairs={{4,0},{0,4},{5,1},{1,5},{6,2},{2,6},{7,3},{3,7},{12,8},{8,12},{13,... | collective-permute-start | bytes 1572872 | tf_op jit(solution)/shard_map/ppermute | solution.py:221
  106.3 35.2 %collective-permute-start.19 = (bf16[256,1024]{1,0:T(8,128)(2,1)S(1)}, bf16[256,1024]{1,0:T(8,128)(2,1)S(1)}, u32[]{:S(2)}, u32[]{:S(2)}) collective-permute-start(bf16[256,1024]{1,0:T(8,128)(2,1)S(1)} %fusion.17), channel_id=1, source_target_pairs={{4,0},{0,4},{5,1},{1,5},{6,2},{2,6},{7,3},{3,7},{12,8},{8,12},{13,... | collective-permute-start | bytes 1572872 | tf_op jit(solution)/shard_map/ppermute | solution.py:221
  106.8 45.9 %collective-permute-start.20 = (bf16[256,1024]{1,0:T(8,128)(2,1)S(1)}, bf16[256,1024]{1,0:T(8,128)(2,1)S(1)}, u32[]{:S(2)}, u32[]{:S(2)}) collective-permute-start(bf16[256,1024]{1,0:T(8,128)(2,1)S(1)} %fusion.20), channel_id=1, source_target_pairs={{4,0},{0,4},{5,1},{1,5},{6,2},{2,6},{7,3},{3,7},{12,8},{8,12},{13,... | collective-permute-start | bytes 1572872 | tf_op jit(solution)/shard_map/ppermute | solution.py:221
  108.3 51.5 %collective-permute-start.21 = (bf16[256,1024]{1,0:T(8,128)(2,1)S(1)}, bf16[256,1024]{1,0:T(8,128)(2,1)S(1)}, u32[]{:S(2)}, u32[]{:S(2)}) collective-permute-start(bf16[256,1024]{1,0:T(8,128)(2,1)S(1)} %fusion.23), channel_id=1, source_target_pairs={{4,0},{0,4},{5,1},{1,5},{6,2},{2,6},{7,3},{3,7},{12,8},{8,12},{13,... | collective-permute-start | bytes 1572872 | tf_op jit(solution)/shard_map/ppermute | solution.py:221
  120.8 3.9 %copy-start.2 = (bf16[1,1,256,5120]{3,2,1,0:T(8,128)(2,1)S(1)}, bf16[1,1,256,5120]{3,2,1,0:T(8,128)(2,1)}, u32[]{:S(2)}) copy-start(bf16[1,1,256,5120]{3,2,1,0:T(8,128)(2,1)} %param.16) | copy-start | bytes 7864324

commit v8 on v7

--- a/solution.py
+++ b/solution.py
@@ -202,9 +202,8 @@
     slots.append((lambda c: jnp.where(c >= final - 1, 1, -1), list(zip(near, far))))
     slots.append((lambda c: jnp.where(c == final, 0, -1), [a for _, a in held]))
 
-    cuts = [len(groups) - 1 if i in (0, 1, len(slots) - 1) else len(groups) - 2 for i in range(len(slots))]
-    early = [(origin, arrays[:cut]) for (origin, arrays), cut in zip(slots, cuts)]
-    late = [(origin, arrays[cut:]) for (origin, arrays), cut in zip(slots, cuts)]
+    early = [(origin, arrays[:1]) for origin, arrays in slots]
+    late = [(origin, arrays[1:]) for origin, arrays in slots]
     states = {}
     for d in range(1, splits):
         states[d] = attend(q_parts[d], early, span_mask, None, False)

time: 161 us -> 162 us (level)
  the two profiles are of different devices: /device:TPU:28 before, /device:TPU:4 now
where the time goes in v8:
time: 162 us
  waiting for transfers between devices  80.4 us (50%)
  starting transfers between devices  31.6 us (20%)
  Pallas kernels  25.6 us (16%)
  matrix products  8.09 us (5%)
  other arithmetic  6.77 us (4%)
  local copies, waits for them, and re-layouts  6.22 us (4%)
  between operations  3.19 us (2%)
    ppermute x3, waiting for transfers between devices, sublayer(): lax.ppermute(pieces[i - low], 'branch', [(b, b ^ low) for b in range(bran...  39.2 us
    ppermute x5, waiting for transfers between devices, sublayer(): returned[j].append(lax.ppermute(partial, 'head', back))  33.1 us
    pallas_call x3, Pallas kernels, attend(): pl.pallas_call(functools.partial(flash_kernel, layout=layout, count=len(a...  25.6 us
    dot_general x6, matrix products, sublayer(): jnp.dot(a, w, preferred_element_type=jnp.float32).astype(jnp.bfloat16)  8.09 us
    ppermute x3, starting transfers between devices, sublayer(): lax.ppermute(pieces[i - low], 'branch', [(b, b ^ low) for b in range(bran...  5.88 us
    ppermute x3, starting transfers between devices, sublayer(): lax.ppermute(a, 'tm', pairs + [(final, final - 1)])  5.74 us
    ppermute x3, waiting for transfers between devices, sublayer(): far = [lax.ppermute(a, 'tm', [(1, final - 1)]) for a in own]  5.43 us
    ppermute x3, starting transfers between devices, sublayer(): near = [lax.ppermute(a, 'tm', [(final - 1, final)]) for a in far]  4.72 us
  transfers between devices with their start and end apart: 22, of which 9 were waited for; matrix products, arithmetic and copies ran while one was open for 7% of the time, Pallas kernels for 10%

profile of v8, /device:TPU:4, one launch (start us, length us, event | category | flops | bytes accessed | tf_op | source)
XLA Modules:
  0.0 161.9 jit_solution(4947888669582350479)
XLA Ops:
  0.0 1.0 copy-done.6
  1.0 0.1 copy-done.5
  1.2 0.8 pad_maximum_fusion.4
  1.9 1.5 collective-permute-start.1
  3.4 0.6 dynamic_slice.40
  6.2 1.4 collective-permute-start
  7.6 1.5 dynamic-slice_bitcast_fusion.1
  9.0 2.7 %collective-permute-done.1 = bf16[2,10,64,128]{3,2,1,0:T(8,128)(2,1)} collective-permute-done((bf16[2,10,64,128]{3,2,1,0:T(8,128)(2,1)}, bf16[2,10,64,128]{3,2,1,0:T(8,128)(2,1)}, u32[]{:S(2)}, u32[]{:S(2)}) %collective-permute-start.1) | collective-permute-done | bytes 327712 | tf_op jit(solution)/shard_map/ppermute | solution.py:153
  11.7 1.4 collective-permute-start.2
  13.1 0.1 pad_maximum_fusion.1
  13.2 1.6 collective-permute-start.5
  15.5 1.0 broadcast_select_fusion.6
  16.5 0.4 broadcast_select_fusion.3
  17.0 2.7 %collective-permute-start.4 = (bf16[2,10,128,128]{3,2,1,0:T(8,128)(2,1)S(1)}, bf16[2,10,128,128]{3,2,1,0:T(8,128)(2,1)S(1)}, u32[]{:S(2)}, u32[]{:S(2)}) collective-permute-start(bf16[2,10,128,128]{3,2,1,0:T(8,128)(2,1)S(1)} %get-tuple-element.41), channel_id=1, source_target_pairs={{0,2},{1,3},{2,0},{3,1},{4,6},{5,7},{6,4},{7,5},{8,10},{9,11},{10,... | collective-permute-start | bytes 1966088 | tf_op jit(solution)/shard_map/ppermute | solution.py:170
  19.6 1.6 collective-permute-start.3
  21.2 27.4 %collective-permute-done.4 = bf16[2,10,128,128]{3,2,1,0:T(8,128)(2,1)S(1)} collective-permute-done((bf16[2,10,128,128]{3,2,1,0:T(8,128)(2,1)S(1)}, bf16[2,10,128,128]{3,2,1,0:T(8,128)(2,1)S(1)}, u32[]{:S(2)}, u32[]{:S(2)}) %collective-permute-start.4) | collective-permute-done | bytes 655392 | tf_op jit(solution)/shard_map/ppermute | solution.py:170
  48.6 0.1 constant_dynamic-update-slice_fusion.1
  48.6 0.1 constant_dynamic-update-slice_fusion
  48.7 1.1 slice.99
  49.9 0.0 slice-start
  49.9 0.8 broadcast_select_fusion
  50.7 0.0 slice-start.1
  50.7 1.6 collective-permute-start.12
  52.3 1.7 %collective-permute-start.6 = (bf16[2,10,128,128]{3,2,1,0:T(8,128)(2,1)S(1)}, bf16[2,10,128,128]{3,2,1,0:T(8,128)(2,1)S(1)}, u32[]{:S(2)}, u32[]{:S(2)}) collective-permute-start(bf16[2,10,128,128]{3,2,1,0:T(8,128)(2,1)S(1)} %collective-permute-done.4), channel_id=1, source_target_pairs={{0,1},{1,0},{2,3},{3,2},{4,5},{5,4},{6,7},{7,6},{8,9},{9,8},{10,11... | collective-permute-start | bytes 1966088 | tf_op jit(solution)/shard_map/ppermute | solution.py:170
  54.0 0.1 dynamic-slice_bitcast_fusion.5
  54.1 0.6 collective-permute-start.16
  54.7 1.9 %collective-permute-start.7 = (bf16[2,10,128,128]{3,2,1,0:T(8,128)(2,1)S(1)}, bf16[2,10,128,128]{3,2,1,0:T(8,128)(2,1)S(1)}, u32[]{:S(2)}, u32[]{:S(2)}) collective-permute-start(bf16[2,10,128,128]{3,2,1,0:T(8,128)(2,1)S(1)} %get-tuple-element.24.refs_13_.refs_5_), channel_id=1, source_target_pairs={{0,8},{16,24},{24,16},{1,9},{17,25},{25,17},{2,10},{18,26},{26,18}... | collective-permute-start | bytes 1966088 | tf_op jit(solution)/shard_map/ppermute | solution.py:188
  56.6 1.3 collective-permute-start.10
  57.9 11.8 %collective-permute-done.6 = bf16[2,10,128,128]{3,2,1,0:T(8,128)(2,1)S(1)} collective-permute-done((bf16[2,10,128,128]{3,2,1,0:T(8,128)(2,1)S(1)}, bf16[2,10,128,128]{3,2,1,0:T(8,128)(2,1)S(1)}, u32[]{:S(2)}, u32[]{:S(2)}) %collective-permute-start.6) | collective-permute-done | bytes 655392 | tf_op jit(solution)/shard_map/ppermute | solution.py:170
  69.7 1.9 %collective-permute-start.8 = (bf16[2,10,256,128]{3,2,1,0:T(8,128)(2,1)S(1)}, bf16[2,10,256,128]{3,2,1,0:T(8,128)(2,1)S(1)}, u32[]{:S(2)}, u32[]{:S(2)}) collective-permute-start(bf16[2,10,256,128]{3,2,1,0:T(8,128)(2,1)S(1)} %get-tuple-element.25.refs_14_.refs_9_), channel_id=1, source_target_pairs={{0,8},{16,24},{24,16},{1,9},{17,25},{25,17},{2,10},{18,26},{26,18}... | collective-permute-start | bytes 3932168 | tf_op jit(solution)/shard_map/ppermute | solution.py:188
  71.7 1.3 broadcast_select_fusion.2
  72.9 1.3 collective-permute-start.14
  74.2 1.9 %collective-permute-start.13 = (bf16[2,10,256,128]{3,2,1,0:T(8,128)(2,1)S(1)}, bf16[2,10,256,128]{3,2,1,0:T(8,128)(2,1)S(1)}, u32[]{:S(2)}, u32[]{:S(2)}) collective-permute-start(bf16[2,10,256,128]{3,2,1,0:T(8,128)(2,1)S(1)} %collective-permute-done.12.refs_10_.refs_6_), channel_id=1, source_target_pairs={{16,24},{17,25},{18,26},{19,27},{20,28},{21,29},{22,30},{23,31}} | collective-permute-start | bytes 3932168 | tf_op jit(solution)/shard_map/ppermute | solution.py:201
  76.1 0.8 collective-permute-done.10.refs_8_.refs_4_
  77.0 1.3 collective-permute-start.11
  78.3 1.9 %collective-permute-start.9 = (bf16[2,10,128,128]{3,2,1,0:T(8,128)(2,1)S(1)}, bf16[2,10,128,128]{3,2,1,0:T(8,128)(2,1)S(1)}, u32[]{:S(2)}, u32[]{:S(2)}) collective-permute-start(bf16[2,10,128,128]{3,2,1,0:T(8,128)(2,1)S(1)} %get-tuple-element.31.refs_15_.refs_10_), channel_id=1, source_target_pairs={{0,8},{16,24},{24,16},{1,9},{17,25},{25,17},{2,10},{18,26},{26,18}... | collective-permute-start | bytes 1966088 | tf_op jit(solution)/shard_map/ppermute | solution.py:188
  80.2 4.6 %collective-permute-done.14.refs_12_.refs_8_ = bf16[2,10,128,128]{3,2,1,0:T(8,128)(2,1)S(1)} collective-permute-done((bf16[2,10,128,128]{3,2,1,0:T(8,128)(2,1)S(1)}, bf16[2,10,128,128]{3,2,1,0:T(8,128)(2,1)S(1)}, u32[]{:S(2)}, u32[]{:S(2)}) %collective-permute-start.14) | collective-permute-done | bytes 655392 | tf_op jit(solution)/shard_map/ppermute | solution.py:200
  84.8 1.5 collective-permute-start.15
  86.4 0.0 slice-start.2
  86.4 4.3 %shard_map.110 = (f32[10,256,128]{2,1,0:T(8,128)S(1)}, f32[10,256,128]{2,1,0:T(8,128)S(1)}, f32[10,256,128]{2,1,0:T(8,128)S(1)}) custom-call(s32[4,4]{1,0:T(4,128)S(1)} %copy-done.1, bf16[10,256,128]{2,1,0:T(8,128)(2,1)S(1)} %collective-permute-done.16.refs_0_, bf16[2,10,128,128]{3,2,1,0:T(8,128)(2,1)S(1)} %get-tuple-element.19.refs_1_, ...), custom_call_target="tpu_custom_call" | custom-call | flops 671088640 | bytes 3932160 | tf_op jit(solution)/shard_map/pallas_call | solution.py:97
  90.7 0.0 slice-start.3
  90.7 9.5 %shard_map.111 = bf16[256,1280]{1,0:T(8,128)(2,1)S(1)} custom-call(s32[4,4]{1,0:T(4,128)S(1)} %copy-done.1, bf16[10,256,128]{2,1,0:T(8,128)(2,1)S(1)} %collective-permute-done.16.refs_0_, bf16[2,10,256,128]{3,2,1,0:T(8,128)(2,1)S(1)} %get-tuple-element.22.refs_2_.refs_1_, bf16[2,10,128,128]{3,2,1,0:T(8,128)(2,1)S(1)} %get-tuple-element.32.refs_3_.refs_2_, ...), custom_call_target="tpu_custom_call" | custom-call | flops 2013265920 | bytes 9175040 | tf_op jit(solution)/shard_map/pallas_call | solution.py:97
  100.2 0.8 fusion.23
  101.1 0.8 fusion.20
  101.9 0.8 fusion.17
  102.8 0.8 fusion.14
  103.6 0.8 fusion.11
  104.5 0.6 collective-permute-start.17
  105.1 1.5 collective-permute-start.18
  106.6 0.5 collective-permute-start.19
  107.1 1.5 collective-permute-start.20
  108.6 0.5 collective-permute-start.21
  109.1 11.9 %shard_map.109 = bf16[256,1280]{1,0:T(8,128)(2,1)S(1)} custom-call(s32[4,4]{1,0:T(4,128)S(1)} %copy-done.1, bf16[10,256,128]{2,1,0:T(8,128)(2,1)S(1)} %get-tuple-element.35.refs_0_, bf16[2,10,128,128]{3,2,1,0:T(8,128)(2,1)S(1)} %get-tuple-element.19.refs_1_, bf16[2,10,256,128]{3,2,1,0:T(8,128)(2,1)S(1)} %get-tuple-element.22.refs_2_.refs_1_, ...), custom_call_target="tpu_custom_call" | custom-call | flops 2684354560 | bytes 11796480 | tf_op jit(solution)/shard_map/pallas_call | solution.py:97
  121.1 3.9 %convolution_convert_fusion = bf16[256,5120]{1,0:T(8,128)(2,1)S(1)} fusion(bf16[256,1280]{1,0:T(8,128)(2,1)S(1)} %shard_map.109, bf16[1280,5120]{1,0:T(8,128)(2,1)S(1)} %bitcast.77), kind=kOutput, calls=%fused_computation | convolution fusion | flops 3356753920 | bytes 16384000 | tf_op jit(solution)/shard_map/dot_general | solution.py:213
  125.0 0.3 fusion.27
  125.3 5.3 %collective-permute-done.18 = bf16[256,1024]{1,0:T(8,128)(2,1)S(1)} collective-permute-done((bf16[256,1024]{1,0:T(8,128)(2,1)S(1)}, bf16[256,1024]{1,0:T(8,128)(2,1)S(1)}, u32[]{:S(2)}, u32[]{:S(2)}) %collective-permute-start.18) | collective-permute-done | bytes 524320 | tf_op jit(solution)/shard_map/ppermute | solution.py:220
  130.6 0.3 fusion.28
  130.9 10.9 %collective-permute-done.19 = bf16[256,1024]{1,0:T(8,128)(2,1)S(1)} collective-permute-done((bf16[256,1024]{1,0:T(8,128)(2,1)S(1)}, bf16[256,1024]{1,0:T(8,128)(2,1)S(1)}, u32[]{:S(2)}, u32[]{:S(2)}) %collective-permute-start.19) | collective-permute-done | bytes 524320 | tf_op jit(solution)/shard_map/ppermute | solution.py:220
  141.8 0.3 fusion.29
  142.1 10.9 %collective-permute-done.20 = bf16[256,1024]{1,0:T(8,128)(2,1)S(1)} collective-permute-done((bf16[256,1024]{1,0:T(8,128)(2,1)S(1)}, bf16[256,1024]{1,0:T(8,128)(2,1)S(1)}, u32[]{:S(2)}, u32[]{:S(2)}) %collective-permute-start.20) | collective-permute-done | bytes 524320 | tf_op jit(solution)/shard_map/ppermute | solution.py:220
  153.1 0.3 fusion.30
  153.4 1.5 copy.17
  154.9 5.9 %collective-permute-done.21 = bf16[256,1024]{1,0:T(8,128)(2,1)S(1)} collective-permute-done((bf16[256,1024]{1,0:T(8,128)(2,1)S(1)}, bf16[256,1024]{1,0:T(8,128)(2,1)S(1)}, u32[]{:S(2)}, u32[]{:S(2)}) %collective-permute-start.21) | collective-permute-done | bytes 524320 | tf_op jit(solution)/shard_map/ppermute | solution.py:220
  160.8 1.1 fusion.32
  (37 shorter events, 0.2 us)
Async XLA Ops:
  0.0 6.1 %copy-start = (f32[16,5120]{1,0:T(8,128)S(1)}, f32[16,5120]{1,0:T(8,128)}, u32[]{:S(2)}) copy-start(f32[16,5120]{1,0:T(8,128)} %param.18) | copy-start | bytes 983044
  0.0 1.0 copy-start.6
  0.0 1.1 copy-start.5
  0.0 3.4 %copy-start.7 = (s32[4]{0:T(128)S(1)}, s32[4]{0:T(128)}, u32[]{:S(2)}) copy-start(s32[4]{0:T(128)} %param.19) | copy-start | bytes 52
  0.0 7.6 %copy-start.4 = (bf16[1,1,256,20,128]{4,2,3,1,0:T(8,128)(2,1)S(1)}, bf16[1,1,256,20,128]{4,2,3,1,0:T(8,128)(2,1)}, u32[]{:S(2)}) copy-start(bf16[1,1,256,20,128]{4,2,3,1,0:T(8,128)(2,1)} %param.13) | copy-start | bytes 3932164
  1.9 9.8 %collective-permute-start.1 = (bf16[2,10,64,128]{3,2,1,0:T(8,128)(2,1)}, bf16[2,10,64,128]{3,2,1,0:T(8,128)(2,1)}, u32[]{:S(2)}, u32[]{:S(2)}) collective-permute-start(bf16[2,10,64,128]{3,2,1,0:T(8,128)(2,1)} %pad_maximum_fusion.4), channel_id=1, source_target_pairs={{0,4},{4,0},{1,5},{5,1},{2,6},{6,2},{3,7},{7,3},{8,12},{12,8},{9,1... | collective-permute-start | bytes 983048 | tf_op jit(solution)/shard_map/ppermute | solution.py:153
  6.2 9.2 %collective-permute-start = (bf16[2,10,64,128]{3,2,1,0:T(8,128)(2,1)S(1)}, bf16[2,10,64,128]{3,2,1,0:T(8,128)(2,1)}, u32[]{:S(2)}, u32[]{:S(2)}) collective-permute-start(bf16[2,10,64,128]{3,2,1,0:T(8,128)(2,1)S(1)} %pad_maximum_fusion.3), channel_id=1, source_target_pairs={{0,24},{1,25},{2,26},{3,27},{4,28},{5,29},{6,30},{7,31}} | collective-permute-start | bytes 983048 | tf_op jit(solution)/shard_map/ppermute | solution.py:165
  11.7 3.8 %collective-permute-start.2 = (bf16[2,10,64,128]{3,2,1,0:T(8,128)(2,1)}, bf16[2,10,64,128]{3,2,1,0:T(8,128)(2,1)}, u32[]{:S(2)}, u32[]{:S(2)}) collective-permute-start(bf16[2,10,64,128]{3,2,1,0:T(8,128)(2,1)} %collective-permute-done.1), channel_id=1, source_target_pairs={{0,24},{1,25},{2,26},{3,27},{4,28},{5,29},{6,30},{7,31}} | collective-permute-start | bytes 983048 | tf_op jit(solution)/shard_map/ppermute | solution.py:165
  13.2 35.5 %collective-permute-start.5 = (bf16[2,10,256,128]{3,2,1,0:T(8,128)(2,1)S(1)}, bf16[2,10,256,128]{3,2,1,0:T(8,128)(2,1)}, u32[]{:S(2)}, u32[]{:S(2)}) collective-permute-start(bf16[2,10,256,128]{3,2,1,0:T(8,128)(2,1)S(1)} %pad_maximum_fusion.1), channel_id=1, source_target_pairs={{0,4},{4,0},{1,5},{5,1},{2,6},{6,2},{3,7},{7,3},{8,12},{12,8},{9,1... | collective-permute-start | bytes 3932168 | tf_op jit(solution)/shard_map/ppermute | solution.py:155
  17.0 31.6 %collective-permute-start.4 = (bf16[2,10,128,128]{3,2,1,0:T(8,128)(2,1)S(1)}, bf16[2,10,128,128]{3,2,1,0:T(8,128)(2,1)S(1)}, u32[]{:S(2)}, u32[]{:S(2)}) collective-permute-start(bf16[2,10,128,128]{3,2,1,0:T(8,128)(2,1)S(1)} %get-tuple-element.41), channel_id=1, source_target_pairs={{0,2},{1,3},{2,0},{3,1},{4,6},{5,7},{6,4},{7,5},{8,10},{9,11},{10,... | collective-permute-start | bytes 1966088 | tf_op jit(solution)/shard_map/ppermute | solution.py:170
  19.6 29.0 %collective-permute-start.3 = (bf16[2,10,128,128]{3,2,1,0:T(8,128)(2,1)S(1)}, bf16[2,10,128,128]{3,2,1,0:T(8,128)(2,1)S(1)}, u32[]{:S(2)}, u32[]{:S(2)}) collective-permute-start(bf16[2,10,128,128]{3,2,1,0:T(8,128)(2,1)S(1)} %get-tuple-element.41), channel_id=1, source_target_pairs={{0,1},{1,0},{2,3},{3,2},{4,5},{5,4},{6,7},{7,6},{8,9},{9,8},{10,11... | collective-permute-start | bytes 1966088 | tf_op jit(solution)/shard_map/ppermute | solution.py:170
  49.9 4.1 %copy-start.3 = (bf16[1,1,256,20,128]{4,2,3,1,0:T(8,128)(2,1)S(1)}, bf16[1,1,256,20,128]{4,2,3,1,0:T(8,128)(2,1)}, u32[]{:S(2)}) copy-start(bf16[1,1,256,20,128]{4,2,3,1,0:T(8,128)(2,1)} %param.11) | copy-start | bytes 3932164
  49.9 50.3 %slice-start = ((s8[13107200]{0:T(1024)(128)(4,1)}), s8[4194304]{0:T(1024)(128)(4,1)S(1)}, s32[]{:S(2)}) async-start(s8[13107200]{0:T(1024)(128)(4,1)} %bitcast.76), calls=%async_computation | async-start | bytes 8388608
  50.7 35.7 %copy-start.1 = (s32[4,4]{1,0:T(4,128)S(1)}, s32[4,4]{1,0:T(4,128)}, u32[]{:S(2)}) copy-start(s32[4,4]{1,0:T(4,128)} %mask.5) | copy-start | bytes 196
  50.7 49.5 %slice-start.1 = ((s8[13107200]{0:T(1024)(128)(4,1)}), s8[4194304]{0:T(1024)(128)(4,1)S(1)}, s32[]{:S(2)}) async-start(s8[13107200]{0:T(1024)(128)(4,1)} %bitcast.76), calls=%async_computation.1 | async-start | bytes 8388608
  50.7 23.5 %collective-permute-start.12 = (bf16[2,10,256,128]{3,2,1,0:T(8,128)(2,1)S(1)}, bf16[2,10,256,128]{3,2,1,0:T(8,128)(2,1)S(1)}, u32[]{:S(2)}, u32[]{:S(2)}) collective-permute-start(bf16[2,10,256,128]{3,2,1,0:T(8,128)(2,1)S(1)} %get-tuple-element.22.refs_2_.refs_1_), channel_id=1, source_target_pairs={{8,16},{9,17},{10,18},{11,19},{12,20},{13,21},{14,22},{15,23}} | collective-permute-start | bytes 3932168 | tf_op jit(solution)/shard_map/ppermute | solution.py:200
  52.3 17.4 %collective-permute-start.6 = (bf16[2,10,128,128]{3,2,1,0:T(8,128)(2,1)S(1)}, bf16[2,10,128,128]{3,2,1,0:T(8,128)(2,1)S(1)}, u32[]{:S(2)}, u32[]{:S(2)}) collective-permute-start(bf16[2,10,128,128]{3,2,1,0:T(8,128)(2,1)S(1)} %collective-permute-done.4), channel_id=1, source_target_pairs={{0,1},{1,0},{2,3},{3,2},{4,5},{5,4},{6,7},{7,6},{8,9},{9,8},{10,11... | collective-permute-start | bytes 1966088 | tf_op jit(solution)/shard_map/ppermute | solution.py:170
  54.1 18.8 %collective-permute-start.16 = (bf16[10,256,128]{2,1,0:T(8,128)(2,1)S(1)}, bf16[10,256,128]{2,1,0:T(8,128)(2,1)S(1)}, u32[]{:S(2)}, u32[]{:S(2)}) collective-permute-start(bf16[10,256,128]{2,1,0:T(8,128)(2,1)S(1)} %get-tuple-element.36), channel_id=1, source_target_pairs={{0,4},{4,0},{1,5},{5,1},{2,6},{6,2},{3,7},{7,3},{8,12},{12,8},{9,1... | collective-permute-start | bytes 1966088 | tf_op jit(solution)/shard_map/ppermute | solution.py:157
  54.7 23.6 %collective-permute-start.7 = (bf16[2,10,128,128]{3,2,1,0:T(8,128)(2,1)S(1)}, bf16[2,10,128,128]{3,2,1,0:T(8,128)(2,1)S(1)}, u32[]{:S(2)}, u32[]{:S(2)}) collective-permute-start(bf16[2,10,128,128]{3,2,1,0:T(8,128)(2,1)S(1)} %get-tuple-element.24.refs_13_.refs_5_), channel_id=1, source_target_pairs={{0,8},{16,24},{24,16},{1,9},{17,25},{25,17},{2,10},{18,26},{26,18}... | collective-permute-start | bytes 1966088 | tf_op jit(solution)/shard_map/ppermute | solution.py:188
  56.6 20.4 %collective-permute-start.10 = (bf16[2,10,128,128]{3,2,1,0:T(8,128)(2,1)S(1)}, bf16[2,10,128,128]{3,2,1,0:T(8,128)(2,1)S(1)}, u32[]{:S(2)}, u32[]{:S(2)}) collective-permute-start(bf16[2,10,128,128]{3,2,1,0:T(8,128)(2,1)S(1)} %get-tuple-element.19.refs_1_), channel_id=1, source_target_pairs={{8,16},{9,17},{10,18},{11,19},{12,20},{13,21},{14,22},{15,23}} | collective-permute-start | bytes 1966088 | tf_op jit(solution)/shard_map/ppermute | solution.py:200
  69.7 20.9 %collective-permute-start.8 = (bf16[2,10,256,128]{3,2,1,0:T(8,128)(2,1)S(1)}, bf16[2,10,256,128]{3,2,1,0:T(8,128)(2,1)S(1)}, u32[]{:S(2)}, u32[]{:S(2)}) collective-permute-start(bf16[2,10,256,128]{3,2,1,0:T(8,128)(2,1)S(1)} %get-tuple-element.25.refs_14_.refs_9_), channel_id=1, source_target_pairs={{0,8},{16,24},{24,16},{1,9},{17,25},{25,17},{2,10},{18,26},{26,18}... | collective-permute-start | bytes 3932168 | tf_op jit(solution)/shard_map/ppermute | solution.py:188
  72.9 11.9 %collective-permute-start.14 = (bf16[2,10,128,128]{3,2,1,0:T(8,128)(2,1)S(1)}, bf16[2,10,128,128]{3,2,1,0:T(8,128)(2,1)S(1)}, u32[]{:S(2)}, u32[]{:S(2)}) collective-permute-start(bf16[2,10,128,128]{3,2,1,0:T(8,128)(2,1)S(1)} %get-tuple-element.32.refs_3_.refs_2_), channel_id=1, source_target_pairs={{8,16},{9,17},{10,18},{11,19},{12,20},{13,21},{14,22},{15,23}} | collective-permute-start | bytes 1966088 | tf_op jit(solution)/shard_map/ppermute | solution.py:200
  74.2 16.5 %collective-permute-start.13 = (bf16[2,10,256,128]{3,2,1,0:T(8,128)(2,1)S(1)}, bf16[2,10,256,128]{3,2,1,0:T(8,128)(2,1)S(1)}, u32[]{:S(2)}, u32[]{:S(2)}) collective-permute-start(bf16[2,10,256,128]{3,2,1,0:T(8,128)(2,1)S(1)} %collective-permute-done.12.refs_10_.refs_6_), channel_id=1, source_target_pairs={{16,24},{17,25},{18,26},{19,27},{20,28},{21,29},{22,30},{23,31}} | collective-permute-start | bytes 3932168 | tf_op jit(solution)/shard_map/ppermute | solution.py:201
  77.0 9.4 %collective-permute-start.11 = (bf16[2,10,128,128]{3,2,1,0:T(8,128)(2,1)S(1)}, bf16[2,10,128,128]{3,2,1,0:T(8,128)(2,1)S(1)}, u32[]{:S(2)}, u32[]{:S(2)}) collective-permute-start(bf16[2,10,128,128]{3,2,1,0:T(8,128)(2,1)S(1)} %collective-permute-done.10.refs_8_.refs_4_), channel_id=1, source_target_pairs={{16,24},{17,25},{18,26},{19,27},{20,28},{21,29},{22,30},{23,31}} | collective-permute-start | bytes 1966088 | tf_op jit(solution)/shard_map/ppermute | solution.py:201
  78.3 12.4 %collective-permute-start.9 = (bf16[2,10,128,128]{3,2,1,0:T(8,128)(2,1)S(1)}, bf16[2,10,128,128]{3,2,1,0:T(8,128)(2,1)S(1)}, u32[]{:S(2)}, u32[]{:S(2)}) collective-permute-start(bf16[2,10,128,128]{3,2,1,0:T(8,128)(2,1)S(1)} %get-tuple-element.31.refs_15_.refs_10_), channel_id=1, source_target_pairs={{0,8},{16,24},{24,16},{1,9},{17,25},{25,17},{2,10},{18,26},{26,18}... | collective-permute-start | bytes 1966088 | tf_op jit(solution)/shard_map/ppermute | solution.py:188
  84.8 5.8 %collective-permute-start.15 = (bf16[2,10,128,128]{3,2,1,0:T(8,128)(2,1)S(1)}, bf16[2,10,128,128]{3,2,1,0:T(8,128)(2,1)S(1)}, u32[]{:S(2)}, u32[]{:S(2)}) collective-permute-start(bf16[2,10,128,128]{3,2,1,0:T(8,128)(2,1)S(1)} %collective-permute-done.14.refs_12_.refs_8_), channel_id=1, source_target_pairs={{16,24},{17,25},{18,26},{19,27},{20,28},{21,29},{22,30},{23,31}} | collective-permute-start | bytes 1966088 | tf_op jit(solution)/shard_map/ppermute | solution.py:201
  86.4 13.8 %slice-start.2 = ((s8[13107200]{0:T(1024)(128)(4,1)}), s8[4194304]{0:T(1024)(128)(4,1)S(1)}, s32[]{:S(2)}) async-start(s8[13107200]{0:T(1024)(128)(4,1)} %bitcast.76), calls=%async_computation.2 | async-start | bytes 8388608
  90.7 9.5 %slice-start.3 = ((s8[13107200]{0:T(1024)(128)(4,1)}), s8[524288]{0:T(1024)(128)(4,1)S(1)}, s32[]{:S(2)}) async-start(s8[13107200]{0:T(1024)(128)(4,1)} %bitcast.76), calls=%async_computation.3 | async-start | bytes 1048576
  104.5 20.5 %collective-permute-start.17 = (bf16[256,1024]{1,0:T(8,128)(2,1)S(1)}, bf16[256,1024]{1,0:T(8,128)(2,1)S(1)}, u32[]{:S(2)}, u32[]{:S(2)}) collective-permute-start(bf16[256,1024]{1,0:T(8,128)(2,1)S(1)} %fusion.11), channel_id=1, source_target_pairs={{4,0},{0,4},{5,1},{1,5},{6,2},{2,6},{7,3},{3,7},{12,8},{8,12},{13,... | collective-permute-start | bytes 1572872 | tf_op jit(solution)/shard_map/ppermute | solution.py:220
  105.1 25.5 %collective-permute-start.18 = (bf16[256,1024]{1,0:T(8,128)(2,1)S(1)}, bf16[256,1024]{1,0:T(8,128)(2,1)S(1)}, u32[]{:S(2)}, u32[]{:S(2)}) collective-permute-start(bf16[256,1024]{1,0:T(8,128)(2,1)S(1)} %fusion.14), channel_id=1, source_target_pairs={{4,0},{0,4},{5,1},{1,5},{6,2},{2,6},{7,3},{3,7},{12,8},{8,12},{13,... | collective-permute-start | bytes 1572872 | tf_op jit(solution)/shard_map/ppermute | solution.py:220
  106.6 35.2 %collective-permute-start.19 = (bf16[256,1024]{1,0:T(8,128)(2,1)S(1)}, bf16[256,1024]{1,0:T(8,128)(2,1)S(1)}, u32[]{:S(2)}, u32[]{:S(2)}) collective-permute-start(bf16[256,1024]{1,0:T(8,128)(2,1)S(1)} %fusion.17), channel_id=1, source_target_pairs={{4,0},{0,4},{5,1},{1,5},{6,2},{2,6},{7,3},{3,7},{12,8},{8,12},{13,... | collective-permute-start | bytes 1572872 | tf_op jit(solution)/shard_map/ppermute | solution.py:220
  107.1 45.9 %collective-permute-start.20 = (bf16[256,1024]{1,0:T(8,128)(2,1)S(1)}, bf16[256,1024]{1,0:T(8,128)(2,1)S(1)}, u32[]{:S(2)}, u32[]{:S(2)}) collective-permute-start(bf16[256,1024]{1,0:T(8,128)(2,1)S(1)} %fusion.20), channel_id=1, source_target_pairs={{4,0},{0,4},{5,1},{1,5},{6,2},{2,6},{7,3},{3,7},{12,8},{8,12},{13,... | collective-permute-start | bytes 1572872 | tf_op jit(solution)/shard_map/ppermute | solution.py:220
  108.6 52.2 %collective-permute-start.21 = (bf16[256,1024]{1,0:T(8,128)(2,1)S(1)}, bf16[256,1024]{1,0:T(8,128)(2,1)S(1)}, u32[]{:S(2)}, u32[]{:S(2)}) collective-permute-start(bf16[256,1024]{1,0:T(8,128)(2,1)S(1)} %fusion.23), channel_id=1, source_target_pairs={{4,0},{0,4},{5,1},{1,5},{6,2},{2,6},{7,3},{3,7},{12,8},{8,12},{13,... | collective-permute-start | bytes 1572872 | tf_op jit(solution)/shard_map/ppermute | solution.py:220
  121.1 3.9 %copy-start.2 = (bf16[1,1,256,5120]{3,2,1,0:T(8,128)(2,1)S(1)}, bf16[1,1,256,5120]{3,2,1,0:T(8,128)(2,1)}, u32[]{:S(2)}) copy-start(bf16[1,1,256,5120]{3,2,1,0:T(8,128)(2,1)} %param.16) | copy-start | bytes 7864324

commit v9 on v7

--- a/solution.py
+++ b/solution.py
@@ -10,7 +10,8 @@
 
 NEG_BIG = -1e30
 LOG2E = 1.4426950408889634
-COL_BLOCKS = 5
+COL_BLOCKS = 2
+ROW_BLOCKS = 2
 HEAD_STEP_SCORES = 1 << 20
 VMEM_MARGIN = 3 << 20
 
@@ -77,8 +78,9 @@
             outs[0][h], outs[1][h], outs[2][h] = top, total, acc
 
 
-def attend(queries, slots, span_mask, state, last):
+def attend(queries, slots, span_mask, state, last, share=(0, 1)):
     heads, rows, dim = queries.shape
+    rows, at_row = rows // share[1], share[0]
     arrays, layout = [], []
     for origin, members in slots:
         places = []
@@ -92,7 +94,7 @@
     read = sum(array.shape[2] for array in arrays)
     blocks = step * dim * (2 * 2 * read + 2 * 2 * rows + 3 * 4 * rows)
     grant = 4 * step * rows * keys + 2 * blocks + VMEM_MARGIN
-    by_head = pl.BlockSpec((step, rows, dim), lambda h, f: (h, 0, 0))
+    by_head = pl.BlockSpec((step, rows, dim), lambda h, f: (h, at_row, 0))
     states = [] if state is None else list(state)
     return pl.pallas_call(
         functools.partial(
@@ -212,23 +214,26 @@
     columns = out_weight.shape[1]
     width = columns // COL_BLOCKS
     project = lambda a, w: jnp.dot(a, w, preferred_element_type=jnp.float32).astype(jnp.bfloat16)
-    returned = [[] for _ in range(COL_BLOCKS)]
-    for d in range(1, splits):
-        attended = attend(q_parts[d], late, span_mask, states[d], True)
+    height = q.shape[1] // ROW_BLOCKS
+    tiles = [(r, j) for r in range(ROW_BLOCKS) for j in range(COL_BLOCKS)]
+    returned = {tile: [] for tile in tiles}
+    for d in range(1, splits):
         back = [((i + d) % splits, i) for i in range(splits)]
-        for j in range(COL_BLOCKS):
+        for r, j in tiles:
+            if j == 0:
+                attended = attend(q_parts[d], late, span_mask, states[d], True, (r, ROW_BLOCKS))
             partial = project(attended, out_weight[:, j * width : (j + 1) * width])
-            returned[j].append(lax.ppermute(partial, "head", back))
+            returned[r, j].append(lax.ppermute(partial, "head", back))
     attended = attend(q_parts[0], slots, span_mask, None, True)
     kept = lax.optimization_barrier(project(attended, out_weight))
     updated = hidden
-    for j in range(COL_BLOCKS):
-        cols = slice(j * width, (j + 1) * width)
-        total = kept[:, cols].astype(jnp.float32)
-        for a in returned[j]:
+    for r, j in tiles:
+        block = slice(r * height, (r + 1) * height), slice(j * width, (j + 1) * width)
+        total = kept[block].astype(jnp.float32)
+        for a in returned[r, j]:
             total = total + a.astype(jnp.float32)
-        fresh = updated[:, cols].astype(jnp.float32) + gate_row[None, cols] * total
-        updated = lax.dynamic_update_slice_in_dim(updated, fresh.astype(jnp.bfloat16), j * width, 1)
+        fresh = updated[block].astype(jnp.float32) + gate_row[None, block[1]] * total
+        updated = lax.dynamic_update_slice(updated, fresh.astype(jnp.bfloat16), (r * height, j * width))
     return updated
 
 

time: 161 us -> 166 us (1.031)
  the two profiles are of different devices: /device:TPU:28 before, /device:TPU:0 now
where the time goes in v9:
time: 166 us; the launch traced here: 163 us
  waiting for transfers between devices  68.3 us (41%)
  starting transfers between devices  42.8 us (26%)
  Pallas kernels  27.9 us (17%)
  matrix products  8.31 us (5%)
  other arithmetic  6.69 us (4%)
  local copies, waits for them, and re-layouts  6.17 us (4%)
  between operations  3 us (2%)
    ppermute x4, waiting for transfers between devices, sublayer(): returned[r, j].append(lax.ppermute(partial, 'head', back))  36.2 us
    ppermute x3, waiting for transfers between devices, sublayer(): lax.ppermute(pieces[i - low], 'branch', [(b, b ^ low) for b in range(bran...  29.5 us
    pallas_call x4, Pallas kernels, attend(): pl.pallas_call(functools.partial(flash_kernel, layout=layout, count=len(a...  27.9 us
    ppermute x3, starting transfers between devices, sublayer(): lax.ppermute(a, 'tm', pairs + [(final, final - 1)])  16.9 us
    dot_general x5, matrix products, sublayer(): jnp.dot(a, w, preferred_element_type=jnp.float32).astype(jnp.bfloat16)  8.31 us
    ppermute x2, starting transfers between devices, sublayer(): lent = [lax.ppermute(a, 'tm', [(0, final)]) for a in ctx_parts]  6.29 us
    ppermute x3, starting transfers between devices, sublayer(): lax.ppermute(pieces[i - low], 'branch', [(b, b ^ low) for b in range(bran...  5.73 us
    ppermute x4, starting transfers between devices, sublayer(): returned[r, j].append(lax.ppermute(partial, 'head', back))  4.12 us
  transfers between devices with their start and end apart: 21, of which 7 were waited for; matrix products, arithmetic and copies ran while one was open for 7% of the time, Pallas kernels for 12%

profile of v9, /device:TPU:0, one launch (start us, length us, event | category | flops | bytes accessed | tf_op | source)
XLA Modules:
  0.0 163.1 jit_solution(4104816305824313304)
XLA Ops:
  0.0 1.0 copy-done.6
  1.0 0.1 copy-done.5
  1.2 0.8 pad_maximum_fusion.4
  1.9 3.0 %collective-permute-start.1 = (bf16[2,10,64,128]{3,2,1,0:T(8,128)(2,1)}, bf16[2,10,64,128]{3,2,1,0:T(8,128)(2,1)}, u32[]{:S(2)}, u32[]{:S(2)}) collective-permute-start(bf16[2,10,64,128]{3,2,1,0:T(8,128)(2,1)} %pad_maximum_fusion.4), channel_id=1, source_target_pairs={{0,4},{4,0},{1,5},{5,1},{2,6},{6,2},{3,7},{7,3},{8,12},{12,8},{9,1... | collective-permute-start | bytes 983048 | tf_op jit(solution)/shard_map/ppermute | solution.py:155
  4.9 0.6 dynamic_slice.40
  7.4 3.3 %collective-permute-start = (bf16[2,10,64,128]{3,2,1,0:T(8,128)(2,1)S(1)}, bf16[2,10,64,128]{3,2,1,0:T(8,128)(2,1)}, u32[]{:S(2)}, u32[]{:S(2)}) collective-permute-start(bf16[2,10,64,128]{3,2,1,0:T(8,128)(2,1)S(1)} %pad_maximum_fusion.3), channel_id=1, source_target_pairs={{0,24},{1,25},{2,26},{3,27},{4,28},{5,29},{6,30},{7,31}} | collective-permute-start | bytes 983048 | tf_op jit(solution)/shard_map/ppermute | solution.py:167
  10.8 1.5 dynamic-slice_bitcast_fusion.1
  12.2 0.7 collective-permute-done.1
  12.9 3.0 %collective-permute-start.2 = (bf16[2,10,64,128]{3,2,1,0:T(8,128)(2,1)}, bf16[2,10,64,128]{3,2,1,0:T(8,128)(2,1)}, u32[]{:S(2)}, u32[]{:S(2)}) collective-permute-start(bf16[2,10,64,128]{3,2,1,0:T(8,128)(2,1)} %collective-permute-done.1), channel_id=1, source_target_pairs={{0,24},{1,25},{2,26},{3,27},{4,28},{5,29},{6,30},{7,31}} | collective-permute-start | bytes 983048 | tf_op jit(solution)/shard_map/ppermute | solution.py:167
  15.9 0.1 pad_maximum_fusion.1
  16.0 1.6 collective-permute-start.5
  18.2 0.0 collective-permute-done
  18.3 1.8 %collective-permute-done.2 = bf16[2,10,64,128]{3,2,1,0:T(8,128)(2,1)} collective-permute-done((bf16[2,10,64,128]{3,2,1,0:T(8,128)(2,1)}, bf16[2,10,64,128]{3,2,1,0:T(8,128)(2,1)}, u32[]{:S(2)}, u32[]{:S(2)}) %collective-permute-start.2) | collective-permute-done | bytes 327712 | tf_op jit(solution)/shard_map/ppermute | solution.py:167
  20.1 1.0 broadcast_select_fusion.6
  21.1 0.0 slice-start
  21.1 0.4 broadcast_select_fusion.3
  21.5 2.7 %collective-permute-start.4 = (bf16[2,10,128,128]{3,2,1,0:T(8,128)(2,1)S(1)}, bf16[2,10,128,128]{3,2,1,0:T(8,128)(2,1)S(1)}, u32[]{:S(2)}, u32[]{:S(2)}) collective-permute-start(bf16[2,10,128,128]{3,2,1,0:T(8,128)(2,1)S(1)} %get-tuple-element.41), channel_id=1, source_target_pairs={{0,2},{1,3},{2,0},{3,1},{4,6},{5,7},{6,4},{7,5},{8,10},{9,11},{10,... | collective-permute-start | bytes 1966088 | tf_op jit(solution)/shard_map/ppermute | solution.py:172
  24.2 1.6 collective-permute-start.3
  25.8 23.1 %collective-permute-done.4 = bf16[2,10,128,128]{3,2,1,0:T(8,128)(2,1)S(1)} collective-permute-done((bf16[2,10,128,128]{3,2,1,0:T(8,128)(2,1)S(1)}, bf16[2,10,128,128]{3,2,1,0:T(8,128)(2,1)S(1)}, u32[]{:S(2)}, u32[]{:S(2)}) %collective-permute-start.4) | collective-permute-done | bytes 655392 | tf_op jit(solution)/shard_map/ppermute | solution.py:172
  48.9 0.2 collective-permute-done.3
  49.1 0.1 constant_dynamic-update-slice_fusion.1
  49.1 0.1 constant_dynamic-update-slice_fusion
  49.2 0.0 collective-permute-done.5
  49.3 1.1 slice.71
  50.4 0.0 copy-start.3
  50.4 0.0 slice-start.1
  50.4 0.8 broadcast_select_fusion
  51.2 0.9 collective-permute-start.12
  52.1 1.5 collective-permute-start.6
  53.6 0.1 dynamic-slice_bitcast_fusion.5
  53.7 0.6 collective-permute-start.16
  54.3 5.5 %collective-permute-start.7 = (bf16[2,10,128,128]{3,2,1,0:T(8,128)(2,1)S(1)}, bf16[2,10,128,128]{3,2,1,0:T(8,128)(2,1)S(1)}, u32[]{:S(2)}, u32[]{:S(2)}) collective-permute-start(bf16[2,10,128,128]{3,2,1,0:T(8,128)(2,1)S(1)} %get-tuple-element.24.refs_13_.refs_7_), channel_id=1, source_target_pairs={{0,8},{16,24},{24,16},{1,9},{17,25},{25,17},{2,10},{18,26},{26,18}... | collective-permute-start | bytes 1966088 | tf_op jit(solution)/shard_map/ppermute | solution.py:190
  59.8 0.7 collective-permute-start.10
  60.5 6.2 %collective-permute-done.6 = bf16[2,10,128,128]{3,2,1,0:T(8,128)(2,1)S(1)} collective-permute-done((bf16[2,10,128,128]{3,2,1,0:T(8,128)(2,1)S(1)}, bf16[2,10,128,128]{3,2,1,0:T(8,128)(2,1)S(1)}, u32[]{:S(2)}, u32[]{:S(2)}) %collective-permute-start.6) | collective-permute-done | bytes 655392 | tf_op jit(solution)/shard_map/ppermute | solution.py:172
  66.8 5.1 %collective-permute-start.8 = (bf16[2,10,256,128]{3,2,1,0:T(8,128)(2,1)S(1)}, bf16[2,10,256,128]{3,2,1,0:T(8,128)(2,1)S(1)}, u32[]{:S(2)}, u32[]{:S(2)}) collective-permute-start(bf16[2,10,256,128]{3,2,1,0:T(8,128)(2,1)S(1)} %get-tuple-element.25.refs_14_.refs_8_), channel_id=1, source_target_pairs={{0,8},{16,24},{24,16},{1,9},{17,25},{25,17},{2,10},{18,26},{26,18}... | collective-permute-start | bytes 3932168 | tf_op jit(solution)/shard_map/ppermute | solution.py:190
  71.9 1.3 broadcast_select_fusion.2
  73.1 0.7 collective-permute-start.14
  73.8 0.0 collective-permute-done.12.refs_10_.refs_4_
  73.9 0.7 collective-permute-start.13
  74.6 0.7 collective-permute-start.11
  75.3 6.3 %collective-permute-start.9 = (bf16[2,10,128,128]{3,2,1,0:T(8,128)(2,1)S(1)}, bf16[2,10,128,128]{3,2,1,0:T(8,128)(2,1)S(1)}, u32[]{:S(2)}, u32[]{:S(2)}) collective-permute-start(bf16[2,10,128,128]{3,2,1,0:T(8,128)(2,1)S(1)} %get-tuple-element.31.refs_15_.refs_7_), channel_id=1, source_target_pairs={{0,8},{16,24},{24,16},{1,9},{17,25},{25,17},{2,10},{18,26},{26,18}... | collective-permute-start | bytes 1966088 | tf_op jit(solution)/shard_map/ppermute | solution.py:190
  81.7 0.9 collective-permute-start.15
  82.6 7.7 %shard_map.110 = (f32[10,256,128]{2,1,0:T(8,128)S(1)}, f32[10,256,128]{2,1,0:T(8,128)S(1)}, f32[10,256,128]{2,1,0:T(8,128)S(1)}) custom-call(s32[4,4]{1,0:T(4,128)S(1)} %copy-done.1, bf16[10,256,128]{2,1,0:T(8,128)(2,1)S(1)} %collective-permute-done.16.refs_0_, bf16[2,10,128,128]{3,2,1,0:T(8,128)(2,1)S(1)} %get-tuple-element.19.refs_1_, ...), custom_call_target="tpu_custom_call" | custom-call | flops 1677721600 | bytes 7864320 | tf_op jit(solution)/shard_map/pallas_call | solution.py:99
  90.3 0.0 slice-start.3
  90.3 4.0 %shard_map.111 = bf16[128,1280]{1,0:T(8,128)(2,1)S(1)} custom-call(s32[4,4]{1,0:T(4,128)S(1)} %copy-done.1, bf16[10,256,128]{2,1,0:T(8,128)(2,1)S(1)} %collective-permute-done.16.refs_0_, bf16[2,10,128,128]{3,2,1,0:T(8,128)(2,1)S(1)} %get-tuple-element.32.refs_3_.refs_1_, bf16[2,10,128,128]{3,2,1,0:T(8,128)(2,1)S(1)} %collective-permute-done.9.refs_6_.refs_2_, ...), custom_call_target="tpu_custom_call" | custom-call | flops 503316480 | bytes 4587520 | tf_op jit(solution)/shard_map/pallas_call | solution.py:99
  94.4 1.1 fusion.14
  95.5 1.1 fusion.8
  96.7 4.0 %shard_map.112 = bf16[128,1280]{1,0:T(8,128)(2,1)S(1)} custom-call(s32[4,4]{1,0:T(4,128)S(1)} %copy-done.1, bf16[10,256,128]{2,1,0:T(8,128)(2,1)S(1)} %collective-permute-done.16.refs_0_, bf16[2,10,128,128]{3,2,1,0:T(8,128)(2,1)S(1)} %get-tuple-element.32.refs_3_.refs_1_, bf16[2,10,128,128]{3,2,1,0:T(8,128)(2,1)S(1)} %collective-permute-done.9.refs_6_.refs_2_, ...), custom_call_target="tpu_custom_call" | custom-call | flops 503316480 | bytes 4587520 | tf_op jit(solution)/shard_map/pallas_call | solution.py:99
  100.7 1.1 fusion.17
  101.8 1.1 fusion.11
  102.9 0.6 collective-permute-start.19
  103.5 1.5 collective-permute-start.20
  105.0 0.5 collective-permute-start.17
  105.5 1.5 collective-permute-start.18
  107.0 12.1 %shard_map.109 = bf16[256,1280]{1,0:T(8,128)(2,1)S(1)} custom-call(s32[4,4]{1,0:T(4,128)S(1)} %copy-done.1, bf16[10,256,128]{2,1,0:T(8,128)(2,1)S(1)} %get-tuple-element.35.refs_0_, bf16[2,10,128,128]{3,2,1,0:T(8,128)(2,1)S(1)} %get-tuple-element.19.refs_1_, bf16[2,10,256,128]{3,2,1,0:T(8,128)(2,1)S(1)} %get-tuple-element.22.refs_2_, ...), custom_call_target="tpu_custom_call" | custom-call | flops 2684354560 | bytes 11796480 | tf_op jit(solution)/shard_map/pallas_call | solution.py:99
  119.2 0.0 copy-start.2
  119.2 3.9 %convolution_convert_fusion = bf16[256,5120]{1,0:T(8,128)(2,1)S(1)} fusion(bf16[256,1280]{1,0:T(8,128)(2,1)S(1)} %shard_map.109, bf16[1280,5120]{1,0:T(8,128)(2,1)S(1)} %bitcast.76), kind=kOutput, calls=%fused_computation | convolution fusion | flops 3356753920 | bytes 16384000 | tf_op jit(solution)/shard_map/dot_general | solution.py:216
  123.1 22.6 %collective-permute-done.17 = bf16[128,2560]{1,0:T(8,128)(2,1)S(1)} collective-permute-done((bf16[128,2560]{1,0:T(8,128)(2,1)S(1)}, bf16[128,2560]{1,0:T(8,128)(2,1)S(1)}, u32[]{:S(2)}, u32[]{:S(2)}) %collective-permute-start.17) | collective-permute-done | bytes 655392 | tf_op jit(solution)/shard_map/ppermute | solution.py:226
  145.7 0.4 fusion.21
  146.1 13.7 %collective-permute-done.18 = bf16[128,2560]{1,0:T(8,128)(2,1)S(1)} collective-permute-done((bf16[128,2560]{1,0:T(8,128)(2,1)S(1)}, bf16[128,2560]{1,0:T(8,128)(2,1)S(1)}, u32[]{:S(2)}, u32[]{:S(2)}) %collective-permute-start.18) | collective-permute-done | bytes 655392 | tf_op jit(solution)/shard_map/ppermute | solution.py:226
  159.7 0.4 fusion.22
  160.1 0.4 fusion.23
  160.5 1.5 copy.16
  162.0 1.1 fusion.25
  (34 shorter events, 0.2 us)
Async XLA Ops:
  0.0 7.3 %copy-start = (f32[16,5120]{1,0:T(8,128)S(1)}, f32[16,5120]{1,0:T(8,128)}, u32[]{:S(2)}) copy-start(f32[16,5120]{1,0:T(8,128)} %param.18) | copy-start | bytes 983044
  0.0 1.0 copy-start.6
  0.0 1.1 copy-start.5
  0.0 4.9 %copy-start.7 = (s32[4]{0:T(128)S(1)}, s32[4]{0:T(128)}, u32[]{:S(2)}) copy-start(s32[4]{0:T(128)} %param.19) | copy-start | bytes 52
  1.1 9.6 %copy-start.4 = (bf16[1,1,256,20,128]{4,2,3,1,0:T(8,128)(2,1)S(1)}, bf16[1,1,256,20,128]{4,2,3,1,0:T(8,128)(2,1)}, u32[]{:S(2)}) copy-start(bf16[1,1,256,20,128]{4,2,3,1,0:T(8,128)(2,1)} %param.13) | copy-start | bytes 3932164
  1.9 11.0 %collective-permute-start.1 = (bf16[2,10,64,128]{3,2,1,0:T(8,128)(2,1)}, bf16[2,10,64,128]{3,2,1,0:T(8,128)(2,1)}, u32[]{:S(2)}, u32[]{:S(2)}) collective-permute-start(bf16[2,10,64,128]{3,2,1,0:T(8,128)(2,1)} %pad_maximum_fusion.4), channel_id=1, source_target_pairs={{0,4},{4,0},{1,5},{5,1},{2,6},{6,2},{3,7},{7,3},{8,12},{12,8},{9,1... | collective-permute-start | bytes 983048 | tf_op jit(solution)/shard_map/ppermute | solution.py:155
  7.4 10.8 %collective-permute-start = (bf16[2,10,64,128]{3,2,1,0:T(8,128)(2,1)S(1)}, bf16[2,10,64,128]{3,2,1,0:T(8,128)(2,1)}, u32[]{:S(2)}, u32[]{:S(2)}) collective-permute-start(bf16[2,10,64,128]{3,2,1,0:T(8,128)(2,1)S(1)} %pad_maximum_fusion.3), channel_id=1, source_target_pairs={{0,24},{1,25},{2,26},{3,27},{4,28},{5,29},{6,30},{7,31}} | collective-permute-start | bytes 983048 | tf_op jit(solution)/shard_map/ppermute | solution.py:167
  12.9 7.1 %collective-permute-start.2 = (bf16[2,10,64,128]{3,2,1,0:T(8,128)(2,1)}, bf16[2,10,64,128]{3,2,1,0:T(8,128)(2,1)}, u32[]{:S(2)}, u32[]{:S(2)}) collective-permute-start(bf16[2,10,64,128]{3,2,1,0:T(8,128)(2,1)} %collective-permute-done.1), channel_id=1, source_target_pairs={{0,24},{1,25},{2,26},{3,27},{4,28},{5,29},{6,30},{7,31}} | collective-permute-start | bytes 983048 | tf_op jit(solution)/shard_map/ppermute | solution.py:167
  16.0 33.2 %collective-permute-start.5 = (bf16[2,10,256,128]{3,2,1,0:T(8,128)(2,1)S(1)}, bf16[2,10,256,128]{3,2,1,0:T(8,128)(2,1)}, u32[]{:S(2)}, u32[]{:S(2)}) collective-permute-start(bf16[2,10,256,128]{3,2,1,0:T(8,128)(2,1)S(1)} %pad_maximum_fusion.1), channel_id=1, source_target_pairs={{0,4},{4,0},{1,5},{5,1},{2,6},{6,2},{3,7},{7,3},{8,12},{12,8},{9,1... | collective-permute-start | bytes 3932168 | tf_op jit(solution)/shard_map/ppermute | solution.py:157
  21.1 73.3 %slice-start = ((s8[13107200]{0:T(1024)(128)(4,1)}), s8[4194304]{0:T(1024)(128)(4,1)S(1)}, s32[]{:S(2)}) async-start(s8[13107200]{0:T(1024)(128)(4,1)} %bitcast.75), calls=%async_computation | async-start | bytes 8388608
  21.5 27.3 %collective-permute-start.4 = (bf16[2,10,128,128]{3,2,1,0:T(8,128)(2,1)S(1)}, bf16[2,10,128,128]{3,2,1,0:T(8,128)(2,1)S(1)}, u32[]{:S(2)}, u32[]{:S(2)}) collective-permute-start(bf16[2,10,128,128]{3,2,1,0:T(8,128)(2,1)S(1)} %get-tuple-element.41), channel_id=1, source_target_pairs={{0,2},{1,3},{2,0},{3,1},{4,6},{5,7},{6,4},{7,5},{8,10},{9,11},{10,... | collective-permute-start | bytes 1966088 | tf_op jit(solution)/shard_map/ppermute | solution.py:172
  24.2 24.9 %collective-permute-start.3 = (bf16[2,10,128,128]{3,2,1,0:T(8,128)(2,1)S(1)}, bf16[2,10,128,128]{3,2,1,0:T(8,128)(2,1)S(1)}, u32[]{:S(2)}, u32[]{:S(2)}) collective-permute-start(bf16[2,10,128,128]{3,2,1,0:T(8,128)(2,1)S(1)} %get-tuple-element.41), channel_id=1, source_target_pairs={{0,1},{1,0},{2,3},{3,2},{4,5},{5,4},{6,7},{7,6},{8,9},{9,8},{10,11... | collective-permute-start | bytes 1966088 | tf_op jit(solution)/shard_map/ppermute | solution.py:172
  50.4 3.2 %copy-start.3 = (bf16[1,1,256,20,128]{4,2,3,1,0:T(8,128)(2,1)S(1)}, bf16[1,1,256,20,128]{4,2,3,1,0:T(8,128)(2,1)}, u32[]{:S(2)}) copy-start(bf16[1,1,256,20,128]{4,2,3,1,0:T(8,128)(2,1)} %param.11) | copy-start | bytes 3932164
  50.4 44.0 %slice-start.1 = ((s8[13107200]{0:T(1024)(128)(4,1)}), s8[4194304]{0:T(1024)(128)(4,1)S(1)}, s32[]{:S(2)}) async-start(s8[13107200]{0:T(1024)(128)(4,1)} %bitcast.75), calls=%async_computation.1 | async-start | bytes 8388608
  51.2 22.6 %collective-permute-start.12 = (bf16[2,10,256,128]{3,2,1,0:T(8,128)(2,1)S(1)}, bf16[2,10,256,128]{3,2,1,0:T(8,128)(2,1)S(1)}, u32[]{:S(2)}, u32[]{:S(2)}) collective-permute-start(bf16[2,10,256,128]{3,2,1,0:T(8,128)(2,1)S(1)} %get-tuple-element.22.refs_2_), channel_id=1, source_target_pairs={{8,16},{9,17},{10,18},{11,19},{12,20},{13,21},{14,22},{15,23}} | collective-permute-start | bytes 3932168 | tf_op jit(solution)/shard_map/ppermute | solution.py:202
  52.1 14.7 %collective-permute-start.6 = (bf16[2,10,128,128]{3,2,1,0:T(8,128)(2,1)S(1)}, bf16[2,10,128,128]{3,2,1,0:T(8,128)(2,1)S(1)}, u32[]{:S(2)}, u32[]{:S(2)}) collective-permute-start(bf16[2,10,128,128]{3,2,1,0:T(8,128)(2,1)S(1)} %collective-permute-done.4), channel_id=1, source_target_pairs={{0,1},{1,0},{2,3},{3,2},{4,5},{5,4},{6,7},{7,6},{8,9},{9,8},{10,11... | collective-permute-start | bytes 1966088 | tf_op jit(solution)/shard_map/ppermute | solution.py:172
  53.7 19.4 %collective-permute-start.16 = (bf16[10,256,128]{2,1,0:T(8,128)(2,1)S(1)}, bf16[10,256,128]{2,1,0:T(8,128)(2,1)S(1)}, u32[]{:S(2)}, u32[]{:S(2)}) collective-permute-start(bf16[10,256,128]{2,1,0:T(8,128)(2,1)S(1)} %get-tuple-element.36), channel_id=1, source_target_pairs={{0,4},{4,0},{1,5},{5,1},{2,6},{6,2},{3,7},{7,3},{8,12},{12,8},{9,1... | collective-permute-start | bytes 1966088 | tf_op jit(solution)/shard_map/ppermute | solution.py:159
  54.3 21.0 %collective-permute-start.7 = (bf16[2,10,128,128]{3,2,1,0:T(8,128)(2,1)S(1)}, bf16[2,10,128,128]{3,2,1,0:T(8,128)(2,1)S(1)}, u32[]{:S(2)}, u32[]{:S(2)}) collective-permute-start(bf16[2,10,128,128]{3,2,1,0:T(8,128)(2,1)S(1)} %get-tuple-element.24.refs_13_.refs_7_), channel_id=1, source_target_pairs={{0,8},{16,24},{24,16},{1,9},{17,25},{25,17},{2,10},{18,26},{26,18}... | collective-permute-start | bytes 1966088 | tf_op jit(solution)/shard_map/ppermute | solution.py:190
  59.8 14.8 %collective-permute-start.10 = (bf16[2,10,128,128]{3,2,1,0:T(8,128)(2,1)S(1)}, bf16[2,10,128,128]{3,2,1,0:T(8,128)(2,1)S(1)}, u32[]{:S(2)}, u32[]{:S(2)}) collective-permute-start(bf16[2,10,128,128]{3,2,1,0:T(8,128)(2,1)S(1)} %get-tuple-element.19.refs_1_), channel_id=1, source_target_pairs={{8,16},{9,17},{10,18},{11,19},{12,20},{13,21},{14,22},{15,23}} | collective-permute-start | bytes 1966088 | tf_op jit(solution)/shard_map/ppermute | solution.py:202
  66.8 15.8 %copy-start.1 = (s32[4,4]{1,0:T(4,128)S(1)}, s32[4,4]{1,0:T(4,128)}, u32[]{:S(2)}) copy-start(s32[4,4]{1,0:T(4,128)} %mask.7) | copy-start | bytes 196
  66.8 27.6 %slice-start.2 = ((s8[13107200]{0:T(1024)(128)(4,1)}), s8[4194304]{0:T(1024)(128)(4,1)S(1)}, s32[]{:S(2)}) async-start(s8[13107200]{0:T(1024)(128)(4,1)} %bitcast.75), calls=%async_computation.2 | async-start | bytes 8388608
  66.8 15.8 %collective-permute-start.8 = (bf16[2,10,256,128]{3,2,1,0:T(8,128)(2,1)S(1)}, bf16[2,10,256,128]{3,2,1,0:T(8,128)(2,1)S(1)}, u32[]{:S(2)}, u32[]{:S(2)}) collective-permute-start(bf16[2,10,256,128]{3,2,1,0:T(8,128)(2,1)S(1)} %get-tuple-element.25.refs_14_.refs_8_), channel_id=1, source_target_pairs={{0,8},{16,24},{24,16},{1,9},{17,25},{25,17},{2,10},{18,26},{26,18}... | collective-permute-start | bytes 3932168 | tf_op jit(solution)/shard_map/ppermute | solution.py:190
  73.1 8.6 %collective-permute-start.14 = (bf16[2,10,128,128]{3,2,1,0:T(8,128)(2,1)S(1)}, bf16[2,10,128,128]{3,2,1,0:T(8,128)(2,1)S(1)}, u32[]{:S(2)}, u32[]{:S(2)}) collective-permute-start(bf16[2,10,128,128]{3,2,1,0:T(8,128)(2,1)S(1)} %get-tuple-element.32.refs_3_.refs_1_), channel_id=1, source_target_pairs={{8,16},{9,17},{10,18},{11,19},{12,20},{13,21},{14,22},{15,23}} | collective-permute-start | bytes 1966088 | tf_op jit(solution)/shard_map/ppermute | solution.py:202
  73.9 16.5 %collective-permute-start.13 = (bf16[2,10,256,128]{3,2,1,0:T(8,128)(2,1)S(1)}, bf16[2,10,256,128]{3,2,1,0:T(8,128)(2,1)S(1)}, u32[]{:S(2)}, u32[]{:S(2)}) collective-permute-start(bf16[2,10,256,128]{3,2,1,0:T(8,128)(2,1)S(1)} %collective-permute-done.12.refs_10_.refs_4_), channel_id=1, source_target_pairs={{16,24},{17,25},{18,26},{19,27},{20,28},{21,29},{22,30},{23,31}} | collective-permute-start | bytes 3932168 | tf_op jit(solution)/shard_map/ppermute | solution.py:203
  74.6 8.0 %collective-permute-start.11 = (bf16[2,10,128,128]{3,2,1,0:T(8,128)(2,1)S(1)}, bf16[2,10,128,128]{3,2,1,0:T(8,128)(2,1)S(1)}, u32[]{:S(2)}, u32[]{:S(2)}) collective-permute-start(bf16[2,10,128,128]{3,2,1,0:T(8,128)(2,1)S(1)} %collective-permute-done.10.refs_8_.refs_6_), channel_id=1, source_target_pairs={{16,24},{17,25},{18,26},{19,27},{20,28},{21,29},{22,30},{23,31}} | collective-permute-start | bytes 1966088 | tf_op jit(solution)/shard_map/ppermute | solution.py:203
  75.3 15.0 %collective-permute-start.9 = (bf16[2,10,128,128]{3,2,1,0:T(8,128)(2,1)S(1)}, bf16[2,10,128,128]{3,2,1,0:T(8,128)(2,1)S(1)}, u32[]{:S(2)}, u32[]{:S(2)}) collective-permute-start(bf16[2,10,128,128]{3,2,1,0:T(8,128)(2,1)S(1)} %get-tuple-element.31.refs_15_.refs_7_), channel_id=1, source_target_pairs={{0,8},{16,24},{24,16},{1,9},{17,25},{25,17},{2,10},{18,26},{26,18}... | collective-permute-start | bytes 1966088 | tf_op jit(solution)/shard_map/ppermute | solution.py:190
  81.7 8.6 %collective-permute-start.15 = (bf16[2,10,128,128]{3,2,1,0:T(8,128)(2,1)S(1)}, bf16[2,10,128,128]{3,2,1,0:T(8,128)(2,1)S(1)}, u32[]{:S(2)}, u32[]{:S(2)}) collective-permute-start(bf16[2,10,128,128]{3,2,1,0:T(8,128)(2,1)S(1)} %collective-permute-done.14.refs_12_.refs_6_), channel_id=1, source_target_pairs={{16,24},{17,25},{18,26},{19,27},{20,28},{21,29},{22,30},{23,31}} | collective-permute-start | bytes 1966088 | tf_op jit(solution)/shard_map/ppermute | solution.py:203
  90.3 4.1 %slice-start.3 = ((s8[13107200]{0:T(1024)(128)(4,1)}), s8[524288]{0:T(1024)(128)(4,1)S(1)}, s32[]{:S(2)}) async-start(s8[13107200]{0:T(1024)(128)(4,1)} %bitcast.75), calls=%async_computation.3 | async-start | bytes 1048576
  102.9 57.2 %collective-permute-start.19 = (bf16[128,2560]{1,0:T(8,128)(2,1)S(1)}, bf16[128,2560]{1,0:T(8,128)(2,1)S(1)}, u32[]{:S(2)}, u32[]{:S(2)}) collective-permute-start(bf16[128,2560]{1,0:T(8,128)(2,1)S(1)} %fusion.11), channel_id=1, source_target_pairs={{4,0},{0,4},{5,1},{1,5},{6,2},{2,6},{7,3},{3,7},{12,8},{8,12},{13,... | collective-permute-start | bytes 1966088 | tf_op jit(solution)/shard_map/ppermute | solution.py:226
  103.5 58.5 %collective-permute-start.20 = (bf16[128,2560]{1,0:T(8,128)(2,1)S(1)}, bf16[128,2560]{1,0:T(8,128)(2,1)S(1)}, u32[]{:S(2)}, u32[]{:S(2)}) collective-permute-start(bf16[128,2560]{1,0:T(8,128)(2,1)S(1)} %fusion.17), channel_id=1, source_target_pairs={{4,0},{0,4},{5,1},{1,5},{6,2},{2,6},{7,3},{3,7},{12,8},{8,12},{13,... | collective-permute-start | bytes 1966088 | tf_op jit(solution)/shard_map/ppermute | solution.py:226
  105.0 40.6 %collective-permute-start.17 = (bf16[128,2560]{1,0:T(8,128)(2,1)S(1)}, bf16[128,2560]{1,0:T(8,128)(2,1)S(1)}, u32[]{:S(2)}, u32[]{:S(2)}) collective-permute-start(bf16[128,2560]{1,0:T(8,128)(2,1)S(1)} %fusion.8), channel_id=1, source_target_pairs={{4,0},{0,4},{5,1},{1,5},{6,2},{2,6},{7,3},{3,7},{12,8},{8,12},{13,... | collective-permute-start | bytes 1966088 | tf_op jit(solution)/shard_map/ppermute | solution.py:226
  105.5 54.2 %collective-permute-start.18 = (bf16[128,2560]{1,0:T(8,128)(2,1)S(1)}, bf16[128,2560]{1,0:T(8,128)(2,1)S(1)}, u32[]{:S(2)}, u32[]{:S(2)}) collective-permute-start(bf16[128,2560]{1,0:T(8,128)(2,1)S(1)} %fusion.14), channel_id=1, source_target_pairs={{4,0},{0,4},{5,1},{1,5},{6,2},{2,6},{7,3},{3,7},{12,8},{8,12},{13,... | collective-permute-start | bytes 1966088 | tf_op jit(solution)/shard_map/ppermute | solution.py:226
  119.2 26.5 %copy-start.2 = (bf16[1,1,256,5120]{3,2,1,0:T(8,128)(2,1)S(1)}, bf16[1,1,256,5120]{3,2,1,0:T(8,128)(2,1)}, u32[]{:S(2)}) copy-start(bf16[1,1,256,5120]{3,2,1,0:T(8,128)(2,1)} %param.16) | copy-start | bytes 7864324
